TPU v7x, 32 devices: a whole 2x2x4 slice. The times are simulated.
32 devices in a mesh: wide: 8 (over y, x, core), narrow: 4 (over z).
Axes of the slice: x: 2, y: 2, z: 4, core: 2. Of those that a mesh axis runs over, the one named last changes fastest.
Arguments:
- tokens: bfloat16 [8, 2048, 768], P('narrow', 'wide'), may hold values from -6 to 6
- cotangent: bfloat16 [8, 2048, 768], P('narrow', 'wide'), may hold values from -6 to 6
- selected: int32 [8, 2048], P('narrow'), may hold values from 0 to 1, as said below
- segments: int32 [8, 2048], P('narrow'), may hold values from 0 to 3, never falling along the last dimension, each value on 1 to 1024 neighbouring positions
- router_vector: bfloat16 [768], replicated, may hold values from -0.21875 to 0.21875
- project_routed: bfloat16 [768, 2304], replicated, may hold values from -0.21875 to 0.21875
- output_routed: bfloat16 [768, 768], replicated, may hold values from -0.875 to 0.875
- prenorm_routed: bfloat16 [768], replicated, may hold values from 0.5 to 1.5
- midnorm_routed: bfloat16 [768], replicated, may hold values from 0.5 to 1.5
- expand_routed: bfloat16 [768, 3072], P(None, 'narrow'), may hold values from -0.21875 to 0.21875
- reduce_routed: bfloat16 [3072, 768], P('narrow'), may hold values from -0.109375 to 0.109375
- project_dense: bfloat16 [768, 2304], replicated, may hold values from -0.21875 to 0.21875
- output_dense: bfloat16 [768, 768], replicated, may hold values from -1.25 to 1.25
- prenorm_dense: bfloat16 [768], replicated, may hold values from 0.5 to 1.5
- midnorm_dense: bfloat16 [768], replicated, may hold values from 0.5 to 1.5
- expand_dense: bfloat16 [768, 3072], P(None, 'narrow'), may hold values from -0.21875 to 0.21875
- reduce_dense: bfloat16 [3072, 768], P('narrow'), may hold values from -0.109375 to 0.109375
Outputs:
- activations: bfloat16 [8, 2048, 768], P('narrow', 'wide')
- tokens_gradient: float32 [8, 2048, 768], P('narrow', 'wide')
- router_gradient: float32 [768], P('wide')
- project_routed_gradient: float32 [768, 2304], P('wide')
- output_routed_gradient: float32 [768, 768], P('wide')
- prenorm_routed_gradient: float32 [768], P('wide')
- midnorm_routed_gradient: float32 [768], P('wide')
- expand_routed_gradient: float32 [768, 3072], P('wide', 'narrow')
- reduce_routed_gradient: float32 [3072, 768], P('narrow', 'wide')
- project_dense_gradient: float32 [768, 2304], P('wide')
- output_dense_gradient: float32 [768, 768], P('wide')
- prenorm_dense_gradient: float32 [768], P('wide')
- midnorm_dense_gradient: float32 [768], P('wide')
- expand_dense_gradient: float32 [768, 3072], P('wide', 'narrow')
- reduce_dense_gradient: float32 [3072, 768], P('narrow', 'wide')
Inputs may be any that keep to these rules, and one draw needn't show every extreme that they name: `selected`: every row holds exactly 256 ones. Of the 256 positions that one index of wide holds in a row, at most 64 are 1, and in every row some index of wide holds exactly 64.
All inputs are finite; a program needn't handle non-finite values.
Results may differ from a plain program's by a relative error of at most 0.024.
Values may be sent and summed in bfloat16 or wider, within the bound.
No kernel may reach another device: no remote copies, remote signals or barrier semaphores. Data moves between devices by JAX's collectives and lax.ppermute only.
A program may use at most 320 MiB of HBM per device.

v0:
```python
from functools import partial

import jax
import jax.numpy as jnp
from jax import lax
from jax.sharding import PartitionSpec as P

H = 12
HD = 64


EPSILON = 1e-06
NEGATIVE = -1e30
SCORE_SCALE = 0.125
PRECISE = lax.Precision.HIGHEST


def rms_gain(vector_in, gain_vector):
    return (
        vector_in
        * lax.rsqrt(jnp.mean(vector_in * vector_in, axis=-1, keepdims=True) + EPSILON)
        * gain_vector
    )


def smooth_gelu(hidden_pre):
    return jax.nn.gelu(hidden_pre, approximate=True)


def split_heads(matrix):
    return matrix.reshape(matrix.shape[0], H, HD)


def allow_mask(query_meta, key_meta):
    query_pos, query_seg, query_valid = query_meta
    key_pos, key_seg, key_valid = key_meta
    inside = (
        (key_pos[None, :] <= query_pos[:, None])
        & (key_seg[None, :] == query_seg[:, None])
        & key_valid[None, :]
    )
    return inside | jnp.logical_not(query_valid)[:, None]


def masked_scores(query_rows, key_rows, allowed):
    raw_scores = (
        jnp.einsum(
            "qhd,khd->hqk",
            split_heads(query_rows),
            split_heads(key_rows),
            preferred_element_type=jnp.float32,
        )
        * SCORE_SCALE
    )
    return jnp.where(allowed[None], raw_scores, NEGATIVE)


def attend_sequence(inputs_seq):
    query_rows, key_rows, value_rows = (inputs_seq[0], inputs_seq[1], inputs_seq[2])
    allowed = allow_mask(inputs_seq[3:6], inputs_seq[6:9])
    scores = masked_scores(query_rows, key_rows, allowed)
    largest = jnp.max(scores, axis=-1, keepdims=True)
    summed = jnp.sum(jnp.exp(scores - largest), axis=-1, keepdims=True)
    log_total = largest + jnp.log(summed)
    weights_soft = jnp.exp(scores - log_total).astype(jnp.bfloat16)
    attended = jnp.einsum(
        "hqk,khd->qhd", weights_soft, split_heads(value_rows), preferred_element_type=jnp.float32
    )
    return (attended.reshape(query_rows.shape[0], -1).astype(jnp.bfloat16), log_total[..., 0])


def query_side(inputs_seq, with_keys):
    query_rows, key_rows, value_rows, grad_rows, log_total = (
        inputs_seq[0],
        inputs_seq[1],
        inputs_seq[2],
        inputs_seq[3],
        inputs_seq[4],
    )
    allowed = allow_mask(inputs_seq[5:8], inputs_seq[8:11])
    softmax = jnp.exp(masked_scores(query_rows, key_rows, allowed) - log_total[..., None])
    grad_soft = jnp.einsum(
        "qhd,khd->hqk",
        split_heads(grad_rows),
        split_heads(value_rows),
        preferred_element_type=jnp.float32,
    )
    row_dot = jnp.sum(softmax * grad_soft, axis=-1)
    grad_scores = (softmax * (grad_soft - row_dot[..., None])).astype(jnp.bfloat16)
    query_grad = (
        jnp.einsum(
            "hqk,khd->qhd", grad_scores, split_heads(key_rows), preferred_element_type=jnp.float32
        )
        * SCORE_SCALE
    )
    query_grad = query_grad.reshape(query_rows.shape[0], -1)
    key_grad = (
        jnp.einsum(
            "hqk,qhd->khd", grad_scores, split_heads(query_rows), preferred_element_type=jnp.float32
        )
        * SCORE_SCALE
    )
    value_grad = jnp.einsum(
        "hqk,qhd->khd",
        softmax.astype(jnp.bfloat16),
        split_heads(grad_rows),
        preferred_element_type=jnp.float32,
    )
    return (
        query_grad,
        key_grad.reshape(key_rows.shape[0], -1),
        value_grad.reshape(key_rows.shape[0], -1),
    )


def mlp_forward(rows_in, expand_part, reduce_part):
    gathered = lax.all_gather(rows_in, "narrow", axis=0, tiled=True)
    hidden_pre = jnp.dot(gathered, expand_part, preferred_element_type=jnp.float32)
    hidden = smooth_gelu(hidden_pre).astype(jnp.bfloat16)
    partial_sum = jnp.dot(hidden, reduce_part, preferred_element_type=jnp.float32)
    reduced = lax.psum_scatter(
        partial_sum.astype(jnp.bfloat16), "narrow", scatter_dimension=0, tiled=True
    ).astype(jnp.float32)
    kept = (gathered, hidden_pre, hidden, expand_part, reduce_part)
    return (reduced, kept)


def mlp_backward(grad_rows, kept):
    rows_used, hidden_pre, hidden, expand_use, reduce_use = kept
    grad_low = grad_rows.astype(jnp.bfloat16)
    grad_low = lax.all_gather(grad_low, "narrow", axis=0, tiled=True)
    grad_hidden = jnp.dot(grad_low, reduce_use.T, preferred_element_type=jnp.float32)
    grad_pre = jax.vjp(smooth_gelu, hidden_pre)[1](grad_hidden)[0].astype(jnp.bfloat16)
    reduce_grad = jnp.dot(hidden.T, grad_low, preferred_element_type=jnp.float32)
    expand_grad = jnp.dot(rows_used.T, grad_pre, preferred_element_type=jnp.float32)
    grad_in = jnp.dot(grad_pre, expand_use.T, preferred_element_type=jnp.float32)
    grad_in = lax.psum_scatter(
        grad_in.astype(jnp.bfloat16), "narrow", scatter_dimension=0, tiled=True
    ).astype(jnp.float32)
    return (grad_in, expand_grad, reduce_grad)


def block_forward(rows_in, weights, query_meta, key_meta):
    project, output, prenorm, midnorm, expand_part, reduce_part = weights
    seq_count, row_count, model_width = rows_in.shape
    normed = rms_gain(rows_in, prenorm.astype(jnp.float32)).astype(jnp.bfloat16)
    projected = jnp.dot(
        normed.reshape(-1, model_width), project, preferred_element_type=jnp.float32
    ).astype(jnp.bfloat16)
    projected = projected.reshape(seq_count, row_count, 3 * model_width)
    queries = projected[..., :model_width]
    keys_own = projected[..., model_width : 2 * model_width]
    values_own = projected[..., 2 * model_width :]
    key_rows, value_rows = (
        lax.all_gather(keys_own, "wide", axis=1, tiled=True),
        lax.all_gather(values_own, "wide", axis=1, tiled=True),
    )
    attended, log_total = lax.map(
        attend_sequence, (queries, key_rows, value_rows) + query_meta + key_meta
    )
    branch = jnp.dot(
        attended.reshape(-1, model_width), output, preferred_element_type=jnp.float32
    ).reshape(seq_count, row_count, model_width)
    middle = rows_in + branch
    normed_mid = rms_gain(middle, midnorm.astype(jnp.float32)).astype(jnp.bfloat16)
    reduced, mlp_kept = mlp_forward(normed_mid.reshape(-1, model_width), expand_part, reduce_part)
    delta = branch + reduced.reshape(seq_count, row_count, model_width)
    kept = (
        rows_in,
        normed,
        queries,
        keys_own,
        values_own,
        key_rows,
        value_rows,
        attended,
        log_total,
        middle,
        mlp_kept,
    )
    return (delta, kept)


def block_backward(grad_delta, kept, weights, query_meta, key_meta):
    project, output, prenorm, midnorm, expand_part, reduce_part = weights
    (
        rows_in,
        normed,
        queries,
        keys_own,
        values_own,
        key_rows,
        value_rows,
        attended,
        log_total,
        middle,
        mlp_kept,
    ) = kept
    seq_count, row_count, model_width = rows_in.shape
    grad_normed_mid, expand_grad, reduce_grad = mlp_backward(
        grad_delta.reshape(-1, model_width), mlp_kept
    )
    mid_pull = jax.vjp(rms_gain, middle, midnorm.astype(jnp.float32))[1]
    grad_middle, midnorm_grad = mid_pull(grad_normed_mid.reshape(seq_count, row_count, model_width))
    grad_branch = (grad_delta + grad_middle).astype(jnp.bfloat16).reshape(-1, model_width)
    output_grad = jnp.dot(
        attended.reshape(-1, model_width).T, grad_branch, preferred_element_type=jnp.float32
    )
    grad_attended = (
        jnp.dot(grad_branch, output.T, preferred_element_type=jnp.float32)
        .astype(jnp.bfloat16)
        .reshape(seq_count, row_count, model_width)
    )
    query_grad, key_terms, value_terms = lax.map(
        partial(query_side, with_keys=True),
        (queries, key_rows, value_rows, grad_attended, log_total) + query_meta + key_meta,
    )
    key_grad, value_grad = (
        lax.psum_scatter(
            key_terms.astype(jnp.bfloat16), "wide", scatter_dimension=1, tiled=True
        ).astype(jnp.float32),
        lax.psum_scatter(
            value_terms.astype(jnp.bfloat16), "wide", scatter_dimension=1, tiled=True
        ).astype(jnp.float32),
    )
    grad_projected = (
        jnp.concatenate([query_grad, key_grad, value_grad], axis=-1)
        .astype(jnp.bfloat16)
        .reshape(-1, 3 * model_width)
    )
    project_grad = jnp.dot(
        normed.reshape(-1, model_width).T, grad_projected, preferred_element_type=jnp.float32
    )
    grad_normed = jnp.dot(grad_projected, project.T, preferred_element_type=jnp.float32).reshape(
        seq_count, row_count, model_width
    )
    first_pull = jax.vjp(rms_gain, rows_in, prenorm.astype(jnp.float32))[1]
    grad_first, prenorm_grad = first_pull(grad_normed)
    return (
        grad_middle + grad_first,
        (project_grad, output_grad, prenorm_grad, midnorm_grad, expand_grad, reduce_grad),
    )


def on_device(
    tokens,
    cotangent,
    selected,
    segments,
    router_vector,
    project_routed,
    output_routed,
    prenorm_routed,
    midnorm_routed,
    expand_routed,
    reduce_routed,
    project_dense,
    output_dense,
    prenorm_dense,
    midnorm_dense,
    expand_dense,
    reduce_dense,
):
    seq_count, span_rows, model_width = tokens.shape
    row_length = selected.shape[1]
    wide_count = lax.axis_size("wide")
    here = lax.axis_index("wide")
    slot_count = span_rows // 4
    grouped = selected.reshape(seq_count, wide_count, span_rows)
    pick_rank = jnp.argsort(1 - grouped, axis=-1, stable=True)[..., :slot_count]
    picked_counts = jnp.sum(grouped, axis=-1)
    slot_index = jnp.arange(slot_count, dtype=jnp.int32)
    valid_all = (slot_index[None, None, :] < picked_counts[..., None]).reshape(seq_count, -1)
    offsets = jnp.arange(wide_count, dtype=jnp.int32) * span_rows
    pos_all = (pick_rank + offsets[None, :, None]).reshape(seq_count, -1)
    seg_all = jnp.take_along_axis(segments, pos_all, axis=1)
    key_meta_routed = (pos_all, seg_all, valid_all)
    query_meta_routed = tuple(
        (
            lax.dynamic_slice_in_dim(meta_part, here * slot_count, slot_count, 1)
            for meta_part in key_meta_routed
        )
    )
    local_picks = query_meta_routed[0] - here * span_rows
    one_hot = local_picks[..., None] == jnp.arange(span_rows, dtype=jnp.int32)[None, None, :]
    placed = (one_hot & query_meta_routed[2][..., None]).astype(jnp.float32)
    picked = jnp.einsum(
        "scp,spd->scd", one_hot.astype(jnp.bfloat16), tokens, preferred_element_type=jnp.float32
    )
    logits = jnp.dot(
        tokens.reshape(-1, model_width), router_vector, preferred_element_type=jnp.float32
    ).reshape(seq_count, span_rows)
    gate = jnp.einsum("scp,sp->sc", placed, logits, precision=PRECISE)
    weights_routed = (
        project_routed,
        output_routed,
        prenorm_routed,
        midnorm_routed,
        expand_routed,
        reduce_routed,
    )
    weights_dense = (
        project_dense,
        output_dense,
        prenorm_dense,
        midnorm_dense,
        expand_dense,
        reduce_dense,
    )
    routed_delta, kept_routed = block_forward(
        picked, weights_routed, query_meta_routed, key_meta_routed
    )
    lifted = jnp.einsum("scp,scd->spd", placed, gate[..., None] * routed_delta, precision=PRECISE)
    mixed = tokens.astype(jnp.float32) + lifted
    own_positions = jnp.broadcast_to(
        here * span_rows + jnp.arange(span_rows, dtype=jnp.int32)[None, :], (seq_count, span_rows)
    )
    own_segments = lax.dynamic_slice_in_dim(segments, here * span_rows, span_rows, 1)
    query_meta_dense = (own_positions, own_segments, jnp.ones((seq_count, span_rows), dtype=bool))
    all_positions = jnp.broadcast_to(
        jnp.arange(row_length, dtype=jnp.int32)[None, :], (seq_count, row_length)
    )
    key_meta_dense = (all_positions, segments, jnp.ones((seq_count, row_length), dtype=bool))
    dense_delta, kept_dense = block_forward(mixed, weights_dense, query_meta_dense, key_meta_dense)
    activations = (mixed + dense_delta).astype(jnp.bfloat16)
    grad_output = cotangent.astype(jnp.float32)
    grad_dense_in, grads_dense = block_backward(
        grad_output, kept_dense, weights_dense, query_meta_dense, key_meta_dense
    )
    grad_mixed = grad_output + grad_dense_in
    grad_lifted = jnp.einsum("scp,spd->scd", placed, grad_mixed, precision=PRECISE)
    grad_routed_delta = gate[..., None] * grad_lifted
    grad_gate = jnp.sum(grad_lifted * routed_delta, axis=-1)
    grad_picked, grads_routed = block_backward(
        grad_routed_delta, kept_routed, weights_routed, query_meta_routed, key_meta_routed
    )
    grad_logits = jnp.einsum("scp,sc->sp", placed, grad_gate, precision=PRECISE)
    tokens_gradient = (
        grad_mixed
        + jnp.einsum("scp,scd->spd", placed, grad_picked, precision=PRECISE)
        + grad_logits[..., None] * router_vector.astype(jnp.float32)
    )
    router_grad = jnp.dot(
        grad_logits.reshape(1, -1),
        tokens.reshape(-1, model_width).astype(jnp.float32),
        precision=PRECISE,
    )[0]
    shares = (
        lax.psum_scatter(
            grads_routed[0].astype(jnp.bfloat16), "wide", scatter_dimension=0, tiled=True
        ).astype(jnp.float32),
        lax.psum_scatter(
            grads_routed[1].astype(jnp.bfloat16), "wide", scatter_dimension=0, tiled=True
        ).astype(jnp.float32),
        lax.psum_scatter(
            grads_dense[0].astype(jnp.bfloat16), "wide", scatter_dimension=0, tiled=True
        ).astype(jnp.float32),
        lax.psum_scatter(
            grads_dense[1].astype(jnp.bfloat16), "wide", scatter_dimension=0, tiled=True
        ).astype(jnp.float32),
        lax.psum_scatter(
            grads_routed[2].astype(jnp.bfloat16), "wide", scatter_dimension=0, tiled=True
        ).astype(jnp.float32),
        lax.psum_scatter(
            grads_routed[3].astype(jnp.bfloat16), "wide", scatter_dimension=0, tiled=True
        ).astype(jnp.float32),
        lax.psum_scatter(
            grads_dense[2].astype(jnp.bfloat16), "wide", scatter_dimension=0, tiled=True
        ).astype(jnp.float32),
        lax.psum_scatter(
            grads_dense[3].astype(jnp.bfloat16), "wide", scatter_dimension=0, tiled=True
        ).astype(jnp.float32),
        lax.psum_scatter(
            router_grad.astype(jnp.bfloat16), "wide", scatter_dimension=0, tiled=True
        ).astype(jnp.float32),
    )
    summed = (
        lax.psum(shares[0].astype(jnp.bfloat16), "narrow").astype(jnp.float32),
        lax.psum(shares[1].astype(jnp.bfloat16), "narrow").astype(jnp.float32),
        lax.psum(shares[2].astype(jnp.bfloat16), "narrow").astype(jnp.float32),
        lax.psum(shares[3].astype(jnp.bfloat16), "narrow").astype(jnp.float32),
        lax.psum(shares[4].astype(jnp.bfloat16), "narrow").astype(jnp.float32),
        lax.psum(shares[5].astype(jnp.bfloat16), "narrow").astype(jnp.float32),
        lax.psum(shares[6].astype(jnp.bfloat16), "narrow").astype(jnp.float32),
        lax.psum(shares[7].astype(jnp.bfloat16), "narrow").astype(jnp.float32),
        lax.psum(shares[8].astype(jnp.bfloat16), "narrow").astype(jnp.float32),
    )
    ffn_grads = (grads_routed[4], grads_dense[4], grads_routed[5], grads_dense[5])
    ffn_summed = (
        lax.psum_scatter(
            ffn_grads[0].astype(jnp.bfloat16), "wide", scatter_dimension=0, tiled=True
        ).astype(jnp.float32),
        lax.psum_scatter(
            ffn_grads[1].astype(jnp.bfloat16), "wide", scatter_dimension=0, tiled=True
        ).astype(jnp.float32),
        lax.psum_scatter(
            ffn_grads[2].astype(jnp.bfloat16), "wide", scatter_dimension=1, tiled=True
        ).astype(jnp.float32),
        lax.psum_scatter(
            ffn_grads[3].astype(jnp.bfloat16), "wide", scatter_dimension=1, tiled=True
        ).astype(jnp.float32),
    )
    return (
        activations,
        tokens_gradient,
        summed[8],
        summed[0],
        summed[1],
        summed[4],
        summed[5],
        ffn_summed[0],
        ffn_summed[2],
        summed[2],
        summed[3],
        summed[6],
        summed[7],
        ffn_summed[1],
        ffn_summed[3],
    )


def solution(mesh):
    return jax.shard_map(
        on_device,
        mesh=mesh,
        in_specs=(
            P("narrow", "wide", None),
            P("narrow", "wide", None),
            P("narrow", None),
            P("narrow", None),
            P(),
            P(),
            P(),
            P(),
            P(),
            P(None, "narrow"),
            P("narrow", None),
            P(),
            P(),
            P(),
            P(),
            P(None, "narrow"),
            P("narrow", None),
        ),
        out_specs=(
            P("narrow", "wide", None),
            P("narrow", "wide", None),
            P("wide"),
            P("wide", None),
            P("wide", None),
            P("wide"),
            P("wide"),
            P("wide", "narrow"),
            P("narrow", "wide"),
            P("wide", None),
            P("wide", None),
            P("wide"),
            P("wide"),
            P("wide", "narrow"),
            P("narrow", "wide"),
        ),
        check_vma=False,
    )
```

profile of v0, /device:TPU:0, one launch (start us, length us, event | category | flops | bytes accessed | tf_op | source)
XLA Modules:
  0.0 1554.5 jit_solution(14536372676720072839)
XLA Ops:
  35.9 13.7 gather_fusion
  55.4 24.8 %all-gather.7.cloned.1.call-done = bf16[2,512,768]{2,0,1:T(2,128)(2,1)} async-done(((bf16[2,64,768]{2,0,1:T(2,128)(2,1)}), bf16[2,512,768]{2,0,1:T(2,128)(2,1)}) %all-gather.7.cloned.1.call-update) | async-done | bytes 1572880 | tf_op jit(solution)/shard_map/all_gather | solution.py:156
  85.2 21.3 %while.56 = (s32[]{:T(128)}, bf16[2,64,768]{1,2,0:T(8,128)(2,1)}, f32[2,12,64]{2,1,0:T(8,128)}, bf16[2,512,768]{1,2,0:T(8,128)(2,1)}, s32[2,512]{1,0:T(2,128)}, ...) while((s32[]{:T(128)}, bf16[2,64,768]{1,2,0:T(8,128)(2,1)}, ...), condition=%wide.region_6.7_spmd, body=%wide.region_3.0_spmd.sunk | while | flops 103628096 | bytes 12693005 | solution.py:158
  110.1 19.5 %all_gather.26 = bf16[512,768]{1,0:T(8,128)(2,1)S(1)} all-gather(bf16[128,768]{1,0:T(8,128)(2,1)S(1)} %bitcast.386), channel_id=1, replica_groups=mesh['wide'=8,'narrow'=4] {'narrow'}, dimensions={0}, use_global_device_ids=true | all-gather | bytes 983040 | tf_op jit(solution)/shard_map/all_gather | solution.py:117
  139.3 17.1 %reduce-scatter.17.cloned.1.call-done = bf16[128,768]{1,0:T(8,128)(2,1)} async-done(((bf16[512,768]{1,0:T(8,128)(2,1)}), bf16[128,768]{1,0:T(8,128)(2,1)}) %reduce-scatter.17.cloned.1.call-update) | async-done | bytes 196624 | tf_op jit(solution)/shard_map/reduce_scatter | solution.py:121
  174.4 37.8 %all-gather.13.cloned.1.call-done = bf16[2,2048,768]{1,2,0:T(8,128)(2,1)} async-done(((bf16[2,256,768]{1,2,0:T(8,128)(2,1)}), bf16[2,2048,768]{1,2,0:T(8,128)(2,1)}) %all-gather.13.cloned.1.call-update) | async-done | bytes 6291472 | tf_op jit(solution)/shard_map/all_gather | solution.py:155
  212.2 49.0 %all-gather.11.cloned.1.call-done = bf16[2,2048,768]{1,2,0:T(8,128)(2,1)} async-done(((bf16[2,256,768]{1,2,0:T(8,128)(2,1)}), bf16[2,2048,768]{1,2,0:T(8,128)(2,1)}) %all-gather.11.cloned.1.call-update) | async-done | bytes 6291472 | tf_op jit(solution)/shard_map/all_gather | solution.py:156
  263.0 82.0 %while.57 = (s32[]{:T(128)}, bf16[2,256,768]{1,2,0:T(8,128)(2,1)}, f32[2,12,256]{2,1,0:T(8,128)}, bf16[2,2048,768]{1,2,0:T(8,128)(2,1)}, s32[2,2048]{1,0:T(2,128...) while((s32[]{:T(128)}, bf16[2,256,768]{1,2,0:T(8,128)(2,1)}, ...), condition=%wide.region_13.14_spmd, body=%wide.region_10.13_spmd.sunk | while | flops 1681585152 | bytes 99195064 | solution.py:158
  269.4 10.7 fusion.221
  280.1 11.7 exponential_reduce_fusion.5
  291.8 11.6 fusion.222
  310.6 10.7 fusion.221
  321.3 11.5 exponential_reduce_fusion.5
  332.9 11.4 fusion.222
  358.9 56.1 %all-gather.15.cloned.1.call-done = bf16[2048,768]{1,0:T(8,128)(2,1)} async-done(((bf16[512,768]{1,0:T(8,128)(2,1)}), bf16[2048,768]{1,0:T(8,128)(2,1)}) %all-gather.15.cloned.1.call-update) | async-done | bytes 3145744 | tf_op jit(solution)/shard_map/all_gather | solution.py:117
  415.0 11.1 fusion.30
  431.8 59.0 %reduce-scatter.21.cloned.1.call-done = bf16[512,768]{1,0:T(8,128)(2,1)} async-done(((bf16[2048,768]{1,0:T(8,128)(2,1)}), bf16[512,768]{1,0:T(8,128)(2,1)}) %reduce-scatter.21.cloned.1.call-update) | async-done | bytes 786448 | tf_op jit(solution)/shard_map/reduce_scatter | solution.py:137
  497.5 252.6 %while.58 = (s32[]{:T(128)}, bf16[2,256,768]{2,1,0:T(8,128)(2,1)}, bf16[2,2048,768]{2,1,0:T(8,128)(2,1)}, bf16[2,2048,768]{2,1,0:T(8,128)(2,1)}, bf16[2,2048,768...) while((s32[]{:T(128)}, bf16[2,256,768]{2,1,0:T(8,128)(2,1)}, ...), condition=%wide.region_20.21_spmd, body=%wide.region_18.20_spmd.sunk | while | flops 4126012416 | bytes 307554688 | solution.py:214
  527.7 10.1 fusion.233
  537.9 12.6 fusion.234
  555.2 19.9 %multiply_reduce_fusion.13 = (f32[12,256]{1,0:T(8,128)}, f32[12,256,2048]{2,1,0:T(8,128)}) fusion(f32[12,256,2048]{2,1,0:T(8,128)} %fusion.233, f32[12,256]{1,0:T(8,128)} %dynamic-slice_bitcast_fusion.4, pred[256,2048]{1,0:T(8,128)(4,1)} %copy-done.7, bf16[256,12,64]{0,2,1:T(8,128)(2,1)} %bitcast.362, bf16[2048,12,64]{0,2,1:T(8,128)(2,1)} %bitcast.344), kind=kOutput, calls=%fused_computation.22.clone.1 | convolution fusion | flops 836760576 | bytes 54419456 | tf_op jit(solution)/shard_map/while/body/eval_jaxpr/qhd,khd->hqk/dot_general | solution.py:82
  575.0 22.3 %multiply_convert_fusion.15 = bf16[12,256,2048]{2,1,0:T(8,128)(2,1)} fusion(f32[12,256,2048]{2,1,0:T(8,128)} %get-tuple-element.1097, f32[12,256,2048]{2,1,0:T(8,128)} %fusion.233, f32[12,256]{1,0:T(8,128)} %get-tuple-element.1098, f32[12,256]{1,0:T(8,128)} %dynamic-slice_bitcast_fusion.4, pred[256,2048]{1,0:T(8,128)(4,1)} %copy-done.7), kind=kLoop, calls=%fused_computation.21.clone.1 | loop fusion | flops 37748736 | bytes 63463424 | tf_op jit(solution)/shard_map/while/body/eval_jaxpr/convert_element_type | solution.py:89
  597.4 9.3 convolution_multiply_fusion.8
  606.7 8.6 convolution_multiply_fusion.9
  647.9 10.1 fusion.233
  658.1 12.6 fusion.234
  675.4 19.9 %multiply_reduce_fusion.13 = (f32[12,256]{1,0:T(8,128)}, f32[12,256,2048]{2,1,0:T(8,128)}) fusion(f32[12,256,2048]{2,1,0:T(8,128)} %fusion.233, f32[12,256]{1,0:T(8,128)} %dynamic-slice_bitcast_fusion.4, pred[256,2048]{1,0:T(8,128)(4,1)} %copy-done.7, bf16[256,12,64]{0,2,1:T(8,128)(2,1)} %bitcast.362, bf16[2048,12,64]{0,2,1:T(8,128)(2,1)} %bitcast.344), kind=kOutput, calls=%fused_computation.22.clone.1 | convolution fusion | flops 836760576 | bytes 54419456 | tf_op jit(solution)/shard_map/while/body/eval_jaxpr/qhd,khd->hqk/dot_general | solution.py:82
  695.2 22.3 %multiply_convert_fusion.15 = bf16[12,256,2048]{2,1,0:T(8,128)(2,1)} fusion(f32[12,256,2048]{2,1,0:T(8,128)} %get-tuple-element.1097, f32[12,256,2048]{2,1,0:T(8,128)} %fusion.233, f32[12,256]{1,0:T(8,128)} %get-tuple-element.1098, f32[12,256]{1,0:T(8,128)} %dynamic-slice_bitcast_fusion.4, pred[256,2048]{1,0:T(8,128)(4,1)} %copy-done.7), kind=kLoop, calls=%fused_computation.21.clone.1 | loop fusion | flops 37748736 | bytes 63463424 | tf_op jit(solution)/shard_map/while/body/eval_jaxpr/convert_element_type | solution.py:89
  717.6 9.3 convolution_multiply_fusion.8
  751.0 8.6 convolution_convert_fusion.4
  759.6 52.5 %reduce-scatter.25.cloned.1.call-done = bf16[2,256,768]{2,1,0:T(8,128)(2,1)} async-done(((bf16[2,2048,768]{2,1,0:T(8,128)(2,1)}), bf16[2,256,768]{2,1,0:T(8,128)(2,1)}) %reduce-scatter.25.cloned.1.call-update) | async-done | bytes 786448 | tf_op jit(solution)/shard_map/reduce_scatter | solution.py:222
  812.1 65.5 %reduce-scatter.23.cloned.1.call-done = bf16[2,256,768]{2,1,0:T(8,128)(2,1)} async-done(((bf16[2,2048,768]{2,1,0:T(8,128)(2,1)}), bf16[2,256,768]{2,1,0:T(8,128)(2,1)}) %reduce-scatter.23.cloned.1.call-update) | async-done | bytes 786448 | tf_op jit(solution)/shard_map/reduce_scatter | solution.py:219
  884.1 55.9 %reduce-scatter.19.cloned.1.call-done = bf16[512,768]{1,0:T(8,128)(2,1)} async-done(((bf16[2048,768]{1,0:T(8,128)(2,1)}), bf16[512,768]{1,0:T(8,128)(2,1)}) %reduce-scatter.19.cloned.1.call-update) | async-done | bytes 786448 | tf_op jit(solution)/shard_map/reduce_scatter | solution.py:121
  947.0 18.3 %all_gather.31 = bf16[512,768]{1,0:T(8,128)(2,1)S(1)} all-gather(bf16[128,768]{1,0:T(8,128)(2,1)S(1)} %bitcast.388), channel_id=1, replica_groups=mesh['wide'=8,'narrow'=4] {'narrow'}, dimensions={0}, use_global_device_ids=true | all-gather | bytes 983040 | tf_op jit(solution)/shard_map/all_gather | solution.py:131
  969.6 23.0 %reduce-scatter.27.cloned.1.call-done = bf16[128,768]{1,0:T(8,128)(2,1)} async-done(((bf16[512,768]{1,0:T(8,128)(2,1)}), bf16[128,768]{1,0:T(8,128)(2,1)}) %reduce-scatter.27.cloned.1.call-update) | async-done | bytes 196624 | tf_op jit(solution)/shard_map/reduce_scatter | solution.py:137
  998.6 58.2 %while.59 = (s32[]{:T(128)}, bf16[2,64,768]{2,1,0:T(8,128)(2,1)}, bf16[2,512,768]{2,1,0:T(8,128)(2,1)}, bf16[2,512,768]{2,1,0:T(8,128)(2,1)}, bf16[2,512,768]{1,...) while((s32[]{:T(128)}, bf16[2,64,768]{2,1,0:T(8,128)(2,1)}, ...), condition=%wide.region_28.29_spmd, body=%wide.region_26.28_spmd.sunk | while | flops 256245056 | bytes 34142720 | solution.py:214
  1084.1 10.6 reduce-scatter.31.cloned.1.call-done
  1094.7 41.6 %reduce-scatter.29.cloned.1.call-done = bf16[2,64,768]{2,1,0:T(8,128)(2,1)} async-done(((bf16[2,512,768]{2,1,0:T(8,128)(2,1)}), bf16[2,64,768]{2,1,0:T(8,128)(2,1)}) %reduce-scatter.29.cloned.1.call-update) | async-done | bytes 196624 | tf_op jit(solution)/shard_map/reduce_scatter | solution.py:219
  1150.0 26.1 %reduce-scatter.47.cloned.1.call-done = bf16[768,96]{0,1:T(8,128)(2,1)} async-done(((bf16[768,768]{0,1:T(8,128)(2,1)}), bf16[768,96]{0,1:T(8,128)(2,1)}) %reduce-scatter.47.cloned.1.call-update) | async-done | bytes 147472 | tf_op jit(solution)/shard_map/reduce_scatter | solution.py:399
  1177.8 38.6 %reduce-scatter.45.cloned.1.call-done = bf16[96,768]{1,0:T(8,128)(2,1)} async-done(((bf16[768,768]{1,0:T(8,128)(2,1)}), bf16[96,768]{1,0:T(8,128)(2,1)}) %reduce-scatter.45.cloned.1.call-update) | async-done | bytes 147472 | tf_op jit(solution)/shard_map/reduce_scatter | solution.py:393
  1218.0 38.2 %reduce-scatter.43.cloned.1.call-done = bf16[96,768]{1,0:T(8,128)(2,1)} async-done(((bf16[768,768]{1,0:T(8,128)(2,1)}), bf16[96,768]{1,0:T(8,128)(2,1)}) %reduce-scatter.43.cloned.1.call-update) | async-done | bytes 147472 | tf_op jit(solution)/shard_map/reduce_scatter | solution.py:358
  1256.3 40.9 %reduce-scatter.35.cloned.1.call-done = bf16[96,768]{1,0:T(8,128)(2,1)} async-done(((bf16[768,768]{1,0:T(8,128)(2,1)}), bf16[96,768]{1,0:T(8,128)(2,1)}) %reduce-scatter.35.cloned.1.call-update) | async-done | bytes 147472 | tf_op jit(solution)/shard_map/reduce_scatter | solution.py:352
  1297.2 51.4 %reduce-scatter.41.cloned.1.call-done = bf16[96,2304]{1,0:T(8,128)(2,1)} async-done(((bf16[768,2304]{1,0:T(8,128)(2,1)}), bf16[96,2304]{1,0:T(8,128)(2,1)}) %reduce-scatter.41.cloned.1.call-update) | async-done | bytes 442384 | tf_op jit(solution)/shard_map/reduce_scatter | solution.py:355
  1348.7 51.6 %reduce-scatter.33.cloned.1.call-done = bf16[96,2304]{1,0:T(8,128)(2,1)} async-done(((bf16[768,2304]{1,0:T(8,128)(2,1)}), bf16[96,2304]{1,0:T(8,128)(2,1)}) %reduce-scatter.33.cloned.1.call-update) | async-done | bytes 442384 | tf_op jit(solution)/shard_map/reduce_scatter | solution.py:349
  1403.4 36.9 %reduce-scatter.39.cloned.1.call-done = bf16[768,96]{0,1:T(8,128)(2,1)} async-done(((bf16[768,768]{0,1:T(8,128)(2,1)}), bf16[768,96]{0,1:T(8,128)(2,1)}) %reduce-scatter.39.cloned.1.call-update) | async-done | bytes 147472 | tf_op jit(solution)/shard_map/reduce_scatter | solution.py:396
  1441.9 38.7 %reduce-scatter.37.cloned.1.call-done = bf16[96,768]{1,0:T(8,128)(2,1)} async-done(((bf16[768,768]{1,0:T(8,128)(2,1)}), bf16[96,768]{1,0:T(8,128)(2,1)}) %reduce-scatter.37.cloned.1.call-update) | async-done | bytes 147472 | tf_op jit(solution)/shard_map/reduce_scatter | solution.py:390
  1487.2 24.1 %all-reduce.5 = (bf16[768]{0:T(1024)(128)(2,1)}, bf16[768]{0:T(1024)(128)(2,1)}, bf16[768]{0:T(1024)(128)(2,1)}, bf16[768]{0:T(1024)(128)(2,1)}, bf16[768]{0:T(1024)(128)(2,1)}) all-reduce(bf16[768]{0:T(1024)(128)(2,1)} %convolution_reduce_fusion, ...), channel_id=10, replica_groups=mesh['wide'=8,'narrow'=4] {'wide'}, use_global_device_ids=true, to_apply=%region_33.34.clone | all-reduce | flops 3840 | bytes 15360
  1517.6 13.1 all-reduce.6
  (508 shorter events, 377.1 us)
Async XLA Ops:
  7.2 153.1 %copy-start = (bf16[768,2304]{1,0:T(8,128)(2,1)S(1)}, bf16[768,2304]{1,0:T(8,128)(2,1)}, u32[]{:S(2)}) copy-start(bf16[768,2304]{1,0:T(8,128)(2,1)} %param.36) | copy-start | bytes 10616836
  9.9 42.9 %all-gather.9.cloned.1.call-start = ((), (), s32[]{:S(2)}) async-start(), calls=%async_computation.17 | async-start | bytes 1769472 | tf_op jit(solution)/shard_map/all_gather | solution.py:155
  22.7 13.3 copy-start.1
  23.5 56.7 %all-gather.7.cloned.1.call-start = ((), (), s32[]{:S(2)}) async-start(), calls=%async_computation.16 | async-start | bytes 1769472 | tf_op jit(solution)/shard_map/all_gather | solution.py:156
  25.4 130.9 %reduce-scatter.17.cloned.1.call-start = ((), (), s32[]{:S(2)}) async-start(), calls=%async_computation.18 | async-start | bytes 983040 | tf_op jit(solution)/shard_map/reduce_scatter | solution.py:121
  106.5 24.0 %copy-start.83 = (bf16[768,768]{1,0:T(8,128)(2,1)S(1)}, bf16[768,768]{1,0:T(8,128)(2,1)}, u32[]{:S(2)}) copy-start(bf16[768,768]{1,0:T(8,128)(2,1)} %param.34) | copy-start | bytes 3538948
  134.4 77.8 %all-gather.13.cloned.1.call-start = ((), (), s32[]{:S(2)}) async-start(), calls=%async_computation.20 | async-start | bytes 7077888 | tf_op jit(solution)/shard_map/all_gather | solution.py:155
  166.1 95.1 %all-gather.11.cloned.1.call-start = ((), (), s32[]{:S(2)}) async-start(), calls=%async_computation.19 | async-start | bytes 7077888 | tf_op jit(solution)/shard_map/all_gather | solution.py:156
  168.5 182.9 %all-gather.17.cloned.1.call-start = ((), (), s32[]{:S(2)}) async-start(), calls=%async_computation.23 | async-start | bytes 3932160 | tf_op jit(solution)/shard_map/all_gather | solution.py:131
  169.2 245.8 %all-gather.15.cloned.1.call-start = ((), (), s32[]{:S(2)}) async-start(), calls=%async_computation.21 | async-start | bytes 3932160 | tf_op jit(solution)/shard_map/all_gather | solution.py:117
  351.3 139.5 %reduce-scatter.21.cloned.1.call-start = ((), (), s32[]{:S(2)}) async-start(), calls=%async_computation.24 | async-start | bytes 3932160 | tf_op jit(solution)/shard_map/reduce_scatter | solution.py:137
  415.0 12.7 copy-start.80
  431.8 380.4 %reduce-scatter.25.cloned.1.call-start = ((), (), s32[]{:S(2)}) async-start(), calls=%async_computation.26 | async-start | bytes 7077888 | tf_op jit(solution)/shard_map/reduce_scatter | solution.py:222
  521.0 16.9 %copy-start.7 = (pred[256,2048]{1,0:T(8,128)(4,1)}, pred[256,2048]{1,0:T(8,128)(4,1)S(1)}, u32[]{:S(2)}) copy-start(pred[256,2048]{1,0:T(8,128)(4,1)S(1)} %compare_and_fusion.5) | copy-start | bytes 1572868 | tf_op jit(solution)/shard_map/while
  575.0 22.3 %copy-start.3 = (bf16[1,2048,768]{1,2,0:T(8,128)(2,1)S(1)}, bf16[1,2048,768]{1,2,0:T(8,128)(2,1)}, u32[]{:S(2)}) copy-start(bf16[1,2048,768]{1,2,0:T(8,128)(2,1)} %copy-done.2) | copy-start | bytes 9437188 | tf_op jit(solution)/shard_map/while
  641.2 16.9 %copy-start.7 = (pred[256,2048]{1,0:T(8,128)(4,1)}, pred[256,2048]{1,0:T(8,128)(4,1)S(1)}, u32[]{:S(2)}) copy-start(pred[256,2048]{1,0:T(8,128)(4,1)S(1)} %compare_and_fusion.5) | copy-start | bytes 1572868 | tf_op jit(solution)/shard_map/while
  695.2 22.3 %copy-start.3 = (bf16[1,2048,768]{1,2,0:T(8,128)(2,1)S(1)}, bf16[1,2048,768]{1,2,0:T(8,128)(2,1)}, u32[]{:S(2)}) copy-start(bf16[1,2048,768]{1,2,0:T(8,128)(2,1)} %copy-done.2) | copy-start | bytes 9437188 | tf_op jit(solution)/shard_map/while
  750.2 127.5 %reduce-scatter.23.cloned.1.call-start = ((), (), s32[]{:S(2)}) async-start(), calls=%async_computation.25 | async-start | bytes 7077888 | tf_op jit(solution)/shard_map/reduce_scatter | solution.py:219
  750.9 189.2 %reduce-scatter.19.cloned.1.call-start = ((), (), s32[]{:S(2)}) async-start(), calls=%async_computation.22 | async-start | bytes 3932160 | tf_op jit(solution)/shard_map/reduce_scatter | solution.py:121
  759.5 118.1 %copy-start.57 = (f32[768]{0:T(1024)S(1)}, f32[768]{0:T(1024)}, u32[]{:S(2)}) copy-start(f32[768]{0:T(1024)} %convert_element_type.287) | copy-start | bytes 9220
  759.6 233.0 %reduce-scatter.27.cloned.1.call-start = ((), (), s32[]{:S(2)}) async-start(), calls=%async_computation.27 | async-start | bytes 983040 | tf_op jit(solution)/shard_map/reduce_scatter | solution.py:137
  877.6 62.4 %copy-start.49 = (f32[768]{0:T(1024)S(1)}, f32[768]{0:T(1024)}, u32[]{:S(2)}) copy-start(f32[768]{0:T(1024)} %convert_element_type.290) | copy-start | bytes 9220
  877.6 62.4 %copy-start.53 = (f32[2,256]{1,0:T(2,128)S(1)}, f32[2,256]{1,0:T(2,128)}, u32[]{:S(2)}) copy-start(f32[2,256]{1,0:T(2,128)} %copy-done.51) | copy-start | bytes 6148
  877.6 62.4 %copy-start.70 = (f32[2,256]{1,0:T(2,128)S(1)}, f32[2,256]{1,0:T(2,128)}, u32[]{:S(2)}) copy-start(f32[2,256]{1,0:T(2,128)} %copy-done.69) | copy-start | bytes 6148
  945.4 21.4 %copy-start.16 = (f32[2,256,768]{2,1,0:T(8,128)}, f32[2,256,768]{2,1,0:T(8,128)S(1)}, u32[]{:S(2)}) copy-start(f32[2,256,768]{2,1,0:T(8,128)S(1)} %get-tuple-element.737) | copy-start | bytes 4718596
  945.4 19.9 %copy-start.82 = (bf16[768,768]{1,0:T(8,128)(2,1)S(1)}, bf16[768,768]{1,0:T(8,128)(2,1)}, u32[]{:S(2)}) copy-start(bf16[768,768]{1,0:T(8,128)(2,1)} %param.35) | copy-start | bytes 3538948
  945.4 19.9 %copy-start.86 = (f32[512,768]{1,0:T(8,128)S(1)}, f32[512,768]{1,0:T(8,128)}, u32[]{:S(2)}) copy-start(f32[512,768]{1,0:T(8,128)} %copy-done.85) | copy-start | bytes 4718596
  967.8 24.8 %copy-start.43 = (f32[768]{0:T(1024)S(1)}, f32[768]{0:T(1024)}, u32[]{:S(2)}) copy-start(f32[768]{0:T(1024)} %convert_element_type.283) | copy-start | bytes 9220
  967.8 24.8 %copy-start.59 = (f32[2,64]{1,0:T(2,128)S(1)}, f32[2,64]{1,0:T(2,128)}, u32[]{:S(2)}) copy-start(f32[2,64]{1,0:T(2,128)} %copy-done.58) | copy-start | bytes 1540
  969.5 29.1 %copy-start.36 = (pred[2,512]{1,0:T(4,128)(4,1)S(1)}, pred[2,512]{1,0:T(4,128)(4,1)}, u32[]{:S(2)}) copy-start(pred[2,512]{1,0:T(4,128)(4,1)} %get-tuple-element.1383) | copy-start | bytes 3076
  969.5 29.1 %copy-start.38 = (s32[2,512]{1,0:T(2,128)S(1)}, s32[2,512]{1,0:T(2,128)}, u32[]{:S(2)}) copy-start(s32[2,512]{1,0:T(2,128)} %get-tuple-element.1384) | copy-start | bytes 12292
  969.5 125.1 %reduce-scatter.31.cloned.1.call-start = ((), (), s32[]{:S(2)}) async-start(), calls=%async_computation.29 | async-start | bytes 1769472 | tf_op jit(solution)/shard_map/reduce_scatter | solution.py:222
  1056.8 79.5 %reduce-scatter.29.cloned.1.call-start = ((), (), s32[]{:S(2)}) async-start(), calls=%async_computation.28 | async-start | bytes 1769472 | tf_op jit(solution)/shard_map/reduce_scatter | solution.py:219
  1057.3 118.8 %reduce-scatter.47.cloned.1.call-start = ((), (), s32[]{:S(2)}) async-start(), calls=%async_computation.37 | async-start | bytes 1327104 | tf_op jit(solution)/shard_map/reduce_scatter | solution.py:399
  1065.3 151.1 %reduce-scatter.45.cloned.1.call-start = ((), (), s32[]{:S(2)}) async-start(), calls=%async_computation.36 | async-start | bytes 1327104 | tf_op jit(solution)/shard_map/reduce_scatter | solution.py:393
  1072.2 184.0 %reduce-scatter.43.cloned.1.call-start = ((), (), s32[]{:S(2)}) async-start(), calls=%async_computation.35 | async-start | bytes 1327104 | tf_op jit(solution)/shard_map/reduce_scatter | solution.py:358
  1075.5 221.7 %reduce-scatter.35.cloned.1.call-start = ((), (), s32[]{:S(2)}) async-start(), calls=%async_computation.31 | async-start | bytes 1327104 | tf_op jit(solution)/shard_map/reduce_scatter | solution.py:352
  1078.1 270.5 %reduce-scatter.41.cloned.1.call-start = ((), (), s32[]{:S(2)}) async-start(), calls=%async_computation.34 | async-start | bytes 3981312 | tf_op jit(solution)/shard_map/reduce_scatter | solution.py:355
  1084.1 316.2 %reduce-scatter.33.cloned.1.call-start = ((), (), s32[]{:S(2)}) async-start(), calls=%async_computation.30 | async-start | bytes 3981312 | tf_op jit(solution)/shard_map/reduce_scatter | solution.py:349
  1140.4 299.9 %reduce-scatter.39.cloned.1.call-start = ((), (), s32[]{:S(2)}) async-start(), calls=%async_computation.33 | async-start | bytes 1327104 | tf_op jit(solution)/shard_map/reduce_scatter | solution.py:396
  1144.1 336.5 %reduce-scatter.37.cloned.1.call-start = ((), (), s32[]{:S(2)}) async-start(), calls=%async_computation.32 | async-start | bytes 1327104 | tf_op jit(solution)/shard_map/reduce_scatter | solution.py:390
  1147.4 252.9 %copy-start.63 = (s32[2,64]{1,0:T(2,128)S(1)}, s32[2,64]{1,0:T(2,128)}, u32[]{:S(2)}) copy-start(s32[2,64]{1,0:T(2,128)} %copy-done.61) | copy-start | bytes 1540
  1147.4 252.9 %copy-start.79 = (pred[2,64]{1,0:T(4,128)(4,1)S(1)}, pred[2,64]{1,0:T(4,128)(4,1)}, u32[]{:S(2)}) copy-start(pred[2,64]{1,0:T(4,128)(4,1)} %get-tuple-element.1409) | copy-start | bytes 388
  1147.4 334.8 %copy-start.55 = (f32[768]{0:T(1024)S(1)}, f32[768]{0:T(1024)}, u32[]{:S(2)}) copy-start(f32[768]{0:T(1024)} %copy-done.54) | copy-start | bytes 9220
  1147.5 393.7 %all-reduce.10.cloned.1.call-start = ((), (), s32[]{:S(2)}) async-start(), calls=%async_computation.38 | async-start | bytes 2359296 | tf_op jit(solution)/shard_map/psum | solution.py:378
  1401.2 79.4 %copy-start.64 = (f32[2,1,256]{2,0,1:T(2,128)}, f32[2,1,256]{2,0,1:T(2,128)S(1)}, u32[]{:S(2)}) copy-start(f32[2,1,256]{2,0,1:T(2,128)S(1)} %copy.155) | copy-start | bytes 6148
  1482.3 54.9 %copy-start.44 = (f32[768]{0:T(1024)S(1)}, f32[768]{0:T(1024)}, u32[]{:S(2)}) copy-start(f32[768]{0:T(1024)} %convert_element_type.283) | copy-start | bytes 9220
  1482.3 54.9 %copy-start.60 = (f32[2,64]{1,0:T(2,128)S(1)}, f32[2,64]{1,0:T(2,128)}, u32[]{:S(2)}) copy-start(f32[2,64]{1,0:T(2,128)} %copy-done.58) | copy-start | bytes 1540
  (85 other events, 292.2 us)
Sparse Core Ops, SparseCore 0:
  11.0 4.8 sort.21.cloned.1.call-done
  23.7 28.3 all-gather.8
  54.6 25.6 all-gather.6
  134.5 21.7 reduce-scatter.16
  166.2 45.9 all-gather.12
  214.5 46.6 all-gather.10
  262.7 63.4 all-gather.16
  351.5 63.4 all-gather.14
  431.9 58.8 reduce-scatter.20
  750.3 61.7 reduce-scatter.24
  815.9 61.7 reduce-scatter.22
  879.8 60.2 reduce-scatter.18
  969.6 22.8 reduce-scatter.26
  1056.9 37.7 reduce-scatter.30
  1097.8 38.4 reduce-scatter.28
  1139.4 36.7 reduce-scatter.46
  1179.6 36.7 reduce-scatter.44
  1219.5 36.7 reduce-scatter.42
  1260.4 36.7 reduce-scatter.34
  1300.5 48.0 reduce-scatter.40
  1352.1 48.0 reduce-scatter.32
  1403.5 36.7 reduce-scatter.38
  1443.8 36.7 reduce-scatter.36
  1483.1 57.6 all-reduce.9
  (1 shorter events, 0.0 us)
where the time goes:
time: 1560 us; the launch traced here: 1550 us
  waiting for transfers between devices  818 us (52%)
  matrix products  293 us (19%)
  local copies, waits for them, and re-layouts  214 us (14%)
  other arithmetic  125 us (8%)
  blocking collectives  75 us (5%)
  between operations  16 us (1%)
    reduce_scatter x2, waiting for transfers between devices, block_backward(): lax.psum_scatter(key_terms.astype(jnp.bfloat16), 'wide', scatter_dimensio...  107 us
    reduce_scatter x2, waiting for transfers between devices, mlp_backward(): lax.psum_scatter(grad_in.astype(jnp.bfloat16), 'narrow', scatter_dimensio...  81.9 us
    all_gather x2, waiting for transfers between devices, block_forward(): lax.all_gather(values_own, 'wide', axis=1, tiled=True)  73.9 us
    reduce_scatter x2, waiting for transfers between devices, mlp_forward(): lax.psum_scatter(partial_sum.astype(jnp.bfloat16), 'narrow', scatter_dime...  73 us
    reduce_scatter x2, waiting for transfers between devices, block_backward(): lax.psum_scatter(value_terms.astype(jnp.bfloat16), 'wide', scatter_dimens...  63 us
    dynamic_update_slice x20, local copies, waits for them, and re-layouts, block_backward(): lax.map(partial(query_side, with_keys=True), (queries, key_rows, value_ro...  58.7 us
    dynamic_slice x48, local copies, waits for them, and re-layouts, block_forward(): lax.map(attend_sequence, (queries, key_rows, value_rows) + query_meta + k...  58 us
    all_gather x1, waiting for transfers between devices, mlp_forward(): gathered = lax.all_gather(rows_in, 'narrow', axis=0, tiled=True)  56.1 us
  transfers between devices with their start and end apart: 23, of which 20 were waited for; matrix products, arithmetic and copies ran while one was open for 14% of the time, Pallas kernels for 0%

commit v1 on v0

v1 whole, which is shorter than its diff:
```python
from functools import partial

import jax
import jax.numpy as jnp
from jax import lax
from jax.experimental import pallas as pl
from jax.experimental.pallas import tpu as pltpu
from jax.sharding import PartitionSpec as P

H = 12
HD = 64
GROUPS = 4
HG = H // GROUPS
GW = HG * HD

EPSILON = 1e-06
NEGATIVE = -1e30
SCORE_SCALE = 0.125
LOG2E = 1.4426950408889634
PRECISE = lax.Precision.HIGHEST
BF = jnp.bfloat16
F32 = jnp.float32
VMEM = 48 << 20


def rms_gain(vector_in, gain_vector):
    return (
        vector_in
        * lax.rsqrt(jnp.mean(vector_in * vector_in, axis=-1, keepdims=True) + EPSILON)
        * gain_vector
    )


def smooth_gelu(hidden_pre):
    return jax.nn.gelu(hidden_pre, approximate=True)


def nt_dot(left, right):
    return lax.dot_general(left, right, (((1,), (1,)), ((), ())), preferred_element_type=F32)


def tn_dot(left, right):
    return lax.dot_general(left, right, (((0,), (0,)), ((), ())), preferred_element_type=F32)


def dot(left, right):
    return jnp.dot(left, right, preferred_element_type=F32)


def head_parts(rows):
    lane = lax.broadcasted_iota(jnp.int32, rows.shape, 1)
    zero = jnp.zeros_like(rows)
    return [
        jnp.where((lane >= h * HD) & (lane < (h + 1) * HD), rows, zero) for h in range(HG)
    ]


def pair_mask(row_ref, col_ref, q_at, k_at, bk, bq):
    k_iota = lax.broadcasted_iota(jnp.int32, (bk, bq), 0) + k_at
    q_iota = lax.broadcasted_iota(jnp.int32, (bk, bq), 1) + q_at
    info = row_ref[0:1, pl.ds(q_at, bq)]
    if col_ref is None:
        return (k_iota >= info) & (k_iota <= q_iota)
    return (col_ref[pl.ds(k_at, bk), :] == info) & (k_iota <= q_iota)


def attend_kernel(bq, bk, by_column, first_ref, x_ref, row_ref, *rest):
    if by_column:
        col_ref, o_ref, lse_ref, k_s, vt_s = rest
    else:
        col_ref = None
        o_ref, lse_ref, k_s, vt_s = rest
    i = pl.program_id(0)

    @pl.when(i == 0)
    def _():
        k_s[...] = x_ref[:, GW : 2 * GW]
        vt_s[...] = x_ref[:, 2 * GW : 3 * GW].T

    q_at = pl.multiple_of(i * bq, bq)
    q_heads = head_parts(x_ref[pl.ds(q_at, bq), 0:GW])

    def step(j, carry):
        k_at = pl.multiple_of(j * bk, bk)
        keys = k_s[pl.ds(k_at, bk), :]
        mask = pair_mask(row_ref, col_ref, q_at, k_at, bk, bq)
        out = []
        for h in range(HG):
            top, total, acc = carry[h]
            scores = nt_dot(keys, q_heads[h]) * (SCORE_SCALE * LOG2E)
            scores = jnp.where(mask, scores, NEGATIVE)
            top_new = jnp.maximum(top, jnp.max(scores, axis=0, keepdims=True))
            weight = jnp.exp2(scores - top_new)
            fade = jnp.exp2(top - top_new)
            total = total * fade + jnp.sum(weight, axis=0, keepdims=True)
            values_t = vt_s[h * HD : (h + 1) * HD, pl.ds(k_at, bk)]
            acc = acc * fade + dot(values_t, weight.astype(BF))
            out.append((top_new, total, acc))
        return tuple(out)

    start = tuple(
        (
            jnp.full((1, bq), NEGATIVE, F32),
            jnp.zeros((1, bq), F32),
            jnp.zeros((HD, bq), F32),
        )
        for _ in range(HG)
    )
    done = lax.fori_loop(first_ref[i], (q_at + bq + bk - 1) // bk, step, start)
    outs = jnp.concatenate([acc / total for _, total, acc in done], axis=0)
    o_ref[...] = outs.T.astype(BF)
    for h in range(HG):
        top, total, _ = done[h]
        lse_ref[h : h + 1, :] = top + jnp.log2(total)


def attend_back_kernel(bq, bk, by_column, first_ref, x_ref, row_ref, *rest):
    if by_column:
        col_ref, o_ref, g_ref, lse_ref, dx_ref, k_s, v_s, dk_s, dv_s = rest
    else:
        col_ref = None
        o_ref, g_ref, lse_ref, dx_ref, k_s, v_s, dk_s, dv_s = rest
    i = pl.program_id(0)

    @pl.when(i == 0)
    def _():
        k_s[...] = x_ref[:, GW : 2 * GW]
        v_s[...] = x_ref[:, 2 * GW : 3 * GW]
        dk_s[...] = jnp.zeros_like(dk_s)
        dv_s[...] = jnp.zeros_like(dv_s)

    q_at = pl.multiple_of(i * bq, bq)
    grad = g_ref[...]
    q_heads = head_parts(x_ref[pl.ds(q_at, bq), 0:GW])
    g_heads = head_parts(grad)
    dots = (grad.astype(F32) * o_ref[...].astype(F32)).T
    row_dot = [
        jnp.sum(dots[h * HD : (h + 1) * HD, :], axis=0, keepdims=True) for h in range(HG)
    ]

    def step(j, dq):
        k_at = pl.multiple_of(j * bk, bk)
        here = pl.ds(k_at, bk)
        keys = k_s[here, :]
        values = v_s[here, :]
        key_heads = head_parts(keys)
        mask = pair_mask(row_ref, col_ref, q_at, k_at, bk, bq)
        dk = dk_s[here, :]
        dv = dv_s[here, :]
        for h in range(HG):
            scores = nt_dot(keys, q_heads[h]) * (SCORE_SCALE * LOG2E)
            scores = jnp.where(mask, scores - lse_ref[h : h + 1, :], NEGATIVE)
            soft = jnp.exp2(scores)
            g_soft = nt_dot(values, g_heads[h])
            g_scores = (soft * (g_soft - row_dot[h])).astype(BF)
            dv = dv + dot(soft.astype(BF), g_heads[h])
            dk = dk + dot(g_scores, q_heads[h])
            dq = dq + tn_dot(g_scores, key_heads[h])
        dk_s[here, :] = dk
        dv_s[here, :] = dv
        return dq

    dq = lax.fori_loop(
        first_ref[i], (q_at + bq + bk - 1) // bk, step, jnp.zeros((bq, GW), F32)
    )
    dx_ref[pl.ds(q_at, bq), 0:GW] = (dq * SCORE_SCALE).astype(BF)

    @pl.when(i == pl.num_programs(0) - 1)
    def _():
        dx_ref[:, GW : 2 * GW] = (dk_s[...] * SCORE_SCALE).astype(BF)
        dx_ref[:, 2 * GW : 3 * GW] = dv_s[...].astype(BF)


def whole(shape):
    return pl.BlockSpec(shape, lambda i, *_: (0, 0))


def attend(x, first, row_info, col_info, bq):
    length = x.shape[0]
    by_column = col_info is not None
    in_specs = [whole(x.shape), whole(row_info.shape)]
    operands = [x, row_info]
    if by_column:
        in_specs.append(whole(col_info.shape))
        operands.append(col_info)
    return pl.pallas_call(
        partial(attend_kernel, bq, bq, by_column),
        out_shape=(
            jax.ShapeDtypeStruct((length, GW), BF),
            jax.ShapeDtypeStruct((8, length), F32),
        ),
        grid_spec=pltpu.PrefetchScalarGridSpec(
            num_scalar_prefetch=1,
            grid=(length // bq,),
            in_specs=in_specs,
            out_specs=(
                pl.BlockSpec((bq, GW), lambda i, *_: (i, 0)),
                pl.BlockSpec((8, bq), lambda i, *_: (0, i)),
            ),
            scratch_shapes=[pltpu.VMEM((length, GW), BF), pltpu.VMEM((GW, length), BF)],
        ),
        compiler_params=pltpu.CompilerParams(vmem_limit_bytes=VMEM),
        cost_estimate=pl.CostEstimate(
            flops=length * length * GW, bytes_accessed=length * GW * 8, transcendentals=0
        ),
        name="attend",
    )(first, *operands)


def attend_back(x, first, row_info, col_info, attended, grad, lse, bq):
    length = x.shape[0]
    by_column = col_info is not None
    in_specs = [whole(x.shape), whole(row_info.shape)]
    operands = [x, row_info]
    if by_column:
        in_specs.append(whole(col_info.shape))
        operands.append(col_info)
    in_specs += [
        pl.BlockSpec((bq, GW), lambda i, *_: (i, 0)),
        pl.BlockSpec((bq, GW), lambda i, *_: (i, 0)),
        pl.BlockSpec((8, bq), lambda i, *_: (0, i)),
    ]
    operands += [attended, grad, lse]
    return pl.pallas_call(
        partial(attend_back_kernel, bq, bq, by_column),
        out_shape=jax.ShapeDtypeStruct(x.shape, BF),
        grid_spec=pltpu.PrefetchScalarGridSpec(
            num_scalar_prefetch=1,
            grid=(length // bq,),
            in_specs=in_specs,
            out_specs=whole(x.shape),
            scratch_shapes=[
                pltpu.VMEM((length, GW), BF),
                pltpu.VMEM((length, GW), BF),
                pltpu.VMEM((length, GW), F32),
                pltpu.VMEM((length, GW), F32),
            ],
        ),
        compiler_params=pltpu.CompilerParams(vmem_limit_bytes=VMEM),
        cost_estimate=pl.CostEstimate(
            flops=3 * length * length * GW, bytes_accessed=length * GW * 16, transcendentals=0
        ),
        name="attend_back",
    )(first, *operands)


def exchange(parts):
    return lax.all_to_all(parts, "wide", 0, 0)


def to_heads(parts):
    groups, rows, width = parts.shape
    wide_count = lax.axis_size("wide")
    parts = parts.reshape(groups * 2, rows // 2, width)
    parts = jnp.tile(parts, (wide_count // (groups * 2), 1, 1))
    return exchange(parts).reshape(-1, width)


def to_rows(rows):
    wide_count = lax.axis_size("wide")
    width = rows.shape[1]
    parts = exchange(rows.reshape(wide_count, -1, width))
    return parts[: GROUPS * 2].reshape(GROUPS, -1, width)


def mlp_forward(rows_in, expand_part, reduce_part):
    gathered = lax.all_gather(rows_in, "narrow", axis=0, tiled=True)
    hidden_pre = jnp.dot(gathered, expand_part, preferred_element_type=jnp.float32)
    hidden = smooth_gelu(hidden_pre).astype(jnp.bfloat16)
    partial_sum = jnp.dot(hidden, reduce_part, preferred_element_type=jnp.float32)
    reduced = lax.psum_scatter(
        partial_sum.astype(jnp.bfloat16), "narrow", scatter_dimension=0, tiled=True
    ).astype(jnp.float32)
    kept = (gathered, hidden_pre, hidden, expand_part, reduce_part)
    return (reduced, kept)


def mlp_backward(grad_rows, kept):
    rows_used, hidden_pre, hidden, expand_use, reduce_use = kept
    grad_low = grad_rows.astype(jnp.bfloat16)
    grad_low = lax.all_gather(grad_low, "narrow", axis=0, tiled=True)
    grad_hidden = jnp.dot(grad_low, reduce_use.T, preferred_element_type=jnp.float32)
    grad_pre = jax.vjp(smooth_gelu, hidden_pre)[1](grad_hidden)[0].astype(jnp.bfloat16)
    reduce_grad = jnp.dot(hidden.T, grad_low, preferred_element_type=jnp.float32)
    expand_grad = jnp.dot(rows_used.T, grad_pre, preferred_element_type=jnp.float32)
    grad_in = jnp.dot(grad_pre, expand_use.T, preferred_element_type=jnp.float32)
    grad_in = lax.psum_scatter(
        grad_in.astype(jnp.bfloat16), "narrow", scatter_dimension=0, tiled=True
    ).astype(jnp.float32)
    return (grad_in, expand_grad, reduce_grad)


def block_forward(rows_in, weights, meta, bq):
    project, output, prenorm, midnorm, expand_part, reduce_part = weights
    first, row_info, col_info = meta
    normed = rms_gain(rows_in, prenorm.astype(F32)).astype(BF)
    projected = jnp.einsum("rd,cdn->crn", normed, project, preferred_element_type=F32).astype(BF)
    x = to_heads(projected)
    attended_h, lse = attend(x, first, row_info, col_info, bq)
    attended = to_rows(attended_h)
    branch = jnp.einsum("crn,cnd->rd", attended, output, preferred_element_type=F32)
    middle = rows_in + branch
    normed_mid = rms_gain(middle, midnorm.astype(F32)).astype(BF)
    reduced, mlp_kept = mlp_forward(normed_mid, expand_part, reduce_part)
    delta = branch + reduced
    return (delta, (rows_in, normed, x, attended_h, lse, attended, middle, mlp_kept))


def block_backward(grad_delta, kept, weights, meta, bq):
    project, output, prenorm, midnorm, expand_part, reduce_part = weights
    first, row_info, col_info = meta
    rows_in, normed, x, attended_h, lse, attended, middle, mlp_kept = kept
    grad_normed_mid, expand_grad, reduce_grad = mlp_backward(grad_delta, mlp_kept)
    mid_pull = jax.vjp(rms_gain, middle, midnorm.astype(F32))[1]
    grad_middle, midnorm_grad = mid_pull(grad_normed_mid)
    grad_branch = (grad_delta + grad_middle).astype(BF)
    output_grad = jnp.einsum("crn,rd->cnd", attended, grad_branch, preferred_element_type=F32)
    grad_attended = jnp.einsum(
        "rd,cnd->crn", grad_branch, output, preferred_element_type=F32
    ).astype(BF)
    dx = attend_back(
        x, first, row_info, col_info, attended_h, to_heads(grad_attended), lse, bq
    )
    grad_projected = to_rows(dx)
    project_grad = jnp.einsum("rd,crn->cdn", normed, grad_projected, preferred_element_type=F32)
    grad_normed = jnp.einsum("crn,cdn->rd", grad_projected, project, preferred_element_type=F32)
    first_pull = jax.vjp(rms_gain, rows_in, prenorm.astype(F32))[1]
    grad_first, prenorm_grad = first_pull(grad_normed)
    model_width = rows_in.shape[1]
    project_grad = (
        project_grad.astype(BF)
        .reshape(GROUPS, model_width, 3, GW)
        .transpose(1, 2, 0, 3)
        .reshape(model_width, 3 * model_width)
    )
    output_grad = output_grad.astype(BF).reshape(model_width, model_width)
    return (
        grad_middle + grad_first,
        (project_grad, output_grad, prenorm_grad, midnorm_grad, expand_grad, reduce_grad),
    )


def on_device(
    tokens,
    cotangent,
    selected,
    segments,
    router_vector,
    project_routed,
    output_routed,
    prenorm_routed,
    midnorm_routed,
    expand_routed,
    reduce_routed,
    project_dense,
    output_dense,
    prenorm_dense,
    midnorm_dense,
    expand_dense,
    reduce_dense,
):
    seq_count, span_rows, model_width = tokens.shape
    row_length = selected.shape[1]
    wide_count = lax.axis_size("wide")
    here = lax.axis_index("wide")
    slot_count = span_rows // 4
    bq_dense = min(256, row_length)
    bq_routed = min(256, slot_count * wide_count)

    def grouped_weights(project, output):
        project = (
            project.reshape(model_width, 3, GROUPS, GW)
            .transpose(2, 0, 1, 3)
            .reshape(GROUPS, model_width, 3 * GW)
        )
        return project, output.reshape(GROUPS, GW, model_width)

    upper = (
        lax.broadcasted_iota(jnp.int32, (span_rows, span_rows), 0)
        <= lax.broadcasted_iota(jnp.int32, (span_rows, span_rows), 1)
    ).astype(BF)
    slots = jnp.arange(slot_count, dtype=jnp.int32)
    own_selected = lax.dynamic_slice_in_dim(selected, here * span_rows, span_rows, 1)
    own_rank = jnp.dot(own_selected.astype(BF), upper, preferred_element_type=F32)
    own_rank = jnp.where(own_selected > 0, own_rank.astype(jnp.int32) - 1, -1)
    one_hot = own_rank[:, None, :] == slots[None, :, None]
    placed = one_hot.astype(F32)

    mine = here % seq_count
    seq_segments = lax.dynamic_slice_in_dim(segments, mine, 1, 0)[0]
    seq_selected = lax.dynamic_slice_in_dim(selected, mine, 1, 0)[0].reshape(wide_count, span_rows)
    seq_rank = jnp.dot(seq_selected.astype(BF), upper, preferred_element_type=F32)
    seq_rank = jnp.where(seq_selected > 0, seq_rank.astype(jnp.int32) - 1, -1)
    slot_segments = (
        jnp.sum(
            jnp.where(
                seq_rank[:, None, :] == slots[None, :, None],
                seq_segments.reshape(wide_count, 1, span_rows) + 1,
                0,
            ),
            axis=-1,
        )
        - 1
    ).reshape(-1)
    meta_routed = (
        jnp.zeros((slot_segments.shape[0] // bq_routed,), jnp.int32),
        jnp.broadcast_to(slot_segments[None], (8, slot_segments.shape[0])),
        slot_segments[:, None],
    )
    starts = sum(
        jnp.where(seq_segments == value, jnp.sum((seq_segments < value).astype(jnp.int32)), 0)
        for value in range(1, 4)
    )
    meta_dense = (
        starts[::bq_dense] // bq_dense,
        jnp.broadcast_to(starts[None], (8, row_length)),
        None,
    )

    picked = jnp.einsum(
        "scp,spd->scd", one_hot.astype(BF), tokens, preferred_element_type=F32
    )
    logits = jnp.dot(
        tokens.reshape(-1, model_width), router_vector, preferred_element_type=F32
    ).reshape(seq_count, span_rows)
    gate = jnp.einsum("scp,sp->sc", placed, logits, precision=PRECISE)
    weights_routed = grouped_weights(project_routed, output_routed) + (
        prenorm_routed,
        midnorm_routed,
        expand_routed,
        reduce_routed,
    )
    weights_dense = grouped_weights(project_dense, output_dense) + (
        prenorm_dense,
        midnorm_dense,
        expand_dense,
        reduce_dense,
    )
    routed_shape = (seq_count, slot_count, model_width)
    routed_delta, kept_routed = block_forward(
        picked.reshape(-1, model_width), weights_routed, meta_routed, bq_routed
    )
    routed_delta = routed_delta.reshape(routed_shape)
    lifted = jnp.einsum("scp,scd->spd", placed, gate[..., None] * routed_delta, precision=PRECISE)
    mixed = tokens.astype(F32) + lifted
    dense_delta, kept_dense = block_forward(
        mixed.reshape(-1, model_width), weights_dense, meta_dense, bq_dense
    )
    activations = (mixed + dense_delta.reshape(mixed.shape)).astype(BF)
    grad_output = cotangent.astype(F32)
    grad_dense_in, grads_dense = block_backward(
        grad_output.reshape(-1, model_width), kept_dense, weights_dense, meta_dense, bq_dense
    )
    grad_mixed = grad_output + grad_dense_in.reshape(grad_output.shape)
    grad_lifted = jnp.einsum("scp,spd->scd", placed, grad_mixed, precision=PRECISE)
    grad_routed_delta = gate[..., None] * grad_lifted
    grad_gate = jnp.sum(grad_lifted * routed_delta, axis=-1)
    grad_picked, grads_routed = block_backward(
        grad_routed_delta.reshape(-1, model_width),
        kept_routed,
        weights_routed,
        meta_routed,
        bq_routed,
    )
    grad_logits = jnp.einsum("scp,sc->sp", placed, grad_gate, precision=PRECISE)
    tokens_gradient = (
        grad_mixed
        + jnp.einsum("scp,scd->spd", placed, grad_picked.reshape(routed_shape), precision=PRECISE)
        + grad_logits[..., None] * router_vector.astype(F32)
    )
    router_grad = jnp.dot(
        grad_logits.reshape(1, -1),
        tokens.reshape(-1, model_width).astype(F32),
        precision=PRECISE,
    )[0]

    def scatter(grad, dimension=0):
        return lax.psum_scatter(
            grad.astype(BF), "wide", scatter_dimension=dimension, tiled=True
        )

    vectors = jnp.stack(
        [grads_routed[2], grads_routed[3], grads_dense[2], grads_dense[3], router_grad], axis=1
    )
    shares = [
        scatter(grads_routed[0]),
        scatter(grads_routed[1]),
        scatter(grads_dense[0]),
        scatter(grads_dense[1]),
        scatter(vectors),
    ]
    summed = [lax.psum(share, "narrow").astype(F32) for share in shares]
    ffn = [
        scatter(grads_routed[4]).astype(F32),
        scatter(grads_dense[4]).astype(F32),
        scatter(grads_routed[5], 1).astype(F32),
        scatter(grads_dense[5], 1).astype(F32),
    ]
    vector_sums = summed[4]
    return (
        activations,
        tokens_gradient,
        vector_sums[:, 4],
        summed[0],
        summed[1],
        vector_sums[:, 0],
        vector_sums[:, 1],
        ffn[0],
        ffn[2],
        summed[2],
        summed[3],
        vector_sums[:, 2],
        vector_sums[:, 3],
        ffn[1],
        ffn[3],
    )


def solution(mesh):
    return jax.shard_map(
        on_device,
        mesh=mesh,
        in_specs=(
            P("narrow", "wide", None),
            P("narrow", "wide", None),
            P("narrow", None),
            P("narrow", None),
            P(),
            P(),
            P(),
            P(),
            P(),
            P(None, "narrow"),
            P("narrow", None),
            P(),
            P(),
            P(),
            P(),
            P(None, "narrow"),
            P("narrow", None),
        ),
        out_specs=(
            P("narrow", "wide", None),
            P("narrow", "wide", None),
            P("wide"),
            P("wide", None),
            P("wide", None),
            P("wide"),
            P("wide"),
            P("wide", "narrow"),
            P("narrow", "wide"),
            P("wide", None),
            P("wide", None),
            P("wide"),
            P("wide"),
            P("wide", "narrow"),
            P("narrow", "wide"),
        ),
        check_vma=False,
    )
```

time: 1560 us -> 1030 us (0.66)
  waiting for transfers between devices: 818 us -> 611 us
  matrix products: 293 us -> 96.4 us
  local copies, waits for them, and re-layouts: 214 us -> 106 us
  other arithmetic: 125 us -> 29.1 us
  Pallas kernels: 0 us -> 54.4 us
  starting transfers between devices: 1.45 us -> 24 us
    reduce_scatter x12 -> x6, waiting for transfers between devices: 493 us -> 164 us  [scatter(): lax.psum_scatter(grad.astype(BF), 'wide', scatter_dimension=dimension, ti...]
    dot_general x42 -> x16, matrix products: 224 us -> 34.8 us  [the longest x2 9.34 us: block_backward(): jnp.einsum('crn,cdn->rd', grad_projected, project, preferred_element_type...]
    unnamed x23 -> x19, waiting for transfers between devices: 2.24 us -> 131 us
    all_gather x4 -> x0, waiting for transfers between devices: 112 us -> none  [the longest x2 73.9 us: block_forward(): lax.all_gather(values_own, 'wide', axis=1, tiled=True)]
    all_to_all x0 -> x5, waiting for transfers between devices: none -> 85.6 us  [exchange(): return lax.all_to_all(parts, 'wide', 0, 0)]
    dynamic_update_slice x24 -> x0, local copies, waits for them, and re-layouts: 60.3 us -> none  [the longest x20 58.7 us: block_backward(): lax.map(partial(query_side, with_keys=True), (queries, key_rows, value_ro...]
    dynamic_slice x51 -> x0, local copies, waits for them, and re-layouts: 59.8 us -> none  [the longest x48 58 us: block_forward(): lax.map(attend_sequence, (queries, key_rows, value_rows) + query_meta + k...]
    psum x1, waiting for transfers between devices: 0.01 us -> 57.6 us  [on_device(): summed = [lax.psum(share, 'narrow').astype(F32) for share in shares]]
  transfers between devices with their start and end apart: 23 -> 21, of which waited for: 20 -> 18; matrix products, arithmetic and copies ran while one was open for 14% -> 14% of each run, Pallas kernels for 0% -> 2%
where the time goes in v1:
time: 1030 us
  waiting for transfers between devices  611 us (59%)
  local copies, waits for them, and re-layouts  106 us (10%)
  matrix products  96.4 us (9%)
  blocking collectives  89.6 us (9%)
  Pallas kernels  54.4 us (5%)
  other arithmetic  29.1 us (3%)
  starting transfers between devices  24 us (2%)
  between operations  15.2 us (1%)
    reduce_scatter x6, waiting for transfers between devices, scatter(): lax.psum_scatter(grad.astype(BF), 'wide', scatter_dimension=dimension, ti...  164 us
    unnamed x19, waiting for transfers between devices  131 us
    all_to_all x5, waiting for transfers between devices, exchange(): return lax.all_to_all(parts, 'wide', 0, 0)  85.6 us
    reduce_scatter x2, waiting for transfers between devices, mlp_forward(): lax.psum_scatter(partial_sum.astype(jnp.bfloat16), 'narrow', scatter_dime...  70.7 us
    psum x1, waiting for transfers between devices, on_device(): summed = [lax.psum(share, 'narrow').astype(F32) for share in shares]  57.6 us
    all_gather x1, waiting for transfers between devices, mlp_forward(): gathered = lax.all_gather(rows_in, 'narrow', axis=0, tiled=True)  52.2 us
    unnamed x148, local copies, waits for them, and re-layouts  50.6 us
    reduce_scatter x2, waiting for transfers between devices, mlp_backward(): lax.psum_scatter(grad_in.astype(jnp.bfloat16), 'narrow', scatter_dimensio...  49.5 us
  transfers between devices with their start and end apart: 21, of which 18 were waited for; matrix products, arithmetic and copies ran while one was open for 14% of the time, Pallas kernels for 2%

profile of v1, /device:TPU:0, one launch (start us, length us, event | category | flops | bytes accessed | tf_op | source)
XLA Modules:
  0.0 1026.1 jit_solution(7405808699653046497)
XLA Ops:
  11.0 5.8 copy.116
  23.0 5.3 all-to-all-start
  29.8 9.6 all-to-all-done
  46.6 6.8 all-to-all-done.1
  56.1 19.9 %all_gather.12 = bf16[512,768]{1,0:T(8,128)(2,1)S(1)} all-gather(bf16[128,768]{1,0:T(8,128)(2,1)S(1)} %multiply_convert_fusion.4), channel_id=1, replica_groups=mesh['wide'=8,'narrow'=4] {'narrow'}, dimensions={0}, use_global_device_ids=true | all-gather | bytes 983040 | tf_op jit(solution)/shard_map/all_gather | solution.py:267
  83.7 5.9 copy.121
  89.6 4.1 copy.122
  93.8 8.2 reduce-scatter.20.cloned.1.call-done
  111.7 5.2 tile_reshape.13
  120.5 4.4 all-to-all-start.2
  127.0 27.4 %all-to-all-done.2 = bf16[8,256,576]{1,2,0:T(8,128)(2,1)} async-done(((bf16[8,256,576]{1,2,0:T(8,128)(2,1)}), bf16[8,256,576]{1,2,0:T(8,128)(2,1)}, u32[]{:S(2)}, u32[]{:S(2)}) %all-to-all-start.2) | async-done | bytes 2359328 | tf_op jit(solution)/shard_map/all_to_all | solution.py:248
  154.3 4.4 copy.125
  160.5 16.1 %attend.3 = (bf16[2048,192]{1,0:T(8,128)(2,1)S(1)}, f32[8,2048]{1,0:T(8,128)S(1)}) custom-call(s32[8]{0:T(128)S(1)} %and_select_fusion.first_ref, bf16[2048,576]{1,0:T(8,128)(2,1)S(1)} %bitcast.203, s32[8,2048]{1,0:T(8,128)S(1)} %broadcast_in_dim.48.row_ref), custom_call_target="tpu_custom_call" | custom-call | flops 805306368 | bytes 3145728 | tf_op jit(solution)/shard_map/attend/pallas_call | solution.py:186
  177.9 4.2 all-to-all-start.3
  182.2 12.5 %all-to-all-done.3 = bf16[8,256,192]{1,2,0:T(8,128)(2,1)} async-done(((bf16[8,256,192]{1,2,0:T(8,128)(2,1)}), bf16[8,256,192]{1,2,0:T(8,128)(2,1)}, u32[]{:S(2)}, u32[]{:S(2)}) %all-to-all-start.3) | async-done | bytes 786464 | tf_op jit(solution)/shard_map/all_to_all | solution.py:248
  206.4 7.5 fusion.75
  213.9 52.2 %all-gather.3.cloned.1.call-done = bf16[2048,768]{1,0:T(8,128)(2,1)} async-done(((bf16[512,768]{1,0:T(8,128)(2,1)}), bf16[2048,768]{1,0:T(8,128)(2,1)}) %all-gather.3.cloned.1.call-update) | async-done | bytes 3145744 | tf_op jit(solution)/shard_map/all_gather | solution.py:267
  266.1 11.7 %fusion.6 = (bf16[2048,768]{1,0:T(8,128)(2,1)S(1)}, f32[2048,768]{1,0:T(8,128)}) fusion(f32[2048,768]{1,0:T(8,128)} %fusion.75, bf16[2048,768]{1,0:T(8,128)(2,1)} %all-gather.3.cloned.1.call-done, bf16[768,768]{1,0:T(8,128)(2,1)S(1)} %copy-done), kind=kOutput, calls=%fused_computation.8 | convolution fusion | flops 2447376384 | bytes 20054016 | tf_op jit(solution)/shard_map/dot_general | solution.py:268
  284.9 8.3 convolution_convert_fusion.1
  293.2 49.5 %reduce-scatter.24.cloned.1.call-done = bf16[512,768]{1,0:T(8,128)(2,1)} async-done(((bf16[2048,768]{1,0:T(8,128)(2,1)}), bf16[512,768]{1,0:T(8,128)(2,1)}) %reduce-scatter.24.cloned.1.call-update) | async-done | bytes 786448 | tf_op jit(solution)/shard_map/reduce_scatter | solution.py:287
  342.7 62.5 %reduce-scatter.22.cloned.1.call-done = bf16[512,768]{1,0:T(8,128)(2,1)} async-done(((bf16[2048,768]{1,0:T(8,128)(2,1)}), bf16[512,768]{1,0:T(8,128)(2,1)}) %reduce-scatter.22.cloned.1.call-update) | async-done | bytes 786448 | tf_op jit(solution)/shard_map/reduce_scatter | solution.py:271
  405.2 4.3 fusion.13
  414.7 16.1 %all_to_all.40 = bf16[8,256,192]{1,2,0:T(8,128)(2,1)} all-to-all(bf16[8,256,192]{1,2,0:T(8,128)(2,1)S(1)} %copy.130), channel_id=1, replica_groups=mesh['wide'=8,'narrow'=4] {'wide'}, dimensions={0} | all-to-all | bytes 1572864 | tf_op jit(solution)/shard_map/all_to_all | solution.py:248
  432.2 29.3 %attend_back.2 = bf16[2048,576]{1,0:T(8,128)(2,1)S(1)} custom-call(s32[8]{0:T(128)S(1)} %and_select_fusion.first_ref, bf16[2048,576]{1,0:T(8,128)(2,1)} %bitcast.202, s32[8,2048]{1,0:T(8,128)S(1)} %broadcast_in_dim.48.row_ref, bf16[2048,192]{1,0:T(8,128)(2,1)S(1)} %get-tuple-element.20.rest_0_, bf16[2048,192]{1,0:T(8,128)(2,1)S(1)} %bitcast.206, ...), custom_call_target="tpu_custom_call" | custom-call | flops 2415919104 | bytes 6291456 | tf_op jit(solution)/shard_map/attend_back/pallas_call | solution.py:224
  463.0 4.4 copy.132
  467.4 4.5 all-to-all-start.5
  472.2 29.2 %all-to-all-done.5 = bf16[8,256,576]{1,2,0:T(8,128)(2,1)} async-done(((bf16[8,256,576]{1,2,0:T(8,128)(2,1)}), bf16[8,256,576]{1,2,0:T(8,128)(2,1)}, u32[]{:S(2)}, u32[]{:S(2)}) %all-to-all-start.5) | async-done | bytes 2359328 | tf_op jit(solution)/shard_map/all_to_all | solution.py:248
  501.4 4.4 copy.133
  505.9 5.6 reshape.359
  511.5 5.9 fusion.22
  519.6 16.4 %all_gather.15 = bf16[512,768]{1,0:T(8,128)(2,1)S(1)} all-gather(bf16[128,768]{1,0:T(8,128)(2,1)S(1)} %bitcast_convert_fusion.1), channel_id=1, replica_groups=mesh['wide'=8,'narrow'=4] {'narrow'}, dimensions={0}, use_global_device_ids=true | all-gather | bytes 983040 | tf_op jit(solution)/shard_map/all_gather | solution.py:281
  540.2 7.9 convolution_convert_fusion.4
  548.4 6.5 convolution_convert_fusion.5
  561.1 5.8 copy.160
  573.1 10.2 all_to_all.41
  583.2 5.4 attend_back.3
  588.7 15.1 %all_to_all.42 = bf16[8,64,576]{2,1,0:T(8,128)(2,1)S(1)} all-to-all(bf16[8,64,576]{2,1,0:T(8,128)(2,1)S(1)} %bitcast.201), channel_id=1, replica_groups=mesh['wide'=8,'narrow'=4] {'wide'}, dimensions={0} | all-to-all | bytes 1179648 | tf_op jit(solution)/shard_map/all_to_all | solution.py:248
  606.9 5.8 copy.158
  632.8 10.1 reduce-scatter.36.cloned.1.call-done
  644.6 50.0 %reduce-scatter.44.cloned.1.call-done = bf16[96,2304]{1,0:T(8,128)(2,1)} async-done(((bf16[768,2304]{1,0:T(8,128)(2,1)}), bf16[96,2304]{1,0:T(8,128)(2,1)}) %reduce-scatter.44.cloned.1.call-update) | async-done | bytes 442384
  696.6 49.4 %reduce-scatter.42.cloned.1.call-done = bf16[96,2304]{1,0:T(8,128)(2,1)} async-done(((bf16[768,2304]{1,0:T(8,128)(2,1)}), bf16[96,2304]{1,0:T(8,128)(2,1)}) %reduce-scatter.42.cloned.1.call-update) | async-done | bytes 442384
  748.1 38.0 %reduce-scatter.34.cloned.1.call-done = bf16[96,768]{1,0:T(8,128)(2,1)} async-done(((bf16[768,768]{1,0:T(8,128)(2,1)}), bf16[96,768]{1,0:T(8,128)(2,1)}) %reduce-scatter.34.cloned.1.call-update) | async-done | bytes 147472 | tf_op jit(solution)/shard_map/reduce_scatter | solution.py:478
  786.0 40.2 %reduce-scatter.28.cloned.1.call-done = bf16[96,768]{1,0:T(8,128)(2,1)} async-done(((bf16[768,768]{1,0:T(8,128)(2,1)}), bf16[96,768]{1,0:T(8,128)(2,1)}) %reduce-scatter.28.cloned.1.call-update) | async-done | bytes 147472 | tf_op jit(solution)/shard_map/reduce_scatter | solution.py:478
  828.7 37.5 %reduce-scatter.32.cloned.1.call-done = bf16[768,96]{0,1:T(8,128)(2,1)} async-done(((bf16[768,768]{0,1:T(8,128)(2,1)}), bf16[768,96]{0,1:T(8,128)(2,1)}) %reduce-scatter.32.cloned.1.call-update) | async-done | bytes 147472 | tf_op jit(solution)/shard_map/reduce_scatter | solution.py:478
  867.9 38.6 %reduce-scatter.30.cloned.1.call-done = bf16[96,768]{1,0:T(8,128)(2,1)} async-done(((bf16[768,768]{1,0:T(8,128)(2,1)}), bf16[96,768]{1,0:T(8,128)(2,1)}) %reduce-scatter.30.cloned.1.call-update) | async-done | bytes 147472 | tf_op jit(solution)/shard_map/reduce_scatter | solution.py:478
  911.6 31.8 %reduce-scatter.40.cloned.1.call-done = bf16[96,5]{1,0:T(8,128)(2,1)} async-done(((bf16[768,5]{1,0:T(8,128)(2,1)}), bf16[96,5]{1,0:T(8,128)(2,1)}) %reduce-scatter.40.cloned.1.call-update) | async-done | bytes 976
  944.2 11.9 %psum.35 = bf16[96,5]{0,1:T(8,128)(2,1)S(1)} all-reduce(bf16[96,5]{0,1:T(8,128)(2,1)S(1)} %copy.157), channel_id=1, replica_groups=mesh['wide'=8,'narrow'=4] {'narrow'}, use_global_device_ids=true, to_apply=%region_22.23 | all-reduce | flops 480 | bytes 1920 | tf_op jit(solution)/shard_map/psum | solution.py:492
  956.7 57.6 %all-reduce.3.cloned.1.call-done = (bf16[96,2304]{0,1:T(8,128)(2,1)}, bf16[96,2304]{0,1:T(8,128)(2,1)}, bf16[96,768]{1,0:T(8,128)(2,1)}, bf16[96,768]{1,0:T(8,128)(2,1)}) async-done(((bf16[96,2304]{0,1:T(8,128)(2,1)}, bf16[96,2304]{0,1:T(8,128)(2,1)}, bf16[96,768]{1,0:T(8,128)(2,1)}, bf16[96,768]{1,0:T(8,128)(2,1)}), (bf16[96,2304]{0,1:T(8,128)(2,1)}, bf16[96,2304]{0,1:T(8,128)(2,1)}, ...) | async-done | bytes 1179664 | tf_op jit(solution)/shard_map/psum | solution.py:492
  (284 shorter events, 137.5 us)
Async XLA Ops:
  7.2 258.9 %copy-start = (bf16[768,768]{1,0:T(8,128)(2,1)S(1)}, bf16[768,768]{1,0:T(8,128)(2,1)}, u32[]{:S(2)}) copy-start(bf16[768,768]{1,0:T(8,128)(2,1)} %param.32) | copy-start | bytes 3538948
  10.3 43.0 %copy-start.19 = (f32[2,64,768]{2,1,0:T(8,128)}, f32[2,64,768]{2,1,0:T(8,128)S(1)}, u32[]{:S(2)}) copy-start(f32[2,64,768]{2,1,0:T(8,128)S(1)} %get-tuple-element.117) | copy-start | bytes 1179652
  21.9 6.4 copy-start.44
  21.9 6.5 copy-start.45
  23.0 23.5 %copy-start.53 = (bf16[768]{0:T(1024)(128)(2,1)S(1)}, bf16[768]{0:T(1024)(128)(2,1)}, u32[]{:S(2)}) copy-start(bf16[768]{0:T(1024)(128)(2,1)} %param.25) | copy-start | bytes 4612
  23.0 16.5 %all-to-all-start = ((bf16[8,64,576]{2,1,0:T(8,128)(2,1)}), bf16[8,64,576]{2,1,0:T(8,128)(2,1)S(1)}, u32[]{:S(2)}, u32[]{:S(2)}) async-start(bf16[8,64,576]{2,1,0:T(8,128)(2,1)} %bitcast.10), calls=%async_computation | async-start | bytes 1310720 | tf_op jit(solution)/shard_map/all_to_all | solution.py:248
  43.1 10.3 %all-to-all-start.1 = ((bf16[8,64,192]{2,1,0:T(8,128)(2,1)}), bf16[8,64,192]{2,1,0:T(8,128)(2,1)S(1)}, u32[]{:S(2)}, u32[]{:S(2)}) async-start(bf16[8,64,192]{2,1,0:T(8,128)(2,1)} %bitcast.12), calls=%async_computation.1 | async-start | bytes 524288 | tf_op jit(solution)/shard_map/all_to_all | solution.py:248
  46.5 55.5 %reduce-scatter.20.cloned.1.call-start = ((), (), s32[]{:S(2)}) async-start(), calls=%async_computation.21 | async-start | bytes 983040 | tf_op jit(solution)/shard_map/reduce_scatter | solution.py:271
  53.4 23.6 %copy-start.62 = (bf16[768,768]{1,0:T(8,128)(2,1)S(1)}, bf16[768,768]{1,0:T(8,128)(2,1)}, u32[]{:S(2)}) copy-start(bf16[768,768]{1,0:T(8,128)(2,1)} %param.26) | copy-start | bytes 3538948
  55.2 22.5 %copy-start.57 = (f32[128]{0:T(128)}, f32[128]{0:T(128)S(1)}, u32[]{:S(2)}) copy-start(f32[128]{0:T(128)S(1)} %get-tuple-element.101) | copy-start | bytes 1540
  55.3 22.4 %copy-start.49 = (f32[128]{0:T(128)}, f32[128]{0:T(128)S(1)}, u32[]{:S(2)}) copy-start(f32[128]{0:T(128)S(1)} %fusion.71) | copy-start | bytes 1540
  80.9 125.5 %all-gather.5.cloned.1.call-start = ((), (), s32[]{:S(2)}) async-start(), calls=%async_computation.24 | async-start | bytes 3932160 | tf_op jit(solution)/shard_map/all_gather | solution.py:281
  83.7 19.3 %copy-start.51 = (f32[2,1,64]{2,1,0:T(1,128)}, f32[2,1,64]{2,1,0:T(1,128)S(1)}, u32[]{:S(2)}) copy-start(f32[2,1,64]{2,1,0:T(1,128)S(1)} %fusion.53) | copy-start | bytes 1540
  120.5 33.9 %all-to-all-start.2 = ((bf16[8,256,576]{1,2,0:T(8,128)(2,1)}), bf16[8,256,576]{1,2,0:T(8,128)(2,1)}, u32[]{:S(2)}, u32[]{:S(2)}) async-start(bf16[8,256,576]{1,2,0:T(8,128)(2,1)} %copy.124), calls=%async_computation.3 | async-start | bytes 4718592 | tf_op jit(solution)/shard_map/all_to_all | solution.py:248
  176.6 5.5 copy-start.55
  177.9 16.8 %all-to-all-start.3 = ((bf16[8,256,192]{1,2,0:T(8,128)(2,1)}), bf16[8,256,192]{1,2,0:T(8,128)(2,1)}, u32[]{:S(2)}, u32[]{:S(2)}) async-start(bf16[8,256,192]{1,2,0:T(8,128)(2,1)} %copy.126), calls=%async_computation.4 | async-start | bytes 1572864 | tf_op jit(solution)/shard_map/all_to_all | solution.py:248
  182.1 84.0 %all-gather.3.cloned.1.call-start = ((), (), s32[]{:S(2)}) async-start(), calls=%async_computation.22 | async-start | bytes 3932160 | tf_op jit(solution)/shard_map/all_gather | solution.py:267
  206.1 136.6 %reduce-scatter.24.cloned.1.call-start = ((), (), s32[]{:S(2)}) async-start(), calls=%async_computation.25 | async-start | bytes 3932160 | tf_op jit(solution)/shard_map/reduce_scatter | solution.py:287
  283.6 121.5 %reduce-scatter.22.cloned.1.call-start = ((), (), s32[]{:S(2)}) async-start(), calls=%async_computation.23 | async-start | bytes 3932160 | tf_op jit(solution)/shard_map/reduce_scatter | solution.py:271
  405.2 4.3 copy-start.9
  405.2 4.4 copy-start.15
  405.2 4.4 copy-start.21
  467.4 4.8 copy-start.48
  467.4 34.0 %all-to-all-start.5 = ((bf16[8,256,576]{1,2,0:T(8,128)(2,1)}), bf16[8,256,576]{1,2,0:T(8,128)(2,1)}, u32[]{:S(2)}, u32[]{:S(2)}) async-start(bf16[8,256,576]{1,2,0:T(8,128)(2,1)} %copy.132), calls=%async_computation.8 | async-start | bytes 4718592 | tf_op jit(solution)/shard_map/all_to_all | solution.py:248
  471.9 95.0 %reduce-scatter.26.cloned.1.call-start = ((), (), s32[]{:S(2)}) async-start(), calls=%async_computation.26 | async-start | bytes 983040 | tf_op jit(solution)/shard_map/reduce_scatter | solution.py:287
  511.5 5.9 copy-start.6
  511.5 5.9 copy-start.10
  511.5 5.9 copy-start.22
  518.6 17.4 %copy-start.65 = (f32[512,768]{1,0:T(8,128)S(1)}, f32[512,768]{1,0:T(8,128)}, u32[]{:S(2)}) copy-start(f32[512,768]{1,0:T(8,128)} %copy-done.64) | copy-start | bytes 4718596
  519.6 18.0 %copy-start.27 = (f32[2,64,768]{2,1,0:T(8,128)}, f32[2,64,768]{2,1,0:T(8,128)S(1)}, u32[]{:S(2)}) copy-start(f32[2,64,768]{2,1,0:T(8,128)S(1)} %get-tuple-element.104) | copy-start | bytes 1179652
  519.6 16.5 %copy-start.61 = (bf16[768,768]{1,0:T(8,128)(2,1)S(1)}, bf16[768,768]{1,0:T(8,128)(2,1)}, u32[]{:S(2)}) copy-start(bf16[768,768]{1,0:T(8,128)(2,1)} %param.27) | copy-start | bytes 3538948
  540.2 91.0 %reduce-scatter.38.cloned.1.call-start = ((), (), s32[]{:S(2)}) async-start(), calls=%async_computation.32 | async-start | bytes 1327104 | tf_op jit(solution)/shard_map/reduce_scatter | solution.py:478
  548.1 6.9 copy-start.37
  548.2 94.8 %reduce-scatter.36.cloned.1.call-start = ((), (), s32[]{:S(2)}) async-start(), calls=%async_computation.31 | async-start | bytes 1327104 | tf_op jit(solution)/shard_map/reduce_scatter | solution.py:478
  555.0 139.6 %reduce-scatter.44.cloned.1.call-start = ((), (), s32[]{:S(2)}) async-start(), calls=%async_computation.35 | async-start | bytes 3981312
  566.9 179.1 %reduce-scatter.42.cloned.1.call-start = ((), (), s32[]{:S(2)}) async-start(), calls=%async_computation.34 | async-start | bytes 3981312
  612.8 4.3 copy-start.30
  612.8 173.2 %reduce-scatter.34.cloned.1.call-start = ((), (), s32[]{:S(2)}) async-start(), calls=%async_computation.30 | async-start | bytes 1327104 | tf_op jit(solution)/shard_map/reduce_scatter | solution.py:478
  617.0 209.2 %reduce-scatter.28.cloned.1.call-start = ((), (), s32[]{:S(2)}) async-start(), calls=%async_computation.27 | async-start | bytes 1327104 | tf_op jit(solution)/shard_map/reduce_scatter | solution.py:478
  618.6 247.6 %reduce-scatter.32.cloned.1.call-start = ((), (), s32[]{:S(2)}) async-start(), calls=%async_computation.29 | async-start | bytes 1327104 | tf_op jit(solution)/shard_map/reduce_scatter | solution.py:478
  622.2 284.3 %reduce-scatter.30.cloned.1.call-start = ((), (), s32[]{:S(2)}) async-start(), calls=%async_computation.28 | async-start | bytes 1327104 | tf_op jit(solution)/shard_map/reduce_scatter | solution.py:478
  625.7 317.7 %reduce-scatter.40.cloned.1.call-start = ((), (), s32[]{:S(2)}) async-start(), calls=%async_computation.33 | async-start | bytes 221184
  626.7 4.4 copy-start.47
  631.1 383.2 %all-reduce.3.cloned.1.call-start = ((), (), s32[]{:S(2)}) async-start(), calls=%async_computation.36 | async-start | bytes 2949120 | tf_op jit(solution)/shard_map/psum | solution.py:492
  644.6 181.7 %copy-start.7 = (f32[2,256,768]{2,1,0:T(8,128)S(1)}, f32[2,256,768]{2,1,0:T(8,128)}, u32[]{:S(2)}) copy-start(f32[2,256,768]{2,1,0:T(8,128)} %copy-done.5) | copy-start | bytes 4718596
  826.3 81.9 %copy-start.33 = (bf16[128,768]{1,0:T(8,128)(2,1)S(1)}, bf16[128,768]{1,0:T(8,128)(2,1)}, u32[]{:S(2)}) copy-start(bf16[128,768]{1,0:T(8,128)(2,1)} %reduce-scatter.26.cloned.1.call-done) | copy-start | bytes 589828
  828.7 80.6 %copy-start.12 = (f32[512,768]{1,0:T(8,128)S(1)}, f32[512,768]{1,0:T(8,128)}, u32[]{:S(2)}) copy-start(f32[512,768]{1,0:T(8,128)} %copy-done.11) | copy-start | bytes 4718596
  1014.3 5.0 copy-start.1
  (41 other events, 76.5 us)
Sparse Core Ops, SparseCore 0:
  81.0 20.9 reduce-scatter.19
  104.1 62.7 all-gather.4
  206.2 59.8 all-gather.2
  283.8 58.8 reduce-scatter.23
  344.9 60.2 reduce-scatter.21
  540.3 22.5 reduce-scatter.25
  566.2 37.3 reduce-scatter.37
  607.2 35.7 reduce-scatter.35
  646.4 48.0 reduce-scatter.43
  697.9 48.0 reduce-scatter.41
  749.2 36.7 reduce-scatter.33
  789.4 36.7 reduce-scatter.27
  829.5 36.7 reduce-scatter.31
  869.7 36.7 reduce-scatter.29
  909.9 33.4 reduce-scatter.39
  947.2 67.0 all-reduce.2

commit v2 on v1

v2 whole, which is shorter than its diff:
```python
from functools import partial

import jax
import jax.numpy as jnp
from jax import lax
from jax.experimental import pallas as pl
from jax.experimental.pallas import tpu as pltpu
from jax.sharding import PartitionSpec as P

H = 12
HD = 64
GROUPS = 4
HG = H // GROUPS
GW = HG * HD

EPSILON = 1e-06
NEGATIVE = -1e30
SCORE_SCALE = 0.125
LOG2E = 1.4426950408889634
GELU_A = 0.7978845608028654
GELU_B = 0.044715
BF = jnp.bfloat16
F32 = jnp.float32
VMEM = 56 << 20


def nt_dot(left, right):
    return lax.dot_general(left, right, (((1,), (1,)), ((), ())), preferred_element_type=F32)


def tn_dot(left, right):
    return lax.dot_general(left, right, (((0,), (0,)), ((), ())), preferred_element_type=F32)


def dot(left, right):
    return jnp.dot(left, right, preferred_element_type=F32)


def sds(shape, dtype):
    return jax.ShapeDtypeStruct(shape, dtype)


def norm_scale(rows):
    return lax.rsqrt(jnp.mean(rows * rows, axis=-1, keepdims=True) + EPSILON)


def norm_back(grad, rows, gain):
    scale = norm_scale(rows)
    inner = grad * gain
    mean = jnp.mean(inner * rows, axis=-1, keepdims=True)
    grad_rows = scale * inner - rows * (scale * scale * scale * mean)
    return grad_rows, jnp.sum(grad * rows * scale, axis=0, keepdims=True)


def gelu(a):
    return 0.5 * a * (1.0 + jnp.tanh(GELU_A * (a + GELU_B * (a * a * a))))


def gelu_both(a):
    square = a * a
    bend = jnp.tanh(GELU_A * (a + GELU_B * (square * a)))
    half = 0.5 * (1.0 + bend)
    slope = half + 0.5 * a * (1.0 - bend * bend) * (GELU_A * (1.0 + 3.0 * GELU_B * square))
    return a * half, slope


def three_parts(x):
    first = x.astype(BF)
    rest = x - first.astype(F32)
    second = rest.astype(BF)
    third = (rest - second.astype(F32)).astype(BF)
    return [first, second, third]


def place(one_hot, x):
    return tn_dot(
        jnp.concatenate([one_hot] * 3, axis=0), jnp.concatenate(three_parts(x), axis=0)
    )


def pick(one_hot, x):
    return dot(jnp.concatenate([one_hot] * 3, axis=1), jnp.concatenate(three_parts(x), axis=0))


def combo(index):
    return lax.rem(lax.div(index, 2), GROUPS), lax.rem(index, 2)


def save_pieces(me, full, parts, pieces):
    rows = full.shape[0] // 2
    thirds = full.shape[1] // (GROUPS * GW)
    for c in range(GROUPS):
        for t in range(thirds):
            at = t * GROUPS * GW + c * GW
            parts[c, :, t * GW : (t + 1) * GW] = full[:, at : at + GW]
    for s, piece in enumerate(pieces):
        c, r = combo(me ^ s)
        piece[...] = parts[c, pl.ds(pl.multiple_of(r * rows, rows), rows), :]


def load_pieces(me, pieces, parts, thirds):
    rows = pieces[0].shape[0]
    for s, piece in enumerate(pieces):
        c, r = combo(me ^ s)
        parts[c, pl.ds(pl.multiple_of(r * rows, rows), rows), :] = piece[...]
    return jnp.concatenate(
        [parts[c, :, t * GW : (t + 1) * GW] for t in range(thirds) for c in range(GROUPS)],
        axis=1,
    )


def stage(body, name, ids, operands, outs, scratch=(), flops=0, grid=None, specs=None):
    kwargs = {}
    if grid is not None:
        kwargs["grid"] = grid
    in_specs = [pl.BlockSpec(memory_space=pltpu.SMEM)]
    for k, operand in enumerate(operands):
        spec = None if specs is None else specs.get(k)
        if spec is None:
            zeros = (0,) * operand.ndim
            spec = pl.BlockSpec(operand.shape, lambda *_, z=zeros: z)
        in_specs.append(spec)
    out_specs = tuple(
        pl.BlockSpec(out.shape, lambda *_, z=(0,) * len(out.shape): z) for out in outs
    )
    moved = sum(a.size * a.dtype.itemsize for a in operands)
    moved += sum(math_prod(a.shape) * a.dtype.itemsize for a in outs)
    return pl.pallas_call(
        body,
        out_shape=tuple(outs),
        in_specs=in_specs,
        out_specs=out_specs,
        scratch_shapes=list(scratch),
        compiler_params=pltpu.CompilerParams(vmem_limit_bytes=VMEM),
        cost_estimate=pl.CostEstimate(flops=flops, bytes_accessed=moved, transcendentals=0),
        name=name,
        **kwargs,
    )(ids, *operands)


def math_prod(shape):
    total = 1
    for size in shape:
        total *= size
    return total


def head_parts(rows):
    lane = lax.broadcasted_iota(jnp.int32, rows.shape, 1)
    zero = jnp.zeros_like(rows)
    return [
        jnp.where((lane >= h * HD) & (lane < (h + 1) * HD), rows, zero) for h in range(HG)
    ]


def pair_mask(row_ref, col_ref, q_at, k_at, bk, bq):
    k_iota = lax.broadcasted_iota(jnp.int32, (bk, bq), 0) + k_at
    q_iota = lax.broadcasted_iota(jnp.int32, (bk, bq), 1) + q_at
    info = row_ref[0:1, pl.ds(q_at, bq)]
    if col_ref is None:
        return (k_iota >= info) & (k_iota <= q_iota)
    return (col_ref[pl.ds(k_at, bk), :] == info) & (k_iota <= q_iota)


def attend_kernel(bq, count, sends, by_column, ids, first_ref, row_ref, *rest):
    rest = list(rest)
    col_ref = rest.pop(0) if by_column else None
    pieces, rest = rest[:count], rest[count:]
    out_pieces, rest = rest[:sends], rest[sends:]
    o_ref, lse_ref, q_s, k_s, v_s, vt_s = rest
    i = pl.program_id(0)
    me = ids[0]
    rows = pieces[0].shape[0]
    bk = bq

    @pl.when(i == 0)
    def _():
        for s in range(count):
            at = pl.ds(pl.multiple_of((me ^ s) * rows, rows), rows)
            q_s[at, :] = pieces[s][:, 0:GW]
            k_s[at, :] = pieces[s][:, GW : 2 * GW]
            v_s[at, :] = pieces[s][:, 2 * GW : 3 * GW]
        vt_s[...] = v_s[...].T

    q_at = pl.multiple_of(i * bq, bq)
    q_heads = head_parts(q_s[pl.ds(q_at, bq), :])

    def step(j, carry):
        k_at = pl.multiple_of(j * bk, bk)
        keys = k_s[pl.ds(k_at, bk), :]
        mask = pair_mask(row_ref, col_ref, q_at, k_at, bk, bq)
        out = []
        for h in range(HG):
            top, total, acc = carry[h]
            scores = nt_dot(keys, q_heads[h]) * (SCORE_SCALE * LOG2E)
            scores = jnp.where(mask, scores, NEGATIVE)
            top_new = jnp.maximum(top, jnp.max(scores, axis=0, keepdims=True))
            weight = jnp.exp2(scores - top_new)
            fade = jnp.exp2(top - top_new)
            total = total * fade + jnp.sum(weight, axis=0, keepdims=True)
            values_t = vt_s[h * HD : (h + 1) * HD, pl.ds(k_at, bk)]
            acc = acc * fade + dot(values_t, weight.astype(BF))
            out.append((top_new, total, acc))
        return tuple(out)

    start = tuple(
        (
            jnp.full((1, bq), NEGATIVE, F32),
            jnp.zeros((1, bq), F32),
            jnp.zeros((HD, bq), F32),
        )
        for _ in range(HG)
    )
    done = lax.fori_loop(first_ref[i], i + 1, step, start)
    outs = jnp.concatenate([acc / total for _, total, acc in done], axis=0)
    o_ref[pl.ds(q_at, bq), :] = outs.T.astype(BF)
    for h in range(HG):
        top, total, _ = done[h]
        lse_ref[h : h + 1, pl.ds(q_at, bq)] = top + jnp.log2(total)

    @pl.when(i == pl.num_programs(0) - 1)
    def _():
        for s in range(sends):
            at = pl.ds(pl.multiple_of((me ^ s) * rows, rows), rows)
            out_pieces[s][...] = o_ref[at, :]


def attend_back_kernel(bq, count, sends, by_column, ids, first_ref, row_ref, *rest):
    rest = list(rest)
    col_ref = rest.pop(0) if by_column else None
    pieces, rest = rest[:count], rest[count:]
    grads, rest = rest[:count], rest[count:]
    o_ref, lse_ref = rest[:2]
    out_pieces, rest = rest[2 : 2 + sends], rest[2 + sends :]
    q_s, k_s, v_s, g_s, dq_s, dk_s, dv_s = rest
    i = pl.program_id(0)
    me = ids[0]
    rows = pieces[0].shape[0]
    bk = bq

    @pl.when(i == 0)
    def _():
        for s in range(count):
            at = pl.ds(pl.multiple_of((me ^ s) * rows, rows), rows)
            q_s[at, :] = pieces[s][:, 0:GW]
            k_s[at, :] = pieces[s][:, GW : 2 * GW]
            v_s[at, :] = pieces[s][:, 2 * GW : 3 * GW]
            g_s[at, :] = grads[s][...]
        dk_s[...] = jnp.zeros_like(dk_s)
        dv_s[...] = jnp.zeros_like(dv_s)

    q_at = pl.multiple_of(i * bq, bq)
    grad = g_s[pl.ds(q_at, bq), :]
    q_heads = head_parts(q_s[pl.ds(q_at, bq), :])
    g_heads = head_parts(grad)
    dots = (grad.astype(F32) * o_ref[pl.ds(q_at, bq), :].astype(F32)).T
    row_dot = [
        jnp.sum(dots[h * HD : (h + 1) * HD, :], axis=0, keepdims=True) for h in range(HG)
    ]
    lse = [lse_ref[h : h + 1, pl.ds(q_at, bq)] for h in range(HG)]

    def step(j, dq):
        k_at = pl.multiple_of(j * bk, bk)
        here = pl.ds(k_at, bk)
        keys = k_s[here, :]
        values = v_s[here, :]
        key_heads = head_parts(keys)
        mask = pair_mask(row_ref, col_ref, q_at, k_at, bk, bq)
        dk = dk_s[here, :]
        dv = dv_s[here, :]
        for h in range(HG):
            scores = nt_dot(keys, q_heads[h]) * (SCORE_SCALE * LOG2E)
            scores = jnp.where(mask, scores - lse[h], NEGATIVE)
            soft = jnp.exp2(scores)
            g_soft = nt_dot(values, g_heads[h])
            g_scores = (soft * (g_soft - row_dot[h])).astype(BF)
            dv = dv + dot(soft.astype(BF), g_heads[h])
            dk = dk + dot(g_scores, q_heads[h])
            dq = dq + tn_dot(g_scores, key_heads[h])
        dk_s[here, :] = dk
        dv_s[here, :] = dv
        return dq

    dq = lax.fori_loop(first_ref[i], i + 1, step, jnp.zeros((bq, GW), F32))
    dq_s[pl.ds(q_at, bq), :] = (dq * SCORE_SCALE).astype(BF)

    @pl.when(i == pl.num_programs(0) - 1)
    def _():
        for s in range(sends):
            at = pl.ds(pl.multiple_of((me ^ s) * rows, rows), rows)
            out_pieces[s][:, 0:GW] = dq_s[at, :]
            out_pieces[s][:, GW : 2 * GW] = (dk_s[at, :] * SCORE_SCALE).astype(BF)
            out_pieces[s][:, 2 * GW : 3 * GW] = dv_s[at, :].astype(BF)


def attend(ids, meta, pieces, bq):
    first, row_info, col_info = meta
    rows = pieces[0].shape[0]
    count, sends = len(pieces), min(len(pieces), 2 * GROUPS)
    length = rows * count
    operands = [first, row_info] + ([] if col_info is None else [col_info]) + list(pieces)
    outs = [sds((rows, GW), BF)] * sends + [sds((length, GW), BF), sds((8, length), F32)]
    got = stage(
        partial(attend_kernel, bq, count, sends, col_info is not None),
        "attend",
        ids,
        operands,
        outs,
        [pltpu.VMEM((length, GW), BF)] * 3 + [pltpu.VMEM((GW, length), BF)],
        flops=length * length * GW * 2,
        grid=(length // bq,),
        specs={0: pl.BlockSpec(memory_space=pltpu.SMEM)},
    )
    return got[:sends], got[sends], got[sends + 1]


def attend_back(ids, meta, pieces, grads, attended, lse, bq):
    first, row_info, col_info = meta
    rows = pieces[0].shape[0]
    count, sends = len(pieces), min(len(pieces), 2 * GROUPS)
    length = rows * count
    operands = [first, row_info] + ([] if col_info is None else [col_info])
    operands += list(pieces) + list(grads) + [attended, lse]
    return stage(
        partial(attend_back_kernel, bq, count, sends, col_info is not None),
        "attend_back",
        ids,
        operands,
        [sds((rows, 3 * GW), BF)] * sends,
        [pltpu.VMEM((length, GW), BF)] * 5 + [pltpu.VMEM((length, GW), F32)] * 2,
        flops=length * length * GW * 5,
        grid=(length // bq,),
        specs={0: pl.BlockSpec(memory_space=pltpu.SMEM)},
    )


def routed_pre_kernel(steps, ids, tok, sel, router, gain, project, *rest):
    pieces = rest[:steps]
    one_hot_ref, picked_ref, normed_ref, parts = rest[steps:]
    seqs, span = sel.shape
    slots = span // 4
    upper = (
        lax.broadcasted_iota(jnp.int32, (span, span), 0)
        <= lax.broadcasted_iota(jnp.int32, (span, span), 1)
    ).astype(F32).astype(BF)
    slot = lax.broadcasted_iota(jnp.int32, (slots, span), 0).astype(F32)
    for q in range(seqs):
        chosen = jnp.broadcast_to(sel[q : q + 1, :].astype(F32), (8, span))
        rank = dot(chosen.astype(BF), upper)[0:1, :] * chosen[0:1, :] - 1.0
        one_hot = (slot == rank).astype(F32).astype(BF)
        one_hot_ref[q * slots : (q + 1) * slots, :] = one_hot
        picked_ref[q * slots : (q + 1) * slots, :] = dot(
            one_hot, tok[q * span : (q + 1) * span, :]
        ).astype(BF)
    picked = picked_ref[...].astype(F32)
    normed = (picked * norm_scale(picked) * gain[...].astype(F32)).astype(BF)
    normed_ref[...] = normed
    save_pieces(ids[0], dot(normed, project[...]).astype(BF), parts, pieces)


def routed_pre(ids, steps, tok, sel, router, gain, project):
    rows, width = sel.shape[0] * sel.shape[1] // 4, tok.shape[1]
    outs = [sds((rows // 2, 3 * GW), BF)] * steps
    outs += [sds((rows, sel.shape[1]), BF), sds((rows, width), BF), sds((rows, width), BF)]
    got = stage(
        partial(routed_pre_kernel, steps),
        "routed_pre",
        ids,
        [tok, sel, router, gain, project],
        outs,
        [pltpu.VMEM((GROUPS, rows, 3 * GW), BF)],
        flops=2 * rows * width * 3 * width,
    )
    return got[:steps], got[steps], got[steps + 1], got[steps + 2]


def routed_mid_kernel(count, ids, *rest):
    pieces = rest[:count]
    output, picked, gain, branch_ref, low_ref, att_ref, parts = rest[count:]
    attended = load_pieces(ids[0], pieces, parts, 1)
    att_ref[...] = attended
    branch = dot(attended, output[...])
    branch_ref[...] = branch
    middle = picked[...].astype(F32) + branch
    low_ref[...] = (middle * norm_scale(middle) * gain[...].astype(F32)).astype(BF)


def routed_mid(ids, pieces, output, picked, gain):
    shape = picked.shape
    return stage(
        partial(routed_mid_kernel, len(pieces)),
        "routed_mid",
        ids,
        list(pieces) + [output, picked, gain],
        [sds(shape, F32), sds(shape, BF), sds(shape, BF)],
        [pltpu.VMEM((GROUPS, shape[0], GW), BF)],
        flops=2 * shape[0] * shape[1] * shape[1],
    )


def hidden_forward_kernel(count, ids, *rest):
    pieces = rest[:count]
    expand, reduce_ref = rest[count : count + 2]
    outs = rest[count + 2 :]
    rows = pieces[0].shape[0]
    low = jnp.concatenate([piece[...] for piece in pieces], axis=0)
    hidden = gelu(dot(low, expand[...])).astype(BF)
    total = dot(hidden, reduce_ref[...]).astype(BF)
    for s, out in enumerate(outs):
        out[...] = total[s * rows : (s + 1) * rows, :]


def hidden_forward(ids, pieces, expand, reduce_part):
    return stage(
        partial(hidden_forward_kernel, len(pieces)),
        "hidden_forward",
        ids,
        list(pieces) + [expand, reduce_part],
        [sds(pieces[0].shape, BF)] * len(pieces),
        flops=4 * len(pieces) * pieces[0].size * expand.shape[1],
    )


def hidden_back_kernel(count, ids, *rest):
    pieces, grads = rest[:count], rest[count : 2 * count]
    expand, reduce_ref = rest[2 * count : 2 * count + 2]
    outs = rest[2 * count + 2 :]
    rows = pieces[0].shape[0]
    low = jnp.concatenate([piece[...] for piece in pieces], axis=0)
    grad = jnp.concatenate([piece[...] for piece in grads], axis=0)
    _, slope = gelu_both(dot(low, expand[...]))
    grad_pre = (nt_dot(grad, reduce_ref[...]) * slope).astype(BF)
    total = nt_dot(grad_pre, expand[...]).astype(BF)
    for s, out in enumerate(outs):
        out[...] = total[s * rows : (s + 1) * rows, :]


def hidden_back(ids, pieces, grads, expand, reduce_part):
    return stage(
        partial(hidden_back_kernel, len(pieces)),
        "hidden_back",
        ids,
        list(pieces) + list(grads) + [expand, reduce_part],
        [sds(pieces[0].shape, BF)] * len(pieces),
        flops=6 * len(pieces) * pieces[0].size * expand.shape[1],
    )


def dense_pre_kernel(steps, shares, ids, tok, one_hot, picked, router, branch, *rest):
    partials = rest[:shares]
    gain, project = rest[shares : shares + 2]
    rest = rest[shares + 2 :]
    pieces = rest[:steps]
    mixed_ref, delta_ref, normed_ref, parts = rest[steps:]
    slots, span = one_hot.shape[0] // 2, one_hot.shape[1]
    delta = branch[...]
    for share in partials:
        delta = delta + share[...].astype(F32)
    delta_ref[...] = delta
    gate = jnp.sum(
        picked[...].astype(F32) * router[...].astype(F32), axis=-1, keepdims=True
    )
    lifted = gate * delta
    for q in range(2):
        at, spots = slice(q * span, (q + 1) * span), slice(q * slots, (q + 1) * slots)
        mixed = tok[at, :].astype(F32) + place(one_hot[spots, :], lifted[spots, :])
        mixed_ref[at, :] = mixed
        normed_ref[at, :] = (mixed * norm_scale(mixed) * gain[...].astype(F32)).astype(BF)
    save_pieces(ids[0], dot(normed_ref[...], project[...]).astype(BF), parts, pieces)


def dense_pre(ids, steps, tok, one_hot, picked, router, branch, partials, gain, project):
    rows, width = tok.shape
    outs = [sds((rows // 2, 3 * GW), BF)] * steps
    outs += [sds(tok.shape, F32), sds(picked.shape, F32), sds(tok.shape, BF)]
    got = stage(
        partial(dense_pre_kernel, steps, len(partials)),
        "dense_pre",
        ids,
        [tok, one_hot, picked, router, branch] + list(partials) + [gain, project],
        outs,
        [pltpu.VMEM((GROUPS, rows, 3 * GW), BF)],
        flops=6 * rows * width * width,
    )
    return got[:steps], got[steps], got[steps + 1], got[steps + 2]


def dense_ffn_kernel(count, steps, split, ids, *rest):
    pieces, rest = rest[:count], rest[count:]
    output, mixed, cot, gain = rest[:4]
    rest = rest[4:]
    weights, rest = rest[:split], rest[split:]
    act_ref, low_ref, back_ref, sum_ref, att_ref, gain_ref = rest[:6]
    g_pieces, rest = rest[6 : 6 + steps], rest[6 + steps :]
    parts, branch_s, delta_s, grad_s = rest[:4]
    n = pl.program_id(0)
    me = ids[0]

    @pl.when(n == 0)
    def _():
        attended = load_pieces(me, pieces, parts, 1)
        att_ref[...] = attended
        branch = dot(attended, output[...])
        branch_s[...] = branch
        middle = mixed[...] + branch
        low_ref[...] = (middle * norm_scale(middle) * gain[...].astype(F32)).astype(BF)
        delta_s[...] = jnp.zeros_like(delta_s)
        grad_s[...] = jnp.zeros_like(grad_s)

    if split == 2:
        expand, reduce_w = weights[0][0], weights[1][0]
    else:
        e_s, r_s = rest[4:]
        rows = weights[0].shape[2]
        for s, weight in enumerate(weights):
            at = pl.ds(pl.multiple_of((me ^ s) * rows, rows), rows)
            e_s[at, :] = weight[0, 0]
            r_s[at, :] = weight[0, 1]
        expand, reduce_w = e_s[...], r_s[...]
    value, slope = gelu_both(dot(low_ref[...], expand))
    delta_s[...] += dot(value.astype(BF), reduce_w)
    grad_pre = (nt_dot(cot[...], reduce_w) * slope).astype(BF)
    grad_s[...] += nt_dot(grad_pre, expand)

    @pl.when(n == pl.num_programs(0) - 1)
    def _():
        middle = mixed[...] + branch_s[...]
        act_ref[...] = (middle + delta_s[...]).astype(BF)
        grad_middle, gain_grad = norm_back(grad_s[...], middle, gain[...].astype(F32))
        gain_ref[...] = jnp.broadcast_to(gain_grad, gain_ref.shape)
        total = cot[...].astype(F32) + grad_middle
        sum_ref[...] = total
        back = total.astype(BF)
        back_ref[...] = back
        save_pieces(me, nt_dot(back, output[...]).astype(BF), parts, g_pieces)


def dense_ffn(ids, steps, pieces, output, mixed, cot, gain, weights):
    rows, width = mixed.shape
    split = len(weights)
    parts_n = weights[0].shape[0]
    hidden = weights[0].shape[-1]
    base = len(pieces) + 4
    specs = {
        base + k: pl.BlockSpec(
            (1,) + w.shape[1:], lambda n, z=(0,) * (w.ndim - 1): (n,) + z
        )
        for k, w in enumerate(weights)
    }
    scratch = [pltpu.VMEM((GROUPS, rows, GW), BF)] + [pltpu.VMEM((rows, width), F32)] * 3
    if split != 2:
        scratch += [pltpu.VMEM((width, hidden), BF)] * 2
    outs = [
        sds((rows, width), BF),
        sds((rows, width), BF),
        sds((rows, width), BF),
        sds((rows, width), F32),
        sds((rows, width), BF),
        sds((8, width), F32),
    ] + [sds((rows // 2, GW), BF)] * steps
    got = stage(
        partial(dense_ffn_kernel, len(pieces), steps, split),
        "dense_ffn",
        ids,
        list(pieces) + [output, mixed, cot, gain] + list(weights),
        outs,
        scratch,
        flops=8 * rows * width * hidden * parts_n + 4 * rows * width * width,
        grid=(parts_n,),
        specs=specs,
    )
    return got[:6], got[6:]


def dense_post_kernel(count, ids, *rest):
    pieces = rest[:count]
    project, gain, mixed, total, one_hot, picked, router, delta = rest[count : count + 8]
    g_mixed_ref, g_proj_ref, g_delta_ref, g_low_ref, g_gate_ref, gain_ref, parts = rest[
        count + 8 :
    ]
    g_proj = load_pieces(ids[0], pieces, parts, 3)
    g_proj_ref[...] = g_proj
    grad_rows, gain_grad = norm_back(
        nt_dot(g_proj, project[...]), mixed[...], gain[...].astype(F32)
    )
    gain_ref[...] = jnp.broadcast_to(gain_grad, gain_ref.shape)
    g_mixed_ref[...] = total[...] + grad_rows
    slots, span = one_hot.shape[0] // 2, one_hot.shape[1]
    gate = jnp.sum(
        picked[...].astype(F32) * router[...].astype(F32), axis=-1, keepdims=True
    )
    for q in range(2):
        at, spots = slice(q * span, (q + 1) * span), slice(q * slots, (q + 1) * slots)
        lifted = pick(one_hot[spots, :], g_mixed_ref[at, :])
        g_delta = gate[spots, :] * lifted
        g_delta_ref[spots, :] = g_delta
        g_low_ref[spots, :] = g_delta.astype(BF)
        g_gate = jnp.sum(lifted * delta[spots, :], axis=-1, keepdims=True)
        g_gate_ref[spots, :] = jnp.broadcast_to(g_gate, (slots, g_gate_ref.shape[1]))


def dense_post(ids, pieces, project, gain, mixed, total, one_hot, picked, router, delta):
    rows, width = mixed.shape
    return stage(
        partial(dense_post_kernel, len(pieces)),
        "dense_post",
        ids,
        list(pieces) + [project, gain, mixed, total, one_hot, picked, router, delta],
        [
            sds((rows, width), F32),
            sds((rows, 3 * width), BF),
            sds(picked.shape, F32),
            sds(picked.shape, BF),
            sds((picked.shape[0], 128), F32),
            sds((8, width), F32),
        ],
        [pltpu.VMEM((GROUPS, rows, 3 * GW), BF)],
        flops=6 * rows * width * width,
    )


def routed_back_kernel(shares, steps, ids, *rest):
    partials = rest[:shares]
    branch, picked, gain, g_delta, output = rest[shares : shares + 5]
    rest = rest[shares + 5 :]
    g_mid_ref, back_ref, gain_ref = rest[:3]
    pieces, parts = rest[3 : 3 + steps], rest[3 + steps]
    grad = partials[0][...].astype(F32)
    for share in partials[1:]:
        grad = grad + share[...].astype(F32)
    middle = picked[...].astype(F32) + branch[...]
    g_middle, gain_grad = norm_back(grad, middle, gain[...].astype(F32))
    gain_ref[...] = jnp.broadcast_to(gain_grad, gain_ref.shape)
    g_mid_ref[...] = g_middle
    back = (g_delta[...] + g_middle).astype(BF)
    back_ref[...] = back
    save_pieces(ids[0], nt_dot(back, output[...]).astype(BF), parts, pieces)


def routed_back(ids, steps, partials, branch, picked, gain, g_delta, output):
    rows, width = branch.shape
    got = stage(
        partial(routed_back_kernel, len(partials), steps),
        "routed_back",
        ids,
        list(partials) + [branch, picked, gain, g_delta, output],
        [sds((rows, width), F32), sds((rows, width), BF), sds((8, width), F32)]
        + [sds((rows // 2, GW), BF)] * steps,
        [pltpu.VMEM((GROUPS, rows, GW), BF)],
        flops=2 * rows * width * width,
    )
    return got[0], got[1], got[2], got[3:]


def routed_post_kernel(count, ids, *rest):
    pieces = rest[:count]
    project, gain, picked, g_mid, g_mixed, one_hot, g_gate, router = rest[count : count + 8]
    out_ref, g_proj_ref, gain_ref, router_ref, parts = rest[count + 8 :]
    g_proj = load_pieces(ids[0], pieces, parts, 3)
    g_proj_ref[...] = g_proj
    rows = picked[...].astype(F32)
    grad_rows, gain_grad = norm_back(
        nt_dot(g_proj, project[...]), rows, gain[...].astype(F32)
    )
    gain_ref[...] = jnp.broadcast_to(gain_grad, gain_ref.shape)
    gate_grad = g_gate[:, 0:1]
    router_ref[...] = jnp.broadcast_to(
        jnp.sum(rows * gate_grad, axis=0, keepdims=True), router_ref.shape
    )
    spread = g_mid[...] + grad_rows + gate_grad * router[...].astype(F32)
    slots, span = one_hot.shape[0] // 2, one_hot.shape[1]
    for q in range(2):
        at, spots = slice(q * span, (q + 1) * span), slice(q * slots, (q + 1) * slots)
        out_ref[at, :] = g_mixed[at, :] + place(one_hot[spots, :], spread[spots, :])


def routed_post(ids, pieces, project, gain, picked, g_mid, g_mixed, one_hot, g_gate, router):
    rows, width = picked.shape
    return stage(
        partial(routed_post_kernel, len(pieces)),
        "routed_post",
        ids,
        list(pieces) + [project, gain, picked, g_mid, g_mixed, one_hot, g_gate, router],
        [
            sds(g_mixed.shape, F32),
            sds((rows, 3 * width), BF),
            sds((8, width), F32),
            sds((8, width), F32),
        ],
        [pltpu.VMEM((GROUPS, rows, 3 * GW), BF)],
        flops=6 * rows * width * width,
    )


def split_rows(me, total, keep, send):
    chips, rows = keep.shape[0], keep.shape[1]
    core = lax.rem(me, 2)
    for c in range(chips):
        mine = pl.multiple_of((2 * c + core) * rows, rows)
        other = pl.multiple_of((2 * c + 1 - core) * rows, rows)
        keep[c] = total[pl.ds(mine, rows), :].astype(BF)
        send[c] = total[pl.ds(other, rows), :].astype(BF)


def hidden_grads_kernel(ids, low, grad, expand, reduce_ref, keep, send, total):
    i = pl.program_id(0)
    hidden = expand.shape[1]

    @pl.when(i == 0)
    def _():
        total[...] = jnp.zeros_like(total)

    value, slope = gelu_both(dot(low[...], expand[...]))
    grad_pre = (nt_dot(grad[...], reduce_ref[...]) * slope).astype(BF)
    total[:, 0:hidden] += tn_dot(low[...], grad_pre)
    total[:, hidden : 2 * hidden] += tn_dot(grad[...], value.astype(BF))

    @pl.when(i == pl.num_programs(0) - 1)
    def _():
        split_rows(ids[0], total, keep, send)


def hidden_grads(ids, wide_count, low, grad, expand, reduce_part):
    width, hidden = expand.shape
    block = min(512, low.shape[0])
    shape = (wide_count // 2, width // wide_count, 2 * hidden)
    row_spec = pl.BlockSpec((block, width), lambda i: (i, 0))
    return stage(
        hidden_grads_kernel,
        "hidden_grads",
        ids,
        [low, grad, expand, reduce_part],
        [sds(shape, BF), sds(shape, BF)],
        [pltpu.VMEM((width, 2 * hidden), F32)],
        flops=8 * low.size * hidden,
        grid=(low.shape[0] // block,),
        specs={0: row_spec, 1: row_spec},
    )


def attend_grads_kernel(vectors, ids, normed, g_proj, att, back, *rest):
    rest = list(rest)
    vecs, rest = rest[:vectors], rest[vectors:]
    keep, send, total = rest
    width = normed.shape[1]
    total[:, 0 : 3 * width] = tn_dot(normed[...], g_proj[...])
    total[:, 3 * width : 4 * width] = tn_dot(att[...], back[...])
    if vectors:
        rows = [vec[0:1, :] for vec in vecs]
        rows.append(jnp.zeros((128 - vectors, width), F32))
        total[:, 4 * width : 4 * width + 128] = jnp.concatenate(rows, axis=0).T
    split_rows(ids[0], total, keep, send)


def attend_grads(ids, wide_count, normed, g_proj, att, back, vecs):
    rows, width = normed.shape
    columns = 4 * width + (128 if vecs else 0)
    shape = (wide_count // 2, width // wide_count, columns)
    return stage(
        partial(attend_grads_kernel, len(vecs)),
        "attend_grads",
        ids,
        [normed, g_proj, att, back] + list(vecs),
        [sds(shape, BF), sds(shape, BF)],
        [pltpu.VMEM((width, columns), F32)],
        flops=8 * rows * width * width,
    )


def join_kernel(chips, ids, keep, came, *outs):
    chip = lax.div(ids[0], 2)
    for s, out in enumerate(outs):
        at = chip ^ s
        out[...] = (keep[at].astype(F32) + came[at].astype(F32)).astype(BF)


def reduce_wide(ids, wide_count, keep, send):
    came = lax.ppermute(send, "wide", [(j, j ^ 1) for j in range(wide_count)])
    chips = keep.shape[0]
    parts = stage(
        partial(join_kernel, chips), "join", ids, [keep, came], [sds(keep.shape[1:], BF)] * chips
    )
    return [parts[0]] + [
        lax.ppermute(parts[s], "wide", [(j, j ^ (2 * s)) for j in range(wide_count)])
        for s in range(1, chips)
    ]


def sum_terms(terms):
    total = terms[0].astype(F32)
    for term in terms[1:]:
        total = total + term.astype(F32)
    return total


def sum_split_kernel(count, ids, *rest):
    terms, outs, total = rest[:count], rest[count:-1], rest[-1]
    got = terms[0][...].astype(F32)
    for term in terms[1:]:
        got = got + term[...].astype(F32)
    total[...] = got
    rows = outs[0].shape[0]
    for s, out in enumerate(outs):
        at = pl.multiple_of((ids[1] ^ s) * rows, rows)
        out[...] = total[pl.ds(at, rows), :].astype(BF)


def sum_kernel(ids, *rest):
    got = rest[0][...].astype(F32)
    for term in rest[1:-1]:
        got = got + term[...].astype(F32)
    rest[-1][...] = got.astype(BF)


def gather_out_kernel(count, ids, *rest):
    pieces, outs = rest[:count], rest[count:]
    rows = pieces[0].shape[0]
    for s, piece in enumerate(pieces):
        at = pl.ds(pl.multiple_of((ids[1] ^ s) * rows, rows), rows)
        low = 0
        for out in outs:
            columns = out.shape[1]
            out[at, :] = piece[:, low : low + columns].astype(F32)
            low += columns


def reduce_narrow(ids, terms, widths):
    narrow_count = lax.axis_size("narrow")
    rows, columns = terms[0].shape
    if rows % (8 * narrow_count):
        total = lax.psum(sum_terms(terms).astype(BF), "narrow").astype(F32)
        outs, low = [], 0
        for size in widths:
            outs.append(total[:, low : low + size])
            low += size
        return outs
    share = rows // narrow_count
    parts = stage(
        partial(sum_split_kernel, len(terms)),
        "sum_split",
        ids,
        terms,
        [sds((share, columns), BF)] * narrow_count,
        [pltpu.VMEM((rows, columns), F32)],
    )
    came = [parts[0]] + [narrow_step(parts[s], s) for s in range(1, narrow_count)]
    (total,) = stage(sum_kernel, "sum_terms", ids, came, [sds((share, columns), BF)])
    pieces = [total] + [narrow_step(total, s) for s in range(1, narrow_count)]
    return stage(
        partial(gather_out_kernel, narrow_count),
        "gather_out",
        ids,
        pieces,
        [sds((rows, size), F32) for size in widths],
    )


def narrow_step(x, s):
    return lax.ppermute(x, "narrow", [(j, j ^ s) for j in range(lax.axis_size("narrow"))])


def narrow_gather(x):
    return [x] + [narrow_step(x, s) for s in range(1, lax.axis_size("narrow"))]


def narrow_return(parts):
    return [parts[0]] + [narrow_step(parts[s], s) for s in range(1, len(parts))]


def exchange(pieces):
    wide_count = lax.axis_size("wide")
    return [pieces[0]] + [
        lax.ppermute(pieces[s], "wide", [(j, j ^ s) for j in range(wide_count)])
        for s in range(1, len(pieces))
    ]


def gather_hidden_weights(expand, reduce_part):
    wide_count = lax.axis_size("wide")
    here = lax.axis_index("wide")
    width, hidden = expand.shape
    rows = width // wide_count
    if width != hidden or rows % 16:
        return [
            lax.all_gather(expand, "narrow", axis=0),
            lax.all_gather(reduce_part, "narrow", axis=0),
        ]
    share = jnp.stack(
        [
            lax.dynamic_slice_in_dim(expand, here * rows, rows, 0),
            lax.dynamic_slice_in_dim(reduce_part, here * rows, rows, 0),
        ]
    )
    mine = lax.all_gather(share, "narrow", axis=0)
    pieces = [None] * wide_count
    pieces[0] = mine
    for s in range(2, wide_count, 2):
        pieces[s] = lax.ppermute(mine, "wide", [(j, j ^ s) for j in range(wide_count)])
    for s in range(1, wide_count, 2):
        pieces[s] = lax.ppermute(
            pieces[s - 1], "wide", [(j, j ^ 1) for j in range(wide_count)]
        )
    return pieces


def on_device(
    tokens,
    cotangent,
    selected,
    segments,
    router_vector,
    project_routed,
    output_routed,
    prenorm_routed,
    midnorm_routed,
    expand_routed,
    reduce_routed,
    project_dense,
    output_dense,
    prenorm_dense,
    midnorm_dense,
    expand_dense,
    reduce_dense,
):
    seq_count, span_rows, width = tokens.shape
    row_length = selected.shape[1]
    hidden = expand_dense.shape[1]
    wide_count = lax.axis_size("wide")
    here = lax.axis_index("wide")
    slot_count = span_rows // 4
    bq_dense = min(256, row_length)
    bq_routed = min(256, slot_count * wide_count)
    ids = jnp.stack([here, lax.axis_index("narrow")]).astype(jnp.int32)
    router = router_vector[None]
    gains = [
        gain[None] for gain in (prenorm_routed, midnorm_routed, prenorm_dense, midnorm_dense)
    ]
    tok = tokens.reshape(-1, width)
    cot = cotangent.reshape(-1, width)

    ffn_weights = gather_hidden_weights(expand_dense, reduce_dense)
    cot_all = lax.all_gather(cot, "narrow", axis=0, tiled=True)

    mine = here % seq_count
    seq_segments = lax.dynamic_slice_in_dim(segments, mine, 1, 0)[0]
    seq_selected = lax.dynamic_slice_in_dim(selected, mine, 1, 0)[0].reshape(wide_count, span_rows)
    upper = (
        lax.broadcasted_iota(jnp.int32, (span_rows, span_rows), 0)
        <= lax.broadcasted_iota(jnp.int32, (span_rows, span_rows), 1)
    ).astype(BF)
    slots = jnp.arange(slot_count, dtype=jnp.int32)
    seq_rank = jnp.dot(seq_selected.astype(BF), upper, preferred_element_type=F32)
    seq_rank = jnp.where(seq_selected > 0, seq_rank.astype(jnp.int32) - 1, -1)
    slot_segments = (
        jnp.sum(
            jnp.where(
                seq_rank[:, None, :] == slots[None, :, None],
                seq_segments.reshape(wide_count, 1, span_rows) + 1,
                0,
            ),
            axis=-1,
        )
        - 1
    ).reshape(-1)
    meta_routed = (
        jnp.zeros((slot_segments.shape[0] // bq_routed,), jnp.int32),
        jnp.broadcast_to(slot_segments[None], (8, slot_segments.shape[0])),
        slot_segments[:, None],
    )
    starts = sum(
        jnp.where(seq_segments == value, jnp.sum((seq_segments < value).astype(jnp.int32)), 0)
        for value in range(1, 4)
    )
    meta_dense = (
        starts[::bq_dense] // bq_dense,
        jnp.broadcast_to(starts[None], (8, row_length)),
        None,
    )

    own_selected = lax.dynamic_slice_in_dim(selected, here * span_rows, span_rows, 1)
    pieces, one_hot, picked, normed_r = routed_pre(
        ids, wide_count, tok, own_selected, router, gains[0], project_routed
    )
    x_r = exchange(pieces)
    pieces, att_seq_r, lse_r = attend(ids, meta_routed, x_r, bq_routed)
    branch_r, low_r, att_r = routed_mid(ids, exchange(pieces), output_routed, picked, gains[1])
    low_pieces = narrow_gather(low_r)
    partials = narrow_return(hidden_forward(ids, low_pieces, expand_routed, reduce_routed))

    pieces, mixed, delta_r, normed_d = dense_pre(
        ids,
        wide_count,
        tok,
        one_hot,
        picked,
        router,
        branch_r,
        partials,
        gains[2],
        project_dense,
    )
    x_d = exchange(pieces)
    pieces, att_seq_d, lse_d = attend(ids, meta_dense, x_d, bq_dense)
    (activations, low_d, back_d, sum_d, att_d, mid_gain_d), pieces = dense_ffn(
        ids, wide_count, exchange(pieces), output_dense, mixed, cot, gains[3], ffn_weights
    )
    low_all = lax.all_gather(low_d, "narrow", axis=0, tiled=True)
    pieces = attend_back(ids, meta_dense, x_d, exchange(pieces), att_seq_d, lse_d, bq_dense)
    g_mixed, g_proj_d, g_delta, g_low, g_gate, pre_gain_d = dense_post(
        ids,
        exchange(pieces),
        project_dense,
        gains[2],
        mixed,
        sum_d,
        one_hot,
        picked,
        router,
        delta_r,
    )
    keep, send = hidden_grads(ids, wide_count, low_all, cot_all, expand_dense, reduce_dense)
    ffn_d = reduce_wide(ids, wide_count, keep, send)

    g_pieces = narrow_gather(g_low)
    partials = narrow_return(
        hidden_back(ids, low_pieces, g_pieces, expand_routed, reduce_routed)
    )
    g_mid_r, back_r, mid_gain_r, pieces = routed_back(
        ids, wide_count, partials, branch_r, picked, gains[1], g_delta, output_routed
    )
    keep, send = attend_grads(ids, wide_count, normed_d, g_proj_d, att_d, back_d, [])
    att_terms_d = reduce_wide(ids, wide_count, keep, send)
    keep, send = hidden_grads(
        ids,
        wide_count,
        jnp.concatenate(low_pieces, axis=0),
        jnp.concatenate(g_pieces, axis=0),
        expand_routed,
        reduce_routed,
    )
    ffn_r = reduce_wide(ids, wide_count, keep, send)
    pieces = attend_back(ids, meta_routed, x_r, exchange(pieces), att_seq_r, lse_r, bq_routed)
    tokens_gradient, g_proj_r, pre_gain_r, router_grad = routed_post(
        ids,
        exchange(pieces),
        project_routed,
        gains[0],
        picked,
        g_mid_r,
        g_mixed,
        one_hot,
        g_gate,
        router,
    )
    keep, send = attend_grads(
        ids,
        wide_count,
        normed_r,
        g_proj_r,
        att_r,
        back_r,
        [pre_gain_r, mid_gain_r, pre_gain_d, mid_gain_d, router_grad],
    )
    att_terms_r = reduce_wide(ids, wide_count, keep, send)

    project_d_grad, output_d_grad = reduce_narrow(ids, att_terms_d, [3 * width, width])
    project_r_grad, output_r_grad, vectors = reduce_narrow(
        ids, att_terms_r, [3 * width, width, 128]
    )
    ffn_r_sum, ffn_d_sum = sum_terms(ffn_r), sum_terms(ffn_d)
    return (
        activations.reshape(tokens.shape),
        tokens_gradient.reshape(tokens.shape),
        vectors[:, 4],
        project_r_grad,
        output_r_grad,
        vectors[:, 0],
        vectors[:, 1],
        ffn_r_sum[:, :hidden],
        ffn_r_sum[:, hidden:].T,
        project_d_grad,
        output_d_grad,
        vectors[:, 2],
        vectors[:, 3],
        ffn_d_sum[:, :hidden],
        ffn_d_sum[:, hidden:].T,
    )


def solution(mesh):
    return jax.shard_map(
        on_device,
        mesh=mesh,
        in_specs=(
            P("narrow", "wide", None),
            P("narrow", "wide", None),
            P("narrow", None),
            P("narrow", None),
            P(),
            P(),
            P(),
            P(),
            P(),
            P(None, "narrow"),
            P("narrow", None),
            P(),
            P(),
            P(),
            P(),
            P(None, "narrow"),
            P("narrow", None),
        ),
        out_specs=(
            P("narrow", "wide", None),
            P("narrow", "wide", None),
            P("wide"),
            P("wide", None),
            P("wide", None),
            P("wide"),
            P("wide"),
            P("wide", "narrow"),
            P("narrow", "wide"),
            P("wide", None),
            P("wide", None),
            P("wide"),
            P("wide"),
            P("wide", "narrow"),
            P("narrow", "wide"),
        ),
        check_vma=False,
    )
```

time: 1030 us -> 608 us (0.59)
  waiting for transfers between devices: 611 us -> 231 us
  Pallas kernels: 54.4 us -> 183 us
  starting transfers between devices: 24 us -> 136 us
  matrix products: 96.4 us -> 0.15 us
  blocking collectives: 89.6 us -> 0 us
  local copies, waits for them, and re-layouts: 106 us -> 26.5 us
  other arithmetic: 29.1 us -> 6.97 us
    reduce_scatter x10 -> x0, waiting for transfers between devices: 285 us -> none  [the longest x6 164 us: scatter(): lax.psum_scatter(grad.astype(BF), 'wide', scatter_dimension=dimension, ti...]
    ppermute x0 -> x103, waiting for transfers between devices: none -> 231 us  [the longest x56 134 us: exchange(): lax.ppermute(pieces[s], 'wide', [(j, j ^ s) for j in range(wide_count)])]
    ppermute x0 -> x103, starting transfers between devices: none -> 136 us  [the longest x56 58.8 us: exchange(): lax.ppermute(pieces[s], 'wide', [(j, j ^ s) for j in range(wide_count)])]
    unnamed x19 -> x3, waiting for transfers between devices: 131 us -> 0.05 us
    pallas_call x4 -> x27, Pallas kernels: 54.4 us -> 183 us  [stage(): pl.pallas_call(body, out_shape=tuple(outs), in_specs=in_specs, out_specs=...]
    dot_general x33 -> x0, matrix products: 96.3 us -> none  [the longest x2 12.5 us: mlp_forward(): jnp.dot(gathered, expand_part, preferred_element_type=jnp.float32)]
    all_to_all x5 -> x0, waiting for transfers between devices: 85.6 us -> none  [exchange(): return lax.all_to_all(parts, 'wide', 0, 0)]
    psum x1 -> x0, waiting for transfers between devices: 57.6 us -> none  [on_device(): summed = [lax.psum(share, 'narrow').astype(F32) for share in shares]]
  transfers between devices with their start and end apart: 21 -> 106, of which waited for: 18 -> 49; matrix products, arithmetic and copies ran while one was open for 14% -> 3% of each run, Pallas kernels for 2% -> 31%
where the time goes in v2:
time: 608 us; the launch traced here: 599 us
  waiting for transfers between devices  231 us (38%)
  Pallas kernels  183 us (30%)
  starting transfers between devices  136 us (22%)
  local copies, waits for them, and re-layouts  26.5 us (4%)
  between operations  15 us (2%)
  other arithmetic  6.97 us (1%)
    pallas_call x27, Pallas kernels, stage(): pl.pallas_call(body, out_shape=tuple(outs), in_specs=in_specs, out_specs=...  183 us
    ppermute x56, waiting for transfers between devices, exchange(): lax.ppermute(pieces[s], 'wide', [(j, j ^ s) for j in range(wide_count)])  134 us
    ppermute x24, waiting for transfers between devices, narrow_step(): lax.ppermute(x, 'narrow', [(j, j ^ s) for j in range(lax.axis_size('narro...  86.4 us
    ppermute x56, starting transfers between devices, exchange(): lax.ppermute(pieces[s], 'wide', [(j, j ^ s) for j in range(wide_count)])  58.8 us
    ppermute x24, starting transfers between devices, narrow_step(): lax.ppermute(x, 'narrow', [(j, j ^ s) for j in range(lax.axis_size('narro...  56.4 us
    ppermute x12, starting transfers between devices, reduce_wide(): lax.ppermute(parts[s], 'wide', [(j, j ^ 2 * s) for j in range(wide_count)])  15.8 us
    unnamed x218, local copies, waits for them, and re-layouts  13.5 us
  transfers between devices with their start and end apart: 106, of which 49 were waited for; matrix products, arithmetic and copies ran while one was open for 3% of the time, Pallas kernels for 31%

profile of v2, /device:TPU:0, one launch (start us, length us, event | category | flops | bytes accessed | tf_op | source)
XLA Modules:
  0.0 598.9 jit_solution(4196796739409178266)
XLA Ops:
  13.4 4.4 routed_pre.1
  33.6 4.5 attend.2
  55.6 13.2 %collective-permute-done.14.rest_1_ = bf16[128,768]{1,0:T(8,128)(2,1)S(1)} collective-permute-done((bf16[128,768]{1,0:T(8,128)(2,1)}, bf16[128,768]{1,0:T(8,128)(2,1)S(1)}, u32[]{:S(2)}, u32[]{:S(2)}) %collective-permute-start.14) | collective-permute-done | bytes 196640 | tf_op jit(solution)/shard_map/ppermute | solution.py:859
  68.8 9.3 %collective-permute-done.15.rest_2_ = bf16[128,768]{1,0:T(8,128)(2,1)S(1)} collective-permute-done((bf16[128,768]{1,0:T(8,128)(2,1)}, bf16[128,768]{1,0:T(8,128)(2,1)S(1)}, u32[]{:S(2)}, u32[]{:S(2)}) %collective-permute-start.15) | collective-permute-done | bytes 196640 | tf_op jit(solution)/shard_map/ppermute | solution.py:859
  82.1 4.3 hidden_forward.1
  86.4 15.5 %collective-permute-start.17 = (bf16[128,768]{1,0:T(8,128)(2,1)}, bf16[128,768]{1,0:T(8,128)(2,1)S(1)}, u32[]{:S(2)}, u32[]{:S(2)}) collective-permute-start(bf16[128,768]{1,0:T(8,128)(2,1)} %get-tuple-element.177), channel_id=1, source_target_pairs={{0,1},{1,0},{2,3},{3,2},{4,5},{5,4},{6,7},{7,6},{8,9},{9,8},{10,11... | collective-permute-start | bytes 589832 | tf_op jit(solution)/shard_map/ppermute | solution.py:859
  106.2 10.6 %collective-permute-done.17.rest_1_ = bf16[128,768]{1,0:T(8,128)(2,1)S(1)} collective-permute-done((bf16[128,768]{1,0:T(8,128)(2,1)}, bf16[128,768]{1,0:T(8,128)(2,1)S(1)}, u32[]{:S(2)}, u32[]{:S(2)}) %collective-permute-start.17) | collective-permute-done | bytes 196640 | tf_op jit(solution)/shard_map/ppermute | solution.py:859
  119.6 6.2 %collective-permute-done.18.rest_2_ = bf16[128,768]{1,0:T(8,128)(2,1)S(1)} collective-permute-done((bf16[128,768]{1,0:T(8,128)(2,1)}, bf16[128,768]{1,0:T(8,128)(2,1)S(1)}, u32[]{:S(2)}, u32[]{:S(2)}) %collective-permute-start.18) | collective-permute-done | bytes 196640 | tf_op jit(solution)/shard_map/ppermute | solution.py:859
  125.8 4.1 collective-permute-done.19.rest_3_
  130.6 7.9 %dense_pre.1 = (bf16[256,576]{1,0:T(8,128)(2,1)}, bf16[256,576]{1,0:T(8,128)(2,1)}, bf16[256,576]{1,0:T(8,128)(2,1)}, bf16[256,576]{1,0:T(8,128)(2,1)}, bf16[256...) custom-call(s32[2]{0:T(128)} %pad_add_fusion.ids, ...), custom_call_target="tpu_custom_call" | custom-call | flops 1811939328 | bytes 10882048 | tf_op jit(solution)/shard_map/dense_pre/pallas_call | solution.py:128
  141.4 24.4 %collective-permute-done.21.rest_2_ = bf16[256,576]{1,0:T(8,128)(2,1)S(1)} collective-permute-done((bf16[256,576]{1,0:T(8,128)(2,1)}, bf16[256,576]{1,0:T(8,128)(2,1)S(1)}, u32[]{:S(2)}, u32[]{:S(2)}) %collective-permute-start.21) | collective-permute-done | bytes 294944 | tf_op jit(solution)/shard_map/ppermute | solution.py:873
  167.7 3.5 collective-permute-start.24
  174.9 11.9 %collective-permute-done.24.rest_5_ = bf16[256,576]{1,0:T(8,128)(2,1)S(1)} collective-permute-done((bf16[256,576]{1,0:T(8,128)(2,1)}, bf16[256,576]{1,0:T(8,128)(2,1)S(1)}, u32[]{:S(2)}, u32[]{:S(2)}) %collective-permute-start.24) | collective-permute-done | bytes 294944 | tf_op jit(solution)/shard_map/ppermute | solution.py:873
  191.6 6.2 %collective-permute-done.26.rest_7_ = bf16[256,576]{1,0:T(8,128)(2,1)} collective-permute-done((bf16[256,576]{1,0:T(8,128)(2,1)}, bf16[256,576]{1,0:T(8,128)(2,1)}, u32[]{:S(2)}, u32[]{:S(2)}) %collective-permute-start.26) | collective-permute-done | bytes 294944 | tf_op jit(solution)/shard_map/ppermute | solution.py:873
  198.3 16.1 %attend.3 = (bf16[256,192]{1,0:T(8,128)(2,1)}, bf16[256,192]{1,0:T(8,128)(2,1)}, bf16[256,192]{1,0:T(8,128)(2,1)}, bf16[256,192]{1,0:T(8,128)(2,1)}, bf16[256,19...) custom-call(s32[2]{0:T(128)} %pad_add_fusion.ids, ...), custom_call_target="tpu_custom_call" | custom-call | flops 1610612736 | bytes 4063264 | tf_op jit(solution)/shard_map/attend/pallas_call | solution.py:128
  214.4 3.3 collective-permute-start.27
  220.3 4.6 collective-permute-done.28.rest_2_
  225.4 5.4 collective-permute-done.29.rest_3_
  230.8 5.6 collective-permute-done.30.rest_4_
  236.4 5.3 collective-permute-done.31.rest_5_
  242.9 5.0 collective-permute-done.32.rest_6_
  249.0 5.1 collective-permute-done.33.rest_7_
  254.7 21.5 %dense_ffn.1 = (bf16[512,768]{1,0:T(8,128)(2,1)}, bf16[512,768]{1,0:T(8,128)(2,1)}, bf16[512,768]{1,0:T(8,128)(2,1)}, f32[512,768]{1,0:T(8,128)}, bf16[512,768]{...) custom-call(s32[2]{0:T(128)} %pad_add_fusion.ids, ...), custom_call_target="tpu_custom_call" | custom-call | flops 10871635968 | bytes 19293696 | tf_op jit(solution)/shard_map/dense_ffn/pallas_call | solution.py:128
  284.8 7.2 %collective-permute-done.45.rest_13_ = bf16[256,192]{1,0:T(8,128)(2,1)S(1)} collective-permute-done((bf16[256,192]{1,0:T(8,128)(2,1)}, bf16[256,192]{1,0:T(8,128)(2,1)S(1)}, u32[]{:S(2)}, u32[]{:S(2)}) %collective-permute-start.45) | collective-permute-done | bytes 98336 | tf_op jit(solution)/shard_map/ppermute | solution.py:873
  292.7 26.4 %attend_back.2 = (bf16[256,576]{1,0:T(8,128)(2,1)}, bf16[256,576]{1,0:T(8,128)(2,1)}, bf16[256,576]{1,0:T(8,128)(2,1)}, bf16[256,576]{1,0:T(8,128)(2,1)}, bf16[2...) custom-call(s32[2]{0:T(128)} %pad_add_fusion.ids, ...), custom_call_target="tpu_custom_call" | custom-call | flops 4026531840 | bytes 6422560 | tf_op jit(solution)/shard_map/attend_back/pallas_call | solution.py:128
  319.2 6.0 collective-permute-start.48
  330.5 5.4 collective-permute-done.49.rest_2_
  335.9 5.7 collective-permute-done.50.rest_3_
  341.6 16.3 %collective-permute-done.52.rest_5_ = bf16[256,576]{1,0:T(8,128)(2,1)S(1)} collective-permute-done((bf16[256,576]{1,0:T(8,128)(2,1)}, bf16[256,576]{1,0:T(8,128)(2,1)S(1)}, u32[]{:S(2)}, u32[]{:S(2)}) %collective-permute-start.52) | collective-permute-done | bytes 294944 | tf_op jit(solution)/shard_map/ppermute | solution.py:873
  358.9 8.3 %dense_post.1 = (f32[512,768]{1,0:T(8,128)}, bf16[512,2304]{1,0:T(8,128)(2,1)}, f32[128,768]{1,0:T(8,128)}, bf16[128,768]{1,0:T(8,128)(2,1)}, f32[128,128]{1,0:T(8,128)}, /*index=5*/f32[8,768]{1,0:T(8,128)}) custom-call(s32[2]{0:T(128)} %pad_add_fusion.ids, bf16[256,576]{1,0:T(8,128)(2,1)} %get-tuple-element.208.rest_0_, bf16[256,576]{1,0:T(8,128)(2,1)} %copy-done.17, ...), custom_call_target="tpu_custom_call" | custom-call | flops 1811939328 | bytes 14314496 | tf_op jit(solution)/shard_map/dense_post/pallas_call | solution.py:128
  371.7 6.8 %collective-permute-done.55.rest_5_ = bf16[128,768]{1,0:T(8,128)(2,1)S(1)} collective-permute-done((bf16[128,768]{1,0:T(8,128)(2,1)}, bf16[128,768]{1,0:T(8,128)(2,1)S(1)}, u32[]{:S(2)}, u32[]{:S(2)}) %collective-permute-start.55) | collective-permute-done | bytes 196640 | tf_op jit(solution)/shard_map/ppermute | solution.py:859
  378.5 6.2 %collective-permute-done.56.rest_6_ = bf16[128,768]{1,0:T(8,128)(2,1)S(1)} collective-permute-done((bf16[128,768]{1,0:T(8,128)(2,1)}, bf16[128,768]{1,0:T(8,128)(2,1)S(1)}, u32[]{:S(2)}, u32[]{:S(2)}) %collective-permute-start.56) | collective-permute-done | bytes 196640 | tf_op jit(solution)/shard_map/ppermute | solution.py:859
  386.1 5.1 hidden_back.1
  397.6 8.1 %attend_grads.3 = (bf16[4,96,3072]{2,1,0:T(8,128)(2,1)}, bf16[4,96,3072]{2,1,0:T(8,128)(2,1)}) custom-call(s32[2]{0:T(128)} %pad_add_fusion.ids, bf16[512,768]{1,0:T(8,128)(2,1)} %get-tuple-element.274.normed, bf16[512,2304]{1,0:T(8,128)(2,1)} %get-tuple-element.275.g_proj, bf16[512,768]{1,0:T(8,128)(2,1)} %get-tuple-element.276.att, ...), custom_call_target="tpu_custom_call" | custom-call | flops 2415919104 | bytes 9437184 | tf_op jit(solution)/shard_map/attend_grads/pallas_call | solution.py:128
  405.7 6.1 %collective-permute-done.59.rest_2_ = bf16[128,768]{1,0:T(8,128)(2,1)S(1)} collective-permute-done((bf16[128,768]{1,0:T(8,128)(2,1)}, bf16[128,768]{1,0:T(8,128)(2,1)S(1)}, u32[]{:S(2)}, u32[]{:S(2)}) %collective-permute-start.59) | collective-permute-done | bytes 196640 | tf_op jit(solution)/shard_map/ppermute | solution.py:859
  412.6 3.5 routed_back.1
  427.3 6.6 %attend_back.3 = (bf16[64,576]{1,0:T(8,128)(2,1)}, bf16[64,576]{1,0:T(8,128)(2,1)}, bf16[64,576]{1,0:T(8,128)(2,1)}, bf16[64,576]{1,0:T(8,128)(2,1)}, bf16[64,57...) custom-call(s32[2]{0:T(128)} %pad_add_fusion.ids, ...), custom_call_target="tpu_custom_call" | custom-call | flops 251658240 | bytes 1607688 | tf_op jit(solution)/shard_map/attend_back/pallas_call | solution.py:128
  442.0 3.4 collective-permute-done.73.rest_6_
  447.2 6.3 %routed_post.1 = (f32[512,768]{1,0:T(8,128)}, bf16[128,2304]{1,0:T(8,128)(2,1)}, f32[8,768]{1,0:T(8,128)}, f32[8,768]{1,0:T(8,128)}) custom-call(s32[2]{0:T(128)} %pad_add_fusion.ids, bf16[64,576]{1,0:T(8,128)(2,1)} %get-tuple-element.234.rest_0_, bf16[64,576]{1,0:T(8,128)(2,1)} %copy-done.55, bf16[64,576]{1,0:T(8,128)(2,1)} %copy-done.56, ...), custom_call_target="tpu_custom_call" | custom-call | flops 452984832 | bytes 8637440 | tf_op jit(solution)/shard_map/routed_post/pallas_call | solution.py:128
  453.5 6.3 %attend_grads.2 = (bf16[4,96,3200]{2,1,0:T(8,128)(2,1)}, bf16[4,96,3200]{2,1,0:T(8,128)(2,1)}) custom-call(s32[2]{0:T(128)} %pad_add_fusion.ids, bf16[128,768]{1,0:T(8,128)(2,1)} %get-tuple-element.246.normed, bf16[128,2304]{1,0:T(8,128)(2,1)} %get-tuple-element.247.g_proj, bf16[128,768]{1,0:T(8,128)(2,1)} %get-tuple-element.248.att, ...), custom_call_target="tpu_custom_call" | custom-call | flops 603979776 | bytes 6217728 | tf_op jit(solution)/shard_map/attend_grads/pallas_call | solution.py:128
  461.5 4.3 join.6
  469.9 7.1 %hidden_grads.2 = (bf16[4,96,1536]{2,1,0:T(8,128)(2,1)}, bf16[4,96,1536]{2,1,0:T(8,128)(2,1)}) custom-call(s32[2]{0:T(128)} %pad_add_fusion.ids, bf16[512,768]{1,0:T(8,128)(2,1)} %pad_maximum_fusion.low, bf16[512,768]{1,0:T(8,128)(2,1)} %pad_maximum_fusion.1.grad, bf16[768,768]{1,0:T(8,128)(2,1)} %expand.2, bf16[768,768]{1,0:T(8,128)(2,1)} %reduce_ref.2), custom_call_target="tpu_custom_call" | custom-call | flops 2415919104 | bytes 6291456 | tf_op jit(solution)/shard_map/hidden_grads/pallas_call | solution.py:128
  479.9 4.0 join.4
  486.0 7.8 %collective-permute-done.91.rest_2_ = bf16[96,3072]{1,0:T(8,128)(2,1)S(1)} collective-permute-done((bf16[96,3072]{1,0:T(8,128)(2,1)}, bf16[96,3072]{1,0:T(8,128)(2,1)S(1)}, u32[]{:S(2)}, u32[]{:S(2)}) %collective-permute-start.91) | collective-permute-done | bytes 589856 | tf_op jit(solution)/shard_map/ppermute | solution.py:784
  497.7 15.4 %hidden_grads.3 = (bf16[4,96,1536]{2,1,0:T(8,128)(2,1)}, bf16[4,96,1536]{2,1,0:T(8,128)(2,1)}) custom-call(s32[2]{0:T(128)} %pad_add_fusion.ids, bf16[2048,768]{1,0:T(8,128)(2,1)} %all-gather.5.cloned.1.call-done.low, bf16[2048,768]{1,0:T(8,128)(2,1)} %all-gather.7.cloned.1.call-done.grad, bf16[768,768]{1,0:T(8,128)(2,1)} %expand.3, bf16[768,768]{1,0:T(8,128)(2,1)} %reduce_ref.3), custom_call_target="tpu_custom_call" | custom-call | flops 9663676416 | bytes 11010048 | tf_op jit(solution)/shard_map/hidden_grads/pallas_call | solution.py:128
  535.7 9.0 %collective-permute-done.94.rest_2_ = bf16[24,3072]{1,0:T(8,128)(2,1)S(1)} collective-permute-done((bf16[24,3072]{1,0:T(8,128)(2,1)S(1)}, bf16[24,3072]{1,0:T(8,128)(2,1)S(1)}, u32[]{:S(2)}, u32[]{:S(2)}) %collective-permute-start.94) | collective-permute-done | bytes 147488 | tf_op jit(solution)/shard_map/ppermute | solution.py:859
  571.4 3.3 collective-permute-done.97.rest_2_
  581.3 4.2 collective-permute-done.83.rest_2_
  (445 shorter events, 196.7 us)
Async XLA Ops:
  7.2 97.2 %all-gather.9.cloned.1.call-start = ((), (), s32[]{:S(2)}) async-start(), calls=%async_computation.2 | async-start | bytes 1474560 | tf_op jit(solution)/shard_map/all_gather | solution.py:894
  9.0 488.7 %all-gather.7.cloned.1.call-start = ((), (), s32[]{:S(2)}) async-start(), calls=%async_computation.1 | async-start | bytes 3932160 | tf_op jit(solution)/shard_map/all_gather | solution.py:942
  22.8 474.9 %all-gather.5.cloned.1.call-start = ((), (), s32[]{:S(2)}) async-start(), calls=%async_computation | async-start | bytes 3932160 | tf_op jit(solution)/shard_map/all_gather | solution.py:1007
  51.2 17.6 %collective-permute-start.14 = (bf16[128,768]{1,0:T(8,128)(2,1)}, bf16[128,768]{1,0:T(8,128)(2,1)S(1)}, u32[]{:S(2)}, u32[]{:S(2)}) collective-permute-start(bf16[128,768]{1,0:T(8,128)(2,1)} %get-tuple-element.175.rest_0_), channel_id=1, source_target_pairs={{0,1},{1,0},{2,3},{3,2},{4,5},{5,4},{6,7},{7,6},{8,9},{9,8},{10,11... | collective-permute-start | bytes 589832 | tf_op jit(solution)/shard_map/ppermute | solution.py:859
  52.5 25.7 %collective-permute-start.15 = (bf16[128,768]{1,0:T(8,128)(2,1)}, bf16[128,768]{1,0:T(8,128)(2,1)S(1)}, u32[]{:S(2)}, u32[]{:S(2)}) collective-permute-start(bf16[128,768]{1,0:T(8,128)(2,1)} %get-tuple-element.175.rest_0_), channel_id=1, source_target_pairs={{0,2},{1,3},{2,0},{3,1},{4,6},{5,7},{6,4},{7,5},{8,10},{9,11},{10,... | collective-permute-start | bytes 589832 | tf_op jit(solution)/shard_map/ppermute | solution.py:859
  55.4 26.0 %collective-permute-start.16 = (bf16[128,768]{1,0:T(8,128)(2,1)}, bf16[128,768]{1,0:T(8,128)(2,1)S(1)}, u32[]{:S(2)}, u32[]{:S(2)}) collective-permute-start(bf16[128,768]{1,0:T(8,128)(2,1)} %get-tuple-element.175.rest_0_), channel_id=1, source_target_pairs={{0,3},{1,2},{2,1},{3,0},{4,7},{5,6},{6,5},{7,4},{8,11},{9,10},{10,... | collective-permute-start | bytes 589832 | tf_op jit(solution)/shard_map/ppermute | solution.py:859
  86.4 30.4 %collective-permute-start.17 = (bf16[128,768]{1,0:T(8,128)(2,1)}, bf16[128,768]{1,0:T(8,128)(2,1)S(1)}, u32[]{:S(2)}, u32[]{:S(2)}) collective-permute-start(bf16[128,768]{1,0:T(8,128)(2,1)} %get-tuple-element.177), channel_id=1, source_target_pairs={{0,1},{1,0},{2,3},{3,2},{4,5},{5,4},{6,7},{7,6},{8,9},{9,8},{10,11... | collective-permute-start | bytes 589832 | tf_op jit(solution)/shard_map/ppermute | solution.py:859
  102.0 23.9 %collective-permute-start.18 = (bf16[128,768]{1,0:T(8,128)(2,1)}, bf16[128,768]{1,0:T(8,128)(2,1)S(1)}, u32[]{:S(2)}, u32[]{:S(2)}) collective-permute-start(bf16[128,768]{1,0:T(8,128)(2,1)} %get-tuple-element.178), channel_id=1, source_target_pairs={{0,2},{1,3},{2,0},{3,1},{4,6},{5,7},{6,4},{7,5},{8,10},{9,11},{10,... | collective-permute-start | bytes 589832 | tf_op jit(solution)/shard_map/ppermute | solution.py:859
  102.1 27.9 %collective-permute-start.19 = (bf16[128,768]{1,0:T(8,128)(2,1)}, bf16[128,768]{1,0:T(8,128)(2,1)S(1)}, u32[]{:S(2)}, u32[]{:S(2)}) collective-permute-start(bf16[128,768]{1,0:T(8,128)(2,1)} %get-tuple-element.179), channel_id=1, source_target_pairs={{0,3},{1,2},{2,1},{3,0},{4,7},{5,6},{6,5},{7,4},{8,11},{9,10},{10,... | collective-permute-start | bytes 589832 | tf_op jit(solution)/shard_map/ppermute | solution.py:859
  104.3 83.6 %collective-permute-start.35 = (bf16[4,2,96,768]{3,2,1,0:T(8,128)(2,1)}, bf16[4,2,96,768]{3,2,1,0:T(8,128)(2,1)S(1)}, u32[]{:S(2)}, u32[]{:S(2)}) collective-permute-start(bf16[4,2,96,768]{3,2,1,0:T(8,128)(2,1)} %bitcast.24), channel_id=1, source_target_pairs={{0,8},{4,12},{8,0},{12,4},{16,24},{20,28},{24,16},{28,20},{1,9},{5... | collective-permute-start | bytes 3538952 | tf_op jit(solution)/shard_map/ppermute | solution.py:898
  105.7 82.8 %collective-permute-start.37 = (bf16[4,2,96,768]{3,2,1,0:T(8,128)(2,1)}, bf16[4,2,96,768]{3,2,1,0:T(8,128)(2,1)}, u32[]{:S(2)}, u32[]{:S(2)}) collective-permute-start(bf16[4,2,96,768]{3,2,1,0:T(8,128)(2,1)} %bitcast.25), channel_id=1, source_target_pairs={{0,16},{4,20},{8,24},{12,28},{16,0},{20,4},{24,8},{28,12},{1,17},{... | collective-permute-start | bytes 3538952 | tf_op jit(solution)/shard_map/ppermute | solution.py:898
  116.9 71.7 %collective-permute-start.39 = (bf16[4,2,96,768]{3,2,1,0:T(8,128)(2,1)}, bf16[4,2,96,768]{3,2,1,0:T(8,128)(2,1)}, u32[]{:S(2)}, u32[]{:S(2)}) collective-permute-start(bf16[4,2,96,768]{3,2,1,0:T(8,128)(2,1)} %bitcast.26), channel_id=1, source_target_pairs={{0,24},{4,28},{8,16},{12,20},{16,8},{20,12},{24,0},{28,4},{1,25},{... | collective-permute-start | bytes 3538952 | tf_op jit(solution)/shard_map/ppermute | solution.py:898
  138.7 27.1 %collective-permute-start.21 = (bf16[256,576]{1,0:T(8,128)(2,1)}, bf16[256,576]{1,0:T(8,128)(2,1)S(1)}, u32[]{:S(2)}, u32[]{:S(2)}) collective-permute-start(bf16[256,576]{1,0:T(8,128)(2,1)} %get-tuple-element.182), channel_id=1, source_target_pairs={{0,8},{4,12},{8,0},{12,4},{16,24},{20,28},{24,16},{28,20},{1,9},{5... | collective-permute-start | bytes 884744 | tf_op jit(solution)/shard_map/ppermute | solution.py:873
  140.5 27.2 %collective-permute-start.22 = (bf16[256,576]{1,0:T(8,128)(2,1)}, bf16[256,576]{1,0:T(8,128)(2,1)S(1)}, u32[]{:S(2)}, u32[]{:S(2)}) collective-permute-start(bf16[256,576]{1,0:T(8,128)(2,1)} %get-tuple-element.183), channel_id=1, source_target_pairs={{0,12},{4,8},{8,4},{12,0},{16,28},{20,24},{24,20},{28,16},{1,13},{... | collective-permute-start | bytes 884744 | tf_op jit(solution)/shard_map/ppermute | solution.py:873
  167.7 19.1 %collective-permute-start.24 = (bf16[256,576]{1,0:T(8,128)(2,1)}, bf16[256,576]{1,0:T(8,128)(2,1)S(1)}, u32[]{:S(2)}, u32[]{:S(2)}) collective-permute-start(bf16[256,576]{1,0:T(8,128)(2,1)} %get-tuple-element.185), channel_id=1, source_target_pairs={{0,20},{4,16},{8,28},{12,24},{16,4},{20,0},{24,12},{28,8},{1,21},{... | collective-permute-start | bytes 884744 | tf_op jit(solution)/shard_map/ppermute | solution.py:873
  187.9 66.2 %collective-permute-start.34 = (bf16[4,2,96,768]{3,2,1,0:T(8,128)(2,1)S(1)}, bf16[4,2,96,768]{3,2,1,0:T(8,128)(2,1)}, u32[]{:S(2)}, u32[]{:S(2)}) collective-permute-start(bf16[4,2,96,768]{3,2,1,0:T(8,128)(2,1)S(1)} %bitcast.28), channel_id=1, source_target_pairs={{0,4},{4,0},{8,12},{12,8},{16,20},{20,16},{24,28},{28,24},{1,5},{5... | collective-permute-start | bytes 3538952 | tf_op jit(solution)/shard_map/ppermute | solution.py:900
  188.0 66.1 %collective-permute-start.36 = (bf16[4,2,96,768]{3,2,1,0:T(8,128)(2,1)S(1)}, bf16[4,2,96,768]{3,2,1,0:T(8,128)(2,1)}, u32[]{:S(2)}, u32[]{:S(2)}) collective-permute-start(bf16[4,2,96,768]{3,2,1,0:T(8,128)(2,1)S(1)} %collective-permute-done.35.rest_14_), channel_id=1, source_target_pairs={{0,4},{4,0},{8,12},{12,8},{16,20},{20,16},{24,28},{28,24},{1,5},{5... | collective-permute-start | bytes 3538952 | tf_op jit(solution)/shard_map/ppermute | solution.py:900
  188.4 65.6 %collective-permute-start.38 = (bf16[4,2,96,768]{3,2,1,0:T(8,128)(2,1)}, bf16[4,2,96,768]{3,2,1,0:T(8,128)(2,1)}, u32[]{:S(2)}, u32[]{:S(2)}) collective-permute-start(bf16[4,2,96,768]{3,2,1,0:T(8,128)(2,1)} %collective-permute-done.37.rest_16_), channel_id=1, source_target_pairs={{0,4},{4,0},{8,12},{12,8},{16,20},{20,16},{24,28},{28,24},{1,5},{5... | collective-permute-start | bytes 3538952 | tf_op jit(solution)/shard_map/ppermute | solution.py:900
  188.5 65.5 %collective-permute-start.40 = (bf16[4,2,96,768]{3,2,1,0:T(8,128)(2,1)}, bf16[4,2,96,768]{3,2,1,0:T(8,128)(2,1)}, u32[]{:S(2)}, u32[]{:S(2)}) collective-permute-start(bf16[4,2,96,768]{3,2,1,0:T(8,128)(2,1)} %collective-permute-done.39.rest_18_), channel_id=1, source_target_pairs={{0,4},{4,0},{8,12},{12,8},{16,20},{20,16},{24,28},{28,24},{1,5},{5... | collective-permute-start | bytes 3538952 | tf_op jit(solution)/shard_map/ppermute | solution.py:900
  326.2 15.4 %collective-permute-start.50 = (bf16[256,576]{1,0:T(8,128)(2,1)}, bf16[256,576]{1,0:T(8,128)(2,1)S(1)}, u32[]{:S(2)}, u32[]{:S(2)}) collective-permute-start(bf16[256,576]{1,0:T(8,128)(2,1)} %get-tuple-element.211), channel_id=1, source_target_pairs={{0,12},{4,8},{8,4},{12,0},{16,28},{20,24},{24,20},{28,16},{1,13},{... | collective-permute-start | bytes 884744 | tf_op jit(solution)/shard_map/ppermute | solution.py:873
  328.0 30.0 %collective-permute-start.52 = (bf16[256,576]{1,0:T(8,128)(2,1)}, bf16[256,576]{1,0:T(8,128)(2,1)S(1)}, u32[]{:S(2)}, u32[]{:S(2)}) collective-permute-start(bf16[256,576]{1,0:T(8,128)(2,1)} %get-tuple-element.213), channel_id=1, source_target_pairs={{0,20},{4,16},{8,28},{12,24},{16,4},{20,0},{24,12},{28,8},{1,21},{... | collective-permute-start | bytes 884744 | tf_op jit(solution)/shard_map/ppermute | solution.py:873
  328.7 29.3 %collective-permute-start.53 = (bf16[256,576]{1,0:T(8,128)(2,1)}, bf16[256,576]{1,0:T(8,128)(2,1)S(1)}, u32[]{:S(2)}, u32[]{:S(2)}) collective-permute-start(bf16[256,576]{1,0:T(8,128)(2,1)} %get-tuple-element.214), channel_id=1, source_target_pairs={{0,24},{4,28},{8,16},{12,20},{16,8},{20,12},{24,0},{28,4},{1,25},{... | collective-permute-start | bytes 884744 | tf_op jit(solution)/shard_map/ppermute | solution.py:873
  335.9 22.0 %collective-permute-start.54 = (bf16[256,576]{1,0:T(8,128)(2,1)}, bf16[256,576]{1,0:T(8,128)(2,1)S(1)}, u32[]{:S(2)}, u32[]{:S(2)}) collective-permute-start(bf16[256,576]{1,0:T(8,128)(2,1)} %get-tuple-element.215), channel_id=1, source_target_pairs={{0,28},{4,24},{8,20},{12,16},{16,12},{20,8},{24,4},{28,0},{1,29},{... | collective-permute-start | bytes 884744 | tf_op jit(solution)/shard_map/ppermute | solution.py:873
  367.3 17.4 %collective-permute-start.56 = (bf16[128,768]{1,0:T(8,128)(2,1)}, bf16[128,768]{1,0:T(8,128)(2,1)S(1)}, u32[]{:S(2)}, u32[]{:S(2)}) collective-permute-start(bf16[128,768]{1,0:T(8,128)(2,1)} %get-tuple-element.218.rest_4_), channel_id=1, source_target_pairs={{0,2},{1,3},{2,0},{3,1},{4,6},{5,7},{6,4},{7,5},{8,10},{9,11},{10,... | collective-permute-start | bytes 589832 | tf_op jit(solution)/shard_map/ppermute | solution.py:859
  369.4 15.4 %collective-permute-start.57 = (bf16[128,768]{1,0:T(8,128)(2,1)}, bf16[128,768]{1,0:T(8,128)(2,1)S(1)}, u32[]{:S(2)}, u32[]{:S(2)}) collective-permute-start(bf16[128,768]{1,0:T(8,128)(2,1)} %get-tuple-element.218.rest_4_), channel_id=1, source_target_pairs={{0,3},{1,2},{2,1},{3,0},{4,7},{5,6},{6,5},{7,4},{8,11},{9,10},{10,... | collective-permute-start | bytes 589832 | tf_op jit(solution)/shard_map/ppermute | solution.py:859
  394.5 17.4 %collective-permute-start.59 = (bf16[128,768]{1,0:T(8,128)(2,1)}, bf16[128,768]{1,0:T(8,128)(2,1)S(1)}, u32[]{:S(2)}, u32[]{:S(2)}) collective-permute-start(bf16[128,768]{1,0:T(8,128)(2,1)} %get-tuple-element.221), channel_id=1, source_target_pairs={{0,2},{1,3},{2,0},{3,1},{4,6},{5,7},{6,4},{7,5},{8,10},{9,11},{10,... | collective-permute-start | bytes 589832 | tf_op jit(solution)/shard_map/ppermute | solution.py:859
  396.2 15.7 %collective-permute-start.60 = (bf16[128,768]{1,0:T(8,128)(2,1)}, bf16[128,768]{1,0:T(8,128)(2,1)S(1)}, u32[]{:S(2)}, u32[]{:S(2)}) collective-permute-start(bf16[128,768]{1,0:T(8,128)(2,1)} %get-tuple-element.222), channel_id=1, source_target_pairs={{0,3},{1,2},{2,1},{3,0},{4,7},{5,6},{6,5},{7,4},{8,11},{9,10},{10,... | collective-permute-start | bytes 589832 | tf_op jit(solution)/shard_map/ppermute | solution.py:859
  405.7 54.3 %collective-permute-start.89 = (bf16[4,96,3072]{2,1,0:T(8,128)(2,1)}, bf16[4,96,3072]{2,1,0:T(8,128)(2,1)S(1)}, u32[]{:S(2)}, u32[]{:S(2)}) collective-permute-start(bf16[4,96,3072]{2,1,0:T(8,128)(2,1)} %get-tuple-element.279), channel_id=1, source_target_pairs={{0,4},{4,0},{8,12},{12,8},{16,20},{20,16},{24,28},{28,24},{1,5},{5... | collective-permute-start | bytes 7077896 | tf_op jit(solution)/shard_map/ppermute | solution.py:778
  459.8 18.6 %collective-permute-start.75 = (bf16[4,96,3200]{2,1,0:T(8,128)(2,1)}, bf16[4,96,3200]{2,1,0:T(8,128)(2,1)S(1)}, u32[]{:S(2)}, u32[]{:S(2)}) collective-permute-start(bf16[4,96,3200]{2,1,0:T(8,128)(2,1)} %get-tuple-element.256), channel_id=1, source_target_pairs={{0,4},{4,0},{8,12},{12,8},{16,20},{20,16},{24,28},{28,24},{1,5},{5... | collective-permute-start | bytes 7372808 | tf_op jit(solution)/shard_map/ppermute | solution.py:778
  465.8 19.1 %collective-permute-start.90 = (bf16[96,3072]{1,0:T(8,128)(2,1)}, bf16[96,3072]{1,0:T(8,128)(2,1)S(1)}, u32[]{:S(2)}, u32[]{:S(2)}) collective-permute-start(bf16[96,3072]{1,0:T(8,128)(2,1)} %get-tuple-element.281), channel_id=1, source_target_pairs={{0,8},{4,12},{8,0},{12,4},{16,24},{20,28},{24,16},{28,20},{1,9},{5... | collective-permute-start | bytes 1769480 | tf_op jit(solution)/shard_map/ppermute | solution.py:784
  466.9 26.9 %collective-permute-start.91 = (bf16[96,3072]{1,0:T(8,128)(2,1)}, bf16[96,3072]{1,0:T(8,128)(2,1)S(1)}, u32[]{:S(2)}, u32[]{:S(2)}) collective-permute-start(bf16[96,3072]{1,0:T(8,128)(2,1)} %get-tuple-element.282), channel_id=1, source_target_pairs={{0,16},{4,20},{8,24},{12,28},{16,0},{20,4},{24,8},{28,12},{1,17},{... | collective-permute-start | bytes 1769480 | tf_op jit(solution)/shard_map/ppermute | solution.py:784
  477.0 52.5 %collective-permute-start.85 = (bf16[4,96,1536]{2,1,0:T(8,128)(2,1)}, bf16[4,96,1536]{2,1,0:T(8,128)(2,1)S(1)}, u32[]{:S(2)}, u32[]{:S(2)}) collective-permute-start(bf16[4,96,1536]{2,1,0:T(8,128)(2,1)} %get-tuple-element.269), channel_id=1, source_target_pairs={{0,4},{4,0},{8,12},{12,8},{16,20},{20,16},{24,28},{28,24},{1,5},{5... | collective-permute-start | bytes 3538952 | tf_op jit(solution)/shard_map/ppermute | solution.py:778
  477.0 36.2 %collective-permute-start.92 = (bf16[96,3072]{1,0:T(8,128)(2,1)}, bf16[96,3072]{1,0:T(8,128)(2,1)}, u32[]{:S(2)}, u32[]{:S(2)}) collective-permute-start(bf16[96,3072]{1,0:T(8,128)(2,1)} %get-tuple-element.283), channel_id=1, source_target_pairs={{0,24},{4,28},{8,16},{12,20},{16,8},{20,12},{24,0},{28,4},{1,25},{... | collective-permute-start | bytes 1769480 | tf_op jit(solution)/shard_map/ppermute | solution.py:784
  483.9 32.2 %collective-permute-start.76 = (bf16[96,3200]{1,0:T(8,128)(2,1)}, bf16[96,3200]{1,0:T(8,128)(2,1)S(1)}, u32[]{:S(2)}, u32[]{:S(2)}) collective-permute-start(bf16[96,3200]{1,0:T(8,128)(2,1)} %get-tuple-element.258), channel_id=1, source_target_pairs={{0,8},{4,12},{8,0},{12,4},{16,24},{20,28},{24,16},{28,20},{1,9},{5... | collective-permute-start | bytes 1843208 | tf_op jit(solution)/shard_map/ppermute | solution.py:784
  484.9 35.3 %collective-permute-start.77 = (bf16[96,3200]{1,0:T(8,128)(2,1)}, bf16[96,3200]{1,0:T(8,128)(2,1)S(1)}, u32[]{:S(2)}, u32[]{:S(2)}) collective-permute-start(bf16[96,3200]{1,0:T(8,128)(2,1)} %get-tuple-element.259), channel_id=1, source_target_pairs={{0,16},{4,20},{8,24},{12,28},{16,0},{20,4},{24,8},{28,12},{1,17},{... | collective-permute-start | bytes 1843208 | tf_op jit(solution)/shard_map/ppermute | solution.py:784
  494.6 26.7 %collective-permute-start.78 = (bf16[96,3200]{1,0:T(8,128)(2,1)}, bf16[96,3200]{1,0:T(8,128)(2,1)S(1)}, u32[]{:S(2)}, u32[]{:S(2)}) collective-permute-start(bf16[96,3200]{1,0:T(8,128)(2,1)} %get-tuple-element.260), channel_id=1, source_target_pairs={{0,24},{4,28},{8,16},{12,20},{16,8},{20,12},{24,0},{28,4},{1,25},{... | collective-permute-start | bytes 1843208 | tf_op jit(solution)/shard_map/ppermute | solution.py:784
  513.2 51.5 %collective-permute-start.99 = (bf16[4,96,1536]{2,1,0:T(8,128)(2,1)}, bf16[4,96,1536]{2,1,0:T(8,128)(2,1)S(1)}, u32[]{:S(2)}, u32[]{:S(2)}) collective-permute-start(bf16[4,96,1536]{2,1,0:T(8,128)(2,1)} %get-tuple-element.292), channel_id=1, source_target_pairs={{0,4},{4,0},{8,12},{12,8},{16,20},{20,16},{24,28},{28,24},{1,5},{5... | collective-permute-start | bytes 3538952 | tf_op jit(solution)/shard_map/ppermute | solution.py:778
  525.1 22.4 %collective-permute-start.79 = (bf16[24,3200]{1,0:T(8,128)(2,1)}, bf16[24,3200]{1,0:T(8,128)(2,1)S(1)}, u32[]{:S(2)}, u32[]{:S(2)}) collective-permute-start(bf16[24,3200]{1,0:T(8,128)(2,1)} %get-tuple-element.262), channel_id=1, source_target_pairs={{0,1},{1,0},{2,3},{3,2},{4,5},{5,4},{6,7},{7,6},{8,9},{9,8},{10,11... | collective-permute-start | bytes 460808 | tf_op jit(solution)/shard_map/ppermute | solution.py:859
  527.8 16.9 %collective-permute-start.94 = (bf16[24,3072]{1,0:T(8,128)(2,1)S(1)}, bf16[24,3072]{1,0:T(8,128)(2,1)S(1)}, u32[]{:S(2)}, u32[]{:S(2)}) collective-permute-start(bf16[24,3072]{1,0:T(8,128)(2,1)S(1)} %copy-done.94), channel_id=1, source_target_pairs={{0,2},{1,3},{2,0},{3,1},{4,6},{5,7},{6,4},{7,5},{8,10},{9,11},{10,... | collective-permute-start | bytes 442376 | tf_op jit(solution)/shard_map/ppermute | solution.py:859
  529.5 16.3 %collective-permute-start.95 = (bf16[24,3072]{1,0:T(8,128)(2,1)S(1)}, bf16[24,3072]{1,0:T(8,128)(2,1)S(1)}, u32[]{:S(2)}, u32[]{:S(2)}) collective-permute-start(bf16[24,3072]{1,0:T(8,128)(2,1)S(1)} %copy-done.93), channel_id=1, source_target_pairs={{0,3},{1,2},{2,1},{3,0},{4,7},{5,6},{6,5},{7,4},{8,11},{9,10},{10,... | collective-permute-start | bytes 442376 | tf_op jit(solution)/shard_map/ppermute | solution.py:859
  531.0 19.0 %collective-permute-start.80 = (bf16[24,3200]{1,0:T(8,128)(2,1)}, bf16[24,3200]{1,0:T(8,128)(2,1)S(1)}, u32[]{:S(2)}, u32[]{:S(2)}) collective-permute-start(bf16[24,3200]{1,0:T(8,128)(2,1)} %get-tuple-element.263), channel_id=1, source_target_pairs={{0,2},{1,3},{2,0},{3,1},{4,6},{5,7},{6,4},{7,5},{8,10},{9,11},{10,... | collective-permute-start | bytes 460808 | tf_op jit(solution)/shard_map/ppermute | solution.py:859
  544.7 15.9 %collective-permute-start.86 = (bf16[96,1536]{1,0:T(8,128)(2,1)}, bf16[96,1536]{1,0:T(8,128)(2,1)S(1)}, u32[]{:S(2)}, u32[]{:S(2)}) collective-permute-start(bf16[96,1536]{1,0:T(8,128)(2,1)} %get-tuple-element.271), channel_id=1, source_target_pairs={{0,8},{4,12},{8,0},{12,4},{16,24},{20,28},{24,16},{28,20},{1,9},{5... | collective-permute-start | bytes 884744 | tf_op jit(solution)/shard_map/ppermute | solution.py:784
  545.8 17.3 %collective-permute-start.87 = (bf16[96,1536]{1,0:T(8,128)(2,1)}, bf16[96,1536]{1,0:T(8,128)(2,1)S(1)}, u32[]{:S(2)}, u32[]{:S(2)}) collective-permute-start(bf16[96,1536]{1,0:T(8,128)(2,1)} %get-tuple-element.272), channel_id=1, source_target_pairs={{0,16},{4,20},{8,24},{12,28},{16,0},{20,4},{24,8},{28,12},{1,17},{... | collective-permute-start | bytes 884744 | tf_op jit(solution)/shard_map/ppermute | solution.py:784
  547.5 16.5 %collective-permute-start.88 = (bf16[96,1536]{1,0:T(8,128)(2,1)}, bf16[96,1536]{1,0:T(8,128)(2,1)S(1)}, u32[]{:S(2)}, u32[]{:S(2)}) collective-permute-start(bf16[96,1536]{1,0:T(8,128)(2,1)} %get-tuple-element.273), channel_id=1, source_target_pairs={{0,24},{4,28},{8,16},{12,20},{16,8},{20,12},{24,0},{28,4},{1,25},{... | collective-permute-start | bytes 884744 | tf_op jit(solution)/shard_map/ppermute | solution.py:784
  564.7 20.8 %collective-permute-start.83 = (bf16[24,3200]{1,0:T(8,128)(2,1)S(1)}, bf16[24,3200]{1,0:T(8,128)(2,1)S(1)}, u32[]{:S(2)}, u32[]{:S(2)}) collective-permute-start(bf16[24,3200]{1,0:T(8,128)(2,1)S(1)} %copy-done.7), channel_id=1, source_target_pairs={{0,2},{1,3},{2,0},{3,1},{4,6},{5,7},{6,4},{7,5},{8,10},{9,11},{10,... | collective-permute-start | bytes 460808 | tf_op jit(solution)/shard_map/ppermute | solution.py:859
  570.5 15.1 %collective-permute-start.84 = (bf16[24,3200]{1,0:T(8,128)(2,1)S(1)}, bf16[24,3200]{1,0:T(8,128)(2,1)S(1)}, u32[]{:S(2)}, u32[]{:S(2)}) collective-permute-start(bf16[24,3200]{1,0:T(8,128)(2,1)S(1)} %copy-done.7), channel_id=1, source_target_pairs={{0,3},{1,2},{2,1},{3,0},{4,7},{5,6},{6,5},{7,4},{8,11},{9,10},{10,... | collective-permute-start | bytes 460808 | tf_op jit(solution)/shard_map/ppermute | solution.py:859
  574.7 16.2 %collective-permute-start.100 = (bf16[96,1536]{1,0:T(8,128)(2,1)}, bf16[96,1536]{1,0:T(8,128)(2,1)S(1)}, u32[]{:S(2)}, u32[]{:S(2)}) collective-permute-start(bf16[96,1536]{1,0:T(8,128)(2,1)} %get-tuple-element.294), channel_id=1, source_target_pairs={{0,8},{4,12},{8,0},{12,4},{16,24},{20,28},{24,16},{28,20},{1,9},{5... | collective-permute-start | bytes 884744 | tf_op jit(solution)/shard_map/ppermute | solution.py:784
  575.7 15.2 %collective-permute-start.101 = (bf16[96,1536]{1,0:T(8,128)(2,1)}, bf16[96,1536]{1,0:T(8,128)(2,1)S(1)}, u32[]{:S(2)}, u32[]{:S(2)}) collective-permute-start(bf16[96,1536]{1,0:T(8,128)(2,1)} %get-tuple-element.295), channel_id=1, source_target_pairs={{0,16},{4,20},{8,24},{12,28},{16,0},{20,4},{24,8},{28,12},{1,17},{... | collective-permute-start | bytes 884744 | tf_op jit(solution)/shard_map/ppermute | solution.py:784
  (167 other events, 1480.1 us)
Sparse Core Ops, SparseCore 0:
  10.2 33.1 all-gather.8
  44.9 95.9 all-gather.6
  283.7 62.7 all-gather.4

commit v3 on v2

--- a/solution.py
+++ b/solution.py
@@ -103,6 +103,18 @@
     for s, piece in enumerate(pieces):
         c, r = combo(me ^ s)
         parts[c, pl.ds(pl.multiple_of(r * rows, rows), rows), :] = piece[...]
+    return jnp.concatenate(
+        [parts[c, :, t * GW : (t + 1) * GW] for t in range(thirds) for c in range(GROUPS)],
+        axis=1,
+    )
+
+
+def load_stack(me, stack, parts, thirds):
+    rows = stack.shape[1]
+    first = lax.div(me, 2 * GROUPS) * (2 * GROUPS)
+    for w in range(2 * GROUPS):
+        c, r = w // 2, w % 2
+        parts[c, r * rows : (r + 1) * rows, :] = stack[first + w]
     return jnp.concatenate(
         [parts[c, :, t * GW : (t + 1) * GW] for t in range(thirds) for c in range(GROUPS)],
         axis=1,
@@ -166,8 +178,9 @@
     rest = list(rest)
     col_ref = rest.pop(0) if by_column else None
     pieces, rest = rest[:count], rest[count:]
+    columns = rest.pop(0)
     out_pieces, rest = rest[:sends], rest[sends:]
-    o_ref, lse_ref, q_s, k_s, v_s, vt_s = rest
+    o_ref, lse_ref, x_ref, k_s, v_s, vt_s = rest
     i = pl.program_id(0)
     me = ids[0]
     rows = pieces[0].shape[0]
@@ -177,13 +190,14 @@
     def _():
         for s in range(count):
             at = pl.ds(pl.multiple_of((me ^ s) * rows, rows), rows)
-            q_s[at, :] = pieces[s][:, 0:GW]
-            k_s[at, :] = pieces[s][:, GW : 2 * GW]
-            v_s[at, :] = pieces[s][:, 2 * GW : 3 * GW]
+            x = dot(pieces[s][...], columns[...]).astype(BF)
+            x_ref[at, :] = x
+            k_s[at, :] = x[:, GW : 2 * GW]
+            v_s[at, :] = x[:, 2 * GW : 3 * GW]
         vt_s[...] = v_s[...].T
 
     q_at = pl.multiple_of(i * bq, bq)
-    q_heads = head_parts(q_s[pl.ds(q_at, bq), :])
+    q_heads = head_parts(x_ref[pl.ds(q_at, bq), 0:GW])
 
     def step(j, carry):
         k_at = pl.multiple_of(j * bk, bk)
@@ -228,30 +242,29 @@
 def attend_back_kernel(bq, count, sends, by_column, ids, first_ref, row_ref, *rest):
     rest = list(rest)
     col_ref = rest.pop(0) if by_column else None
-    pieces, rest = rest[:count], rest[count:]
+    x_ref = rest.pop(0)
     grads, rest = rest[:count], rest[count:]
     o_ref, lse_ref = rest[:2]
     out_pieces, rest = rest[2 : 2 + sends], rest[2 + sends :]
-    q_s, k_s, v_s, g_s, dq_s, dk_s, dv_s = rest
+    dx_ref, k_s, v_s, g_s, dk_s, dv_s = rest
     i = pl.program_id(0)
     me = ids[0]
-    rows = pieces[0].shape[0]
+    rows = grads[0].shape[0]
     bk = bq
 
     @pl.when(i == 0)
     def _():
+        k_s[...] = x_ref[:, GW : 2 * GW]
+        v_s[...] = x_ref[:, 2 * GW : 3 * GW]
         for s in range(count):
             at = pl.ds(pl.multiple_of((me ^ s) * rows, rows), rows)
-            q_s[at, :] = pieces[s][:, 0:GW]
-            k_s[at, :] = pieces[s][:, GW : 2 * GW]
-            v_s[at, :] = pieces[s][:, 2 * GW : 3 * GW]
             g_s[at, :] = grads[s][...]
         dk_s[...] = jnp.zeros_like(dk_s)
         dv_s[...] = jnp.zeros_like(dv_s)
 
     q_at = pl.multiple_of(i * bq, bq)
     grad = g_s[pl.ds(q_at, bq), :]
-    q_heads = head_parts(q_s[pl.ds(q_at, bq), :])
+    q_heads = head_parts(x_ref[pl.ds(q_at, bq), 0:GW])
     g_heads = head_parts(grad)
     dots = (grad.astype(F32) * o_ref[pl.ds(q_at, bq), :].astype(F32)).T
     row_dot = [
@@ -282,62 +295,129 @@
         return dq
 
     dq = lax.fori_loop(first_ref[i], i + 1, step, jnp.zeros((bq, GW), F32))
-    dq_s[pl.ds(q_at, bq), :] = (dq * SCORE_SCALE).astype(BF)
+    dx_ref[pl.ds(q_at, bq), 0:GW] = (dq * SCORE_SCALE).astype(BF)
 
     @pl.when(i == pl.num_programs(0) - 1)
     def _():
+        dx_ref[:, GW : 2 * GW] = (dk_s[...] * SCORE_SCALE).astype(BF)
+        dx_ref[:, 2 * GW : 3 * GW] = dv_s[...].astype(BF)
         for s in range(sends):
             at = pl.ds(pl.multiple_of((me ^ s) * rows, rows), rows)
-            out_pieces[s][:, 0:GW] = dq_s[at, :]
-            out_pieces[s][:, GW : 2 * GW] = (dk_s[at, :] * SCORE_SCALE).astype(BF)
-            out_pieces[s][:, 2 * GW : 3 * GW] = dv_s[at, :].astype(BF)
-
-
-def attend(ids, meta, pieces, bq):
+            out_pieces[s][...] = dx_ref[at, :]
+
+
+def attend(ids, meta, pieces, columns, bq):
     first, row_info, col_info = meta
-    rows = pieces[0].shape[0]
+    rows, width = pieces[0].shape
     count, sends = len(pieces), min(len(pieces), 2 * GROUPS)
     length = rows * count
-    operands = [first, row_info] + ([] if col_info is None else [col_info]) + list(pieces)
-    outs = [sds((rows, GW), BF)] * sends + [sds((length, GW), BF), sds((8, length), F32)]
+    operands = [first, row_info] + ([] if col_info is None else [col_info])
+    operands += list(pieces) + [columns]
+    outs = [sds((rows, GW), BF)] * sends + [
+        sds((length, GW), BF),
+        sds((8, length), F32),
+        sds((length, 3 * GW), BF),
+    ]
     got = stage(
         partial(attend_kernel, bq, count, sends, col_info is not None),
         "attend",
         ids,
         operands,
         outs,
-        [pltpu.VMEM((length, GW), BF)] * 3 + [pltpu.VMEM((GW, length), BF)],
-        flops=length * length * GW * 2,
+        [pltpu.VMEM((length, GW), BF)] * 2 + [pltpu.VMEM((GW, length), BF)],
+        flops=length * length * GW * 2 + 6 * length * width * GW,
         grid=(length // bq,),
         specs={0: pl.BlockSpec(memory_space=pltpu.SMEM)},
     )
-    return got[:sends], got[sends], got[sends + 1]
-
-
-def attend_back(ids, meta, pieces, grads, attended, lse, bq):
+    return got[:sends], got[sends:]
+
+
+def attend_back(ids, meta, kept, grads, bq, send=True):
     first, row_info, col_info = meta
-    rows = pieces[0].shape[0]
-    count, sends = len(pieces), min(len(pieces), 2 * GROUPS)
+    attended, lse, x = kept
+    rows = grads[0].shape[0]
+    count, sends = len(grads), min(len(grads), 2 * GROUPS) if send else 0
     length = rows * count
     operands = [first, row_info] + ([] if col_info is None else [col_info])
-    operands += list(pieces) + list(grads) + [attended, lse]
-    return stage(
+    operands += [x] + list(grads) + [attended, lse]
+    got = stage(
         partial(attend_back_kernel, bq, count, sends, col_info is not None),
         "attend_back",
         ids,
         operands,
-        [sds((rows, 3 * GW), BF)] * sends,
-        [pltpu.VMEM((length, GW), BF)] * 5 + [pltpu.VMEM((length, GW), F32)] * 2,
+        [sds((rows, 3 * GW), BF)] * sends + [sds(x.shape, BF)],
+        [pltpu.VMEM((length, GW), BF)] * 3 + [pltpu.VMEM((length, GW), F32)] * 2,
         flops=length * length * GW * 5,
         grid=(length // bq,),
         specs={0: pl.BlockSpec(memory_space=pltpu.SMEM)},
     )
-
-
-def routed_pre_kernel(steps, ids, tok, sel, router, gain, project, *rest):
-    pieces = rest[:steps]
-    one_hot_ref, picked_ref, normed_ref, parts = rest[steps:]
-    seqs, span = sel.shape
+    return got[:sends], got[sends]
+
+
+def project_grads_kernel(count, ids, dx_ref, *rest):
+    pieces, (keep, send, total) = rest[:count], rest[count:]
+    rows = pieces[0].shape[0]
+    for s, piece in enumerate(pieces):
+        at = pl.ds(pl.multiple_of((ids[0] ^ s) * rows, rows), rows)
+        term = tn_dot(piece[...], dx_ref[at, :])
+        total[...] = term if s == 0 else total[...] + term
+    split_rows(ids[0], total, keep, send)
+
+
+def project_grads(ids, wide_count, pieces, dx):
+    rows, width = pieces[0].shape
+    shape = (wide_count // 2, width // wide_count, 3 * GW)
+    return stage(
+        partial(project_grads_kernel, len(pieces)),
+        "project_grads",
+        ids,
+        [dx] + list(pieces),
+        [sds(shape, BF)] * 2,
+        [pltpu.VMEM((width, 3 * GW), F32)],
+        flops=6 * dx.size * width // 3,
+    )
+
+
+def group_columns_kernel(ids, project, out):
+    group, _ = combo(ids[0])
+    width = GROUPS * GW
+    for c in range(GROUPS):
+
+        @pl.when(group == c)
+        def _():
+            for t in range(3):
+                at = t * width + c * GW
+                out[:, t * GW : (t + 1) * GW] = project[:, at : at + GW]
+
+
+def group_columns(ids, project):
+    (out,) = stage(
+        group_columns_kernel,
+        "group_columns",
+        ids,
+        [project],
+        [sds((project.shape[0], 3 * GW), BF)],
+    )
+    return out
+
+
+def save_halves(me, normed, mine_ref, other_ref):
+    rows = mine_ref.shape[0]
+    core = lax.rem(me, 2)
+    mine_ref[...] = normed[pl.ds(pl.multiple_of(core * rows, rows), rows), :]
+    other_ref[...] = normed[pl.ds(pl.multiple_of((1 - core) * rows, rows), rows), :]
+
+
+def routed_pre_kernel(count, ids, tok, sel, *rest):
+    vectors, rest = rest[:count], rest[count:]
+    mine_ref, other_ref, one_hot_ref, picked_ref, vecs, normed = rest
+    rows = [vector[...].astype(F32).reshape(1, -1) for vector in vectors]
+    rows.append(jnp.zeros((8 - count, tok.shape[1]), F32))
+    vecs[...] = jnp.concatenate(rows, axis=0)
+    span = one_hot_ref.shape[1]
+    seqs = sel.shape[0]
+    if sel.shape[1] != span:
+        sel = sel[:, pl.ds(pl.multiple_of(ids[0] * span, span), span)]
     slots = span // 4
     upper = (
         lax.broadcasted_iota(jnp.int32, (span, span), 0)
@@ -353,45 +433,51 @@
             one_hot, tok[q * span : (q + 1) * span, :]
         ).astype(BF)
     picked = picked_ref[...].astype(F32)
-    normed = (picked * norm_scale(picked) * gain[...].astype(F32)).astype(BF)
-    normed_ref[...] = normed
-    save_pieces(ids[0], dot(normed, project[...]).astype(BF), parts, pieces)
-
-
-def routed_pre(ids, steps, tok, sel, router, gain, project):
-    rows, width = sel.shape[0] * sel.shape[1] // 4, tok.shape[1]
-    outs = [sds((rows // 2, 3 * GW), BF)] * steps
-    outs += [sds((rows, sel.shape[1]), BF), sds((rows, width), BF), sds((rows, width), BF)]
-    got = stage(
-        partial(routed_pre_kernel, steps),
+    normed[...] = (picked * norm_scale(picked) * gain_of(vecs, 1)).astype(BF)
+    save_halves(ids[0], normed, mine_ref, other_ref)
+
+
+def gain_of(vecs, k):
+    return vecs[k : k + 1, :]
+
+
+def routed_pre(ids, tok, sel, span, vectors):
+    rows, width = tok.shape[0] // 4, tok.shape[1]
+    return stage(
+        partial(routed_pre_kernel, len(vectors)),
         "routed_pre",
         ids,
-        [tok, sel, router, gain, project],
-        outs,
-        [pltpu.VMEM((GROUPS, rows, 3 * GW), BF)],
-        flops=2 * rows * width * 3 * width,
-    )
-    return got[:steps], got[steps], got[steps + 1], got[steps + 2]
+        [tok, sel] + vectors,
+        [
+            sds((rows // 2, width), BF),
+            sds((rows // 2, width), BF),
+            sds((rows, span), BF),
+            sds((rows, width), BF),
+            sds((8, width), F32),
+        ],
+        [pltpu.VMEM((rows, width), BF)],
+        flops=4 * rows * width * span,
+    )
 
 
 def routed_mid_kernel(count, ids, *rest):
     pieces = rest[:count]
-    output, picked, gain, branch_ref, low_ref, att_ref, parts = rest[count:]
+    output, picked, vecs, branch_ref, low_ref, att_ref, parts = rest[count:]
     attended = load_pieces(ids[0], pieces, parts, 1)
     att_ref[...] = attended
     branch = dot(attended, output[...])
     branch_ref[...] = branch
     middle = picked[...].astype(F32) + branch
-    low_ref[...] = (middle * norm_scale(middle) * gain[...].astype(F32)).astype(BF)
-
-
-def routed_mid(ids, pieces, output, picked, gain):
+    low_ref[...] = (middle * norm_scale(middle) * gain_of(vecs, 2)).astype(BF)
+
+
+def routed_mid(ids, pieces, output, picked, vecs):
     shape = picked.shape
     return stage(
         partial(routed_mid_kernel, len(pieces)),
         "routed_mid",
         ids,
-        list(pieces) + [output, picked, gain],
+        list(pieces) + [output, picked, vecs],
         [sds(shape, F32), sds(shape, BF), sds(shape, BF)],
         [pltpu.VMEM((GROUPS, shape[0], GW), BF)],
         flops=2 * shape[0] * shape[1] * shape[1],
@@ -446,48 +532,80 @@
     )
 
 
-def dense_pre_kernel(steps, shares, ids, tok, one_hot, picked, router, branch, *rest):
+def dense_pre_kernel(shares, ids, tok, one_hot, picked, vecs, branch, *rest):
     partials = rest[:shares]
-    gain, project = rest[shares : shares + 2]
-    rest = rest[shares + 2 :]
-    pieces = rest[:steps]
-    mixed_ref, delta_ref, normed_ref, parts = rest[steps:]
+    mine_ref, other_ref, mixed_ref, delta_ref, normed = rest[shares:]
     slots, span = one_hot.shape[0] // 2, one_hot.shape[1]
     delta = branch[...]
     for share in partials:
         delta = delta + share[...].astype(F32)
     delta_ref[...] = delta
-    gate = jnp.sum(
-        picked[...].astype(F32) * router[...].astype(F32), axis=-1, keepdims=True
-    )
+    gate = jnp.sum(picked[...].astype(F32) * gain_of(vecs, 0), axis=-1, keepdims=True)
     lifted = gate * delta
     for q in range(2):
         at, spots = slice(q * span, (q + 1) * span), slice(q * slots, (q + 1) * slots)
         mixed = tok[at, :].astype(F32) + place(one_hot[spots, :], lifted[spots, :])
         mixed_ref[at, :] = mixed
-        normed_ref[at, :] = (mixed * norm_scale(mixed) * gain[...].astype(F32)).astype(BF)
-    save_pieces(ids[0], dot(normed_ref[...], project[...]).astype(BF), parts, pieces)
-
-
-def dense_pre(ids, steps, tok, one_hot, picked, router, branch, partials, gain, project):
+        normed[at, :] = (mixed * norm_scale(mixed) * gain_of(vecs, 3)).astype(BF)
+    save_halves(ids[0], normed, mine_ref, other_ref)
+
+
+def dense_pre(ids, tok, one_hot, picked, vecs, branch, partials):
     rows, width = tok.shape
-    outs = [sds((rows // 2, 3 * GW), BF)] * steps
-    outs += [sds(tok.shape, F32), sds(picked.shape, F32), sds(tok.shape, BF)]
-    got = stage(
-        partial(dense_pre_kernel, steps, len(partials)),
+    return stage(
+        partial(dense_pre_kernel, len(partials)),
         "dense_pre",
         ids,
-        [tok, one_hot, picked, router, branch] + list(partials) + [gain, project],
-        outs,
-        [pltpu.VMEM((GROUPS, rows, 3 * GW), BF)],
-        flops=6 * rows * width * width,
-    )
-    return got[:steps], got[steps], got[steps + 1], got[steps + 2]
+        [tok, one_hot, picked, vecs, branch] + list(partials),
+        [
+            sds((rows // 2, width), BF),
+            sds((rows // 2, width), BF),
+            sds(tok.shape, F32),
+            sds(picked.shape, F32),
+        ],
+        [pltpu.VMEM((rows, width), BF)],
+        flops=6 * rows * width * one_hot.shape[0],
+    )
+
+
+def this_part(me, weights, scratch):
+    if not scratch:
+        return weights[0][0], weights[1][0]
+    e_s, r_s = scratch
+    chips, rows = weights[0].shape[0], weights[0].shape[3]
+    core = lax.rem(me, 2)
+    for c in range(chips):
+        for weight, at in ((weights[0], 2 * c + core), (weights[1], 2 * c + 1 - core)):
+            at = pl.ds(pl.multiple_of(at * rows, rows), rows)
+            e_s[at, :] = weight[c, 0, 0]
+            r_s[at, :] = weight[c, 0, 1]
+    return e_s[...], r_s[...]
+
+
+def part_specs(base, weights):
+    if weights[0].ndim == 3:
+        return {
+            base + k: pl.BlockSpec((1,) + w.shape[1:], lambda n: (n, 0, 0))
+            for k, w in enumerate(weights)
+        }
+    return {
+        base + k: pl.BlockSpec(
+            (w.shape[0], 1) + w.shape[2:], lambda n: (0, n, 0, 0, 0)
+        )
+        for k, w in enumerate(weights)
+    }
+
+
+def part_scratch(width, weights):
+    if weights[0].ndim == 3:
+        return []
+    return [pltpu.VMEM((width, weights[0].shape[-1]), BF)] * 2
 
 
 def dense_ffn_kernel(count, steps, split, ids, *rest):
     pieces, rest = rest[:count], rest[count:]
-    output, mixed, cot, gain = rest[:4]
+    output, mixed, cot, vecs = rest[:4]
+    gain = gain_of(vecs, 4)
     rest = rest[4:]
     weights, rest = rest[:split], rest[split:]
     act_ref, low_ref, back_ref, sum_ref, att_ref, gain_ref = rest[:6]
@@ -503,20 +621,11 @@
         branch = dot(attended, output[...])
         branch_s[...] = branch
         middle = mixed[...] + branch
-        low_ref[...] = (middle * norm_scale(middle) * gain[...].astype(F32)).astype(BF)
+        low_ref[...] = (middle * norm_scale(middle) * gain).astype(BF)
         delta_s[...] = jnp.zeros_like(delta_s)
         grad_s[...] = jnp.zeros_like(grad_s)
 
-    if split == 2:
-        expand, reduce_w = weights[0][0], weights[1][0]
-    else:
-        e_s, r_s = rest[4:]
-        rows = weights[0].shape[2]
-        for s, weight in enumerate(weights):
-            at = pl.ds(pl.multiple_of((me ^ s) * rows, rows), rows)
-            e_s[at, :] = weight[0, 0]
-            r_s[at, :] = weight[0, 1]
-        expand, reduce_w = e_s[...], r_s[...]
+    expand, reduce_w = this_part(me, weights, rest[4:])
     value, slope = gelu_both(dot(low_ref[...], expand))
     delta_s[...] += dot(value.astype(BF), reduce_w)
     grad_pre = (nt_dot(cot[...], reduce_w) * slope).astype(BF)
@@ -526,7 +635,7 @@
     def _():
         middle = mixed[...] + branch_s[...]
         act_ref[...] = (middle + delta_s[...]).astype(BF)
-        grad_middle, gain_grad = norm_back(grad_s[...], middle, gain[...].astype(F32))
+        grad_middle, gain_grad = norm_back(grad_s[...], middle, gain)
         gain_ref[...] = jnp.broadcast_to(gain_grad, gain_ref.shape)
         total = cot[...].astype(F32) + grad_middle
         sum_ref[...] = total
@@ -535,21 +644,15 @@
         save_pieces(me, nt_dot(back, output[...]).astype(BF), parts, g_pieces)
 
 
-def dense_ffn(ids, steps, pieces, output, mixed, cot, gain, weights):
+def dense_ffn(ids, steps, pieces, output, mixed, cot, vecs, weights):
     rows, width = mixed.shape
     split = len(weights)
-    parts_n = weights[0].shape[0]
+    parts_n = weights[0].shape[0 if weights[0].ndim == 3 else 1]
     hidden = weights[0].shape[-1]
     base = len(pieces) + 4
-    specs = {
-        base + k: pl.BlockSpec(
-            (1,) + w.shape[1:], lambda n, z=(0,) * (w.ndim - 1): (n,) + z
-        )
-        for k, w in enumerate(weights)
-    }
+    specs = part_specs(base, weights)
     scratch = [pltpu.VMEM((GROUPS, rows, GW), BF)] + [pltpu.VMEM((rows, width), F32)] * 3
-    if split != 2:
-        scratch += [pltpu.VMEM((width, hidden), BF)] * 2
+    scratch += part_scratch(width, weights)
     outs = [
         sds((rows, width), BF),
         sds((rows, width), BF),
@@ -562,7 +665,7 @@
         partial(dense_ffn_kernel, len(pieces), steps, split),
         "dense_ffn",
         ids,
-        list(pieces) + [output, mixed, cot, gain] + list(weights),
+        list(pieces) + [output, mixed, cot, vecs] + list(weights),
         outs,
         scratch,
         flops=8 * rows * width * hidden * parts_n + 4 * rows * width * width,
@@ -572,23 +675,16 @@
     return got[:6], got[6:]
 
 
-def dense_post_kernel(count, ids, *rest):
-    pieces = rest[:count]
-    project, gain, mixed, total, one_hot, picked, router, delta = rest[count : count + 8]
-    g_mixed_ref, g_proj_ref, g_delta_ref, g_low_ref, g_gate_ref, gain_ref, parts = rest[
-        count + 8 :
-    ]
-    g_proj = load_pieces(ids[0], pieces, parts, 3)
-    g_proj_ref[...] = g_proj
-    grad_rows, gain_grad = norm_back(
-        nt_dot(g_proj, project[...]), mixed[...], gain[...].astype(F32)
-    )
-    gain_ref[...] = jnp.broadcast_to(gain_grad, gain_ref.shape)
+def dense_post_kernel(ids, stack, *rest):
+    project, vecs, mixed, total, one_hot, picked, delta = rest[:7]
+    g_mixed_ref, g_delta_ref, g_low_ref, g_gate_ref, router_ref, parts = rest[7:]
+    g_proj = load_stack(ids[0], stack, parts, 3)
+    grad_rows, _ = norm_back(nt_dot(g_proj, project[...]), mixed[...], gain_of(vecs, 3))
     g_mixed_ref[...] = total[...] + grad_rows
     slots, span = one_hot.shape[0] // 2, one_hot.shape[1]
-    gate = jnp.sum(
-        picked[...].astype(F32) * router[...].astype(F32), axis=-1, keepdims=True
-    )
+    rows = picked[...].astype(F32)
+    gate = jnp.sum(rows * gain_of(vecs, 0), axis=-1, keepdims=True)
+    router = jnp.zeros((1, rows.shape[1]), F32)
     for q in range(2):
         at, spots = slice(q * span, (q + 1) * span), slice(q * slots, (q + 1) * slots)
         lifted = pick(one_hot[spots, :], g_mixed_ref[at, :])
@@ -597,18 +693,19 @@
         g_low_ref[spots, :] = g_delta.astype(BF)
         g_gate = jnp.sum(lifted * delta[spots, :], axis=-1, keepdims=True)
         g_gate_ref[spots, :] = jnp.broadcast_to(g_gate, (slots, g_gate_ref.shape[1]))
-
-
-def dense_post(ids, pieces, project, gain, mixed, total, one_hot, picked, router, delta):
+        router = router + jnp.sum(rows[spots, :] * g_gate, axis=0, keepdims=True)
+    router_ref[...] = jnp.broadcast_to(router, router_ref.shape)
+
+
+def dense_post(ids, stack, project, vecs, mixed, total, one_hot, picked, delta):
     rows, width = mixed.shape
     return stage(
-        partial(dense_post_kernel, len(pieces)),
+        dense_post_kernel,
         "dense_post",
         ids,
-        list(pieces) + [project, gain, mixed, total, one_hot, picked, router, delta],
+        [stack, project, vecs, mixed, total, one_hot, picked, delta],
         [
             sds((rows, width), F32),
-            sds((rows, 3 * width), BF),
             sds(picked.shape, F32),
             sds(picked.shape, BF),
             sds((picked.shape[0], 128), F32),
@@ -621,7 +718,7 @@
 
 def routed_back_kernel(shares, steps, ids, *rest):
     partials = rest[:shares]
-    branch, picked, gain, g_delta, output = rest[shares : shares + 5]
+    branch, picked, vecs, g_delta, output = rest[shares : shares + 5]
     rest = rest[shares + 5 :]
     g_mid_ref, back_ref, gain_ref = rest[:3]
     pieces, parts = rest[3 : 3 + steps], rest[3 + steps]
@@ -629,7 +726,7 @@
     for share in partials[1:]:
         grad = grad + share[...].astype(F32)
     middle = picked[...].astype(F32) + branch[...]
-    g_middle, gain_grad = norm_back(grad, middle, gain[...].astype(F32))
+    g_middle, gain_grad = norm_back(grad, middle, gain_of(vecs, 2))
     gain_ref[...] = jnp.broadcast_to(gain_grad, gain_ref.shape)
     g_mid_ref[...] = g_middle
     back = (g_delta[...] + g_middle).astype(BF)
@@ -637,13 +734,13 @@
     save_pieces(ids[0], nt_dot(back, output[...]).astype(BF), parts, pieces)
 
 
-def routed_back(ids, steps, partials, branch, picked, gain, g_delta, output):
+def routed_back(ids, steps, partials, branch, picked, vecs, g_delta, output):
     rows, width = branch.shape
     got = stage(
         partial(routed_back_kernel, len(partials), steps),
         "routed_back",
         ids,
-        list(partials) + [branch, picked, gain, g_delta, output],
+        list(partials) + [branch, picked, vecs, g_delta, output],
         [sds((rows, width), F32), sds((rows, width), BF), sds((8, width), F32)]
         + [sds((rows // 2, GW), BF)] * steps,
         [pltpu.VMEM((GROUPS, rows, GW), BF)],
@@ -654,42 +751,30 @@
 
 def routed_post_kernel(count, ids, *rest):
     pieces = rest[:count]
-    project, gain, picked, g_mid, g_mixed, one_hot, g_gate, router = rest[count : count + 8]
-    out_ref, g_proj_ref, gain_ref, router_ref, parts = rest[count + 8 :]
+    project, vecs, picked, g_mid, g_mixed, one_hot, g_gate = rest[count : count + 7]
+    out_ref, parts = rest[count + 7 :]
     g_proj = load_pieces(ids[0], pieces, parts, 3)
-    g_proj_ref[...] = g_proj
     rows = picked[...].astype(F32)
-    grad_rows, gain_grad = norm_back(
-        nt_dot(g_proj, project[...]), rows, gain[...].astype(F32)
-    )
-    gain_ref[...] = jnp.broadcast_to(gain_grad, gain_ref.shape)
-    gate_grad = g_gate[:, 0:1]
-    router_ref[...] = jnp.broadcast_to(
-        jnp.sum(rows * gate_grad, axis=0, keepdims=True), router_ref.shape
-    )
-    spread = g_mid[...] + grad_rows + gate_grad * router[...].astype(F32)
+    grad_rows, _ = norm_back(nt_dot(g_proj, project[...]), rows, gain_of(vecs, 1))
+    spread = g_mid[...] + grad_rows + g_gate[:, 0:1] * gain_of(vecs, 0)
     slots, span = one_hot.shape[0] // 2, one_hot.shape[1]
     for q in range(2):
         at, spots = slice(q * span, (q + 1) * span), slice(q * slots, (q + 1) * slots)
         out_ref[at, :] = g_mixed[at, :] + place(one_hot[spots, :], spread[spots, :])
 
 
-def routed_post(ids, pieces, project, gain, picked, g_mid, g_mixed, one_hot, g_gate, router):
+def routed_post(ids, pieces, project, vecs, picked, g_mid, g_mixed, one_hot, g_gate):
     rows, width = picked.shape
-    return stage(
+    (out,) = stage(
         partial(routed_post_kernel, len(pieces)),
         "routed_post",
         ids,
-        list(pieces) + [project, gain, picked, g_mid, g_mixed, one_hot, g_gate, router],
-        [
-            sds(g_mixed.shape, F32),
-            sds((rows, 3 * width), BF),
-            sds((8, width), F32),
-            sds((8, width), F32),
-        ],
+        list(pieces) + [project, vecs, picked, g_mid, g_mixed, one_hot, g_gate],
+        [sds(g_mixed.shape, F32)],
         [pltpu.VMEM((GROUPS, rows, 3 * GW), BF)],
         flops=6 * rows * width * width,
     )
+    return out
 
 
 def split_rows(me, total, keep, send):
@@ -702,7 +787,7 @@
         send[c] = total[pl.ds(other, rows), :].astype(BF)
 
 
-def hidden_grads_kernel(ids, low, grad, expand, reduce_ref, keep, send, total):
+def hidden_grads_kernel(ids, low, grad, expand, reduce_ref, out, total):
     i = pl.program_id(0)
     hidden = expand.shape[1]
 
@@ -717,53 +802,52 @@
 
     @pl.when(i == pl.num_programs(0) - 1)
     def _():
-        split_rows(ids[0], total, keep, send)
-
-
-def hidden_grads(ids, wide_count, low, grad, expand, reduce_part):
+        out[...] = total[...].astype(BF)
+
+
+def hidden_grads(ids, low, grad, expand, reduce_part):
     width, hidden = expand.shape
     block = min(512, low.shape[0])
-    shape = (wide_count // 2, width // wide_count, 2 * hidden)
     row_spec = pl.BlockSpec((block, width), lambda i: (i, 0))
-    return stage(
+    (out,) = stage(
         hidden_grads_kernel,
         "hidden_grads",
         ids,
         [low, grad, expand, reduce_part],
-        [sds(shape, BF), sds(shape, BF)],
+        [sds((width, 2 * hidden), BF)],
         [pltpu.VMEM((width, 2 * hidden), F32)],
         flops=8 * low.size * hidden,
         grid=(low.shape[0] // block,),
         specs={0: row_spec, 1: row_spec},
     )
-
-
-def attend_grads_kernel(vectors, ids, normed, g_proj, att, back, *rest):
+    return out
+
+
+def output_grads_kernel(vectors, ids, att_d, back_d, att_r, back_r, *rest):
     rest = list(rest)
     vecs, rest = rest[:vectors], rest[vectors:]
     keep, send, total = rest
-    width = normed.shape[1]
-    total[:, 0 : 3 * width] = tn_dot(normed[...], g_proj[...])
-    total[:, 3 * width : 4 * width] = tn_dot(att[...], back[...])
-    if vectors:
-        rows = [vec[0:1, :] for vec in vecs]
-        rows.append(jnp.zeros((128 - vectors, width), F32))
-        total[:, 4 * width : 4 * width + 128] = jnp.concatenate(rows, axis=0).T
+    width = att_d.shape[1]
+    total[:, 0:width] = tn_dot(att_d[...], back_d[...])
+    total[:, width : 2 * width] = tn_dot(att_r[...], back_r[...])
+    rows = [vec[0:1, :] for vec in vecs]
+    rows.append(jnp.zeros((128 - vectors, width), F32))
+    total[:, 2 * width : 2 * width + 128] = jnp.concatenate(rows, axis=0).T
     split_rows(ids[0], total, keep, send)
 
 
-def attend_grads(ids, wide_count, normed, g_proj, att, back, vecs):
-    rows, width = normed.shape
-    columns = 4 * width + (128 if vecs else 0)
+def output_grads(ids, wide_count, att_d, back_d, att_r, back_r, vecs):
+    rows, width = att_d.shape
+    columns = 2 * width + 128
     shape = (wide_count // 2, width // wide_count, columns)
     return stage(
-        partial(attend_grads_kernel, len(vecs)),
-        "attend_grads",
-        ids,
-        [normed, g_proj, att, back] + list(vecs),
+        partial(output_grads_kernel, len(vecs)),
+        "output_grads",
+        ids,
+        [att_d, back_d, att_r, back_r] + list(vecs),
         [sds(shape, BF), sds(shape, BF)],
         [pltpu.VMEM((width, columns), F32)],
-        flops=8 * rows * width * width,
+        flops=3 * rows * width * width,
     )
 
 
@@ -774,16 +858,15 @@
         out[...] = (keep[at].astype(F32) + came[at].astype(F32)).astype(BF)
 
 
-def reduce_wide(ids, wide_count, keep, send):
-    came = lax.ppermute(send, "wide", [(j, j ^ 1) for j in range(wide_count)])
+def join_chips(ids, keep, came):
     chips = keep.shape[0]
-    parts = stage(
+    return stage(
         partial(join_kernel, chips), "join", ids, [keep, came], [sds(keep.shape[1:], BF)] * chips
     )
-    return [parts[0]] + [
-        lax.ppermute(parts[s], "wide", [(j, j ^ (2 * s)) for j in range(wide_count)])
-        for s in range(1, chips)
-    ]
+
+
+def chips_return(parts):
+    return [parts[0]] + [chip_step(parts[s], s) for s in range(1, len(parts))]
 
 
 def sum_terms(terms):
@@ -813,15 +896,17 @@
 
 
 def gather_out_kernel(count, ids, *rest):
-    pieces, outs = rest[:count], rest[count:]
+    pieces, outs, wide_s = rest[:count], rest[count:-1], rest[-1]
     rows = pieces[0].shape[0]
     for s, piece in enumerate(pieces):
         at = pl.ds(pl.multiple_of((ids[1] ^ s) * rows, rows), rows)
         low = 0
-        for out in outs:
+        for out in outs[:-1]:
             columns = out.shape[1]
             out[at, :] = piece[:, low : low + columns].astype(F32)
             low += columns
+        wide_s[at, :] = piece[:, low:].astype(F32)
+    outs[-1][...] = wide_s[...].T[: outs[-1].shape[0], :]
 
 
 def reduce_narrow(ids, terms, widths):
@@ -833,6 +918,7 @@
         for size in widths:
             outs.append(total[:, low : low + size])
             low += size
+        outs[-1] = outs[-1].T[:8]
         return outs
     share = rows // narrow_count
     parts = stage(
@@ -851,8 +937,111 @@
         "gather_out",
         ids,
         pieces,
-        [sds((rows, size), F32) for size in widths],
-    )
+        [sds((rows, size), F32) for size in widths[:-1]] + [sds((8, rows), F32)],
+        [pltpu.VMEM((rows, widths[-1]), F32)],
+    )
+
+
+def join_narrow_kernel(count, ids, keep, came, *outs):
+    each = outs[0].shape[0]
+    for t, out in enumerate(outs):
+        for j in range(each):
+            at = (ids[1] ^ t) * each + j
+            out[j] = (keep[at].astype(F32) + came[at].astype(F32)).astype(BF)
+
+
+def route_kernel(count, ids, *rest):
+    pieces, outs, blocks = rest[:count], rest[count:-1], rest[-1]
+    each = pieces[0].shape[0]
+    for t, piece in enumerate(pieces):
+        for j in range(each):
+            blocks[(ids[1] ^ t) * each + j] = piece[j]
+    chip = lax.div(ids[0], 2)
+    for s, out in enumerate(outs):
+        out[...] = blocks[chip ^ s]
+
+
+def unpack_kernel(ids, *rest):
+    pieces, own, own_gain, out, gain_ref, parts = (rest[:GROUPS],) + rest[GROUPS:]
+    for s, piece in enumerate(pieces):
+        group = lax.rem(lax.div(ids[0], 2) ^ s, GROUPS)
+        parts[group] = piece[...].astype(F32)
+    rows = out.shape[0]
+    total = jnp.zeros((rows, GW), F32)
+    for t in range(3):
+        for c in range(GROUPS):
+            at = (t * GROUPS + c) * GW
+            part = parts[c, :, t * GW : (t + 1) * GW]
+            out[:, at : at + GW] = part
+            total = total + part * own[:, at : at + GW].astype(F32)
+    sums = jnp.broadcast_to(jnp.sum(total, axis=1, keepdims=True), (rows, 128)).T
+    gain_ref[...] = sums[0:8, :] / own_gain[...]
+
+
+def unpack(ids, pieces, own, own_gain):
+    rows, columns = pieces[0].shape
+    return stage(
+        unpack_kernel,
+        "unpack",
+        ids,
+        list(pieces) + [own, own_gain],
+        [sds((rows, GROUPS * columns), F32), sds((8, rows), F32)],
+        [pltpu.VMEM((GROUPS, rows, columns), F32)],
+    )
+
+
+def split_narrow(ids, keep, came):
+    narrow_count = lax.axis_size("narrow")
+    chips, rows, columns = keep.shape
+    shape = (chips // narrow_count, rows, columns)
+    return stage(
+        partial(join_narrow_kernel, narrow_count),
+        "join_narrow",
+        ids,
+        [keep, came],
+        [sds(shape, BF)] * narrow_count,
+    )
+
+
+def sum_project(ids, parts):
+    (total,) = stage(
+        sum_kernel, "sum_terms", ids, narrow_return(parts), [sds(parts[0].shape, BF)]
+    )
+    return total
+
+
+def route_project(ids, gathered, chips):
+    rows, columns = gathered[0].shape[1:]
+    return stage(
+        partial(route_kernel, len(gathered)),
+        "route",
+        ids,
+        gathered,
+        [sds((rows, columns), BF)] * GROUPS,
+        [pltpu.VMEM((chips, rows, columns), BF)],
+    )
+
+
+def finish_hidden_kernel(ids, dense, routed, e_d, r_d, e_r, r_r):
+    hidden = e_d.shape[1]
+    for total, e_ref, r_ref in ((dense, e_d, r_d), (routed, e_r, r_r)):
+        e_ref[...] = total[:, 0:hidden].astype(F32)
+        r_ref[...] = total[:, hidden : 2 * hidden].astype(F32)
+
+
+def finish_hidden(ids, dense, routed):
+    rows, columns = dense.shape
+    return stage(
+        finish_hidden_kernel,
+        "finish_hidden",
+        ids,
+        [dense, routed],
+        [sds((rows, columns // 2), F32)] * 4,
+    )
+
+
+def tie(x, *first):
+    return lax.optimization_barrier((x, first))[0]
 
 
 def narrow_step(x, s):
@@ -875,32 +1064,40 @@
     ]
 
 
-def gather_hidden_weights(expand, reduce_part):
+def exchange_rows(mine, other):
+    wide_count = lax.axis_size("wide")
+    if wide_count != 8:
+        return exchange([mine, other] * (wide_count // 2))
+    beside = core_step(other)
+    from_x = [chip_step(mine, 1), chip_step(beside, 1)]
+    from_y = [chip_step(mine, 2), chip_step(beside, 2)]
+    corner = [chip_step(from_y[0], 1), chip_step(from_x[1], 2)]
+    return [mine, beside] + from_x + from_y + corner
+
+
+def hidden_share(expand, reduce_part):
     wide_count = lax.axis_size("wide")
     here = lax.axis_index("wide")
     width, hidden = expand.shape
     rows = width // wide_count
     if width != hidden or rows % 16:
-        return [
-            lax.all_gather(expand, "narrow", axis=0),
-            lax.all_gather(reduce_part, "narrow", axis=0),
-        ]
-    share = jnp.stack(
+        return None
+    return jnp.stack(
         [
             lax.dynamic_slice_in_dim(expand, here * rows, rows, 0),
             lax.dynamic_slice_in_dim(reduce_part, here * rows, rows, 0),
         ]
     )
-    mine = lax.all_gather(share, "narrow", axis=0)
-    pieces = [None] * wide_count
-    pieces[0] = mine
-    for s in range(2, wide_count, 2):
-        pieces[s] = lax.ppermute(mine, "wide", [(j, j ^ s) for j in range(wide_count)])
-    for s in range(1, wide_count, 2):
-        pieces[s] = lax.ppermute(
-            pieces[s - 1], "wide", [(j, j ^ 1) for j in range(wide_count)]
-        )
-    return pieces
+
+
+def chip_step(x, s):
+    return lax.ppermute(
+        x, "wide", [(j, j ^ (2 * s)) for j in range(lax.axis_size("wide"))]
+    )
+
+
+def core_step(x):
+    return lax.ppermute(x, "wide", [(j, j ^ 1) for j in range(lax.axis_size("wide"))])
 
 
 def on_device(
@@ -931,15 +1128,13 @@
     bq_dense = min(256, row_length)
     bq_routed = min(256, slot_count * wide_count)
     ids = jnp.stack([here, lax.axis_index("narrow")]).astype(jnp.int32)
-    router = router_vector[None]
-    gains = [
-        gain[None] for gain in (prenorm_routed, midnorm_routed, prenorm_dense, midnorm_dense)
-    ]
     tok = tokens.reshape(-1, width)
     cot = cotangent.reshape(-1, width)
 
-    ffn_weights = gather_hidden_weights(expand_dense, reduce_dense)
-    cot_all = lax.all_gather(cot, "narrow", axis=0, tiled=True)
+    share_d = hidden_share(expand_dense, reduce_dense)
+    staged = share_d is not None
+    if staged:
+        own_d = lax.all_gather(share_d, "narrow", axis=0)
 
     mine = here % seq_count
     seq_segments = lax.dynamic_slice_in_dim(segments, mine, 1, 0)[0]
@@ -967,8 +1162,33 @@
         jnp.broadcast_to(slot_segments[None], (8, slot_segments.shape[0])),
         slot_segments[:, None],
     )
+    own_selected = selected
+    if span_rows % 128:
+        own_selected = lax.dynamic_slice_in_dim(selected, here * span_rows, span_rows, 1)
+    mine_r, other_r, one_hot, picked, vecs = routed_pre(
+        ids,
+        tok,
+        own_selected,
+        span_rows,
+        [router_vector, prenorm_routed, midnorm_routed, prenorm_dense, midnorm_dense],
+    )
+    columns_r = group_columns(ids, tie(project_routed, mine_r))
+    rows_r = exchange([mine_r, other_r] * (wide_count // 2))
+    rows_r, meta_routed = lax.optimization_barrier((rows_r, meta_routed))
+    pieces, kept_r = attend(ids, meta_routed, rows_r, columns_r, bq_routed)
+    pieces = exchange(pieces)
+    if staged:
+        pieces, own_d = lax.optimization_barrier((pieces, own_d))
+        chips_d = lax.all_gather(
+            own_d,
+            "wide",
+            axis=0,
+            axis_index_groups=[list(range(r, wide_count, 2)) for r in range(2)],
+        )
+    branch_r, low_r, att_r = routed_mid(ids, pieces, output_routed, picked, vecs)
+    dense_segments = tie(seq_segments, low_r)
     starts = sum(
-        jnp.where(seq_segments == value, jnp.sum((seq_segments < value).astype(jnp.int32)), 0)
+        jnp.where(dense_segments == value, jnp.sum((dense_segments < value).astype(jnp.int32)), 0)
         for value in range(1, 4)
     )
     meta_dense = (
@@ -977,113 +1197,125 @@
         None,
     )
 
-    own_selected = lax.dynamic_slice_in_dim(selected, here * span_rows, span_rows, 1)
-    pieces, one_hot, picked, normed_r = routed_pre(
-        ids, wide_count, tok, own_selected, router, gains[0], project_routed
-    )
-    x_r = exchange(pieces)
-    pieces, att_seq_r, lse_r = attend(ids, meta_routed, x_r, bq_routed)
-    branch_r, low_r, att_r = routed_mid(ids, exchange(pieces), output_routed, picked, gains[1])
-    low_pieces = narrow_gather(low_r)
+    own_at = here * (width // wide_count)
+
+    def own_slice(x):
+        return lax.dynamic_slice_in_dim(tie(x, low_r), own_at, width // wide_count, 0)
+
+    own_rows = (
+        own_slice(project_routed),
+        own_slice(project_dense),
+        own_slice(prenorm_routed).astype(F32)[None],
+        own_slice(prenorm_dense).astype(F32)[None],
+    )
+    columns_d = group_columns(ids, tie(project_dense, low_r))
+    low_pieces, columns_d, meta_dense, own_rows = lax.optimization_barrier(
+        (narrow_gather(low_r), columns_d, meta_dense, own_rows)
+    )
     partials = narrow_return(hidden_forward(ids, low_pieces, expand_routed, reduce_routed))
 
-    pieces, mixed, delta_r, normed_d = dense_pre(
-        ids,
-        wide_count,
-        tok,
-        one_hot,
-        picked,
-        router,
-        branch_r,
-        partials,
-        gains[2],
-        project_dense,
-    )
-    x_d = exchange(pieces)
-    pieces, att_seq_d, lse_d = attend(ids, meta_dense, x_d, bq_dense)
+    mine_d, other_d, mixed, delta_r = dense_pre(
+        ids, tok, one_hot, picked, vecs, branch_r, partials
+    )
+    if staged:
+        mine_d, other_d, chips_d = lax.optimization_barrier((mine_d, other_d, chips_d))
+    cot_all = lax.all_gather(tie(cot, mine_d), "narrow", axis=0, tiled=True)
+    rows_d = exchange_rows(mine_d, other_d)
+    if staged:
+        weights_d = [chips_d, core_step(chips_d)]
+    else:
+        weights_d = [
+            lax.all_gather(expand_dense, "narrow", axis=0),
+            lax.all_gather(reduce_dense, "narrow", axis=0),
+        ]
+    pieces, kept_d = attend(ids, meta_dense, rows_d, columns_d, bq_dense)
+    pieces, weights_d = lax.optimization_barrier((pieces, weights_d))
+    pieces, cot_all = lax.optimization_barrier((exchange(pieces), cot_all))
     (activations, low_d, back_d, sum_d, att_d, mid_gain_d), pieces = dense_ffn(
-        ids, wide_count, exchange(pieces), output_dense, mixed, cot, gains[3], ffn_weights
+        ids, wide_count, pieces, output_dense, mixed, cot, vecs, weights_d
     )
     low_all = lax.all_gather(low_d, "narrow", axis=0, tiled=True)
-    pieces = attend_back(ids, meta_dense, x_d, exchange(pieces), att_seq_d, lse_d, bq_dense)
-    g_mixed, g_proj_d, g_delta, g_low, g_gate, pre_gain_d = dense_post(
-        ids,
-        exchange(pieces),
-        project_dense,
-        gains[2],
-        mixed,
-        sum_d,
-        one_hot,
-        picked,
-        router,
-        delta_r,
-    )
-    keep, send = hidden_grads(ids, wide_count, low_all, cot_all, expand_dense, reduce_dense)
-    ffn_d = reduce_wide(ids, wide_count, keep, send)
+    _, dx_d = attend_back(ids, meta_dense, kept_d, exchange(pieces), bq_dense, send=False)
+    stack = lax.all_to_all(dx_d.reshape(wide_count, span_rows, 3 * GW), "wide", 0, 0)
+    keep, send = project_grads(ids, wide_count, rows_d, dx_d)
+    project_d = sum_project(ids, split_narrow(ids, keep, core_step(send)))
+    stack, project_d = lax.optimization_barrier((stack, project_d))
+    project_d_parts = route_project(ids, narrow_gather(project_d), keep.shape[0])
+    g_mixed, g_delta, g_low, g_gate, router_grad = dense_post(
+        ids, stack, project_dense, vecs, mixed, sum_d, one_hot, picked, delta_r
+    )
 
     g_pieces = narrow_gather(g_low)
-    partials = narrow_return(
-        hidden_back(ids, low_pieces, g_pieces, expand_routed, reduce_routed)
-    )
-    g_mid_r, back_r, mid_gain_r, pieces = routed_back(
-        ids, wide_count, partials, branch_r, picked, gains[1], g_delta, output_routed
-    )
-    keep, send = attend_grads(ids, wide_count, normed_d, g_proj_d, att_d, back_d, [])
-    att_terms_d = reduce_wide(ids, wide_count, keep, send)
-    keep, send = hidden_grads(
-        ids,
-        wide_count,
+    hidden_d = hidden_grads(ids, tie(low_all, g_low), cot_all, expand_dense, reduce_dense)
+    g_pieces, hidden_d, project_d_parts = lax.optimization_barrier(
+        (g_pieces, hidden_d, project_d_parts)
+    )
+    project_d_grad, pre_gain_d = unpack(
+        ids, chips_return(project_d_parts), own_rows[1], own_rows[3]
+    )
+    ffn_d = lax.psum_scatter(hidden_d, "wide", scatter_dimension=0, tiled=True)
+    partials = hidden_back(ids, low_pieces, g_pieces, expand_routed, reduce_routed)
+    hidden_r = hidden_grads(
+        ids,
         jnp.concatenate(low_pieces, axis=0),
         jnp.concatenate(g_pieces, axis=0),
         expand_routed,
         reduce_routed,
     )
-    ffn_r = reduce_wide(ids, wide_count, keep, send)
-    pieces = attend_back(ids, meta_routed, x_r, exchange(pieces), att_seq_r, lse_r, bq_routed)
-    tokens_gradient, g_proj_r, pre_gain_r, router_grad = routed_post(
-        ids,
-        exchange(pieces),
-        project_routed,
-        gains[0],
-        picked,
-        g_mid_r,
-        g_mixed,
-        one_hot,
-        g_gate,
-        router,
-    )
-    keep, send = attend_grads(
+    partials, hidden_r, project_d_grad = lax.optimization_barrier(
+        (narrow_return(partials), hidden_r, project_d_grad)
+    )
+    ffn_r = lax.psum_scatter(hidden_r, "wide", scatter_dimension=0, tiled=True)
+    g_mid_r, back_r, mid_gain_r, pieces = routed_back(
+        ids, wide_count, partials, branch_r, picked, vecs, g_delta, output_routed
+    )
+    keep_o, send_o = output_grads(
         ids,
         wide_count,
-        normed_r,
-        g_proj_r,
+        att_d,
+        back_d,
         att_r,
         back_r,
-        [pre_gain_r, mid_gain_r, pre_gain_d, mid_gain_d, router_grad],
-    )
-    att_terms_r = reduce_wide(ids, wide_count, keep, send)
-
-    project_d_grad, output_d_grad = reduce_narrow(ids, att_terms_d, [3 * width, width])
-    project_r_grad, output_r_grad, vectors = reduce_narrow(
-        ids, att_terms_r, [3 * width, width, 128]
-    )
-    ffn_r_sum, ffn_d_sum = sum_terms(ffn_r), sum_terms(ffn_d)
+        [mid_gain_r, mid_gain_d, router_grad],
+    )
+    pieces, keep_o, send_o = lax.optimization_barrier((exchange(pieces), keep_o, send_o))
+    pieces, dx_r = attend_back(ids, meta_routed, kept_r, pieces, bq_routed)
+    keep, send = project_grads(ids, wide_count, rows_r, dx_r)
+    output_parts = join_chips(ids, tie(keep_o, send), core_step(send_o))
+    project_parts = split_narrow(ids, keep, core_step(tie(send, output_parts)))
+    output_terms, pieces, project_parts = lax.optimization_barrier(
+        (chips_return(output_parts), pieces, project_parts)
+    )
+    project_r = sum_project(ids, project_parts)
+    project_r_terms = chips_return(
+        route_project(ids, narrow_gather(project_r), keep.shape[0])
+    )
+    output_d_grad, output_r_grad, vectors = reduce_narrow(
+        ids, output_terms, [width, width, 128]
+    )
+    project_r_grad, pre_gain_r = unpack(ids, project_r_terms, own_rows[0], own_rows[2])
+    tokens_gradient = routed_post(
+        ids, exchange(pieces), project_routed, vecs, picked, g_mid_r, g_mixed, one_hot, g_gate
+    )
+    expand_d_grad, reduce_d_grad, expand_r_grad, reduce_r_grad = finish_hidden(
+        ids, ffn_d, ffn_r
+    )
     return (
         activations.reshape(tokens.shape),
         tokens_gradient.reshape(tokens.shape),
-        vectors[:, 4],
+        vectors[2],
         project_r_grad,
         output_r_grad,
-        vectors[:, 0],
-        vectors[:, 1],
-        ffn_r_sum[:, :hidden],
-        ffn_r_sum[:, hidden:].T,
+        pre_gain_r[0],
+        vectors[0],
+        expand_r_grad,
+        reduce_r_grad.T,
         project_d_grad,
         output_d_grad,
-        vectors[:, 2],
-        vectors[:, 3],
-        ffn_d_sum[:, :hidden],
-        ffn_d_sum[:, hidden:].T,
+        pre_gain_d[0],
+        vectors[1],
+        expand_d_grad,
+        reduce_d_grad.T,
     )
 
 

time: 608 us -> 494 us (0.81)
  waiting for transfers between devices: 231 us -> 114 us
  starting transfers between devices: 136 us -> 116 us
  Pallas kernels: 183 us -> 198 us
  local copies, waits for them, and re-layouts: 26.5 us -> 34.7 us
    ppermute x56 -> x42, waiting for transfers between devices: 134 us -> 28.9 us  [exchange(): lax.ppermute(pieces[s], 'wide', [(j, j ^ s) for j in range(wide_count)])]
    ppermute x24 -> x30, waiting for transfers between devices: 86.4 us -> 28.5 us  [narrow_step(): lax.ppermute(x, 'narrow', [(j, j ^ s) for j in range(lax.axis_size('narro...]
    ppermute x23 -> x20, waiting for transfers between devices: 10.1 us -> 50 us  [the longest x15 42.3 us: chip_step(): lax.ppermute(x, 'wide', [(j, j ^ 2 * s) for j in range(lax.axis_size('wid...]
    ppermute x56 -> x42, starting transfers between devices: 58.8 us -> 38.1 us  [exchange(): lax.ppermute(pieces[s], 'wide', [(j, j ^ s) for j in range(wide_count)])]
    pallas_call x27 -> x33, Pallas kernels: 183 us -> 198 us  [stage(): pl.pallas_call(body, out_shape=tuple(outs), in_specs=in_specs, out_specs=...]
    ppermute x24 -> x30, starting transfers between devices: 56.4 us -> 52.5 us  [narrow_step(): lax.ppermute(x, 'narrow', [(j, j ^ s) for j in range(lax.axis_size('narro...]
    unnamed x218 -> x226, local copies, waits for them, and re-layouts: 13.5 us -> 16.2 us
    ppermute x23 -> x20, starting transfers between devices: 21.1 us -> 20.4 us  [the longest x15 18.5 us: chip_step(): lax.ppermute(x, 'wide', [(j, j ^ 2 * s) for j in range(lax.axis_size('wid...]
  transfers between devices with their start and end apart: 106 -> 99, of which waited for: 49 -> 33; matrix products, arithmetic and copies ran while one was open for 3% -> 5% of each run, Pallas kernels for 31% -> 36%
where the time goes in v3:
time: 494 us; the launch traced here: 487 us
  Pallas kernels  198 us (40%)
  starting transfers between devices  116 us (23%)
  waiting for transfers between devices  114 us (23%)
  local copies, waits for them, and re-layouts  34.7 us (7%)
  between operations  15.5 us (3%)
  other arithmetic  9.24 us (2%)
    pallas_call x33, Pallas kernels, stage(): pl.pallas_call(body, out_shape=tuple(outs), in_specs=in_specs, out_specs=...  198 us
    ppermute x30, starting transfers between devices, narrow_step(): lax.ppermute(x, 'narrow', [(j, j ^ s) for j in range(lax.axis_size('narro...  52.5 us
    ppermute x15, waiting for transfers between devices, chip_step(): lax.ppermute(x, 'wide', [(j, j ^ 2 * s) for j in range(lax.axis_size('wid...  42.3 us
    ppermute x42, starting transfers between devices, exchange(): lax.ppermute(pieces[s], 'wide', [(j, j ^ s) for j in range(wide_count)])  38.1 us
    ppermute x42, waiting for transfers between devices, exchange(): lax.ppermute(pieces[s], 'wide', [(j, j ^ s) for j in range(wide_count)])  28.9 us
    ppermute x30, waiting for transfers between devices, narrow_step(): lax.ppermute(x, 'narrow', [(j, j ^ s) for j in range(lax.axis_size('narro...  28.5 us
    ppermute x15, starting transfers between devices, chip_step(): lax.ppermute(x, 'wide', [(j, j ^ 2 * s) for j in range(lax.axis_size('wid...  18.5 us
    unnamed x226, local copies, waits for them, and re-layouts  16.2 us
  transfers between devices with their start and end apart: 99, of which 33 were waited for; matrix products, arithmetic and copies ran while one was open for 5% of the time, Pallas kernels for 36%

profile of v3, /device:TPU:0, one launch (start us, length us, event | category | flops | bytes accessed | tf_op | source)
XLA Modules:
  0.0 487.4 jit_solution(9864603836482501736)
XLA Ops:
  12.2 2.9 collective-permute-start.1
  22.2 3.1 group_columns.2.rest_9_
  29.1 6.4 %attend.2 = (bf16[64,192]{1,0:T(8,128)(2,1)}, bf16[64,192]{1,0:T(8,128)(2,1)}, bf16[64,192]{1,0:T(8,128)(2,1)}, bf16[64,192]{1,0:T(8,128)(2,1)}, bf16[64,192]{1,...) custom-call(s32[2]{0:T(128)} %pad_add_fusion.ids, ...), custom_call_target="tpu_custom_call" | custom-call | flops 553648128 | bytes 2689032 | tf_op jit(solution)/shard_map/attend/pallas_call | solution.py:140
  55.5 3.2 group_columns.3.rest_8_
  68.1 4.3 hidden_forward.1
  72.4 3.7 collective-permute-start.17
  78.5 4.7 collective-permute-done.17.rest_1_
  83.2 10.2 %collective-permute-done.18.rest_2_ = bf16[128,768]{1,0:T(8,128)(2,1)S(1)} collective-permute-done((bf16[128,768]{1,0:T(8,128)(2,1)}, bf16[128,768]{1,0:T(8,128)(2,1)S(1)}, u32[]{:S(2)}, u32[]{:S(2)}) %collective-permute-start.18) | collective-permute-done | bytes 196640 | tf_op jit(solution)/shard_map/ppermute | solution.py:1048
  94.1 3.8 dense_pre.1
  97.9 4.9 %all-gather.13.cloned.1.call-done = bf16[16,2,96,768]{3,2,1,0:T(8,128)(2,1)} async-done(((bf16[4,2,96,768]{3,2,1,0:T(8,128)(2,1)}), bf16[16,2,96,768]{3,2,1,0:T(8,128)(2,1)}) %all-gather.13.cloned.1.call-update) | async-done | bytes 4718608 | tf_op jit(solution)/shard_map/all_gather | solution.py:1182
  105.4 6.0 %collective-permute-done.20.rest_1_ = bf16[256,768]{1,0:T(8,128)(2,1)S(1)} collective-permute-done((bf16[256,768]{1,0:T(8,128)(2,1)}, bf16[256,768]{1,0:T(8,128)(2,1)S(1)}, u32[]{:S(2)}, u32[]{:S(2)}) %collective-permute-start.20) | collective-permute-done | bytes 393248 | tf_op jit(solution)/shard_map/ppermute | solution.py:1100
  116.8 6.6 %collective-permute-done.22.rest_3_ = bf16[256,768]{1,0:T(8,128)(2,1)S(1)} collective-permute-done((bf16[256,768]{1,0:T(8,128)(2,1)S(1)}, bf16[256,768]{1,0:T(8,128)(2,1)S(1)}, u32[]{:S(2)}, u32[]{:S(2)}) %collective-permute-start.22) | collective-permute-done | bytes 393248 | tf_op jit(solution)/shard_map/ppermute | solution.py:1094
  124.9 7.0 %collective-permute-done.21.rest_2_ = bf16[256,768]{1,0:T(8,128)(2,1)S(1)} collective-permute-done((bf16[256,768]{1,0:T(8,128)(2,1)}, bf16[256,768]{1,0:T(8,128)(2,1)S(1)}, u32[]{:S(2)}, u32[]{:S(2)}) %collective-permute-start.21) | collective-permute-done | bytes 393248 | tf_op jit(solution)/shard_map/ppermute | solution.py:1094
  131.8 7.6 %collective-permute-done.25.rest_6_ = bf16[256,768]{1,0:T(8,128)(2,1)S(1)} collective-permute-done((bf16[256,768]{1,0:T(8,128)(2,1)S(1)}, bf16[256,768]{1,0:T(8,128)(2,1)S(1)}, u32[]{:S(2)}, u32[]{:S(2)}) %collective-permute-start.25) | collective-permute-done | bytes 393248 | tf_op jit(solution)/shard_map/ppermute | solution.py:1094
  141.0 22.8 %attend.3 = (bf16[256,192]{1,0:T(8,128)(2,1)}, bf16[256,192]{1,0:T(8,128)(2,1)}, bf16[256,192]{1,0:T(8,128)(2,1)}, bf16[256,192]{1,0:T(8,128)(2,1)}, bf16[256,19...) custom-call(s32[2]{0:T(128)} %pad_add_fusion.ids, ...), custom_call_target="tpu_custom_call" | custom-call | flops 3422552064 | bytes 8093728 | tf_op jit(solution)/shard_map/attend/pallas_call | solution.py:140
  172.4 7.2 %collective-permute-done.32.rest_5_ = bf16[256,192]{1,0:T(8,128)(2,1)S(1)} collective-permute-done((bf16[256,192]{1,0:T(8,128)(2,1)}, bf16[256,192]{1,0:T(8,128)(2,1)S(1)}, u32[]{:S(2)}, u32[]{:S(2)}) %collective-permute-start.32) | collective-permute-done | bytes 98336 | tf_op jit(solution)/shard_map/ppermute | solution.py:1062
  180.3 20.8 %dense_ffn.1 = (bf16[512,768]{1,0:T(8,128)(2,1)}, bf16[512,768]{1,0:T(8,128)(2,1)}, bf16[512,768]{1,0:T(8,128)(2,1)}, f32[512,768]{1,0:T(8,128)}, bf16[512,768]{...) custom-call(s32[2]{0:T(128)} %pad_add_fusion.ids, ...), custom_call_target="tpu_custom_call" | custom-call | flops 10871635968 | bytes 19316736 | tf_op jit(solution)/shard_map/dense_ffn/pallas_call | solution.py:140
  210.3 7.4 %collective-permute-done.39.rest_6_ = bf16[256,192]{1,0:T(8,128)(2,1)S(1)} collective-permute-done((bf16[256,192]{1,0:T(8,128)(2,1)}, bf16[256,192]{1,0:T(8,128)(2,1)S(1)}, u32[]{:S(2)}, u32[]{:S(2)}) %collective-permute-start.39) | collective-permute-done | bytes 98336 | tf_op jit(solution)/shard_map/ppermute | solution.py:1062
  218.4 31.5 %attend_back.2.dx_ref = bf16[2048,576]{1,0:T(8,128)(2,1)} custom-call(s32[2]{0:T(128)} %pad_add_fusion.ids, s32[8]{0:T(128)} %and_select_fusion.first_ref, s32[8,2048]{1,0:T(8,128)} %broadcast_in_dim.62.row_ref, bf16[2048,576]{1,0:T(8,128)(2,1)} %get-tuple-element.329.rest_0_, bf16[256,192]{1,0:T(8,128)(2,1)} %get-tuple-element.330.rest_1_, ...), custom_call_target="tpu_custom_call" | custom-call | flops 4026531840 | bytes 6422560 | tf_op jit(solution)/shard_map/attend_back/pallas_call | solution.py:140
  249.9 4.3 copy.39
  254.3 3.6 all-to-all-start
  258.0 6.6 %project_grads.2 = (bf16[4,96,576]{2,1,0:T(8,128)(2,1)}, bf16[4,96,576]{2,1,0:T(8,128)(2,1)}) custom-call(s32[2]{0:T(128)} %pad_add_fusion.ids, bf16[2048,576]{1,0:T(8,128)(2,1)} %attend_back.2.dx_ref, bf16[256,768]{1,0:T(8,128)(2,1)} %get-tuple-element.296.rest_0_, bf16[256,768]{1,0:T(8,128)(2,1)} %copy-done.81, bf16[256,768]{1,0:T(8,128)(2,1)} %copy-done.84, ...), custom_call_target="tpu_custom_call" | custom-call | flops 1811939328 | bytes 6389760 | tf_op jit(solution)/shard_map/project_grads/pallas_call | solution.py:140
  269.5 3.9 collective-permute-start.44
  273.9 3.7 collective-permute-done.43.rest_1_
  277.5 5.5 %collective-permute-done.44.rest_2_ = bf16[1,96,576]{2,1,0:T(8,128)(2,1)S(1)} collective-permute-done((bf16[1,96,576]{2,1,0:T(8,128)(2,1)}, bf16[1,96,576]{2,1,0:T(8,128)(2,1)S(1)}, u32[]{:S(2)}, u32[]{:S(2)}) %collective-permute-start.44) | collective-permute-done | bytes 110624 | tf_op jit(solution)/shard_map/ppermute | solution.py:1048
  288.1 3.1 collective-permute-start.50
  291.7 2.8 copy.40.stack
  294.5 8.2 %dense_post.1 = (f32[512,768]{1,0:T(8,128)}, f32[128,768]{1,0:T(8,128)}, bf16[128,768]{1,0:T(8,128)(2,1)}, f32[128,128]{1,0:T(8,128)}, f32[8,768]{1,0:T(8,128)}) custom-call(s32[2]{0:T(128)} %pad_add_fusion.ids, bf16[8,256,576]{2,1,0:T(8,128)(2,1)} %copy.40.stack, bf16[768,2304]{1,0:T(8,128)(2,1)} %rest_0_.3, ...), custom_call_target="tpu_custom_call" | custom-call | flops 1811939328 | bytes 11976704 | tf_op jit(solution)/shard_map/dense_post/pallas_call | solution.py:140
  302.7 3.8 collective-permute-start.47
  310.4 15.2 %hidden_grads.2 = bf16[768,1536]{1,0:T(8,128)(2,1)} custom-call(s32[2]{0:T(128)} %pad_add_fusion.ids, bf16[2048,768]{1,0:T(8,128)(2,1)} %all-gather.9.cloned.1.call-done.low, bf16[2048,768]{1,0:T(8,128)(2,1)} %all-gather.7.cloned.1.call-done.grad, bf16[768,768]{1,0:T(8,128)(2,1)} %expand.2, bf16[768,768]{1,0:T(8,128)(2,1)} %reduce_ref.2), custom_call_target="tpu_custom_call" | custom-call | flops 9663676416 | bytes 11010048 | tf_op jit(solution)/shard_map/hidden_grads/pallas_call | solution.py:140
  331.6 5.5 %hidden_back.1 = (bf16[128,768]{1,0:T(8,128)(2,1)}, bf16[128,768]{1,0:T(8,128)(2,1)}, bf16[128,768]{1,0:T(8,128)(2,1)}, bf16[128,768]{1,0:T(8,128)(2,1)}) custom-call(s32[2]{0:T(128)} %pad_add_fusion.ids, bf16[128,768]{1,0:T(8,128)(2,1)} %get-tuple-element.285.rest_0_, bf16[128,768]{1,0:T(8,128)(2,1)} %copy-done.7, bf16[128,768]{1,0:T(8,128)(2,1)} %copy-done.9, ...), custom_call_target="tpu_custom_call" | custom-call | flops 1811939328 | bytes 4718592 | tf_op jit(solution)/shard_map/hidden_back/pallas_call | solution.py:140
  337.1 3.8 collective-permute-start.53
  342.5 6.3 %hidden_grads.3 = bf16[768,1536]{1,0:T(8,128)(2,1)} custom-call(s32[2]{0:T(128)} %pad_add_fusion.ids, bf16[512,768]{1,0:T(8,128)(2,1)} %pad_maximum_fusion.low, bf16[512,768]{1,0:T(8,128)(2,1)} %pad_maximum_fusion.1.grad, bf16[768,768]{1,0:T(8,128)(2,1)} %expand.3, bf16[768,768]{1,0:T(8,128)(2,1)} %reduce_ref.3), custom_call_target="tpu_custom_call" | custom-call | flops 2415919104 | bytes 6291456 | tf_op jit(solution)/shard_map/hidden_grads/pallas_call | solution.py:140
  350.1 2.9 unpack.2
  353.8 3.5 routed_back.1
  363.7 5.1 %output_grads.1 = (bf16[4,96,1664]{2,1,0:T(8,128)(2,1)}, bf16[4,96,1664]{2,1,0:T(8,128)(2,1)}) custom-call(s32[2]{0:T(128)} %pad_add_fusion.ids, bf16[512,768]{1,0:T(8,128)(2,1)} %get-tuple-element.386.att_d, bf16[512,768]{1,0:T(8,128)(2,1)} %get-tuple-element.387.back_d, bf16[128,768]{1,0:T(8,128)(2,1)} %get-tuple-element.388.att_r, ...), custom_call_target="tpu_custom_call" | custom-call | flops 905969664 | bytes 4595712 | tf_op jit(solution)/shard_map/output_grads/pallas_call | solution.py:140
  369.5 6.9 %attend_back.3 = (bf16[64,576]{1,0:T(8,128)(2,1)}, bf16[64,576]{1,0:T(8,128)(2,1)}, bf16[64,576]{1,0:T(8,128)(2,1)}, bf16[64,576]{1,0:T(8,128)(2,1)}, bf16[64,57...) custom-call(s32[2]{0:T(128)} %pad_add_fusion.ids, ...), custom_call_target="tpu_custom_call" | custom-call | flops 251658240 | bytes 2197512 | tf_op jit(solution)/shard_map/attend_back/pallas_call | solution.py:140
  376.4 4.9 %project_grads.3 = (bf16[4,96,576]{2,1,0:T(8,128)(2,1)}, bf16[4,96,576]{2,1,0:T(8,128)(2,1)}) custom-call(s32[2]{0:T(128)} %pad_add_fusion.ids, bf16[512,576]{1,0:T(8,128)(2,1)} %get-tuple-element.407.dx_ref, bf16[64,768]{1,0:T(8,128)(2,1)} %get-tuple-element.248.rest_1_.rest_0_, bf16[64,768]{1,0:T(8,128)(2,1)} %copy-done.47, bf16[64,768]{1,0:T(8,128)(2,1)} %copy-done.44, ...), custom_call_target="tpu_custom_call" | custom-call | flops 452984832 | bytes 2260992 | tf_op jit(solution)/shard_map/project_grads/pallas_call | solution.py:140
  382.4 3.0 join.1
  392.2 4.3 collective-permute-done.66.rest_1_
  396.5 6.3 %collective-permute-done.67.rest_2_ = bf16[96,1664]{1,0:T(8,128)(2,1)S(1)} collective-permute-done((bf16[96,1664]{1,0:T(8,128)(2,1)}, bf16[96,1664]{1,0:T(8,128)(2,1)S(1)}, u32[]{:S(2)}, u32[]{:S(2)}) %collective-permute-start.67) | collective-permute-done | bytes 319520 | tf_op jit(solution)/shard_map/ppermute | solution.py:1094
  402.9 5.5 %collective-permute-done.68.rest_3_ = bf16[96,1664]{1,0:T(8,128)(2,1)S(1)} collective-permute-done((bf16[96,1664]{1,0:T(8,128)(2,1)}, bf16[96,1664]{1,0:T(8,128)(2,1)S(1)}, u32[]{:S(2)}, u32[]{:S(2)}) %collective-permute-start.68) | collective-permute-done | bytes 319520 | tf_op jit(solution)/shard_map/ppermute | solution.py:1094
  411.3 4.0 collective-permute-start.77
  429.9 4.7 collective-permute-start.80
  441.1 2.9 collective-permute-start.81
  451.1 6.3 %routed_post.1 = f32[512,768]{1,0:T(8,128)} custom-call(s32[2]{0:T(128)} %pad_add_fusion.ids, bf16[64,576]{1,0:T(8,128)(2,1)} %get-tuple-element.429.rest_0_, bf16[64,576]{1,0:T(8,128)(2,1)} %copy-done.51, bf16[64,576]{1,0:T(8,128)(2,1)} %copy-done.52, bf16[64,576]{1,0:T(8,128)(2,1)} %copy-done.53, bf16[64,576]{1,0:T(8,128)(2,1)} %copy-done.54, ...), custom_call_target="tpu_custom_call" | custom-call | flops 452984832 | bytes 8019968 | tf_op jit(solution)/shard_map/routed_post/pallas_call | solution.py:140
  469.7 3.5 collective-permute-done.90.rest_2_
  473.9 2.9 unpack.3
  (448 shorter events, 164.6 us)
Async XLA Ops:
  7.2 37.8 %all-gather.11.cloned.1.call-start = ((), (), s32[]{:S(2)}) async-start(), calls=%async_computation.7 | async-start | bytes 1474560 | tf_op jit(solution)/shard_map/all_gather | solution.py:1137
  9.0 93.8 %all-gather.13.cloned.1.call-start = ((), (), s32[]{:S(2)}) async-start(), calls=%async_computation.8 | async-start | bytes 5898240 | tf_op jit(solution)/shard_map/all_gather | solution.py:1182
  45.0 125.7 %all-gather.7.cloned.1.call-start = ((), (), s32[]{:S(2)}) async-start(), calls=%async_computation.3 | async-start | bytes 3932160 | tf_op jit(solution)/shard_map/all_gather | solution.py:1222
  48.4 17.0 %collective-permute-start.14 = (bf16[128,768]{1,0:T(8,128)(2,1)}, bf16[128,768]{1,0:T(8,128)(2,1)S(1)}, u32[]{:S(2)}, u32[]{:S(2)}) collective-permute-start(bf16[128,768]{1,0:T(8,128)(2,1)} %get-tuple-element.285.rest_0_), channel_id=1, source_target_pairs={{0,1},{1,0},{2,3},{3,2},{4,5},{5,4},{6,7},{7,6},{8,9},{9,8},{10,11... | collective-permute-start | bytes 589832 | tf_op jit(solution)/shard_map/ppermute | solution.py:1048
  50.0 17.3 %collective-permute-start.15 = (bf16[128,768]{1,0:T(8,128)(2,1)}, bf16[128,768]{1,0:T(8,128)(2,1)S(1)}, u32[]{:S(2)}, u32[]{:S(2)}) collective-permute-start(bf16[128,768]{1,0:T(8,128)(2,1)} %get-tuple-element.285.rest_0_), channel_id=1, source_target_pairs={{0,2},{1,3},{2,0},{3,1},{4,6},{5,7},{6,4},{7,5},{8,10},{9,11},{10,... | collective-permute-start | bytes 589832 | tf_op jit(solution)/shard_map/ppermute | solution.py:1048
  52.7 14.7 %collective-permute-start.16 = (bf16[128,768]{1,0:T(8,128)(2,1)}, bf16[128,768]{1,0:T(8,128)(2,1)S(1)}, u32[]{:S(2)}, u32[]{:S(2)}) collective-permute-start(bf16[128,768]{1,0:T(8,128)(2,1)} %get-tuple-element.285.rest_0_), channel_id=1, source_target_pairs={{0,3},{1,2},{2,1},{3,0},{4,7},{5,6},{6,5},{7,4},{8,11},{9,10},{10,... | collective-permute-start | bytes 589832 | tf_op jit(solution)/shard_map/ppermute | solution.py:1048
  76.1 17.3 %collective-permute-start.18 = (bf16[128,768]{1,0:T(8,128)(2,1)}, bf16[128,768]{1,0:T(8,128)(2,1)S(1)}, u32[]{:S(2)}, u32[]{:S(2)}) collective-permute-start(bf16[128,768]{1,0:T(8,128)(2,1)} %get-tuple-element.291), channel_id=1, source_target_pairs={{0,2},{1,3},{2,0},{3,1},{4,6},{5,7},{6,4},{7,5},{8,10},{9,11},{10,... | collective-permute-start | bytes 589832 | tf_op jit(solution)/shard_map/ppermute | solution.py:1048
  77.0 16.4 %collective-permute-start.19 = (bf16[128,768]{1,0:T(8,128)(2,1)}, bf16[128,768]{1,0:T(8,128)(2,1)S(1)}, u32[]{:S(2)}, u32[]{:S(2)}) collective-permute-start(bf16[128,768]{1,0:T(8,128)(2,1)} %get-tuple-element.292), channel_id=1, source_target_pairs={{0,3},{1,2},{2,1},{3,0},{4,7},{5,6},{6,5},{7,4},{8,11},{9,10},{10,... | collective-permute-start | bytes 589832 | tf_op jit(solution)/shard_map/ppermute | solution.py:1048
  102.9 60.9 %collective-permute-start.27 = (bf16[4,4,2,96,768]{4,3,2,1,0:T(8,128)(2,1)}, bf16[4,4,2,96,768]{4,3,2,1,0:T(8,128)(2,1)}, u32[]{:S(2)}, u32[]{:S(2)}) collective-permute-start(bf16[4,4,2,96,768]{4,3,2,1,0:T(8,128)(2,1)} %bitcast.42), channel_id=1, source_target_pairs={{0,4},{4,0},{8,12},{12,8},{16,20},{20,16},{24,28},{28,24},{1,5},{5... | collective-permute-start | bytes 14155784 | tf_op jit(solution)/shard_map/ppermute | solution.py:1100
  102.9 207.5 %all-gather.9.cloned.1.call-start = ((), (), s32[]{:S(2)}) async-start(), calls=%async_computation.4 | async-start | bytes 3932160 | tf_op jit(solution)/shard_map/all_gather | solution.py:1237
  104.0 11.3 %collective-permute-start.23 = (bf16[256,768]{1,0:T(8,128)(2,1)}, bf16[256,768]{1,0:T(8,128)(2,1)S(1)}, u32[]{:S(2)}, u32[]{:S(2)}) collective-permute-start(bf16[256,768]{1,0:T(8,128)(2,1)} %get-tuple-element.296.rest_0_), channel_id=1, source_target_pairs={{0,16},{4,20},{8,24},{12,28},{16,0},{20,4},{24,8},{28,12},{1,17},{... | collective-permute-start | bytes 1179656 | tf_op jit(solution)/shard_map/ppermute | solution.py:1094
  111.4 12.0 %collective-permute-start.22 = (bf16[256,768]{1,0:T(8,128)(2,1)S(1)}, bf16[256,768]{1,0:T(8,128)(2,1)S(1)}, u32[]{:S(2)}, u32[]{:S(2)}) collective-permute-start(bf16[256,768]{1,0:T(8,128)(2,1)S(1)} %collective-permute-done.20.rest_1_), channel_id=1, source_target_pairs={{0,8},{4,12},{8,0},{12,4},{16,24},{20,28},{24,16},{28,20},{1,9},{5... | collective-permute-start | bytes 1179656 | tf_op jit(solution)/shard_map/ppermute | solution.py:1094
  112.9 18.9 %collective-permute-start.21 = (bf16[256,768]{1,0:T(8,128)(2,1)}, bf16[256,768]{1,0:T(8,128)(2,1)S(1)}, u32[]{:S(2)}, u32[]{:S(2)}) collective-permute-start(bf16[256,768]{1,0:T(8,128)(2,1)} %get-tuple-element.296.rest_0_), channel_id=1, source_target_pairs={{0,8},{4,12},{8,0},{12,4},{16,24},{20,28},{24,16},{28,20},{1,9},{5... | collective-permute-start | bytes 1179656 | tf_op jit(solution)/shard_map/ppermute | solution.py:1094
  113.5 18.4 %collective-permute-start.24 = (bf16[256,768]{1,0:T(8,128)(2,1)S(1)}, bf16[256,768]{1,0:T(8,128)(2,1)S(1)}, u32[]{:S(2)}, u32[]{:S(2)}) collective-permute-start(bf16[256,768]{1,0:T(8,128)(2,1)S(1)} %collective-permute-done.20.rest_1_), channel_id=1, source_target_pairs={{0,16},{4,20},{8,24},{12,28},{16,0},{20,4},{24,8},{28,12},{1,17},{... | collective-permute-start | bytes 1179656 | tf_op jit(solution)/shard_map/ppermute | solution.py:1094
  115.3 24.2 %collective-permute-start.25 = (bf16[256,768]{1,0:T(8,128)(2,1)S(1)}, bf16[256,768]{1,0:T(8,128)(2,1)S(1)}, u32[]{:S(2)}, u32[]{:S(2)}) collective-permute-start(bf16[256,768]{1,0:T(8,128)(2,1)S(1)} %collective-permute-done.23.rest_4_), channel_id=1, source_target_pairs={{0,8},{4,12},{8,0},{12,4},{16,24},{20,28},{24,16},{28,20},{1,9},{5... | collective-permute-start | bytes 1179656 | tf_op jit(solution)/shard_map/ppermute | solution.py:1094
  123.4 16.1 %collective-permute-start.26 = (bf16[256,768]{1,0:T(8,128)(2,1)S(1)}, bf16[256,768]{1,0:T(8,128)(2,1)S(1)}, u32[]{:S(2)}, u32[]{:S(2)}) collective-permute-start(bf16[256,768]{1,0:T(8,128)(2,1)S(1)} %collective-permute-done.22.rest_3_), channel_id=1, source_target_pairs={{0,16},{4,20},{8,24},{12,28},{16,0},{20,4},{24,8},{28,12},{1,17},{... | collective-permute-start | bytes 1179656 | tf_op jit(solution)/shard_map/ppermute | solution.py:1094
  167.2 12.3 %collective-permute-start.32 = (bf16[256,192]{1,0:T(8,128)(2,1)}, bf16[256,192]{1,0:T(8,128)(2,1)S(1)}, u32[]{:S(2)}, u32[]{:S(2)}) collective-permute-start(bf16[256,192]{1,0:T(8,128)(2,1)} %get-tuple-element.313), channel_id=1, source_target_pairs={{0,20},{4,16},{8,28},{12,24},{16,4},{20,0},{24,12},{28,8},{1,21},{... | collective-permute-start | bytes 294920 | tf_op jit(solution)/shard_map/ppermute | solution.py:1062
  167.4 12.1 %collective-permute-start.33 = (bf16[256,192]{1,0:T(8,128)(2,1)}, bf16[256,192]{1,0:T(8,128)(2,1)S(1)}, u32[]{:S(2)}, u32[]{:S(2)}) collective-permute-start(bf16[256,192]{1,0:T(8,128)(2,1)} %get-tuple-element.314), channel_id=1, source_target_pairs={{0,24},{4,28},{8,16},{12,20},{16,8},{20,12},{24,0},{28,4},{1,25},{... | collective-permute-start | bytes 294920 | tf_op jit(solution)/shard_map/ppermute | solution.py:1062
  204.7 13.0 %collective-permute-start.39 = (bf16[256,192]{1,0:T(8,128)(2,1)}, bf16[256,192]{1,0:T(8,128)(2,1)S(1)}, u32[]{:S(2)}, u32[]{:S(2)}) collective-permute-start(bf16[256,192]{1,0:T(8,128)(2,1)} %get-tuple-element.335), channel_id=1, source_target_pairs={{0,20},{4,16},{8,28},{12,24},{16,4},{20,0},{24,12},{28,8},{1,21},{... | collective-permute-start | bytes 294920 | tf_op jit(solution)/shard_map/ppermute | solution.py:1062
  205.3 12.4 %collective-permute-start.40 = (bf16[256,192]{1,0:T(8,128)(2,1)}, bf16[256,192]{1,0:T(8,128)(2,1)S(1)}, u32[]{:S(2)}, u32[]{:S(2)}) collective-permute-start(bf16[256,192]{1,0:T(8,128)(2,1)} %get-tuple-element.336), channel_id=1, source_target_pairs={{0,24},{4,28},{8,16},{12,20},{16,8},{20,12},{24,0},{28,4},{1,25},{... | collective-permute-start | bytes 294920 | tf_op jit(solution)/shard_map/ppermute | solution.py:1062
  254.3 33.0 %all-to-all-start = ((bf16[8,256,576]{1,2,0:T(8,128)(2,1)}), bf16[8,256,576]{1,2,0:T(8,128)(2,1)S(1)}, u32[]{:S(2)}, u32[]{:S(2)}) async-start(bf16[8,256,576]{1,2,0:T(8,128)(2,1)} %copy.39), calls=%async_computation | async-start | bytes 4718592 | tf_op jit(solution)/shard_map/all_to_all | solution.py:1239
  257.9 220.0 %reduce-scatter.3.cloned.1.call-start = ((), (), s32[]{:S(2)}) async-start(), calls=%async_computation.5 | async-start | bytes 2654208 | tf_op jit(solution)/shard_map/reduce_scatter | solution.py:1256
  269.5 13.5 %collective-permute-start.44 = (bf16[1,96,576]{2,1,0:T(8,128)(2,1)}, bf16[1,96,576]{2,1,0:T(8,128)(2,1)S(1)}, u32[]{:S(2)}, u32[]{:S(2)}) collective-permute-start(bf16[1,96,576]{2,1,0:T(8,128)(2,1)} %get-tuple-element.344), channel_id=1, source_target_pairs={{0,2},{1,3},{2,0},{3,1},{4,6},{5,7},{6,4},{7,5},{8,10},{9,11},{10,... | collective-permute-start | bytes 331784 | tf_op jit(solution)/shard_map/ppermute | solution.py:1048
  287.3 19.3 %collective-permute-start.49 = (bf16[1,96,576]{2,1,0:T(8,128)(2,1)}, bf16[1,96,576]{2,1,0:T(8,128)(2,1)S(1)}, u32[]{:S(2)}, u32[]{:S(2)}) collective-permute-start(bf16[1,96,576]{2,1,0:T(8,128)(2,1)} %sum_terms.3.rest_0_), channel_id=1, source_target_pairs={{0,1},{1,0},{2,3},{3,2},{4,5},{5,4},{6,7},{7,6},{8,9},{9,8},{10,11... | collective-permute-start | bytes 331784 | tf_op jit(solution)/shard_map/ppermute | solution.py:1048
  288.1 19.0 %collective-permute-start.50 = (bf16[1,96,576]{2,1,0:T(8,128)(2,1)}, bf16[1,96,576]{2,1,0:T(8,128)(2,1)S(1)}, u32[]{:S(2)}, u32[]{:S(2)}) collective-permute-start(bf16[1,96,576]{2,1,0:T(8,128)(2,1)} %sum_terms.3.rest_0_), channel_id=1, source_target_pairs={{0,2},{1,3},{2,0},{3,1},{4,6},{5,7},{6,4},{7,5},{8,10},{9,11},{10,... | collective-permute-start | bytes 331784 | tf_op jit(solution)/shard_map/ppermute | solution.py:1048
  291.2 15.9 %collective-permute-start.51 = (bf16[1,96,576]{2,1,0:T(8,128)(2,1)}, bf16[1,96,576]{2,1,0:T(8,128)(2,1)S(1)}, u32[]{:S(2)}, u32[]{:S(2)}) collective-permute-start(bf16[1,96,576]{2,1,0:T(8,128)(2,1)} %sum_terms.3.rest_0_), channel_id=1, source_target_pairs={{0,3},{1,2},{2,1},{3,0},{4,7},{5,6},{6,5},{7,4},{8,11},{9,10},{10,... | collective-permute-start | bytes 331784 | tf_op jit(solution)/shard_map/ppermute | solution.py:1048
  302.7 22.9 %collective-permute-start.46 = (bf16[128,768]{1,0:T(8,128)(2,1)}, bf16[128,768]{1,0:T(8,128)(2,1)S(1)}, u32[]{:S(2)}, u32[]{:S(2)}) collective-permute-start(bf16[128,768]{1,0:T(8,128)(2,1)} %get-tuple-element.358.rest_4_), channel_id=1, source_target_pairs={{0,1},{1,0},{2,3},{3,2},{4,5},{5,4},{6,7},{7,6},{8,9},{9,8},{10,11... | collective-permute-start | bytes 589832 | tf_op jit(solution)/shard_map/ppermute | solution.py:1048
  302.7 22.9 %collective-permute-start.47 = (bf16[128,768]{1,0:T(8,128)(2,1)}, bf16[128,768]{1,0:T(8,128)(2,1)S(1)}, u32[]{:S(2)}, u32[]{:S(2)}) collective-permute-start(bf16[128,768]{1,0:T(8,128)(2,1)} %get-tuple-element.358.rest_4_), channel_id=1, source_target_pairs={{0,2},{1,3},{2,0},{3,1},{4,6},{5,7},{6,4},{7,5},{8,10},{9,11},{10,... | collective-permute-start | bytes 589832 | tf_op jit(solution)/shard_map/ppermute | solution.py:1048
  306.6 19.1 %collective-permute-start.48 = (bf16[128,768]{1,0:T(8,128)(2,1)}, bf16[128,768]{1,0:T(8,128)(2,1)S(1)}, u32[]{:S(2)}, u32[]{:S(2)}) collective-permute-start(bf16[128,768]{1,0:T(8,128)(2,1)} %get-tuple-element.358.rest_4_), channel_id=1, source_target_pairs={{0,3},{1,2},{2,1},{3,0},{4,7},{5,6},{6,5},{7,4},{8,11},{9,10},{10,... | collective-permute-start | bytes 589832 | tf_op jit(solution)/shard_map/ppermute | solution.py:1048
  325.8 152.2 %reduce-scatter.5.cloned.1.call-start = ((), (), s32[]{:S(2)}) async-start(), calls=%async_computation.6 | async-start | bytes 2654208 | tf_op jit(solution)/shard_map/reduce_scatter | solution.py:1268
  328.0 13.9 %collective-permute-start.55 = (bf16[96,576]{1,0:T(8,128)(2,1)S(1)}, bf16[96,576]{1,0:T(8,128)(2,1)S(1)}, u32[]{:S(2)}, u32[]{:S(2)}) collective-permute-start(bf16[96,576]{1,0:T(8,128)(2,1)S(1)} %copy-done.105), channel_id=1, source_target_pairs={{0,8},{4,12},{8,0},{12,4},{16,24},{20,28},{24,16},{28,20},{1,9},{5... | collective-permute-start | bytes 331784 | tf_op jit(solution)/shard_map/ppermute | solution.py:1094
  328.6 20.2 %collective-permute-start.56 = (bf16[96,576]{1,0:T(8,128)(2,1)S(1)}, bf16[96,576]{1,0:T(8,128)(2,1)S(1)}, u32[]{:S(2)}, u32[]{:S(2)}) collective-permute-start(bf16[96,576]{1,0:T(8,128)(2,1)S(1)} %copy-done.104), channel_id=1, source_target_pairs={{0,16},{4,20},{8,24},{12,28},{16,0},{20,4},{24,8},{28,12},{1,17},{... | collective-permute-start | bytes 331784 | tf_op jit(solution)/shard_map/ppermute | solution.py:1094
  330.1 18.7 %collective-permute-start.57 = (bf16[96,576]{1,0:T(8,128)(2,1)S(1)}, bf16[96,576]{1,0:T(8,128)(2,1)S(1)}, u32[]{:S(2)}, u32[]{:S(2)}) collective-permute-start(bf16[96,576]{1,0:T(8,128)(2,1)S(1)} %copy-done.103), channel_id=1, source_target_pairs={{0,24},{4,28},{8,16},{12,20},{16,8},{20,12},{24,0},{28,4},{1,25},{... | collective-permute-start | bytes 331784 | tf_op jit(solution)/shard_map/ppermute | solution.py:1094
  337.1 15.9 %collective-permute-start.52 = (bf16[128,768]{1,0:T(8,128)(2,1)}, bf16[128,768]{1,0:T(8,128)(2,1)S(1)}, u32[]{:S(2)}, u32[]{:S(2)}) collective-permute-start(bf16[128,768]{1,0:T(8,128)(2,1)} %get-tuple-element.363), channel_id=1, source_target_pairs={{0,1},{1,0},{2,3},{3,2},{4,5},{5,4},{6,7},{7,6},{8,9},{9,8},{10,11... | collective-permute-start | bytes 589832 | tf_op jit(solution)/shard_map/ppermute | solution.py:1048
  337.1 15.9 %collective-permute-start.53 = (bf16[128,768]{1,0:T(8,128)(2,1)}, bf16[128,768]{1,0:T(8,128)(2,1)S(1)}, u32[]{:S(2)}, u32[]{:S(2)}) collective-permute-start(bf16[128,768]{1,0:T(8,128)(2,1)} %get-tuple-element.364), channel_id=1, source_target_pairs={{0,2},{1,3},{2,0},{3,1},{4,6},{5,7},{6,4},{7,5},{8,10},{9,11},{10,... | collective-permute-start | bytes 589832 | tf_op jit(solution)/shard_map/ppermute | solution.py:1048
  341.9 11.1 %collective-permute-start.54 = (bf16[128,768]{1,0:T(8,128)(2,1)S(1)}, bf16[128,768]{1,0:T(8,128)(2,1)S(1)}, u32[]{:S(2)}, u32[]{:S(2)}) collective-permute-start(bf16[128,768]{1,0:T(8,128)(2,1)S(1)} %copy-done.88), channel_id=1, source_target_pairs={{0,3},{1,2},{2,1},{3,0},{4,7},{5,6},{6,5},{7,4},{8,11},{9,10},{10,... | collective-permute-start | bytes 589832 | tf_op jit(solution)/shard_map/ppermute | solution.py:1048
  368.9 12.4 %collective-permute-start.65 = (bf16[4,96,1664]{2,1,0:T(8,128)(2,1)}, bf16[4,96,1664]{2,1,0:T(8,128)(2,1)S(1)}, u32[]{:S(2)}, u32[]{:S(2)}) collective-permute-start(bf16[4,96,1664]{2,1,0:T(8,128)(2,1)} %get-tuple-element.410), channel_id=1, source_target_pairs={{0,4},{4,0},{8,12},{12,8},{16,20},{20,16},{24,28},{28,24},{1,5},{5... | collective-permute-start | bytes 3833864 | tf_op jit(solution)/shard_map/ppermute | solution.py:1100
  387.2 15.7 %collective-permute-start.67 = (bf16[96,1664]{1,0:T(8,128)(2,1)}, bf16[96,1664]{1,0:T(8,128)(2,1)S(1)}, u32[]{:S(2)}, u32[]{:S(2)}) collective-permute-start(bf16[96,1664]{1,0:T(8,128)(2,1)} %get-tuple-element.413), channel_id=1, source_target_pairs={{0,16},{4,20},{8,24},{12,28},{16,0},{20,4},{24,8},{28,12},{1,17},{... | collective-permute-start | bytes 958472 | tf_op jit(solution)/shard_map/ppermute | solution.py:1094
  387.9 20.5 %collective-permute-start.68 = (bf16[96,1664]{1,0:T(8,128)(2,1)}, bf16[96,1664]{1,0:T(8,128)(2,1)S(1)}, u32[]{:S(2)}, u32[]{:S(2)}) collective-permute-start(bf16[96,1664]{1,0:T(8,128)(2,1)} %get-tuple-element.414), channel_id=1, source_target_pairs={{0,24},{4,28},{8,16},{12,20},{16,8},{20,12},{24,0},{28,4},{1,25},{... | collective-permute-start | bytes 958472 | tf_op jit(solution)/shard_map/ppermute | solution.py:1094
  417.9 17.2 %collective-permute-start.83 = (bf16[1,96,576]{2,1,0:T(8,128)(2,1)}, bf16[1,96,576]{2,1,0:T(8,128)(2,1)S(1)}, u32[]{:S(2)}, u32[]{:S(2)}) collective-permute-start(bf16[1,96,576]{2,1,0:T(8,128)(2,1)} %get-tuple-element.450), channel_id=1, source_target_pairs={{0,1},{1,0},{2,3},{3,2},{4,5},{5,4},{6,7},{7,6},{8,9},{9,8},{10,11... | collective-permute-start | bytes 331784 | tf_op jit(solution)/shard_map/ppermute | solution.py:1048
  418.8 16.9 %collective-permute-start.84 = (bf16[1,96,576]{2,1,0:T(8,128)(2,1)}, bf16[1,96,576]{2,1,0:T(8,128)(2,1)S(1)}, u32[]{:S(2)}, u32[]{:S(2)}) collective-permute-start(bf16[1,96,576]{2,1,0:T(8,128)(2,1)} %get-tuple-element.451), channel_id=1, source_target_pairs={{0,2},{1,3},{2,0},{3,1},{4,6},{5,7},{6,4},{7,5},{8,10},{9,11},{10,... | collective-permute-start | bytes 331784 | tf_op jit(solution)/shard_map/ppermute | solution.py:1048
  420.9 16.3 %collective-permute-start.85 = (bf16[1,96,576]{2,1,0:T(8,128)(2,1)}, bf16[1,96,576]{2,1,0:T(8,128)(2,1)S(1)}, u32[]{:S(2)}, u32[]{:S(2)}) collective-permute-start(bf16[1,96,576]{2,1,0:T(8,128)(2,1)} %get-tuple-element.452), channel_id=1, source_target_pairs={{0,3},{1,2},{2,1},{3,0},{4,7},{5,6},{6,5},{7,4},{8,11},{9,10},{10,... | collective-permute-start | bytes 331784 | tf_op jit(solution)/shard_map/ppermute | solution.py:1048
  429.9 18.5 %collective-permute-start.80 = (bf16[24,1664]{1,0:T(8,128)(2,1)}, bf16[24,1664]{1,0:T(8,128)(2,1)S(1)}, u32[]{:S(2)}, u32[]{:S(2)}) collective-permute-start(bf16[24,1664]{1,0:T(8,128)(2,1)} %sum_terms.4.rest_0_), channel_id=1, source_target_pairs={{0,1},{1,0},{2,3},{3,2},{4,5},{5,4},{6,7},{7,6},{8,9},{9,8},{10,11... | collective-permute-start | bytes 239624 | tf_op jit(solution)/shard_map/ppermute | solution.py:1048
  441.1 16.4 %collective-permute-start.81 = (bf16[24,1664]{1,0:T(8,128)(2,1)}, bf16[24,1664]{1,0:T(8,128)(2,1)S(1)}, u32[]{:S(2)}, u32[]{:S(2)}) collective-permute-start(bf16[24,1664]{1,0:T(8,128)(2,1)} %sum_terms.4.rest_0_), channel_id=1, source_target_pairs={{0,2},{1,3},{2,0},{3,1},{4,6},{5,7},{6,4},{7,5},{8,10},{9,11},{10,... | collective-permute-start | bytes 239624 | tf_op jit(solution)/shard_map/ppermute | solution.py:1048
  444.0 13.5 %collective-permute-start.82 = (bf16[24,1664]{1,0:T(8,128)(2,1)}, bf16[24,1664]{1,0:T(8,128)(2,1)S(1)}, u32[]{:S(2)}, u32[]{:S(2)}) collective-permute-start(bf16[24,1664]{1,0:T(8,128)(2,1)} %sum_terms.4.rest_0_), channel_id=1, source_target_pairs={{0,3},{1,2},{2,1},{3,0},{4,7},{5,6},{6,5},{7,4},{8,11},{9,10},{10,... | collective-permute-start | bytes 239624 | tf_op jit(solution)/shard_map/ppermute | solution.py:1048
  445.5 15.1 %collective-permute-start.86 = (bf16[1,96,576]{2,1,0:T(8,128)(2,1)}, bf16[1,96,576]{2,1,0:T(8,128)(2,1)S(1)}, u32[]{:S(2)}, u32[]{:S(2)}) collective-permute-start(bf16[1,96,576]{2,1,0:T(8,128)(2,1)} %sum_terms.5.rest_0_), channel_id=1, source_target_pairs={{0,1},{1,0},{2,3},{3,2},{4,5},{5,4},{6,7},{7,6},{8,9},{9,8},{10,11... | collective-permute-start | bytes 331784 | tf_op jit(solution)/shard_map/ppermute | solution.py:1048
  446.2 14.5 %collective-permute-start.87 = (bf16[1,96,576]{2,1,0:T(8,128)(2,1)}, bf16[1,96,576]{2,1,0:T(8,128)(2,1)S(1)}, u32[]{:S(2)}, u32[]{:S(2)}) collective-permute-start(bf16[1,96,576]{2,1,0:T(8,128)(2,1)} %sum_terms.5.rest_0_), channel_id=1, source_target_pairs={{0,2},{1,3},{2,0},{3,1},{4,6},{5,7},{6,4},{7,5},{8,10},{9,11},{10,... | collective-permute-start | bytes 331784 | tf_op jit(solution)/shard_map/ppermute | solution.py:1048
  448.4 12.2 %collective-permute-start.88 = (bf16[1,96,576]{2,1,0:T(8,128)(2,1)}, bf16[1,96,576]{2,1,0:T(8,128)(2,1)S(1)}, u32[]{:S(2)}, u32[]{:S(2)}) collective-permute-start(bf16[1,96,576]{2,1,0:T(8,128)(2,1)} %sum_terms.5.rest_0_), channel_id=1, source_target_pairs={{0,3},{1,2},{2,1},{3,0},{4,7},{5,6},{6,5},{7,4},{8,11},{9,10},{10,... | collective-permute-start | bytes 331784 | tf_op jit(solution)/shard_map/ppermute | solution.py:1048
  (164 other events, 1177.3 us)
Sparse Core Ops, SparseCore 0:
  10.2 33.1 all-gather.10
  45.2 57.6 all-gather.12
  104.4 63.4 all-gather.6
  201.3 63.7 all-gather.8
  325.9 43.6 reduce-scatter.2
  373.1 49.8 reduce-scatter.4

commit v4 on v3

--- a/solution.py
+++ b/solution.py
@@ -109,12 +109,27 @@
     )
 
 
+def save_stack(full, parts, stack):
+    rows = full.shape[0] // 2
+    thirds = full.shape[1] // (GROUPS * GW)
+    half, columns = rows // 2, thirds * GW
+    for c in range(GROUPS):
+        for t in range(thirds):
+            at = t * GROUPS * GW + c * GW
+            parts[c, :, t * GW : (t + 1) * GW] = full[:, at : at + GW]
+    for b in range(stack.shape[0]):
+        c, at = (b // 2) % GROUPS, (b % 2) * rows
+        stack[b, :, 0:columns] = parts[c, at : at + half, :]
+        stack[b, :, columns : 2 * columns] = parts[c, at + half : at + rows, :]
+
+
 def load_stack(me, stack, parts, thirds):
-    rows = stack.shape[1]
+    half, columns = stack.shape[1], stack.shape[2] // 2
     first = lax.div(me, 2 * GROUPS) * (2 * GROUPS)
     for w in range(2 * GROUPS):
-        c, r = w // 2, w % 2
-        parts[c, r * rows : (r + 1) * rows, :] = stack[first + w]
+        c, at = w // 2, (w % 2) * 2 * half
+        parts[c, at : at + half, :] = stack[first + w, :, 0:columns]
+        parts[c, at + half : at + 2 * half, :] = stack[first + w, :, columns : 2 * columns]
     return jnp.concatenate(
         [parts[c, :, t * GW : (t + 1) * GW] for t in range(thirds) for c in range(GROUPS)],
         axis=1,
@@ -174,12 +189,13 @@
     return (col_ref[pl.ds(k_at, bk), :] == info) & (k_iota <= q_iota)
 
 
-def attend_kernel(bq, count, sends, by_column, ids, first_ref, row_ref, *rest):
+def attend_kernel(bq, count, sends, stacked, by_column, ids, first_ref, row_ref, *rest):
     rest = list(rest)
     col_ref = rest.pop(0) if by_column else None
     pieces, rest = rest[:count], rest[count:]
     columns = rest.pop(0)
     out_pieces, rest = rest[:sends], rest[sends:]
+    stack_ref = rest.pop(0) if stacked else None
     o_ref, lse_ref, x_ref, k_s, v_s, vt_s = rest
     i = pl.program_id(0)
     me = ids[0]
@@ -237,19 +253,27 @@
         for s in range(sends):
             at = pl.ds(pl.multiple_of((me ^ s) * rows, rows), rows)
             out_pieces[s][...] = o_ref[at, :]
-
-
-def attend_back_kernel(bq, count, sends, by_column, ids, first_ref, row_ref, *rest):
+        if stacked:
+            half = rows // 2
+            for b in range(count):
+                at = b * rows
+                stack_ref[b, :, 0:GW] = o_ref[at : at + half, :]
+                stack_ref[b, :, GW : 2 * GW] = o_ref[at + half : at + rows, :]
+
+
+def attend_back_kernel(bq, count, sends, stacked, by_column, ids, first_ref, row_ref, *rest):
     rest = list(rest)
     col_ref = rest.pop(0) if by_column else None
     x_ref = rest.pop(0)
-    grads, rest = rest[:count], rest[count:]
+    given = 1 if stacked else count
+    grads, rest = rest[:given], rest[given:]
     o_ref, lse_ref = rest[:2]
     out_pieces, rest = rest[2 : 2 + sends], rest[2 + sends :]
+    stack_ref = rest.pop(0) if stacked else None
     dx_ref, k_s, v_s, g_s, dk_s, dv_s = rest
     i = pl.program_id(0)
     me = ids[0]
-    rows = grads[0].shape[0]
+    rows = g_s.shape[0] // count
     bk = bq
 
     @pl.when(i == 0)
@@ -257,8 +281,13 @@
         k_s[...] = x_ref[:, GW : 2 * GW]
         v_s[...] = x_ref[:, 2 * GW : 3 * GW]
         for s in range(count):
-            at = pl.ds(pl.multiple_of((me ^ s) * rows, rows), rows)
-            g_s[at, :] = grads[s][...]
+            if stacked:
+                half = rows // 2
+                g_s[s * rows : s * rows + half, :] = grads[0][s, :, 0:GW]
+                g_s[s * rows + half : (s + 1) * rows, :] = grads[0][s, :, GW : 2 * GW]
+            else:
+                at = pl.ds(pl.multiple_of((me ^ s) * rows, rows), rows)
+                g_s[at, :] = grads[s][...]
         dk_s[...] = jnp.zeros_like(dk_s)
         dv_s[...] = jnp.zeros_like(dv_s)
 
@@ -304,22 +333,31 @@
         for s in range(sends):
             at = pl.ds(pl.multiple_of((me ^ s) * rows, rows), rows)
             out_pieces[s][...] = dx_ref[at, :]
-
-
-def attend(ids, meta, pieces, columns, bq):
+        if stacked:
+            half = rows // 2
+            for b in range(count):
+                at = b * rows
+                stack_ref[b, :, 0 : 3 * GW] = dx_ref[at : at + half, :]
+                stack_ref[b, :, 3 * GW : 6 * GW] = dx_ref[at + half : at + rows, :]
+
+
+def attend(ids, meta, pieces, columns, bq, stacked=False):
     first, row_info, col_info = meta
     rows, width = pieces[0].shape
-    count, sends = len(pieces), min(len(pieces), 2 * GROUPS)
+    count = len(pieces)
+    sends = 0 if stacked else min(count, 2 * GROUPS)
     length = rows * count
     operands = [first, row_info] + ([] if col_info is None else [col_info])
     operands += list(pieces) + [columns]
-    outs = [sds((rows, GW), BF)] * sends + [
+    outs = [sds((rows, GW), BF)] * sends
+    outs += [sds((count, rows // 2, 2 * GW), BF)] if stacked else []
+    outs += [
         sds((length, GW), BF),
         sds((8, length), F32),
         sds((length, 3 * GW), BF),
     ]
     got = stage(
-        partial(attend_kernel, bq, count, sends, col_info is not None),
+        partial(attend_kernel, bq, count, sends, stacked, col_info is not None),
         "attend",
         ids,
         operands,
@@ -329,29 +367,32 @@
         grid=(length // bq,),
         specs={0: pl.BlockSpec(memory_space=pltpu.SMEM)},
     )
-    return got[:sends], got[sends:]
-
-
-def attend_back(ids, meta, kept, grads, bq, send=True):
+    return got[:-3], got[-3:]
+
+
+def attend_back(ids, meta, kept, grads, bq, stacked=False):
     first, row_info, col_info = meta
     attended, lse, x = kept
-    rows = grads[0].shape[0]
-    count, sends = len(grads), min(len(grads), 2 * GROUPS) if send else 0
+    count = grads[0].shape[0] if stacked else len(grads)
+    rows = attended.shape[0] // count
+    sends = 0 if stacked else min(count, 2 * GROUPS)
     length = rows * count
     operands = [first, row_info] + ([] if col_info is None else [col_info])
     operands += [x] + list(grads) + [attended, lse]
     got = stage(
-        partial(attend_back_kernel, bq, count, sends, col_info is not None),
+        partial(attend_back_kernel, bq, count, sends, stacked, col_info is not None),
         "attend_back",
         ids,
         operands,
-        [sds((rows, 3 * GW), BF)] * sends + [sds(x.shape, BF)],
+        [sds((rows, 3 * GW), BF)] * sends
+        + ([sds((count, rows // 2, 6 * GW), BF)] if stacked else [])
+        + [sds(x.shape, BF)],
         [pltpu.VMEM((length, GW), BF)] * 3 + [pltpu.VMEM((length, GW), F32)] * 2,
         flops=length * length * GW * 5,
         grid=(length // bq,),
         specs={0: pl.BlockSpec(memory_space=pltpu.SMEM)},
     )
-    return got[:sends], got[sends]
+    return got[:-1], got[-1]
 
 
 def project_grads_kernel(count, ids, dx_ref, *rest):
@@ -507,31 +548,6 @@
     )
 
 
-def hidden_back_kernel(count, ids, *rest):
-    pieces, grads = rest[:count], rest[count : 2 * count]
-    expand, reduce_ref = rest[2 * count : 2 * count + 2]
-    outs = rest[2 * count + 2 :]
-    rows = pieces[0].shape[0]
-    low = jnp.concatenate([piece[...] for piece in pieces], axis=0)
-    grad = jnp.concatenate([piece[...] for piece in grads], axis=0)
-    _, slope = gelu_both(dot(low, expand[...]))
-    grad_pre = (nt_dot(grad, reduce_ref[...]) * slope).astype(BF)
-    total = nt_dot(grad_pre, expand[...]).astype(BF)
-    for s, out in enumerate(outs):
-        out[...] = total[s * rows : (s + 1) * rows, :]
-
-
-def hidden_back(ids, pieces, grads, expand, reduce_part):
-    return stage(
-        partial(hidden_back_kernel, len(pieces)),
-        "hidden_back",
-        ids,
-        list(pieces) + list(grads) + [expand, reduce_part],
-        [sds(pieces[0].shape, BF)] * len(pieces),
-        flops=6 * len(pieces) * pieces[0].size * expand.shape[1],
-    )
-
-
 def dense_pre_kernel(shares, ids, tok, one_hot, picked, vecs, branch, *rest):
     partials = rest[:shares]
     mine_ref, other_ref, mixed_ref, delta_ref, normed = rest[shares:]
@@ -602,21 +618,20 @@
     return [pltpu.VMEM((width, weights[0].shape[-1]), BF)] * 2
 
 
-def dense_ffn_kernel(count, steps, split, ids, *rest):
-    pieces, rest = rest[:count], rest[count:]
+def dense_ffn_kernel(split, ids, stack, *rest):
     output, mixed, cot, vecs = rest[:4]
     gain = gain_of(vecs, 4)
     rest = rest[4:]
     weights, rest = rest[:split], rest[split:]
     act_ref, low_ref, back_ref, sum_ref, att_ref, gain_ref = rest[:6]
-    g_pieces, rest = rest[6 : 6 + steps], rest[6 + steps :]
+    g_stack, rest = rest[6], rest[7:]
     parts, branch_s, delta_s, grad_s = rest[:4]
     n = pl.program_id(0)
     me = ids[0]
 
     @pl.when(n == 0)
     def _():
-        attended = load_pieces(me, pieces, parts, 1)
+        attended = load_stack(me, stack, parts, 1)
         att_ref[...] = attended
         branch = dot(attended, output[...])
         branch_s[...] = branch
@@ -641,15 +656,15 @@
         sum_ref[...] = total
         back = total.astype(BF)
         back_ref[...] = back
-        save_pieces(me, nt_dot(back, output[...]).astype(BF), parts, g_pieces)
-
-
-def dense_ffn(ids, steps, pieces, output, mixed, cot, vecs, weights):
+        save_stack(nt_dot(back, output[...]).astype(BF), parts, g_stack)
+
+
+def dense_ffn(ids, stack, output, mixed, cot, vecs, weights):
     rows, width = mixed.shape
     split = len(weights)
     parts_n = weights[0].shape[0 if weights[0].ndim == 3 else 1]
     hidden = weights[0].shape[-1]
-    base = len(pieces) + 4
+    base = 5
     specs = part_specs(base, weights)
     scratch = [pltpu.VMEM((GROUPS, rows, GW), BF)] + [pltpu.VMEM((rows, width), F32)] * 3
     scratch += part_scratch(width, weights)
@@ -660,19 +675,20 @@
         sds((rows, width), F32),
         sds((rows, width), BF),
         sds((8, width), F32),
-    ] + [sds((rows // 2, GW), BF)] * steps
+        sds(stack.shape, BF),
+    ]
     got = stage(
-        partial(dense_ffn_kernel, len(pieces), steps, split),
+        partial(dense_ffn_kernel, split),
         "dense_ffn",
         ids,
-        list(pieces) + [output, mixed, cot, vecs] + list(weights),
+        [stack, output, mixed, cot, vecs] + list(weights),
         outs,
         scratch,
         flops=8 * rows * width * hidden * parts_n + 4 * rows * width * width,
         grid=(parts_n,),
         specs=specs,
     )
-    return got[:6], got[6:]
+    return got[:6], got[6]
 
 
 def dense_post_kernel(ids, stack, *rest):
@@ -716,44 +732,57 @@
     )
 
 
-def routed_back_kernel(shares, steps, ids, *rest):
-    partials = rest[:shares]
-    branch, picked, vecs, g_delta, output = rest[shares : shares + 5]
-    rest = rest[shares + 5 :]
-    g_mid_ref, back_ref, gain_ref = rest[:3]
-    pieces, parts = rest[3 : 3 + steps], rest[3 + steps]
-    grad = partials[0][...].astype(F32)
-    for share in partials[1:]:
-        grad = grad + share[...].astype(F32)
-    middle = picked[...].astype(F32) + branch[...]
-    g_middle, gain_grad = norm_back(grad, middle, gain_of(vecs, 2))
-    gain_ref[...] = jnp.broadcast_to(gain_grad, gain_ref.shape)
-    g_mid_ref[...] = g_middle
-    back = (g_delta[...] + g_middle).astype(BF)
-    back_ref[...] = back
-    save_pieces(ids[0], nt_dot(back, output[...]).astype(BF), parts, pieces)
-
-
-def routed_back(ids, steps, partials, branch, picked, vecs, g_delta, output):
+def routed_back_kernel(split, ids, low, g_low, branch, picked, vecs, g_delta, output, *rest):
+    weights, rest = rest[:split], rest[split:]
+    g_mid_ref, back_ref, gain_ref, stack, parts, grad_s = rest[:6]
+    n = pl.program_id(0)
+
+    @pl.when(n == 0)
+    def _():
+        grad_s[...] = jnp.zeros_like(grad_s)
+
+    expand, reduce_w = this_part(ids[0], weights, rest[6:])
+    _, slope = gelu_both(dot(low[...], expand))
+    grad_pre = (nt_dot(g_low[...], reduce_w) * slope).astype(BF)
+    grad_s[...] += nt_dot(grad_pre, expand)
+
+    @pl.when(n == pl.num_programs(0) - 1)
+    def _():
+        middle = picked[...].astype(F32) + branch[...]
+        g_middle, gain_grad = norm_back(grad_s[...], middle, gain_of(vecs, 2))
+        gain_ref[...] = jnp.broadcast_to(gain_grad, gain_ref.shape)
+        g_mid_ref[...] = g_middle
+        back = (g_delta[...] + g_middle).astype(BF)
+        back_ref[...] = back
+        save_stack(nt_dot(back, output[...]).astype(BF), parts, stack)
+
+
+def routed_back(ids, wide_count, low, g_low, branch, picked, vecs, g_delta, output, weights):
     rows, width = branch.shape
-    got = stage(
-        partial(routed_back_kernel, len(partials), steps),
+    parts_n = weights[0].shape[0 if weights[0].ndim == 3 else 1]
+    return stage(
+        partial(routed_back_kernel, len(weights)),
         "routed_back",
         ids,
-        list(partials) + [branch, picked, vecs, g_delta, output],
-        [sds((rows, width), F32), sds((rows, width), BF), sds((8, width), F32)]
-        + [sds((rows // 2, GW), BF)] * steps,
-        [pltpu.VMEM((GROUPS, rows, GW), BF)],
-        flops=2 * rows * width * width,
-    )
-    return got[0], got[1], got[2], got[3:]
-
-
-def routed_post_kernel(count, ids, *rest):
-    pieces = rest[:count]
-    project, vecs, picked, g_mid, g_mixed, one_hot, g_gate = rest[count : count + 7]
-    out_ref, parts = rest[count + 7 :]
-    g_proj = load_pieces(ids[0], pieces, parts, 3)
+        [low, g_low, branch, picked, vecs, g_delta, output] + list(weights),
+        [
+            sds((rows, width), F32),
+            sds((rows, width), BF),
+            sds((8, width), F32),
+            sds((wide_count, rows // 4, 2 * GW), BF),
+        ],
+        [pltpu.VMEM((GROUPS, rows, GW), BF), pltpu.VMEM((rows, width), F32)]
+        + part_scratch(width, weights),
+        flops=6 * rows * width * parts_n * weights[0].shape[-1],
+        grid=(parts_n,),
+        specs=part_specs(7, weights),
+    )
+
+
+def routed_post_kernel(ids, stack, *rest):
+    project, vecs, picked, g_mid, g_mixed, one_hot, g_gate = rest[:7]
+    out_ref, parts = rest[7:]
+    g_proj = load_stack(ids[0], stack, parts, 3)
     rows = picked[...].astype(F32)
     grad_rows, _ = norm_back(nt_dot(g_proj, project[...]), rows, gain_of(vecs, 1))
     spread = g_mid[...] + grad_rows + g_gate[:, 0:1] * gain_of(vecs, 0)
@@ -763,13 +792,13 @@
         out_ref[at, :] = g_mixed[at, :] + place(one_hot[spots, :], spread[spots, :])
 
 
-def routed_post(ids, pieces, project, vecs, picked, g_mid, g_mixed, one_hot, g_gate):
+def routed_post(ids, stack, project, vecs, picked, g_mid, g_mixed, one_hot, g_gate):
     rows, width = picked.shape
     (out,) = stage(
-        partial(routed_post_kernel, len(pieces)),
+        routed_post_kernel,
         "routed_post",
         ids,
-        list(pieces) + [project, vecs, picked, g_mid, g_mixed, one_hot, g_gate],
+        [stack, project, vecs, picked, g_mid, g_mixed, one_hot, g_gate],
         [sds(g_mixed.shape, F32)],
         [pltpu.VMEM((GROUPS, rows, 3 * GW), BF)],
         flops=6 * rows * width * width,
@@ -787,81 +816,103 @@
         send[c] = total[pl.ds(other, rows), :].astype(BF)
 
 
-def hidden_grads_kernel(ids, low, grad, expand, reduce_ref, out, total):
-    i = pl.program_id(0)
+def hidden_grads_kernel(spans, ids, *rest):
+    count = len(spans)
+    grads, rest = rest[:count], rest[count:]
+    lows, (expand, reduce_ref, out, total) = rest[:-4], rest[-4:]
     hidden = expand.shape[1]
-
-    @pl.when(i == 0)
-    def _():
-        total[...] = jnp.zeros_like(total)
-
-    value, slope = gelu_both(dot(low[...], expand[...]))
-    grad_pre = (nt_dot(grad[...], reduce_ref[...]) * slope).astype(BF)
-    total[:, 0:hidden] += tn_dot(low[...], grad_pre)
-    total[:, hidden : 2 * hidden] += tn_dot(grad[...], value.astype(BF))
-
-    @pl.when(i == pl.num_programs(0) - 1)
-    def _():
-        out[...] = total[...].astype(BF)
-
-
-def hidden_grads(ids, low, grad, expand, reduce_part):
+    for k, (step, low_at, rows, whole) in enumerate(spans):
+        grad = grads[k][...]
+        if len(lows) == count:
+            low = lows[k][...]
+        else:
+            at = pl.multiple_of((ids[1] ^ step) * whole + low_at, rows)
+            low = lows[0][pl.ds(at, rows), :]
+        value, slope = gelu_both(dot(low, expand[...]))
+        grad_pre = (nt_dot(grad, reduce_ref[...]) * slope).astype(BF)
+        e_term = tn_dot(low, grad_pre)
+        r_term = tn_dot(grad, value.astype(BF))
+        if k:
+            e_term, r_term = total[:, 0:hidden] + e_term, total[:, hidden:] + r_term
+        if k < count - 1:
+            total[:, 0:hidden] = e_term
+            total[:, hidden:] = r_term
+        else:
+            out[:, 0:hidden] = e_term.astype(BF)
+            out[:, hidden:] = r_term.astype(BF)
+
+
+def hidden_grads(ids, lows, grads, expand, reduce_part, halved=None):
     width, hidden = expand.shape
-    block = min(512, low.shape[0])
-    row_spec = pl.BlockSpec((block, width), lambda i: (i, 0))
+    whole_rows = grads[0].shape[0]
+    spans, flat = [], []
+    for step, grad in enumerate(grads):
+        low_at = 0
+        for part in grad if step == halved else [grad]:
+            spans.append((step, low_at, part.shape[0], whole_rows))
+            flat.append(part)
+            low_at += part.shape[0]
     (out,) = stage(
-        hidden_grads_kernel,
+        partial(hidden_grads_kernel, spans),
         "hidden_grads",
         ids,
-        [low, grad, expand, reduce_part],
+        flat + list(lows) + [expand, reduce_part],
         [sds((width, 2 * hidden), BF)],
         [pltpu.VMEM((width, 2 * hidden), F32)],
-        flops=8 * low.size * hidden,
-        grid=(low.shape[0] // block,),
-        specs={0: row_spec, 1: row_spec},
+        flops=8 * len(grads) * grads[0].size * hidden,
     )
     return out
 
 
-def output_grads_kernel(vectors, ids, att_d, back_d, att_r, back_r, *rest):
+def output_grads_kernel(vectors, ids, att, back, *rest):
     rest = list(rest)
     vecs, rest = rest[:vectors], rest[vectors:]
     keep, send, total = rest
-    width = att_d.shape[1]
-    total[:, 0:width] = tn_dot(att_d[...], back_d[...])
-    total[:, width : 2 * width] = tn_dot(att_r[...], back_r[...])
-    rows = [vec[0:1, :] for vec in vecs]
-    rows.append(jnp.zeros((128 - vectors, width), F32))
-    total[:, 2 * width : 2 * width + 128] = jnp.concatenate(rows, axis=0).T
+    width = att.shape[1]
+    total[:, 0:width] = tn_dot(att[...], back[...])
+    if vectors:
+        rows = [vec[0:1, :] for vec in vecs]
+        rows.append(jnp.zeros((128 - vectors, width), F32))
+        total[:, width : width + 128] = jnp.concatenate(rows, axis=0).T
     split_rows(ids[0], total, keep, send)
 
 
-def output_grads(ids, wide_count, att_d, back_d, att_r, back_r, vecs):
-    rows, width = att_d.shape
-    columns = 2 * width + 128
+def output_grads(ids, wide_count, att, back, vecs):
+    rows, width = att.shape
+    columns = width + (128 if vecs else 0)
     shape = (wide_count // 2, width // wide_count, columns)
     return stage(
         partial(output_grads_kernel, len(vecs)),
         "output_grads",
         ids,
-        [att_d, back_d, att_r, back_r] + list(vecs),
+        [att, back] + list(vecs),
         [sds(shape, BF), sds(shape, BF)],
         [pltpu.VMEM((width, columns), F32)],
         flops=3 * rows * width * width,
     )
 
 
-def join_kernel(chips, ids, keep, came, *outs):
+def join_kernel(pairs, ids, *rest):
+    keeps, cames, outs = rest[:pairs], rest[pairs : 2 * pairs], rest[2 * pairs :]
     chip = lax.div(ids[0], 2)
     for s, out in enumerate(outs):
-        at = chip ^ s
-        out[...] = (keep[at].astype(F32) + came[at].astype(F32)).astype(BF)
-
-
-def join_chips(ids, keep, came):
-    chips = keep.shape[0]
+        low = 0
+        for keep, came in zip(keeps, cames):
+            columns = keep.shape[2]
+            total = keep[chip ^ s].astype(F32) + came[chip ^ s].astype(F32)
+            out[:, low : low + columns] = total.astype(BF)
+            low += columns
+
+
+def join_chips(ids, keeps, cames):
+    chips, rows = keeps[0].shape[:2]
+    columns = sum(keep.shape[2] for keep in keeps)
     return stage(
-        partial(join_kernel, chips), "join", ids, [keep, came], [sds(keep.shape[1:], BF)] * chips
+        partial(join_kernel, len(keeps)),
+        "join",
+        ids,
+        list(keeps) + list(cames),
+        [sds((rows, columns), BF)] * chips,
     )
 
 
@@ -895,58 +946,69 @@
     rest[-1][...] = got.astype(BF)
 
 
-def gather_out_kernel(count, ids, *rest):
-    pieces, outs, wide_s = rest[:count], rest[count:-1], rest[-1]
+def gather_out_kernel(count, vectors, ids, *rest):
+    pieces, outs = rest[:count], rest[count : -1 - vectors]
+    vecs, wide_s = rest[-1 - vectors : -1], rest[-1]
     rows = pieces[0].shape[0]
     for s, piece in enumerate(pieces):
         at = pl.ds(pl.multiple_of((ids[1] ^ s) * rows, rows), rows)
         low = 0
-        for out in outs[:-1]:
+        for out in outs:
             columns = out.shape[1]
             out[at, :] = piece[:, low : low + columns].astype(F32)
             low += columns
         wide_s[at, :] = piece[:, low:].astype(F32)
-    outs[-1][...] = wide_s[...].T[: outs[-1].shape[0], :]
-
-
-def reduce_narrow(ids, terms, widths):
+    turned = wide_s[...].T
+    for k, vec in enumerate(vecs):
+        vec[...] = turned[k : k + 1, :].reshape(vec.shape[0])
+
+
+def narrow_terms(ids, terms):
     narrow_count = lax.axis_size("narrow")
     rows, columns = terms[0].shape
     if rows % (8 * narrow_count):
-        total = lax.psum(sum_terms(terms).astype(BF), "narrow").astype(F32)
+        return [sum_terms(terms).astype(BF)]
+    return stage(
+        partial(sum_split_kernel, len(terms)),
+        "sum_split",
+        ids,
+        terms,
+        [sds((rows // narrow_count, columns), BF)] * narrow_count,
+        [pltpu.VMEM((rows, columns), F32)],
+    )
+
+
+def sum_narrow(ids, parts, first):
+    if len(parts) == 1:
+        return lax.psum(parts[0], "narrow")
+    return sum_parts(ids, tie(narrow_return(parts), first))
+
+
+def spread_narrow(ids, total, rows, widths, vectors):
+    narrow_count = lax.axis_size("narrow")
+    if total.shape[0] == rows:
+        total = total.astype(F32)
         outs, low = [], 0
         for size in widths:
             outs.append(total[:, low : low + size])
             low += size
-        outs[-1] = outs[-1].T[:8]
-        return outs
-    share = rows // narrow_count
-    parts = stage(
-        partial(sum_split_kernel, len(terms)),
-        "sum_split",
-        ids,
-        terms,
-        [sds((share, columns), BF)] * narrow_count,
-        [pltpu.VMEM((rows, columns), F32)],
-    )
-    came = [parts[0]] + [narrow_step(parts[s], s) for s in range(1, narrow_count)]
-    (total,) = stage(sum_kernel, "sum_terms", ids, came, [sds((share, columns), BF)])
-    pieces = [total] + [narrow_step(total, s) for s in range(1, narrow_count)]
+        return outs[:-1] + [outs[-1][:, k] for k in range(vectors)]
     return stage(
-        partial(gather_out_kernel, narrow_count),
+        partial(gather_out_kernel, narrow_count, vectors),
         "gather_out",
         ids,
-        pieces,
-        [sds((rows, size), F32) for size in widths[:-1]] + [sds((8, rows), F32)],
+        narrow_gather(total),
+        [sds((rows, size), F32) for size in widths[:-1]] + [sds((rows,), F32)] * vectors,
         [pltpu.VMEM((rows, widths[-1]), F32)],
     )
 
 
-def join_narrow_kernel(count, ids, keep, came, *outs):
+def join_narrow_kernel(turned, ids, keep, came, *outs):
     each = outs[0].shape[0]
+    turn = lax.div(ids[0], 2) if turned else 0
     for t, out in enumerate(outs):
         for j in range(each):
-            at = (ids[1] ^ t) * each + j
+            at = ((ids[1] ^ t) * each + j) ^ turn
             out[j] = (keep[at].astype(F32) + came[at].astype(F32)).astype(BF)
 
 
@@ -961,31 +1023,33 @@
         out[...] = blocks[chip ^ s]
 
 
-def unpack_kernel(ids, *rest):
-    pieces, own, own_gain, out, gain_ref, parts = (rest[:GROUPS],) + rest[GROUPS:]
+def unpack_kernel(turned, ids, *rest):
+    pieces, (own, gain, out, gain_out, parts) = rest[:GROUPS], rest[GROUPS:]
+    at = lax.div(ids[0], 2)
+    if turned:
+        at = at ^ ids[1]
+    rows = out.shape[0]
     for s, piece in enumerate(pieces):
-        group = lax.rem(lax.div(ids[0], 2) ^ s, GROUPS)
-        parts[group] = piece[...].astype(F32)
-    rows = out.shape[0]
+        parts[lax.rem(at ^ s, GROUPS)] = piece[...].astype(F32)
     total = jnp.zeros((rows, GW), F32)
     for t in range(3):
         for c in range(GROUPS):
-            at = (t * GROUPS + c) * GW
+            low = (t * GROUPS + c) * GW
             part = parts[c, :, t * GW : (t + 1) * GW]
-            out[:, at : at + GW] = part
-            total = total + part * own[:, at : at + GW].astype(F32)
+            out[:, low : low + GW] = part
+            total = total + part * own[:, low : low + GW].astype(F32)
     sums = jnp.broadcast_to(jnp.sum(total, axis=1, keepdims=True), (rows, 128)).T
-    gain_ref[...] = sums[0:8, :] / own_gain[...]
-
-
-def unpack(ids, pieces, own, own_gain):
+    gain_out[...] = (sums[0:1, :] / gain[...]).reshape(rows)
+
+
+def unpack(ids, pieces, own, gain):
     rows, columns = pieces[0].shape
     return stage(
-        unpack_kernel,
+        partial(unpack_kernel, direct_delivery()),
         "unpack",
         ids,
-        list(pieces) + [own, own_gain],
-        [sds((rows, GROUPS * columns), F32), sds((8, rows), F32)],
+        list(pieces) + [own, gain],
+        [sds((rows, GROUPS * columns), F32), sds((rows,), F32)],
         [pltpu.VMEM((GROUPS, rows, columns), F32)],
     )
 
@@ -995,7 +1059,7 @@
     chips, rows, columns = keep.shape
     shape = (chips // narrow_count, rows, columns)
     return stage(
-        partial(join_narrow_kernel, narrow_count),
+        partial(join_narrow_kernel, direct_delivery()),
         "join_narrow",
         ids,
         [keep, came],
@@ -1003,10 +1067,8 @@
     )
 
 
-def sum_project(ids, parts):
-    (total,) = stage(
-        sum_kernel, "sum_terms", ids, narrow_return(parts), [sds(parts[0].shape, BF)]
-    )
+def sum_parts(ids, terms):
+    (total,) = stage(sum_kernel, "sum_terms", ids, terms, [sds(terms[0].shape, BF)])
     return total
 
 
@@ -1020,6 +1082,28 @@
         [sds((rows, columns), BF)] * GROUPS,
         [pltpu.VMEM((chips, rows, columns), BF)],
     )
+
+
+def direct_delivery():
+    return lax.axis_size("narrow") == GROUPS and lax.axis_size("wide") == 2 * GROUPS
+
+
+def deliver(ids, total, chips):
+    narrow_count = lax.axis_size("narrow")
+    if not direct_delivery():
+        return chips_return(route_project(ids, narrow_gather(total), chips))
+    total = total[0]
+
+    def moves(k):
+        pairs = []
+        for chip in range(chips):
+            for core in range(2):
+                for n in range(narrow_count):
+                    to = (2 * (chip ^ n) + core) * narrow_count + (n ^ k)
+                    pairs.append(((2 * chip + core) * narrow_count + n, to))
+        return pairs
+
+    return [lax.ppermute(total, ("wide", "narrow"), moves(k)) for k in range(narrow_count)]
 
 
 def finish_hidden_kernel(ids, dense, routed, e_d, r_d, e_r, r_r):
@@ -1088,6 +1172,11 @@
             lax.dynamic_slice_in_dim(reduce_part, here * rows, rows, 0),
         ]
     )
+
+
+def all_chips(x):
+    groups = [list(range(core, lax.axis_size("wide"), 2)) for core in range(2)]
+    return lax.all_gather(x, "wide", axis=0, axis_index_groups=groups)
 
 
 def chip_step(x, s):
@@ -1123,6 +1212,7 @@
     row_length = selected.shape[1]
     hidden = expand_dense.shape[1]
     wide_count = lax.axis_size("wide")
+    narrow_count = lax.axis_size("narrow")
     here = lax.axis_index("wide")
     slot_count = span_rows // 4
     bq_dense = min(256, row_length)
@@ -1179,12 +1269,7 @@
     pieces = exchange(pieces)
     if staged:
         pieces, own_d = lax.optimization_barrier((pieces, own_d))
-        chips_d = lax.all_gather(
-            own_d,
-            "wide",
-            axis=0,
-            axis_index_groups=[list(range(r, wide_count, 2)) for r in range(2)],
-        )
+        chips_d = all_chips(own_d)
     branch_r, low_r, att_r = routed_mid(ids, pieces, output_routed, picked, vecs)
     dense_segments = tie(seq_segments, low_r)
     starts = sum(
@@ -1219,83 +1304,117 @@
     )
     if staged:
         mine_d, other_d, chips_d = lax.optimization_barrier((mine_d, other_d, chips_d))
-    cot_all = lax.all_gather(tie(cot, mine_d), "narrow", axis=0, tiled=True)
-    rows_d = exchange_rows(mine_d, other_d)
-    if staged:
+        share_r = hidden_share(tie(expand_routed, mine_d), reduce_routed)
+        own_r = lax.all_gather(share_r, "narrow", axis=0)
+        rows_d, own_r = lax.optimization_barrier((exchange_rows(mine_d, other_d), own_r))
+        chips_r = all_chips(own_r)
         weights_d = [chips_d, core_step(chips_d)]
     else:
+        rows_d = exchange_rows(mine_d, other_d)
         weights_d = [
             lax.all_gather(expand_dense, "narrow", axis=0),
             lax.all_gather(reduce_dense, "narrow", axis=0),
         ]
-    pieces, kept_d = attend(ids, meta_dense, rows_d, columns_d, bq_dense)
-    pieces, weights_d = lax.optimization_barrier((pieces, weights_d))
-    pieces, cot_all = lax.optimization_barrier((exchange(pieces), cot_all))
-    (activations, low_d, back_d, sum_d, att_d, mid_gain_d), pieces = dense_ffn(
-        ids, wide_count, pieces, output_dense, mixed, cot, vecs, weights_d
-    )
+        weights_r = [
+            lax.all_gather(expand_routed, "narrow", axis=0),
+            lax.all_gather(reduce_routed, "narrow", axis=0),
+        ]
+    cot_halves = cot.reshape(2, -1, width)
+    cot_first = tie(cot, rows_d)
+    cot_pieces = [cot] + [narrow_step(cot_first, s) for s in range(1, narrow_count)]
+    cot_pieces[2] = [narrow_step(tie(cot_halves[0], rows_d), 2), None]
+    (stack,), kept_d = attend(ids, meta_dense, rows_d, columns_d, bq_dense, stacked=True)
+    stack, weights_d, cot_pieces[1] = lax.optimization_barrier(
+        (stack, weights_d, cot_pieces[1])
+    )
+    stack, cot_pieces[2][0], cot_pieces[3:] = lax.optimization_barrier(
+        (lax.all_to_all(stack, "wide", 0, 0), cot_pieces[2][0], cot_pieces[3:])
+    )
+    cot_pieces[2][1] = narrow_step(tie(cot_halves[1], stack), 2)
+    (activations, low_d, back_d, sum_d, att_d, mid_gain_d), stack = dense_ffn(
+        ids, stack, output_dense, mixed, cot, vecs, weights_d
+    )
+    stack, low_d, cot_pieces = lax.optimization_barrier((stack, low_d, cot_pieces))
+    if staged:
+        stack, chips_r, low_d = lax.optimization_barrier((stack, chips_r, low_d))
     low_all = lax.all_gather(low_d, "narrow", axis=0, tiled=True)
-    _, dx_d = attend_back(ids, meta_dense, kept_d, exchange(pieces), bq_dense, send=False)
-    stack = lax.all_to_all(dx_d.reshape(wide_count, span_rows, 3 * GW), "wide", 0, 0)
+    keep_d, send_d = output_grads(ids, wide_count, att_d, back_d, [])
+    stack, keep_d, send_d = lax.optimization_barrier(
+        (lax.all_to_all(stack, "wide", 0, 0), keep_d, send_d)
+    )
+    came_d = core_step(send_d)
+    if staged:
+        weights_r = [chips_r, core_step(chips_r)]
+    (stack,), dx_d = attend_back(ids, meta_dense, kept_d, [stack], bq_dense, stacked=True)
+    stack, dx_d, weights_r, came_d = lax.optimization_barrier(
+        (stack, dx_d, weights_r, came_d)
+    )
+    stack = lax.all_to_all(stack, "wide", 0, 0)
     keep, send = project_grads(ids, wide_count, rows_d, dx_d)
-    project_d = sum_project(ids, split_narrow(ids, keep, core_step(send)))
-    stack, project_d = lax.optimization_barrier((stack, project_d))
-    project_d_parts = route_project(ids, narrow_gather(project_d), keep.shape[0])
+    project_d_parts = split_narrow(ids, keep, core_step(send))
+    hidden_d = hidden_grads(
+        ids, [tie(low_all, project_d_parts)], cot_pieces, expand_dense, reduce_dense, 2
+    )
+    project_d = sum_parts(ids, tie(narrow_return(project_d_parts), hidden_d))
+    stack, project_d, hidden_d = lax.optimization_barrier((stack, project_d, hidden_d))
+    ffn_d = lax.psum_scatter(hidden_d, "wide", scatter_dimension=0, tiled=True)
+    delivered_d = deliver(ids, project_d, keep.shape[0])
     g_mixed, g_delta, g_low, g_gate, router_grad = dense_post(
         ids, stack, project_dense, vecs, mixed, sum_d, one_hot, picked, delta_r
     )
 
-    g_pieces = narrow_gather(g_low)
-    hidden_d = hidden_grads(ids, tie(low_all, g_low), cot_all, expand_dense, reduce_dense)
-    g_pieces, hidden_d, project_d_parts = lax.optimization_barrier(
-        (g_pieces, hidden_d, project_d_parts)
-    )
+    g_mid_r, back_r, mid_gain_r, stack = routed_back(
+        ids,
+        wide_count,
+        low_r,
+        g_low,
+        branch_r,
+        picked,
+        vecs,
+        g_delta,
+        output_routed,
+        weights_r,
+    )
+    stack, delivered_d, back_r = lax.optimization_barrier((stack, delivered_d, back_r))
+    keep_r, send_r = output_grads(
+        ids, wide_count, att_r, back_r, [mid_gain_r, mid_gain_d, router_grad]
+    )
+    came_r = core_step(send_r)
+    g_pieces = narrow_gather(tie(g_low, keep_r))
+    stack, keep_r, send_r = lax.optimization_barrier(
+        (lax.all_to_all(stack, "wide", 0, 0), keep_r, send_r)
+    )
+    (stack,), dx_r = attend_back(ids, meta_routed, kept_r, [stack], bq_routed, stacked=True)
+    stack, dx_r, g_pieces, came_r = lax.optimization_barrier((stack, dx_r, g_pieces, came_r))
+    keep, send = project_grads(ids, wide_count, rows_r, dx_r)
+    came = core_step(send)
+    output_parts = join_chips(ids, tie([keep_d, keep_r], send), [came_d, came_r])
+    hidden_r = hidden_grads(
+        ids, tie(low_pieces, output_parts), g_pieces, expand_routed, reduce_routed
+    )
+    ffn_r = lax.psum_scatter(hidden_r, "wide", scatter_dimension=0, tiled=True)
+    output_parts = narrow_terms(ids, tie(chips_return(output_parts), hidden_r))
+    project_parts = split_narrow(ids, tie(keep, output_parts), came)
+    stack, project_parts, output_parts = lax.optimization_barrier(
+        (stack, project_parts, output_parts)
+    )
+    stack = lax.all_to_all(stack, "wide", 0, 0)
+    returned, stack = lax.optimization_barrier((narrow_return(project_parts), stack))
+    project_r = sum_parts(ids, returned)
+    output_total = sum_narrow(ids, tie(output_parts, project_parts), project_r)
+    stack, output_total = lax.optimization_barrier((stack, output_total))
+    tokens_gradient = routed_post(
+        ids, stack, project_routed, vecs, picked, g_mid_r, g_mixed, one_hot, g_gate
+    )
+    delivered_r = deliver(ids, project_r, keep.shape[0])
     project_d_grad, pre_gain_d = unpack(
-        ids, chips_return(project_d_parts), own_rows[1], own_rows[3]
-    )
-    ffn_d = lax.psum_scatter(hidden_d, "wide", scatter_dimension=0, tiled=True)
-    partials = hidden_back(ids, low_pieces, g_pieces, expand_routed, reduce_routed)
-    hidden_r = hidden_grads(
-        ids,
-        jnp.concatenate(low_pieces, axis=0),
-        jnp.concatenate(g_pieces, axis=0),
-        expand_routed,
-        reduce_routed,
-    )
-    partials, hidden_r, project_d_grad = lax.optimization_barrier(
-        (narrow_return(partials), hidden_r, project_d_grad)
-    )
-    ffn_r = lax.psum_scatter(hidden_r, "wide", scatter_dimension=0, tiled=True)
-    g_mid_r, back_r, mid_gain_r, pieces = routed_back(
-        ids, wide_count, partials, branch_r, picked, vecs, g_delta, output_routed
-    )
-    keep_o, send_o = output_grads(
-        ids,
-        wide_count,
-        att_d,
-        back_d,
-        att_r,
-        back_r,
-        [mid_gain_r, mid_gain_d, router_grad],
-    )
-    pieces, keep_o, send_o = lax.optimization_barrier((exchange(pieces), keep_o, send_o))
-    pieces, dx_r = attend_back(ids, meta_routed, kept_r, pieces, bq_routed)
-    keep, send = project_grads(ids, wide_count, rows_r, dx_r)
-    output_parts = join_chips(ids, tie(keep_o, send), core_step(send_o))
-    project_parts = split_narrow(ids, keep, core_step(tie(send, output_parts)))
-    output_terms, pieces, project_parts = lax.optimization_barrier(
-        (chips_return(output_parts), pieces, project_parts)
-    )
-    project_r = sum_project(ids, project_parts)
-    project_r_terms = chips_return(
-        route_project(ids, narrow_gather(project_r), keep.shape[0])
-    )
-    output_d_grad, output_r_grad, vectors = reduce_narrow(
-        ids, output_terms, [width, width, 128]
-    )
-    project_r_grad, pre_gain_r = unpack(ids, project_r_terms, own_rows[0], own_rows[2])
-    tokens_gradient = routed_post(
-        ids, exchange(pieces), project_routed, vecs, picked, g_mid_r, g_mixed, one_hot, g_gate
+        ids, tie(delivered_d, project_r), own_rows[1], own_rows[3]
+    )
+    output_d_grad, output_r_grad, mid_r_grad, mid_d_grad, router_grad = spread_narrow(
+        ids, output_total, width // wide_count, [width, width, 128], 3
+    )
+    project_r_grad, pre_gain_r = unpack(
+        ids, tie(delivered_r, tokens_gradient), own_rows[0], own_rows[2]
     )
     expand_d_grad, reduce_d_grad, expand_r_grad, reduce_r_grad = finish_hidden(
         ids, ffn_d, ffn_r
@@ -1303,17 +1422,17 @@
     return (
         activations.reshape(tokens.shape),
         tokens_gradient.reshape(tokens.shape),
-        vectors[2],
+        router_grad,
         project_r_grad,
         output_r_grad,
-        pre_gain_r[0],
-        vectors[0],
+        pre_gain_r,
+        mid_r_grad,
         expand_r_grad,
         reduce_r_grad.T,
         project_d_grad,
         output_d_grad,
-        pre_gain_d[0],
-        vectors[1],
+        pre_gain_d,
+        mid_d_grad,
         expand_d_grad,
         reduce_d_grad.T,
     )

time: 494 us -> 474 us (0.960)
  blocking collectives: 0 us -> 10.4 us
  local copies, waits for them, and re-layouts: 34.7 us -> 25.4 us
  starting transfers between devices: 116 us -> 108 us
  waiting for transfers between devices: 114 us -> 106 us
    ppermute x42 -> x14, waiting for transfers between devices: 28.9 us -> 5.26 us  [exchange(): lax.ppermute(pieces[s], 'wide', [(j, j ^ s) for j in range(wide_count)])]
    ppermute x42 -> x14, starting transfers between devices: 38.1 us -> 15 us  [exchange(): lax.ppermute(pieces[s], 'wide', [(j, j ^ s) for j in range(wide_count)])]
    ppermute x30 -> x25, waiting for transfers between devices: 28.5 us -> 48.5 us  [narrow_step(): lax.ppermute(x, 'narrow', [(j, j ^ s) for j in range(lax.axis_size('narro...]
    ppermute x0 -> x8, starting transfers between devices: none -> 17 us  [deliver(): lax.ppermute(total, ('wide', 'narrow'), moves(k))]
    all_to_all x1 -> x4, starting transfers between devices: 3.61 us -> 18.1 us  [the longest x2 9.52 us: on_device(): stack = lax.all_to_all(stack, 'wide', 0, 0)]
    all_to_all x0 -> x1, blocking collectives: none -> 10.4 us  [on_device(): lax.all_to_all(stack, 'wide', 0, 0)]
    ppermute x30 -> x25, starting transfers between devices: 52.5 us -> 43.7 us  [narrow_step(): lax.ppermute(x, 'narrow', [(j, j ^ s) for j in range(lax.axis_size('narro...]
    ppermute x15 -> x9, waiting for transfers between devices: 42.3 us -> 35.1 us  [chip_step(): lax.ppermute(x, 'wide', [(j, j ^ 2 * s) for j in range(lax.axis_size('wid...]
  transfers between devices with their start and end apart: 99 -> 74, of which waited for: 33 -> 24; matrix products, arithmetic and copies ran while one was open for 5% -> 3% of each run, Pallas kernels for 36% -> 41%
where the time goes in v4:
time: 474 us; the launch traced here: 467 us
  Pallas kernels  194 us (41%)
  starting transfers between devices  108 us (23%)
  waiting for transfers between devices  106 us (22%)
  local copies, waits for them, and re-layouts  25.4 us (5%)
  between operations  15.1 us (3%)
  blocking collectives  10.4 us (2%)
  other arithmetic  8.17 us (2%)
    pallas_call x31, Pallas kernels, stage(): pl.pallas_call(body, out_shape=tuple(outs), in_specs=in_specs, out_specs=...  194 us
    ppermute x25, waiting for transfers between devices, narrow_step(): lax.ppermute(x, 'narrow', [(j, j ^ s) for j in range(lax.axis_size('narro...  48.5 us
    ppermute x25, starting transfers between devices, narrow_step(): lax.ppermute(x, 'narrow', [(j, j ^ s) for j in range(lax.axis_size('narro...  43.7 us
    ppermute x9, waiting for transfers between devices, chip_step(): lax.ppermute(x, 'wide', [(j, j ^ 2 * s) for j in range(lax.axis_size('wid...  35.1 us
    ppermute x8, starting transfers between devices, deliver(): lax.ppermute(total, ('wide', 'narrow'), moves(k))  17 us
    unnamed x152, local copies, waits for them, and re-layouts  15.9 us
    ppermute x14, starting transfers between devices, exchange(): lax.ppermute(pieces[s], 'wide', [(j, j ^ s) for j in range(wide_count)])  15 us
    ppermute x9, starting transfers between devices, chip_step(): lax.ppermute(x, 'wide', [(j, j ^ 2 * s) for j in range(lax.axis_size('wid...  11.4 us
  transfers between devices with their start and end apart: 74, of which 24 were waited for; matrix products, arithmetic and copies ran while one was open for 3% of the time, Pallas kernels for 41%

profile of v4, /device:TPU:0, one launch (start us, length us, event | category | flops | bytes accessed | tf_op | source)
XLA Modules:
  0.0 466.7 jit_solution(1104325093877487088)
XLA Ops:
  12.2 2.9 collective-permute-start.1
  22.3 3.1 group_columns.2.rest_9_
  29.1 6.4 %attend.2 = (bf16[64,192]{1,0:T(8,128)(2,1)}, bf16[64,192]{1,0:T(8,128)(2,1)}, bf16[64,192]{1,0:T(8,128)(2,1)}, bf16[64,192]{1,0:T(8,128)(2,1)}, bf16[64,192]{1,...) custom-call(s32[2]{0:T(128)} %pad_add_fusion.ids, ...), custom_call_target="tpu_custom_call" | custom-call | flops 553648128 | bytes 2689032 | tf_op jit(solution)/shard_map/attend/pallas_call | solution.py:155
  45.5 2.8 routed_mid.1
  55.5 3.2 group_columns.3.rest_8_
  68.1 4.3 hidden_forward.1
  72.4 3.6 collective-permute-start.17
  79.4 3.7 collective-permute-done.17.rest_1_
  83.1 10.3 %collective-permute-done.18.rest_2_ = bf16[128,768]{1,0:T(8,128)(2,1)S(1)} collective-permute-done((bf16[128,768]{1,0:T(8,128)(2,1)}, bf16[128,768]{1,0:T(8,128)(2,1)S(1)}, u32[]{:S(2)}, u32[]{:S(2)}) %collective-permute-start.18) | collective-permute-done | bytes 196640 | tf_op jit(solution)/shard_map/ppermute | solution.py:1132
  94.1 3.8 dense_pre.1
  98.0 4.9 %all-gather.14.cloned.1.call-done = bf16[16,2,96,768]{3,2,1,0:T(8,128)(2,1)} async-done(((bf16[4,2,96,768]{3,2,1,0:T(8,128)(2,1)}), bf16[16,2,96,768]{3,2,1,0:T(8,128)(2,1)}) %all-gather.14.cloned.1.call-update) | async-done | bytes 4718608 | tf_op jit(solution)/shard_map/all_gather | solution.py:1179
  110.3 6.8 %collective-permute-done.23.rest_4_ = bf16[256,768]{1,0:T(8,128)(2,1)S(1)} collective-permute-done((bf16[256,768]{1,0:T(8,128)(2,1)}, bf16[256,768]{1,0:T(8,128)(2,1)S(1)}, u32[]{:S(2)}, u32[]{:S(2)}) %collective-permute-start.23) | collective-permute-done | bytes 393248 | tf_op jit(solution)/shard_map/ppermute | solution.py:1183
  120.2 7.0 %collective-permute-done.21.rest_2_ = bf16[256,768]{1,0:T(8,128)(2,1)S(1)} collective-permute-done((bf16[256,768]{1,0:T(8,128)(2,1)}, bf16[256,768]{1,0:T(8,128)(2,1)S(1)}, u32[]{:S(2)}, u32[]{:S(2)}) %collective-permute-start.21) | collective-permute-done | bytes 393248 | tf_op jit(solution)/shard_map/ppermute | solution.py:1183
  127.2 7.6 %collective-permute-done.25.rest_6_ = bf16[256,768]{1,0:T(8,128)(2,1)S(1)} collective-permute-done((bf16[256,768]{1,0:T(8,128)(2,1)S(1)}, bf16[256,768]{1,0:T(8,128)(2,1)S(1)}, u32[]{:S(2)}, u32[]{:S(2)}) %collective-permute-start.25) | collective-permute-done | bytes 393248 | tf_op jit(solution)/shard_map/ppermute | solution.py:1183
  139.5 19.7 %attend.3 = (bf16[8,128,384]{2,1,0:T(8,128)(2,1)}, bf16[2048,192]{1,0:T(8,128)(2,1)}, f32[8,2048]{1,0:T(8,128)}, bf16[2048,576]{1,0:T(8,128)(2,1)}) custom-call(s32[2]{0:T(128)} %pad_add_fusion.ids, s32[8]{0:T(128)} %and_select_fusion.first_ref, s32[8,2048]{1,0:T(8,128)} %broadcast_in_dim.62.row_ref, bf16[256,768]{1,0:T(8,128)(2,1)} %get-tuple-element.304.rest_0_, ...), custom_call_target="tpu_custom_call" | custom-call | flops 3422552064 | bytes 8093728 | tf_op jit(solution)/shard_map/attend/pallas_call | solution.py:155
  160.1 4.9 %all-to-all-start = ((bf16[8,128,384]{2,1,0:T(8,128)(2,1)}), bf16[8,128,384]{2,1,0:T(8,128)(2,1)S(1)}, u32[]{:S(2)}, u32[]{:S(2)}) async-start(bf16[8,128,384]{2,1,0:T(8,128)(2,1)} %get-tuple-element.316), calls=%async_computation | async-start | bytes 1572864 | tf_op jit(solution)/shard_map/all_to_all | solution.py:1331
  166.3 24.2 %collective-permute-done.29.rest_2_ = bf16[256,768]{1,0:T(8,128)(2,1)S(1)} collective-permute-done((bf16[256,768]{1,0:T(8,128)(2,1)S(1)}, bf16[256,768]{1,0:T(8,128)(2,1)S(1)}, u32[]{:S(2)}, u32[]{:S(2)}) %collective-permute-start.29) | collective-permute-done | bytes 393248 | tf_op jit(solution)/shard_map/ppermute | solution.py:1132
  191.5 20.8 %dense_ffn.1 = (bf16[512,768]{1,0:T(8,128)(2,1)}, bf16[512,768]{1,0:T(8,128)(2,1)}, bf16[512,768]{1,0:T(8,128)(2,1)}, f32[512,768]{1,0:T(8,128)}, bf16[512,768]{...) custom-call(s32[2]{0:T(128)} %pad_add_fusion.ids, bf16[8,128,384]{2,1,0:T(8,128)(2,1)} %copy-done.3, ...), custom_call_target="tpu_custom_call" | custom-call | flops 10871635968 | bytes 19316736 | tf_op jit(solution)/shard_map/dense_ffn/pallas_call | solution.py:155
  213.4 3.7 all-to-all-start.1
  217.1 3.7 output_grads.2
  220.8 8.9 %all-to-all-done.1.rest_1_ = bf16[8,128,384]{2,1,0:T(8,128)(2,1)S(1)} async-done(((bf16[8,128,384]{2,1,0:T(8,128)(2,1)}), bf16[8,128,384]{2,1,0:T(8,128)(2,1)S(1)}, u32[]{:S(2)}, u32[]{:S(2)}) %all-to-all-start.1) | async-done | bytes 786464 | tf_op jit(solution)/shard_map/all_to_all | solution.py:1343
  230.6 26.8 %attend_back.2 = (bf16[8,128,1152]{2,1,0:T(8,128)(2,1)}, bf16[2048,576]{1,0:T(8,128)(2,1)}) custom-call(s32[2]{0:T(128)} %pad_add_fusion.ids, s32[8]{0:T(128)} %and_select_fusion.first_ref, s32[8,2048]{1,0:T(8,128)} %broadcast_in_dim.62.row_ref, bf16[2048,576]{1,0:T(8,128)(2,1)} %get-tuple-element.324.rest_0_, bf16[8,128,384]{2,1,0:T(8,128)(2,1)} %copy-done.4, ...), custom_call_target="tpu_custom_call" | custom-call | flops 4026531840 | bytes 8781856 | tf_op jit(solution)/shard_map/attend_back/pallas_call | solution.py:155
  258.2 6.0 %all-to-all-start.2 = ((bf16[8,128,1152]{2,1,0:T(8,128)(2,1)}), bf16[8,128,1152]{2,1,0:T(8,128)(2,1)S(1)}, u32[]{:S(2)}, u32[]{:S(2)}) async-start(bf16[8,128,1152]{2,1,0:T(8,128)(2,1)} %get-tuple-element.346), calls=%async_computation.2 | async-start | bytes 4718592 | tf_op jit(solution)/shard_map/all_to_all | solution.py:1352
  264.4 6.6 %project_grads.2 = (bf16[4,96,576]{2,1,0:T(8,128)(2,1)}, bf16[4,96,576]{2,1,0:T(8,128)(2,1)}) custom-call(s32[2]{0:T(128)} %pad_add_fusion.ids, bf16[2048,576]{1,0:T(8,128)(2,1)} %get-tuple-element.347.dx_ref, bf16[256,768]{1,0:T(8,128)(2,1)} %get-tuple-element.304.rest_0_, bf16[256,768]{1,0:T(8,128)(2,1)} %copy-done.56, bf16[256,768]{1,0:T(8,128)(2,1)} %copy-done.59, ...), custom_call_target="tpu_custom_call" | custom-call | flops 1811939328 | bytes 6389760 | tf_op jit(solution)/shard_map/project_grads/pallas_call | solution.py:155
  277.2 3.8 collective-permute-start.35
  283.4 16.9 %hidden_grads.2 = bf16[768,1536]{1,0:T(8,128)(2,1)} custom-call(s32[2]{0:T(128)} %pad_add_fusion.ids, bf16[512,768]{1,0:T(8,128)(2,1)} %bitcast.42, bf16[512,768]{1,0:T(8,128)(2,1)} %copy-done.53, bf16[256,768]{1,0:T(8,128)(2,1)} %copy-done.62, bf16[256,768]{1,0:T(8,128)(2,1)} %copy-done.63, bf16[512,768]{1,0:T(8,128)(2,1)} %copy-done.54, ...), custom_call_target="tpu_custom_call" | custom-call | flops 9663676416 | bytes 11010048 | tf_op jit(solution)/shard_map/hidden_grads/pallas_call | solution.py:155
  305.1 4.3 collective-permute-start.39
  312.7 8.9 %dense_post.1 = (f32[512,768]{1,0:T(8,128)}, f32[128,768]{1,0:T(8,128)}, bf16[128,768]{1,0:T(8,128)(2,1)}, f32[128,128]{1,0:T(8,128)}, f32[8,768]{1,0:T(8,128)}) custom-call(s32[2]{0:T(128)} %pad_add_fusion.ids, bf16[8,128,1152]{2,1,0:T(8,128)(2,1)} %copy-done, bf16[768,2304]{1,0:T(8,128)(2,1)} %rest_0_.6, ...), custom_call_target="tpu_custom_call" | custom-call | flops 1811939328 | bytes 11976704 | tf_op jit(solution)/shard_map/dense_post/pallas_call | solution.py:155
  321.6 10.1 %routed_back.1 = (f32[128,768]{1,0:T(8,128)}, bf16[128,768]{1,0:T(8,128)(2,1)}, f32[8,768]{1,0:T(8,128)}, bf16[8,32,384]{2,1,0:T(8,128)(2,1)}) custom-call(s32[2]{0:T(128)} %pad_add_fusion.ids, bf16[128,768]{1,0:T(8,128)(2,1)} %get-tuple-element.407.rest_0_.low.rest_4_, bf16[128,768]{1,0:T(8,128)(2,1)} %get-tuple-element.403.g_low.rest_0_, ...), custom_call_target="tpu_custom_call" | custom-call | flops 1811939328 | bytes 12828672 | tf_op jit(solution)/shard_map/routed_back/pallas_call | solution.py:155
  331.8 3.3 output_grads.3
  336.3 3.4 collective-permute-start.43
  339.7 10.4 %all_to_all.25.rest_2_ = bf16[8,32,384]{2,1,0:T(8,128)(2,1)} all-to-all(bf16[8,32,384]{2,1,0:T(8,128)(2,1)} %get-tuple-element.375), channel_id=1, replica_groups=mesh['wide'=8,'narrow'=4] {'wide'}, dimensions={0} | all-to-all | bytes 393216 | tf_op jit(solution)/shard_map/all_to_all | solution.py:1385
  350.1 6.6 %attend_back.3 = (bf16[8,32,1152]{2,1,0:T(8,128)(2,1)}, bf16[512,576]{1,0:T(8,128)(2,1)}) custom-call(s32[2]{0:T(128)} %pad_add_fusion.ids, s32[2]{0:T(128)} %broadcast.58.first_ref, s32[8,512]{1,0:T(8,128)} %broadcast_in_dim.57.row_ref, s32[512,1]{1,0:T(8,128)} %copy.36.rest_0_, bf16[512,576]{1,0:T(8,128)(2,1)} %get-tuple-element.323.rest_1_, ...), custom_call_target="tpu_custom_call" | custom-call | flops 251658240 | bytes 2197512 | tf_op jit(solution)/shard_map/attend_back/pallas_call | solution.py:155
  356.8 5.3 %project_grads.3 = (bf16[4,96,576]{2,1,0:T(8,128)(2,1)}, bf16[4,96,576]{2,1,0:T(8,128)(2,1)}) custom-call(s32[2]{0:T(128)} %pad_add_fusion.ids, bf16[512,576]{1,0:T(8,128)(2,1)} %get-tuple-element.390.dx_ref, bf16[64,768]{1,0:T(8,128)(2,1)} %get-tuple-element.253.rest_1_.rest_0_, bf16[64,768]{1,0:T(8,128)(2,1)} %copy-done.34, bf16[64,768]{1,0:T(8,128)(2,1)} %copy-done.31, ...), custom_call_target="tpu_custom_call" | custom-call | flops 452984832 | bytes 2260992 | tf_op jit(solution)/shard_map/project_grads/pallas_call | solution.py:155
  362.1 2.8 join.1
  365.0 8.6 %hidden_grads.3 = bf16[768,1536]{1,0:T(8,128)(2,1)} custom-call(s32[2]{0:T(128)} %pad_add_fusion.ids, bf16[128,768]{1,0:T(8,128)(2,1)} %get-tuple-element.403.g_low.rest_0_, bf16[128,768]{1,0:T(8,128)(2,1)} %copy-done.70, bf16[128,768]{1,0:T(8,128)(2,1)} %copy-done.71, bf16[128,768]{1,0:T(8,128)(2,1)} %copy-done.72, ...), custom_call_target="tpu_custom_call" | custom-call | flops 2415919104 | bytes 6291456 | tf_op jit(solution)/shard_map/hidden_grads/pallas_call | solution.py:155
  378.2 6.8 %collective-permute-done.46.rest_1_ = bf16[96,1664]{1,0:T(8,128)(2,1)S(1)} collective-permute-done((bf16[96,1664]{1,0:T(8,128)(2,1)S(1)}, bf16[96,1664]{1,0:T(8,128)(2,1)S(1)}, u32[]{:S(2)}, u32[]{:S(2)}) %collective-permute-start.46) | collective-permute-done | bytes 319520 | tf_op jit(solution)/shard_map/ppermute | solution.py:1183
  385.0 6.7 %collective-permute-done.47.rest_2_ = bf16[96,1664]{1,0:T(8,128)(2,1)S(1)} collective-permute-done((bf16[96,1664]{1,0:T(8,128)(2,1)S(1)}, bf16[96,1664]{1,0:T(8,128)(2,1)S(1)}, u32[]{:S(2)}, u32[]{:S(2)}) %collective-permute-start.47) | collective-permute-done | bytes 319520 | tf_op jit(solution)/shard_map/ppermute | solution.py:1183
  398.2 3.5 all-to-all-start.4
  407.6 3.0 collective-permute-start.54
  410.6 3.0 collective-permute-start.55
  413.6 3.2 collective-permute-done.51.rest_2_
  419.5 5.0 %collective-permute-done.54.rest_2_ = bf16[24,1664]{1,0:T(8,128)(2,1)S(1)} collective-permute-done((bf16[24,1664]{1,0:T(8,128)(2,1)S(1)}, bf16[24,1664]{1,0:T(8,128)(2,1)S(1)}, u32[]{:S(2)}, u32[]{:S(2)}) %collective-permute-start.54) | collective-permute-done | bytes 79904 | tf_op jit(solution)/shard_map/ppermute | solution.py:1132
  431.9 3.7 collective-permute-start.60
  439.1 2.8 collective-permute-start.58
  441.9 2.9 unpack.3
  444.7 6.0 %routed_post.1 = f32[512,768]{1,0:T(8,128)} custom-call(s32[2]{0:T(128)} %pad_add_fusion.ids, bf16[8,32,1152]{2,1,0:T(8,128)(2,1)} %copy-done.1, bf16[768,2304]{1,0:T(8,128)(2,1)} %rest_0_.7, f32[8,768]{1,0:T(8,128)} %get-tuple-element.279.rest_10_.vecs.rest_3_.rest_1_, bf16[128,768]{1,0:T(8,128)(2,1)} %get-tuple-element.278.rest_9_.picked.rest_5_.rest_2_, ...), custom_call_target="tpu_custom_call" | custom-call | flops 452984832 | bytes 8019968 | tf_op jit(solution)/shard_map/routed_post/pallas_call | solution.py:155
  454.7 2.9 unpack.2
  (321 shorter events, 122.0 us)
Async XLA Ops:
  7.2 37.7 %all-gather.12.cloned.1.call-start = ((), (), s32[]{:S(2)}) async-start(), calls=%async_computation.10 | async-start | bytes 1474560 | tf_op jit(solution)/shard_map/all_gather | solution.py:1227
  9.0 93.9 %all-gather.14.cloned.1.call-start = ((), (), s32[]{:S(2)}) async-start(), calls=%async_computation.11 | async-start | bytes 5898240 | tf_op jit(solution)/shard_map/all_gather | solution.py:1179
  45.0 90.6 %all-gather.16.cloned.1.call-start = ((), (), s32[]{:S(2)}) async-start(), calls=%async_computation.12 | async-start | bytes 1474560 | tf_op jit(solution)/shard_map/all_gather | solution.py:1308
  48.4 17.0 %collective-permute-start.14 = (bf16[128,768]{1,0:T(8,128)(2,1)}, bf16[128,768]{1,0:T(8,128)(2,1)S(1)}, u32[]{:S(2)}, u32[]{:S(2)}) collective-permute-start(bf16[128,768]{1,0:T(8,128)(2,1)} %get-tuple-element.407.rest_0_.low.rest_4_), channel_id=1, source_target_pairs={{0,1},{1,0},{2,3},{3,2},{4,5},{5,4},{6,7},{7,6},{8,9},{9,8},{10,11... | collective-permute-start | bytes 589832 | tf_op jit(solution)/shard_map/ppermute | solution.py:1132
  50.0 17.3 %collective-permute-start.15 = (bf16[128,768]{1,0:T(8,128)(2,1)}, bf16[128,768]{1,0:T(8,128)(2,1)S(1)}, u32[]{:S(2)}, u32[]{:S(2)}) collective-permute-start(bf16[128,768]{1,0:T(8,128)(2,1)} %get-tuple-element.407.rest_0_.low.rest_4_), channel_id=1, source_target_pairs={{0,2},{1,3},{2,0},{3,1},{4,6},{5,7},{6,4},{7,5},{8,10},{9,11},{10,... | collective-permute-start | bytes 589832 | tf_op jit(solution)/shard_map/ppermute | solution.py:1132
  52.6 14.7 %collective-permute-start.16 = (bf16[128,768]{1,0:T(8,128)(2,1)}, bf16[128,768]{1,0:T(8,128)(2,1)S(1)}, u32[]{:S(2)}, u32[]{:S(2)}) collective-permute-start(bf16[128,768]{1,0:T(8,128)(2,1)} %get-tuple-element.407.rest_0_.low.rest_4_), channel_id=1, source_target_pairs={{0,3},{1,2},{2,1},{3,0},{4,7},{5,6},{6,5},{7,4},{8,11},{9,10},{10,... | collective-permute-start | bytes 589832 | tf_op jit(solution)/shard_map/ppermute | solution.py:1132
  76.1 17.3 %collective-permute-start.18 = (bf16[128,768]{1,0:T(8,128)(2,1)}, bf16[128,768]{1,0:T(8,128)(2,1)S(1)}, u32[]{:S(2)}, u32[]{:S(2)}) collective-permute-start(bf16[128,768]{1,0:T(8,128)(2,1)} %get-tuple-element.296), channel_id=1, source_target_pairs={{0,2},{1,3},{2,0},{3,1},{4,6},{5,7},{6,4},{7,5},{8,10},{9,11},{10,... | collective-permute-start | bytes 589832 | tf_op jit(solution)/shard_map/ppermute | solution.py:1132
  77.0 16.4 %collective-permute-start.19 = (bf16[128,768]{1,0:T(8,128)(2,1)}, bf16[128,768]{1,0:T(8,128)(2,1)S(1)}, u32[]{:S(2)}, u32[]{:S(2)}) collective-permute-start(bf16[128,768]{1,0:T(8,128)(2,1)} %get-tuple-element.297), channel_id=1, source_target_pairs={{0,3},{1,2},{2,1},{3,0},{4,7},{5,6},{6,5},{7,4},{8,11},{9,10},{10,... | collective-permute-start | bytes 589832 | tf_op jit(solution)/shard_map/ppermute | solution.py:1132
  104.6 108.5 %all-gather.18.cloned.1.call-start = ((), (), s32[]{:S(2)}) async-start(), calls=%async_computation.13 | async-start | bytes 5898240 | tf_op jit(solution)/shard_map/all_gather | solution.py:1179
  108.3 18.9 %collective-permute-start.21 = (bf16[256,768]{1,0:T(8,128)(2,1)}, bf16[256,768]{1,0:T(8,128)(2,1)S(1)}, u32[]{:S(2)}, u32[]{:S(2)}) collective-permute-start(bf16[256,768]{1,0:T(8,128)(2,1)} %get-tuple-element.304.rest_0_), channel_id=1, source_target_pairs={{0,8},{4,12},{8,0},{12,4},{16,24},{20,28},{24,16},{28,20},{1,9},{5... | collective-permute-start | bytes 1179656 | tf_op jit(solution)/shard_map/ppermute | solution.py:1183
  108.8 18.4 %collective-permute-start.24 = (bf16[256,768]{1,0:T(8,128)(2,1)S(1)}, bf16[256,768]{1,0:T(8,128)(2,1)S(1)}, u32[]{:S(2)}, u32[]{:S(2)}) collective-permute-start(bf16[256,768]{1,0:T(8,128)(2,1)S(1)} %collective-permute-done.20.rest_1_), channel_id=1, source_target_pairs={{0,16},{4,20},{8,24},{12,28},{16,0},{20,4},{24,8},{28,12},{1,17},{... | collective-permute-start | bytes 1179656 | tf_op jit(solution)/shard_map/ppermute | solution.py:1183
  117.1 17.7 %collective-permute-start.25 = (bf16[256,768]{1,0:T(8,128)(2,1)S(1)}, bf16[256,768]{1,0:T(8,128)(2,1)S(1)}, u32[]{:S(2)}, u32[]{:S(2)}) collective-permute-start(bf16[256,768]{1,0:T(8,128)(2,1)S(1)} %collective-permute-done.23.rest_4_), channel_id=1, source_target_pairs={{0,8},{4,12},{8,0},{12,4},{16,24},{20,28},{24,16},{28,20},{1,9},{5... | collective-permute-start | bytes 1179656 | tf_op jit(solution)/shard_map/ppermute | solution.py:1183
  118.8 16.1 %collective-permute-start.26 = (bf16[256,768]{1,0:T(8,128)(2,1)S(1)}, bf16[256,768]{1,0:T(8,128)(2,1)}, u32[]{:S(2)}, u32[]{:S(2)}) collective-permute-start(bf16[256,768]{1,0:T(8,128)(2,1)S(1)} %collective-permute-done.22.rest_3_), channel_id=1, source_target_pairs={{0,16},{4,20},{8,24},{12,28},{16,0},{20,4},{24,8},{28,12},{1,17},{... | collective-permute-start | bytes 1179656 | tf_op jit(solution)/shard_map/ppermute | solution.py:1183
  135.6 24.6 %collective-permute-start.27 = (bf16[4,4,2,96,768]{4,3,2,1,0:T(8,128)(2,1)}, bf16[4,4,2,96,768]{4,3,2,1,0:T(8,128)(2,1)}, u32[]{:S(2)}, u32[]{:S(2)}) collective-permute-start(bf16[4,4,2,96,768]{4,3,2,1,0:T(8,128)(2,1)} %bitcast.55), channel_id=1, source_target_pairs={{0,4},{4,0},{8,12},{12,8},{16,20},{20,16},{24,28},{28,24},{1,5},{5... | collective-permute-start | bytes 14155784 | tf_op jit(solution)/shard_map/ppermute | solution.py:1189
  135.7 23.5 %collective-permute-start.28 = (bf16[512,768]{1,0:T(8,128)(2,1)S(1)}, bf16[512,768]{1,0:T(8,128)(2,1)S(1)}, u32[]{:S(2)}, u32[]{:S(2)}) collective-permute-start(bf16[512,768]{1,0:T(8,128)(2,1)S(1)} %bitcast.43), channel_id=1, source_target_pairs={{0,1},{1,0},{2,3},{3,2},{4,5},{5,4},{6,7},{7,6},{8,9},{9,8},{10,11... | collective-permute-start | bytes 2359304 | tf_op jit(solution)/shard_map/ppermute | solution.py:1132
  137.1 53.4 %collective-permute-start.30 = (bf16[512,768]{1,0:T(8,128)(2,1)S(1)}, bf16[512,768]{1,0:T(8,128)(2,1)S(1)}, u32[]{:S(2)}, u32[]{:S(2)}) collective-permute-start(bf16[512,768]{1,0:T(8,128)(2,1)S(1)} %bitcast.44), channel_id=1, source_target_pairs={{0,3},{1,2},{2,1},{3,0},{4,7},{5,6},{6,5},{7,4},{8,11},{9,10},{10,... | collective-permute-start | bytes 2359304 | tf_op jit(solution)/shard_map/ppermute | solution.py:1132
  160.1 30.4 %all-to-all-start = ((bf16[8,128,384]{2,1,0:T(8,128)(2,1)}), bf16[8,128,384]{2,1,0:T(8,128)(2,1)S(1)}, u32[]{:S(2)}, u32[]{:S(2)}) async-start(bf16[8,128,384]{2,1,0:T(8,128)(2,1)} %get-tuple-element.316), calls=%async_computation | async-start | bytes 1572864 | tf_op jit(solution)/shard_map/all_to_all | solution.py:1331
  165.0 118.4 %all-gather.10.cloned.1.call-start = ((), (), s32[]{:S(2)}) async-start(), calls=%async_computation.7 | async-start | bytes 3932160 | tf_op jit(solution)/shard_map/all_gather | solution.py:1340
  165.1 25.4 %collective-permute-start.29 = (bf16[256,768]{1,0:T(8,128)(2,1)S(1)}, bf16[256,768]{1,0:T(8,128)(2,1)S(1)}, u32[]{:S(2)}, u32[]{:S(2)}) collective-permute-start(bf16[256,768]{1,0:T(8,128)(2,1)S(1)} %get-tuple-element.317), channel_id=1, source_target_pairs={{0,2},{1,3},{2,0},{3,1},{4,6},{5,7},{6,4},{7,5},{8,10},{9,11},{10,... | collective-permute-start | bytes 1179656 | tf_op jit(solution)/shard_map/ppermute | solution.py:1132
  190.6 21.8 %collective-permute-start.31 = (bf16[256,768]{1,0:T(8,128)(2,1)S(1)}, bf16[256,768]{1,0:T(8,128)(2,1)S(1)}, u32[]{:S(2)}, u32[]{:S(2)}) collective-permute-start(bf16[256,768]{1,0:T(8,128)(2,1)S(1)} %get-tuple-element.329), channel_id=1, source_target_pairs={{0,2},{1,3},{2,0},{3,1},{4,6},{5,7},{6,4},{7,5},{8,10},{9,11},{10,... | collective-permute-start | bytes 1179656 | tf_op jit(solution)/shard_map/ppermute | solution.py:1132
  213.1 44.3 %collective-permute-start.32 = (bf16[4,4,2,96,768]{4,3,2,1,0:T(8,128)(2,1)}, bf16[4,4,2,96,768]{4,3,2,1,0:T(8,128)(2,1)}, u32[]{:S(2)}, u32[]{:S(2)}) collective-permute-start(bf16[4,4,2,96,768]{4,3,2,1,0:T(8,128)(2,1)} %bitcast.34), channel_id=1, source_target_pairs={{0,4},{4,0},{8,12},{12,8},{16,20},{20,16},{24,28},{28,24},{1,5},{5... | collective-permute-start | bytes 14155784 | tf_op jit(solution)/shard_map/ppermute | solution.py:1189
  213.4 16.3 %all-to-all-start.1 = ((bf16[8,128,384]{2,1,0:T(8,128)(2,1)}), bf16[8,128,384]{2,1,0:T(8,128)(2,1)S(1)}, u32[]{:S(2)}, u32[]{:S(2)}) async-start(bf16[8,128,384]{2,1,0:T(8,128)(2,1)} %get-tuple-element.334), calls=%async_computation.1 | async-start | bytes 1572864 | tf_op jit(solution)/shard_map/all_to_all | solution.py:1343
  229.7 27.7 %collective-permute-start.33 = (bf16[4,96,768]{2,1,0:T(8,128)(2,1)}, bf16[4,96,768]{2,1,0:T(8,128)(2,1)S(1)}, u32[]{:S(2)}, u32[]{:S(2)}) collective-permute-start(bf16[4,96,768]{2,1,0:T(8,128)(2,1)} %get-tuple-element.345), channel_id=1, source_target_pairs={{0,4},{4,0},{8,12},{12,8},{16,20},{20,16},{24,28},{28,24},{1,5},{5... | collective-permute-start | bytes 1769480 | tf_op jit(solution)/shard_map/ppermute | solution.py:1189
  258.2 45.3 %all-to-all-start.2 = ((bf16[8,128,1152]{2,1,0:T(8,128)(2,1)}), bf16[8,128,1152]{2,1,0:T(8,128)(2,1)S(1)}, u32[]{:S(2)}, u32[]{:S(2)}) async-start(bf16[8,128,1152]{2,1,0:T(8,128)(2,1)} %get-tuple-element.346), calls=%async_computation.2 | async-start | bytes 4718592 | tf_op jit(solution)/shard_map/all_to_all | solution.py:1352
  264.2 193.4 %reduce-scatter.3.cloned.1.call-start = ((), (), s32[]{:S(2)}) async-start(), calls=%async_computation.8 | async-start | bytes 2654208 | tf_op jit(solution)/shard_map/reduce_scatter | solution.py:1360
  277.2 23.1 %collective-permute-start.35 = (bf16[1,96,576]{2,1,0:T(8,128)(2,1)}, bf16[1,96,576]{2,1,0:T(8,128)(2,1)S(1)}, u32[]{:S(2)}, u32[]{:S(2)}) collective-permute-start(bf16[1,96,576]{2,1,0:T(8,128)(2,1)} %get-tuple-element.351), channel_id=1, source_target_pairs={{0,1},{1,0},{2,3},{3,2},{4,5},{5,4},{6,7},{7,6},{8,9},{9,8},{10,11... | collective-permute-start | bytes 331784 | tf_op jit(solution)/shard_map/ppermute | solution.py:1132
  281.0 19.3 %collective-permute-start.36 = (bf16[1,96,576]{2,1,0:T(8,128)(2,1)}, bf16[1,96,576]{2,1,0:T(8,128)(2,1)S(1)}, u32[]{:S(2)}, u32[]{:S(2)}) collective-permute-start(bf16[1,96,576]{2,1,0:T(8,128)(2,1)} %get-tuple-element.352), channel_id=1, source_target_pairs={{0,2},{1,3},{2,0},{3,1},{4,6},{5,7},{6,4},{7,5},{8,10},{9,11},{10,... | collective-permute-start | bytes 331784 | tf_op jit(solution)/shard_map/ppermute | solution.py:1132
  281.8 18.5 %collective-permute-start.37 = (bf16[1,96,576]{2,1,0:T(8,128)(2,1)}, bf16[1,96,576]{2,1,0:T(8,128)(2,1)S(1)}, u32[]{:S(2)}, u32[]{:S(2)}) collective-permute-start(bf16[1,96,576]{2,1,0:T(8,128)(2,1)} %get-tuple-element.353), channel_id=1, source_target_pairs={{0,3},{1,2},{2,1},{3,0},{4,7},{5,6},{6,5},{7,4},{8,11},{9,10},{10,... | collective-permute-start | bytes 331784 | tf_op jit(solution)/shard_map/ppermute | solution.py:1132
  303.5 154.0 %reduce-scatter.5.cloned.1.call-start = ((), (), s32[]{:S(2)}) async-start(), calls=%async_computation.9 | async-start | bytes 2654208 | tf_op jit(solution)/shard_map/reduce_scatter | solution.py:1395
  304.5 27.3 %collective-permute-start.38 = (bf16[96,576]{1,0:T(8,128)(2,1)S(1)}, bf16[96,576]{1,0:T(8,128)(2,1)S(1)}, u32[]{:S(2)}, u32[]{:S(2)}) collective-permute-start(bf16[96,576]{1,0:T(8,128)(2,1)S(1)} %bitcast.49), channel_id=1, source_target_pairs={{0,0},{1,9},{2,18},{3,27},{4,4},{5,13},{6,22},{7,31},{8,8},{9,1},{... | collective-permute-start | bytes 331784 | tf_op jit(solution)/shard_map/ppermute | solution.py:1106
  305.1 26.6 %collective-permute-start.39 = (bf16[96,576]{1,0:T(8,128)(2,1)S(1)}, bf16[96,576]{1,0:T(8,128)(2,1)S(1)}, u32[]{:S(2)}, u32[]{:S(2)}) collective-permute-start(bf16[96,576]{1,0:T(8,128)(2,1)S(1)} %bitcast.50), channel_id=1, source_target_pairs={{0,1},{1,8},{2,19},{3,26},{4,5},{5,12},{6,23},{7,30},{8,9},{9,0},{... | collective-permute-start | bytes 331784 | tf_op jit(solution)/shard_map/ppermute | solution.py:1106
  309.4 22.4 %collective-permute-start.40 = (bf16[96,576]{1,0:T(8,128)(2,1)S(1)}, bf16[96,576]{1,0:T(8,128)(2,1)S(1)}, u32[]{:S(2)}, u32[]{:S(2)}) collective-permute-start(bf16[96,576]{1,0:T(8,128)(2,1)S(1)} %bitcast.51), channel_id=1, source_target_pairs={{0,2},{1,11},{2,16},{3,25},{4,6},{5,15},{6,20},{7,29},{8,10},{9,3}... | collective-permute-start | bytes 331784 | tf_op jit(solution)/shard_map/ppermute | solution.py:1106
  312.0 19.8 %collective-permute-start.41 = (bf16[96,576]{1,0:T(8,128)(2,1)S(1)}, bf16[96,576]{1,0:T(8,128)(2,1)S(1)}, u32[]{:S(2)}, u32[]{:S(2)}) collective-permute-start(bf16[96,576]{1,0:T(8,128)(2,1)S(1)} %bitcast.52), channel_id=1, source_target_pairs={{0,3},{1,10},{2,17},{3,24},{4,7},{5,14},{6,21},{7,28},{8,11},{9,2}... | collective-permute-start | bytes 331784 | tf_op jit(solution)/shard_map/ppermute | solution.py:1106
  335.1 21.7 %collective-permute-start.45 = (bf16[4,96,896]{2,1,0:T(8,128)(2,1)}, bf16[4,96,896]{2,1,0:T(8,128)(2,1)S(1)}, u32[]{:S(2)}, u32[]{:S(2)}) collective-permute-start(bf16[4,96,896]{2,1,0:T(8,128)(2,1)} %get-tuple-element.382), channel_id=1, source_target_pairs={{0,4},{4,0},{8,12},{12,8},{16,20},{20,16},{24,28},{28,24},{1,5},{5... | collective-permute-start | bytes 2064392 | tf_op jit(solution)/shard_map/ppermute | solution.py:1189
  335.1 21.6 %collective-permute-start.42 = (bf16[128,768]{1,0:T(8,128)(2,1)S(1)}, bf16[128,768]{1,0:T(8,128)(2,1)S(1)}, u32[]{:S(2)}, u32[]{:S(2)}) collective-permute-start(bf16[128,768]{1,0:T(8,128)(2,1)S(1)} %copy-done.15), channel_id=1, source_target_pairs={{0,1},{1,0},{2,3},{3,2},{4,5},{5,4},{6,7},{7,6},{8,9},{9,8},{10,11... | collective-permute-start | bytes 589832 | tf_op jit(solution)/shard_map/ppermute | solution.py:1132
  336.3 20.5 %collective-permute-start.43 = (bf16[128,768]{1,0:T(8,128)(2,1)S(1)}, bf16[128,768]{1,0:T(8,128)(2,1)S(1)}, u32[]{:S(2)}, u32[]{:S(2)}) collective-permute-start(bf16[128,768]{1,0:T(8,128)(2,1)S(1)} %copy-done.15), channel_id=1, source_target_pairs={{0,2},{1,3},{2,0},{3,1},{4,6},{5,7},{6,4},{7,5},{8,10},{9,11},{10,... | collective-permute-start | bytes 589832 | tf_op jit(solution)/shard_map/ppermute | solution.py:1132
  339.7 17.1 %collective-permute-start.44 = (bf16[128,768]{1,0:T(8,128)(2,1)S(1)}, bf16[128,768]{1,0:T(8,128)(2,1)S(1)}, u32[]{:S(2)}, u32[]{:S(2)}) collective-permute-start(bf16[128,768]{1,0:T(8,128)(2,1)S(1)} %copy-done.15), channel_id=1, source_target_pairs={{0,3},{1,2},{2,1},{3,0},{4,7},{5,6},{6,5},{7,4},{8,11},{9,10},{10,... | collective-permute-start | bytes 589832 | tf_op jit(solution)/shard_map/ppermute | solution.py:1132
  374.6 20.8 %collective-permute-start.49 = (bf16[4,96,576]{2,1,0:T(8,128)(2,1)S(1)}, bf16[4,96,576]{2,1,0:T(8,128)(2,1)S(1)}, u32[]{:S(2)}, u32[]{:S(2)}) collective-permute-start(bf16[4,96,576]{2,1,0:T(8,128)(2,1)S(1)} %copy-done.55), channel_id=1, source_target_pairs={{0,4},{4,0},{8,12},{12,8},{16,20},{20,16},{24,28},{28,24},{1,5},{5... | collective-permute-start | bytes 1327112 | tf_op jit(solution)/shard_map/ppermute | solution.py:1189
  375.3 16.4 %collective-permute-start.47 = (bf16[96,1664]{1,0:T(8,128)(2,1)S(1)}, bf16[96,1664]{1,0:T(8,128)(2,1)S(1)}, u32[]{:S(2)}, u32[]{:S(2)}) collective-permute-start(bf16[96,1664]{1,0:T(8,128)(2,1)S(1)} %copy-done.65), channel_id=1, source_target_pairs={{0,16},{4,20},{8,24},{12,28},{16,0},{20,4},{24,8},{28,12},{1,17},{... | collective-permute-start | bytes 958472 | tf_op jit(solution)/shard_map/ppermute | solution.py:1183
  375.8 15.9 %collective-permute-start.48 = (bf16[96,1664]{1,0:T(8,128)(2,1)S(1)}, bf16[96,1664]{1,0:T(8,128)(2,1)S(1)}, u32[]{:S(2)}, u32[]{:S(2)}) collective-permute-start(bf16[96,1664]{1,0:T(8,128)(2,1)S(1)} %copy-done.64), channel_id=1, source_target_pairs={{0,24},{4,28},{8,16},{12,20},{16,8},{20,12},{24,0},{28,4},{1,25},{... | collective-permute-start | bytes 958472 | tf_op jit(solution)/shard_map/ppermute | solution.py:1183
  398.2 18.6 %all-to-all-start.4 = ((bf16[8,32,1152]{2,1,0:T(8,128)(2,1)}), bf16[8,32,1152]{2,1,0:T(8,128)(2,1)S(1)}, u32[]{:S(2)}, u32[]{:S(2)}) async-start(bf16[8,32,1152]{2,1,0:T(8,128)(2,1)} %get-tuple-element.428), calls=%async_computation.4 | async-start | bytes 1179648 | tf_op jit(solution)/shard_map/all_to_all | solution.py:1401
  406.6 12.9 %collective-permute-start.53 = (bf16[24,1664]{1,0:T(8,128)(2,1)S(1)}, bf16[24,1664]{1,0:T(8,128)(2,1)S(1)}, u32[]{:S(2)}, u32[]{:S(2)}) collective-permute-start(bf16[24,1664]{1,0:T(8,128)(2,1)S(1)} %copy-done.75), channel_id=1, source_target_pairs={{0,1},{1,0},{2,3},{3,2},{4,5},{5,4},{6,7},{7,6},{8,9},{9,8},{10,11... | collective-permute-start | bytes 239624 | tf_op jit(solution)/shard_map/ppermute | solution.py:1132
  407.6 16.8 %collective-permute-start.54 = (bf16[24,1664]{1,0:T(8,128)(2,1)S(1)}, bf16[24,1664]{1,0:T(8,128)(2,1)S(1)}, u32[]{:S(2)}, u32[]{:S(2)}) collective-permute-start(bf16[24,1664]{1,0:T(8,128)(2,1)S(1)} %copy-done.74), channel_id=1, source_target_pairs={{0,2},{1,3},{2,0},{3,1},{4,6},{5,7},{6,4},{7,5},{8,10},{9,11},{10,... | collective-permute-start | bytes 239624 | tf_op jit(solution)/shard_map/ppermute | solution.py:1132
  410.6 13.9 %collective-permute-start.55 = (bf16[24,1664]{1,0:T(8,128)(2,1)S(1)}, bf16[24,1664]{1,0:T(8,128)(2,1)S(1)}, u32[]{:S(2)}, u32[]{:S(2)}) collective-permute-start(bf16[24,1664]{1,0:T(8,128)(2,1)S(1)} %copy-done.73), channel_id=1, source_target_pairs={{0,3},{1,2},{2,1},{3,0},{4,7},{5,6},{6,5},{7,4},{8,11},{9,10},{10,... | collective-permute-start | bytes 239624 | tf_op jit(solution)/shard_map/ppermute | solution.py:1132
  430.4 22.9 %collective-permute-start.59 = (bf16[96,576]{1,0:T(8,128)(2,1)}, bf16[96,576]{1,0:T(8,128)(2,1)S(1)}, u32[]{:S(2)}, u32[]{:S(2)}) collective-permute-start(bf16[96,576]{1,0:T(8,128)(2,1)} %bitcast.45), channel_id=1, source_target_pairs={{0,0},{1,9},{2,18},{3,27},{4,4},{5,13},{6,22},{7,31},{8,8},{9,1},{... | collective-permute-start | bytes 331784 | tf_op jit(solution)/shard_map/ppermute | solution.py:1106
  431.9 21.4 %collective-permute-start.60 = (bf16[96,576]{1,0:T(8,128)(2,1)}, bf16[96,576]{1,0:T(8,128)(2,1)S(1)}, u32[]{:S(2)}, u32[]{:S(2)}) collective-permute-start(bf16[96,576]{1,0:T(8,128)(2,1)} %bitcast.46), channel_id=1, source_target_pairs={{0,1},{1,8},{2,19},{3,26},{4,5},{5,12},{6,23},{7,30},{8,9},{9,0},{... | collective-permute-start | bytes 331784 | tf_op jit(solution)/shard_map/ppermute | solution.py:1106
  435.5 17.8 %collective-permute-start.61 = (bf16[96,576]{1,0:T(8,128)(2,1)}, bf16[96,576]{1,0:T(8,128)(2,1)S(1)}, u32[]{:S(2)}, u32[]{:S(2)}) collective-permute-start(bf16[96,576]{1,0:T(8,128)(2,1)} %bitcast.47), channel_id=1, source_target_pairs={{0,2},{1,11},{2,16},{3,25},{4,6},{5,15},{6,20},{7,29},{8,10},{9,3}... | collective-permute-start | bytes 331784 | tf_op jit(solution)/shard_map/ppermute | solution.py:1106
  436.9 16.4 %collective-permute-start.62 = (bf16[96,576]{1,0:T(8,128)(2,1)}, bf16[96,576]{1,0:T(8,128)(2,1)S(1)}, u32[]{:S(2)}, u32[]{:S(2)}) collective-permute-start(bf16[96,576]{1,0:T(8,128)(2,1)} %bitcast.48), channel_id=1, source_target_pairs={{0,3},{1,10},{2,17},{3,24},{4,7},{5,14},{6,21},{7,28},{8,11},{9,2}... | collective-permute-start | bytes 331784 | tf_op jit(solution)/shard_map/ppermute | solution.py:1106
  (102 other events, 762.1 us)
Sparse Core Ops, SparseCore 0:
  10.2 33.1 all-gather.11
  45.2 57.6 all-gather.13
  105.0 30.4 all-gather.15
  137.2 64.6 all-gather.17
  213.5 63.0 all-gather.9
  303.6 42.7 reduce-scatter.2
  373.8 42.5 reduce-scatter.4

commit v5 on v4

--- a/solution.py
+++ b/solution.py
@@ -588,13 +588,19 @@
     if not scratch:
         return weights[0][0], weights[1][0]
     e_s, r_s = scratch
-    chips, rows = weights[0].shape[0], weights[0].shape[3]
     core = lax.rem(me, 2)
-    for c in range(chips):
-        for weight, at in ((weights[0], 2 * c + core), (weights[1], 2 * c + 1 - core)):
-            at = pl.ds(pl.multiple_of(at * rows, rows), rows)
-            e_s[at, :] = weight[c, 0, 0]
-            r_s[at, :] = weight[c, 0, 1]
+    rows = weights[0].shape[-2]
+    if len(weights) == 2:
+        blocks = []
+        for c in range(weights[0].shape[0]):
+            blocks.append((weights[0], c, 2 * c + core))
+            blocks.append((weights[1], c, 2 * c + 1 - core))
+    else:
+        blocks = [(weight, 0, me ^ s) for s, weight in enumerate(weights)]
+    for weight, c, at in blocks:
+        at = pl.ds(pl.multiple_of(at * rows, rows), rows)
+        e_s[at, :] = weight[c, 0, 0]
+        r_s[at, :] = weight[c, 0, 1]
     return e_s[...], r_s[...]
 
 
@@ -816,50 +822,38 @@
         send[c] = total[pl.ds(other, rows), :].astype(BF)
 
 
-def hidden_grads_kernel(spans, ids, *rest):
-    count = len(spans)
-    grads, rest = rest[:count], rest[count:]
-    lows, (expand, reduce_ref, out, total) = rest[:-4], rest[-4:]
+def hidden_grads_kernel(ids, low, grad, expand, reduce_ref, out, total):
+    i = pl.program_id(0)
     hidden = expand.shape[1]
-    for k, (step, low_at, rows, whole) in enumerate(spans):
-        grad = grads[k][...]
-        if len(lows) == count:
-            low = lows[k][...]
-        else:
-            at = pl.multiple_of((ids[1] ^ step) * whole + low_at, rows)
-            low = lows[0][pl.ds(at, rows), :]
-        value, slope = gelu_both(dot(low, expand[...]))
-        grad_pre = (nt_dot(grad, reduce_ref[...]) * slope).astype(BF)
-        e_term = tn_dot(low, grad_pre)
-        r_term = tn_dot(grad, value.astype(BF))
-        if k:
-            e_term, r_term = total[:, 0:hidden] + e_term, total[:, hidden:] + r_term
-        if k < count - 1:
-            total[:, 0:hidden] = e_term
-            total[:, hidden:] = r_term
-        else:
-            out[:, 0:hidden] = e_term.astype(BF)
-            out[:, hidden:] = r_term.astype(BF)
-
-
-def hidden_grads(ids, lows, grads, expand, reduce_part, halved=None):
+
+    @pl.when(i == 0)
+    def _():
+        total[...] = jnp.zeros_like(total)
+
+    value, slope = gelu_both(dot(low[...], expand[...]))
+    grad_pre = (nt_dot(grad[...], reduce_ref[...]) * slope).astype(BF)
+    total[:, 0:hidden] += tn_dot(low[...], grad_pre)
+    total[:, hidden : 2 * hidden] += tn_dot(grad[...], value.astype(BF))
+
+    @pl.when(i == pl.num_programs(0) - 1)
+    def _():
+        out[...] = total[...].astype(BF)
+
+
+def hidden_grads(ids, low, grad, expand, reduce_part):
     width, hidden = expand.shape
-    whole_rows = grads[0].shape[0]
-    spans, flat = [], []
-    for step, grad in enumerate(grads):
-        low_at = 0
-        for part in grad if step == halved else [grad]:
-            spans.append((step, low_at, part.shape[0], whole_rows))
-            flat.append(part)
-            low_at += part.shape[0]
+    block = min(512, low.shape[0])
+    row_spec = pl.BlockSpec((block, width), lambda i: (i, 0))
     (out,) = stage(
-        partial(hidden_grads_kernel, spans),
+        hidden_grads_kernel,
         "hidden_grads",
         ids,
-        flat + list(lows) + [expand, reduce_part],
+        [low, grad, expand, reduce_part],
         [sds((width, 2 * hidden), BF)],
         [pltpu.VMEM((width, 2 * hidden), F32)],
-        flops=8 * len(grads) * grads[0].size * hidden,
+        flops=8 * low.size * hidden,
+        grid=(low.shape[0] // block,),
+        specs={0: row_spec, 1: row_spec},
     )
     return out
 
@@ -984,7 +978,7 @@
     return sum_parts(ids, tie(narrow_return(parts), first))
 
 
-def spread_narrow(ids, total, rows, widths, vectors):
+def spread_narrow(ids, total, rows, widths, vectors, first):
     narrow_count = lax.axis_size("narrow")
     if total.shape[0] == rows:
         total = total.astype(F32)
@@ -997,7 +991,7 @@
         partial(gather_out_kernel, narrow_count, vectors),
         "gather_out",
         ids,
-        narrow_gather(total),
+        tie(narrow_gather(total), first),
         [sds((rows, size), F32) for size in widths[:-1]] + [sds((rows,), F32)] * vectors,
         [pltpu.VMEM((rows, widths[-1]), F32)],
     )
@@ -1065,6 +1059,23 @@
         [keep, came],
         [sds(shape, BF)] * narrow_count,
     )
+
+
+def join_all_kernel(turned, ids, keep, came, out):
+    turn = lax.div(ids[0], 2) if turned else 0
+    for n in range(out.shape[0]):
+        out[n] = (keep[n ^ turn].astype(F32) + came[n ^ turn].astype(F32)).astype(BF)
+
+
+def join_all(ids, keep, came):
+    (total,) = stage(
+        partial(join_all_kernel, direct_delivery()),
+        "join_all",
+        ids,
+        [keep, came],
+        [sds(keep.shape, BF)],
+    )
+    return total
 
 
 def sum_parts(ids, terms):
@@ -1294,8 +1305,9 @@
         own_slice(prenorm_dense).astype(F32)[None],
     )
     columns_d = group_columns(ids, tie(project_dense, low_r))
-    low_pieces, columns_d, meta_dense, own_rows = lax.optimization_barrier(
-        (narrow_gather(low_r), columns_d, meta_dense, own_rows)
+    share_r = hidden_share(tie(expand_routed, low_r), reduce_routed)
+    low_pieces, columns_d, meta_dense, own_rows, share_r = lax.optimization_barrier(
+        (narrow_gather(low_r), columns_d, meta_dense, own_rows, share_r)
     )
     partials = narrow_return(hidden_forward(ids, low_pieces, expand_routed, reduce_routed))
 
@@ -1304,10 +1316,8 @@
     )
     if staged:
         mine_d, other_d, chips_d = lax.optimization_barrier((mine_d, other_d, chips_d))
-        share_r = hidden_share(tie(expand_routed, mine_d), reduce_routed)
-        own_r = lax.all_gather(share_r, "narrow", axis=0)
+        own_r = lax.all_gather(tie(share_r, mine_d), "narrow", axis=0)[None]
         rows_d, own_r = lax.optimization_barrier((exchange_rows(mine_d, other_d), own_r))
-        chips_r = all_chips(own_r)
         weights_d = [chips_d, core_step(chips_d)]
     else:
         rows_d = exchange_rows(mine_d, other_d)
@@ -1319,24 +1329,20 @@
             lax.all_gather(expand_routed, "narrow", axis=0),
             lax.all_gather(reduce_routed, "narrow", axis=0),
         ]
-    cot_halves = cot.reshape(2, -1, width)
-    cot_first = tie(cot, rows_d)
-    cot_pieces = [cot] + [narrow_step(cot_first, s) for s in range(1, narrow_count)]
-    cot_pieces[2] = [narrow_step(tie(cot_halves[0], rows_d), 2), None]
+    cot_all = lax.all_gather(tie(cot, rows_d), "narrow", axis=0, tiled=True)
     (stack,), kept_d = attend(ids, meta_dense, rows_d, columns_d, bq_dense, stacked=True)
-    stack, weights_d, cot_pieces[1] = lax.optimization_barrier(
-        (stack, weights_d, cot_pieces[1])
-    )
-    stack, cot_pieces[2][0], cot_pieces[3:] = lax.optimization_barrier(
-        (lax.all_to_all(stack, "wide", 0, 0), cot_pieces[2][0], cot_pieces[3:])
-    )
-    cot_pieces[2][1] = narrow_step(tie(cot_halves[1], stack), 2)
+    stack, weights_d = lax.optimization_barrier((stack, weights_d))
+    stack = lax.all_to_all(stack, "wide", 0, 0)
+    if staged:
+        stack, own_r = lax.optimization_barrier((stack, own_r))
+        corner_r = chip_step(own_r, 3)
     (activations, low_d, back_d, sum_d, att_d, mid_gain_d), stack = dense_ffn(
         ids, stack, output_dense, mixed, cot, vecs, weights_d
     )
-    stack, low_d, cot_pieces = lax.optimization_barrier((stack, low_d, cot_pieces))
     if staged:
-        stack, chips_r, low_d = lax.optimization_barrier((stack, chips_r, low_d))
+        stack, low_d, cot_all, corner_r = lax.optimization_barrier(
+            (stack, low_d, cot_all, corner_r)
+        )
     low_all = lax.all_gather(low_d, "narrow", axis=0, tiled=True)
     keep_d, send_d = output_grads(ids, wide_count, att_d, back_d, [])
     stack, keep_d, send_d = lax.optimization_barrier(
@@ -1344,25 +1350,30 @@
     )
     came_d = core_step(send_d)
     if staged:
-        weights_r = [chips_r, core_step(chips_r)]
+        stack, own_r = lax.optimization_barrier((stack, own_r))
+        sides_r = [chip_step(own_r, 1), chip_step(own_r, 2)]
+        corner_r = [corner_r, core_step(corner_r)]
+        weights_r = [own_r, core_step(own_r)]
     (stack,), dx_d = attend_back(ids, meta_dense, kept_d, [stack], bq_dense, stacked=True)
     stack, dx_d, weights_r, came_d = lax.optimization_barrier(
         (stack, dx_d, weights_r, came_d)
     )
+    if staged:
+        stack, dx_d, sides_r = lax.optimization_barrier((stack, dx_d, sides_r))
+        weights_r += [w for own in sides_r for w in (own, core_step(own))] + corner_r
     stack = lax.all_to_all(stack, "wide", 0, 0)
     keep, send = project_grads(ids, wide_count, rows_d, dx_d)
-    project_d_parts = split_narrow(ids, keep, core_step(send))
-    hidden_d = hidden_grads(
-        ids, [tie(low_all, project_d_parts)], cot_pieces, expand_dense, reduce_dense, 2
-    )
-    project_d = sum_parts(ids, tie(narrow_return(project_d_parts), hidden_d))
-    stack, project_d, hidden_d = lax.optimization_barrier((stack, project_d, hidden_d))
+    project_d = join_all(ids, keep, core_step(send))
+    low_all, project_d = lax.optimization_barrier((low_all, project_d))
+    project_d = lax.psum_scatter(project_d, "narrow", scatter_dimension=0, tiled=True)
+    hidden_d = hidden_grads(ids, low_all, cot_all, expand_dense, reduce_dense)
+    stack, hidden_d, weights_r = lax.optimization_barrier((stack, hidden_d, weights_r))
     ffn_d = lax.psum_scatter(hidden_d, "wide", scatter_dimension=0, tiled=True)
-    delivered_d = deliver(ids, project_d, keep.shape[0])
     g_mixed, g_delta, g_low, g_gate, router_grad = dense_post(
         ids, stack, project_dense, vecs, mixed, sum_d, one_hot, picked, delta_r
     )
 
+    g_pieces = narrow_gather(g_low)
     g_mid_r, back_r, mid_gain_r, stack = routed_back(
         ids,
         wide_count,
@@ -1375,46 +1386,58 @@
         output_routed,
         weights_r,
     )
-    stack, delivered_d, back_r = lax.optimization_barrier((stack, delivered_d, back_r))
+    back_r, g_pieces = lax.optimization_barrier((back_r, g_pieces))
     keep_r, send_r = output_grads(
         ids, wide_count, att_r, back_r, [mid_gain_r, mid_gain_d, router_grad]
     )
     came_r = core_step(send_r)
-    g_pieces = narrow_gather(tie(g_low, keep_r))
-    stack, keep_r, send_r = lax.optimization_barrier(
-        (lax.all_to_all(stack, "wide", 0, 0), keep_r, send_r)
-    )
+    hidden_r = hidden_grads(
+        ids,
+        jnp.concatenate(tie(low_pieces, keep_r), axis=0),
+        jnp.concatenate(g_pieces, axis=0),
+        expand_routed,
+        reduce_routed,
+    )
+    stack, keep_r, send_r, hidden_r = lax.optimization_barrier(
+        (lax.all_to_all(stack, "wide", 0, 0), keep_r, send_r, hidden_r)
+    )
+    delivered_d = deliver(ids, tie(project_d, back_r), wide_count // 2)
     (stack,), dx_r = attend_back(ids, meta_routed, kept_r, [stack], bq_routed, stacked=True)
-    stack, dx_r, g_pieces, came_r = lax.optimization_barrier((stack, dx_r, g_pieces, came_r))
+    stack, dx_r, came_r, delivered_d = lax.optimization_barrier(
+        (stack, dx_r, came_r, delivered_d)
+    )
+    ffn_r = lax.psum_scatter(tie(hidden_r, dx_r), "wide", scatter_dimension=0, tiled=True)
     keep, send = project_grads(ids, wide_count, rows_r, dx_r)
     came = core_step(send)
     output_parts = join_chips(ids, tie([keep_d, keep_r], send), [came_d, came_r])
-    hidden_r = hidden_grads(
-        ids, tie(low_pieces, output_parts), g_pieces, expand_routed, reduce_routed
-    )
-    ffn_r = lax.psum_scatter(hidden_r, "wide", scatter_dimension=0, tiled=True)
-    output_parts = narrow_terms(ids, tie(chips_return(output_parts), hidden_r))
     project_parts = split_narrow(ids, tie(keep, output_parts), came)
-    stack, project_parts, output_parts = lax.optimization_barrier(
-        (stack, project_parts, output_parts)
-    )
-    stack = lax.all_to_all(stack, "wide", 0, 0)
-    returned, stack = lax.optimization_barrier((narrow_return(project_parts), stack))
-    project_r = sum_parts(ids, returned)
-    output_total = sum_narrow(ids, tie(output_parts, project_parts), project_r)
-    stack, output_total = lax.optimization_barrier((stack, output_total))
+    returned = narrow_return(project_parts)
+    project_d_grad, pre_gain_d = unpack(
+        ids, tie(delivered_d, project_parts), own_rows[1], own_rows[3]
+    )
+    stack = lax.all_to_all(tie(stack, project_parts), "wide", 0, 0)
+    project_r = sum_parts(ids, tie(returned, project_d_grad))
+    output_parts = narrow_terms(ids, tie(chips_return(output_parts), project_r))
     tokens_gradient = routed_post(
-        ids, stack, project_routed, vecs, picked, g_mid_r, g_mixed, one_hot, g_gate
-    )
-    delivered_r = deliver(ids, project_r, keep.shape[0])
-    project_d_grad, pre_gain_d = unpack(
-        ids, tie(delivered_d, project_r), own_rows[1], own_rows[3]
+        ids,
+        tie(stack, output_parts),
+        project_routed,
+        vecs,
+        picked,
+        g_mid_r,
+        g_mixed,
+        one_hot,
+        g_gate,
+    )
+    output_total = sum_narrow(ids, output_parts, tokens_gradient)
+    project_r_grad, pre_gain_r = unpack(
+        ids,
+        tie(deliver(ids, project_r, keep.shape[0]), output_total),
+        own_rows[0],
+        own_rows[2],
     )
     output_d_grad, output_r_grad, mid_r_grad, mid_d_grad, router_grad = spread_narrow(
-        ids, output_total, width // wide_count, [width, width, 128], 3
-    )
-    project_r_grad, pre_gain_r = unpack(
-        ids, tie(delivered_r, tokens_gradient), own_rows[0], own_rows[2]
+        ids, output_total, width // wide_count, [width, width, 128], 3, project_r_grad
     )
     expand_d_grad, reduce_d_grad, expand_r_grad, reduce_r_grad = finish_hidden(
         ids, ffn_d, ffn_r

time: 474 us -> 451 us (0.951)
  waiting for transfers between devices: 106 us -> 92.8 us
  starting transfers between devices: 108 us -> 98.4 us
  blocking collectives: 10.4 us -> 17.3 us
  local copies, waits for them, and re-layouts: 25.4 us -> 19.4 us
    ppermute x25 -> x18, waiting for transfers between devices: 48.5 us -> 26.8 us  [narrow_step(): lax.ppermute(x, 'narrow', [(j, j ^ s) for j in range(lax.axis_size('narro...]
    ppermute x25 -> x18, starting transfers between devices: 43.7 us -> 29 us  [narrow_step(): lax.ppermute(x, 'narrow', [(j, j ^ s) for j in range(lax.axis_size('narro...]
    all_to_all x1, blocking collectives: 10.4 us -> 17.3 us  [on_device(): stack = lax.all_to_all(stack, 'wide', 0, 0)]
    unnamed x152 -> x138, local copies, waits for them, and re-layouts: 15.9 us -> 10 us
    ppermute x7 -> x10, waiting for transfers between devices: 2.11 us -> 7.34 us  [core_step(): lax.ppermute(x, 'wide', [(j, j ^ 1) for j in range(lax.axis_size('wide'))])]
    pallas_call x31 -> x30, Pallas kernels: 194 us -> 190 us  [stage(): pl.pallas_call(body, out_shape=tuple(outs), in_specs=in_specs, out_specs=...]
    ppermute x9 -> x12, starting transfers between devices: 11.4 us -> 13.5 us  [chip_step(): lax.ppermute(x, 'wide', [(j, j ^ 2 * s) for j in range(lax.axis_size('wid...]
    all_to_all x2 -> x1, starting transfers between devices: 9.52 us -> 8.2 us  [on_device(): stack = lax.all_to_all(stack, 'wide', 0, 0)]
  transfers between devices with their start and end apart: 74 -> 74, of which waited for: 24 -> 26; matrix products, arithmetic and copies ran while one was open for 3% -> 4% of each run, Pallas kernels for 41% -> 42%
where the time goes in v5:
time: 451 us; the launch traced here: 443 us
  Pallas kernels  190 us (42%)
  starting transfers between devices  98.4 us (22%)
  waiting for transfers between devices  92.8 us (21%)
  local copies, waits for them, and re-layouts  19.4 us (4%)
  blocking collectives  17.3 us (4%)
  between operations  15.4 us (3%)
  other arithmetic  9.98 us (2%)
    pallas_call x30, Pallas kernels, stage(): pl.pallas_call(body, out_shape=tuple(outs), in_specs=in_specs, out_specs=...  190 us
    ppermute x12, waiting for transfers between devices, chip_step(): lax.ppermute(x, 'wide', [(j, j ^ 2 * s) for j in range(lax.axis_size('wid...  34.3 us
    ppermute x18, starting transfers between devices, narrow_step(): lax.ppermute(x, 'narrow', [(j, j ^ s) for j in range(lax.axis_size('narro...  29 us
    ppermute x18, waiting for transfers between devices, narrow_step(): lax.ppermute(x, 'narrow', [(j, j ^ s) for j in range(lax.axis_size('narro...  26.8 us
    ppermute x8, starting transfers between devices, deliver(): lax.ppermute(total, ('wide', 'narrow'), moves(k))  19.2 us
    all_to_all x1, blocking collectives, on_device(): stack = lax.all_to_all(stack, 'wide', 0, 0)  17.3 us
    ppermute x14, starting transfers between devices, exchange(): lax.ppermute(pieces[s], 'wide', [(j, j ^ s) for j in range(wide_count)])  15 us
    ppermute x12, starting transfers between devices, chip_step(): lax.ppermute(x, 'wide', [(j, j ^ 2 * s) for j in range(lax.axis_size('wid...  13.5 us
  transfers between devices with their start and end apart: 74, of which 26 were waited for; matrix products, arithmetic and copies ran while one was open for 4% of the time, Pallas kernels for 42%

profile of v5, /device:TPU:0, one launch (start us, length us, event | category | flops | bytes accessed | tf_op | source)
XLA Modules:
  0.0 443.0 jit_solution(8292003301681248419)
XLA Ops:
  12.2 2.9 collective-permute-start.1
  22.2 3.1 group_columns.2.rest_9_
  29.1 6.4 %attend.2 = (bf16[64,192]{1,0:T(8,128)(2,1)}, bf16[64,192]{1,0:T(8,128)(2,1)}, bf16[64,192]{1,0:T(8,128)(2,1)}, bf16[64,192]{1,0:T(8,128)(2,1)}, bf16[64,192]{1,...) custom-call(s32[2]{0:T(128)} %pad_add_fusion.ids, ...), custom_call_target="tpu_custom_call" | custom-call | flops 553648128 | bytes 2689032 | tf_op jit(solution)/shard_map/attend/pallas_call | solution.py:155
  46.0 2.8 routed_mid.1
  50.5 2.7 collective-permute-start.15
  56.0 3.2 group_columns.3.rest_8_
  68.6 4.3 hidden_forward.1
  72.9 3.6 collective-permute-start.17
  79.0 4.7 %collective-permute-done.17.rest_1_ = bf16[128,768]{1,0:T(8,128)(2,1)S(1)} collective-permute-done((bf16[128,768]{1,0:T(8,128)(2,1)}, bf16[128,768]{1,0:T(8,128)(2,1)S(1)}, u32[]{:S(2)}, u32[]{:S(2)}) %collective-permute-start.17) | collective-permute-done | bytes 196640 | tf_op jit(solution)/shard_map/ppermute | solution.py:1143
  83.7 10.2 %collective-permute-done.18.rest_2_ = bf16[128,768]{1,0:T(8,128)(2,1)S(1)} collective-permute-done((bf16[128,768]{1,0:T(8,128)(2,1)}, bf16[128,768]{1,0:T(8,128)(2,1)S(1)}, u32[]{:S(2)}, u32[]{:S(2)}) %collective-permute-start.18) | collective-permute-done | bytes 196640 | tf_op jit(solution)/shard_map/ppermute | solution.py:1143
  94.6 3.8 dense_pre.1
  98.5 4.4 %all-gather.15.cloned.1.call-done = bf16[16,2,96,768]{3,2,1,0:T(8,128)(2,1)} async-done(((bf16[4,2,96,768]{3,2,1,0:T(8,128)(2,1)}), bf16[16,2,96,768]{3,2,1,0:T(8,128)(2,1)}) %all-gather.15.cloned.1.call-update) | async-done | bytes 4718608 | tf_op jit(solution)/shard_map/all_gather | solution.py:1190
  105.0 6.2 %collective-permute-done.20.rest_1_ = bf16[256,768]{1,0:T(8,128)(2,1)S(1)} collective-permute-done((bf16[256,768]{1,0:T(8,128)(2,1)}, bf16[256,768]{1,0:T(8,128)(2,1)S(1)}, u32[]{:S(2)}, u32[]{:S(2)}) %collective-permute-start.20) | collective-permute-done | bytes 393248 | tf_op jit(solution)/shard_map/ppermute | solution.py:1200
  116.3 6.8 %collective-permute-done.22.rest_3_ = bf16[256,768]{1,0:T(8,128)(2,1)S(1)} collective-permute-done((bf16[256,768]{1,0:T(8,128)(2,1)S(1)}, bf16[256,768]{1,0:T(8,128)(2,1)S(1)}, u32[]{:S(2)}, u32[]{:S(2)}) %collective-permute-start.22) | collective-permute-done | bytes 393248 | tf_op jit(solution)/shard_map/ppermute | solution.py:1194
  124.6 7.0 %collective-permute-done.21.rest_2_ = bf16[256,768]{1,0:T(8,128)(2,1)S(1)} collective-permute-done((bf16[256,768]{1,0:T(8,128)(2,1)}, bf16[256,768]{1,0:T(8,128)(2,1)S(1)}, u32[]{:S(2)}, u32[]{:S(2)}) %collective-permute-start.21) | collective-permute-done | bytes 393248 | tf_op jit(solution)/shard_map/ppermute | solution.py:1194
  131.6 7.9 %collective-permute-done.25.rest_6_ = bf16[256,768]{1,0:T(8,128)(2,1)S(1)} collective-permute-done((bf16[256,768]{1,0:T(8,128)(2,1)S(1)}, bf16[256,768]{1,0:T(8,128)(2,1)S(1)}, u32[]{:S(2)}, u32[]{:S(2)}) %collective-permute-start.25) | collective-permute-done | bytes 393248 | tf_op jit(solution)/shard_map/ppermute | solution.py:1194
  140.4 20.2 %attend.3 = (bf16[8,128,384]{2,1,0:T(8,128)(2,1)}, bf16[2048,192]{1,0:T(8,128)(2,1)}, f32[8,2048]{1,0:T(8,128)}, bf16[2048,576]{1,0:T(8,128)(2,1)}) custom-call(s32[2]{0:T(128)} %pad_add_fusion.ids, s32[8]{0:T(128)} %and_select_fusion.first_ref, s32[8,2048]{1,0:T(8,128)} %broadcast_in_dim.65.row_ref, bf16[256,768]{1,0:T(8,128)(2,1)} %get-tuple-element.295.rest_0_, ...), custom_call_target="tpu_custom_call" | custom-call | flops 3422552064 | bytes 8093728 | tf_op jit(solution)/shard_map/attend/pallas_call | solution.py:155
  160.6 17.3 %all_to_all.25.stack = bf16[8,128,384]{2,1,0:T(8,128)(2,1)} all-to-all(bf16[8,128,384]{2,1,0:T(8,128)(2,1)} %get-tuple-element.306), channel_id=1, replica_groups=mesh['wide'=8,'narrow'=4] {'wide'}, dimensions={0} | all-to-all | bytes 1572864 | tf_op jit(solution)/shard_map/all_to_all | solution.py:1335
  178.9 20.8 %dense_ffn.1 = (bf16[512,768]{1,0:T(8,128)(2,1)}, bf16[512,768]{1,0:T(8,128)(2,1)}, bf16[512,768]{1,0:T(8,128)(2,1)}, f32[512,768]{1,0:T(8,128)}, bf16[512,768]{...) custom-call(s32[2]{0:T(128)} %pad_add_fusion.ids, bf16[8,128,384]{2,1,0:T(8,128)(2,1)} %all_to_all.25.stack, ...), custom_call_target="tpu_custom_call" | custom-call | flops 10871635968 | bytes 19316736 | tf_op jit(solution)/shard_map/dense_ffn/pallas_call | solution.py:155
  199.7 3.5 all-gather.9.cloned.1.call-done.grad
  205.7 3.7 all-to-all-start.1
  209.5 3.7 output_grads.2
  213.1 8.9 %all-to-all-done.1.rest_1_ = bf16[8,128,384]{2,1,0:T(8,128)(2,1)S(1)} async-done(((bf16[8,128,384]{2,1,0:T(8,128)(2,1)}), bf16[8,128,384]{2,1,0:T(8,128)(2,1)S(1)}, u32[]{:S(2)}, u32[]{:S(2)}) %all-to-all-start.1) | async-done | bytes 786464 | tf_op jit(solution)/shard_map/all_to_all | solution.py:1349
  223.2 27.9 %attend_back.2 = (bf16[8,128,1152]{2,1,0:T(8,128)(2,1)}, bf16[2048,576]{1,0:T(8,128)(2,1)}) custom-call(s32[2]{0:T(128)} %pad_add_fusion.ids, s32[8]{0:T(128)} %and_select_fusion.first_ref, s32[8,2048]{1,0:T(8,128)} %broadcast_in_dim.65.row_ref, bf16[2048,576]{1,0:T(8,128)(2,1)} %get-tuple-element.314.rest_0_, bf16[8,128,384]{2,1,0:T(8,128)(2,1)} %copy-done.7, ...), custom_call_target="tpu_custom_call" | custom-call | flops 4026531840 | bytes 8781856 | tf_op jit(solution)/shard_map/attend_back/pallas_call | solution.py:155
  252.2 8.2 %all-to-all-start.2 = ((bf16[8,128,1152]{2,1,0:T(8,128)(2,1)}), bf16[8,128,1152]{2,1,0:T(8,128)(2,1)S(1)}, u32[]{:S(2)}, u32[]{:S(2)}) async-start(bf16[8,128,1152]{2,1,0:T(8,128)(2,1)} %get-tuple-element.334), calls=%async_computation.2 | async-start | bytes 4718592 | tf_op jit(solution)/shard_map/all_to_all | solution.py:1364
  260.5 6.7 %project_grads.2 = (bf16[4,96,576]{2,1,0:T(8,128)(2,1)}, bf16[4,96,576]{2,1,0:T(8,128)(2,1)}) custom-call(s32[2]{0:T(128)} %pad_add_fusion.ids, bf16[2048,576]{1,0:T(8,128)(2,1)} %get-tuple-element.336.dx_ref, bf16[256,768]{1,0:T(8,128)(2,1)} %get-tuple-element.295.rest_0_, bf16[256,768]{1,0:T(8,128)(2,1)} %copy-done.59, bf16[256,768]{1,0:T(8,128)(2,1)} %copy-done.62, ...), custom_call_target="tpu_custom_call" | custom-call | flops 1811939328 | bytes 6389760 | tf_op jit(solution)/shard_map/project_grads/pallas_call | solution.py:155
  272.6 15.2 %hidden_grads.2 = bf16[768,1536]{1,0:T(8,128)(2,1)} custom-call(s32[2]{0:T(128)} %pad_add_fusion.ids, bf16[2048,768]{1,0:T(8,128)(2,1)} %all-gather.11.cloned.1.call-done.low, bf16[2048,768]{1,0:T(8,128)(2,1)} %all-gather.9.cloned.1.call-done.grad, bf16[768,768]{1,0:T(8,128)(2,1)} %expand.2, bf16[768,768]{1,0:T(8,128)(2,1)} %reduce_ref.2), custom_call_target="tpu_custom_call" | custom-call | flops 9663676416 | bytes 11010048 | tf_op jit(solution)/shard_map/hidden_grads/pallas_call | solution.py:155
  291.3 8.5 %dense_post.1 = (f32[512,768]{1,0:T(8,128)}, f32[128,768]{1,0:T(8,128)}, bf16[128,768]{1,0:T(8,128)(2,1)}, f32[128,128]{1,0:T(8,128)}, f32[8,768]{1,0:T(8,128)}) custom-call(s32[2]{0:T(128)} %pad_add_fusion.ids, bf16[8,128,1152]{2,1,0:T(8,128)(2,1)} %copy-done, bf16[768,2304]{1,0:T(8,128)(2,1)} %rest_0_.6, ...), custom_call_target="tpu_custom_call" | custom-call | flops 1811939328 | bytes 11976704 | tf_op jit(solution)/shard_map/dense_post/pallas_call | solution.py:155
  299.8 3.7 collective-permute-start.37
  306.0 10.2 %routed_back.1 = (f32[128,768]{1,0:T(8,128)}, bf16[128,768]{1,0:T(8,128)(2,1)}, f32[8,768]{1,0:T(8,128)}, bf16[8,32,384]{2,1,0:T(8,128)(2,1)}) custom-call(s32[2]{0:T(128)} %pad_add_fusion.ids, bf16[128,768]{1,0:T(8,128)(2,1)} %get-tuple-element.368.rest_0_.low, bf16[128,768]{1,0:T(8,128)(2,1)} %get-tuple-element.372.g_low, ...), custom_call_target="tpu_custom_call" | custom-call | flops 1811939328 | bytes 12828672 | tf_op jit(solution)/shard_map/routed_back/pallas_call | solution.py:155
  316.2 3.8 collective-permute-done.38
  320.0 3.4 output_grads.3
  323.4 3.4 all-to-all-start.3
  330.3 5.4 %collective-permute-start.42 = (bf16[96,576]{1,0:T(8,128)(2,1)}, bf16[96,576]{1,0:T(8,128)(2,1)S(1)}, u32[]{:S(2)}, u32[]{:S(2)}) collective-permute-start(bf16[96,576]{1,0:T(8,128)(2,1)} %bitcast.51), channel_id=1, source_target_pairs={{0,1},{1,8},{2,19},{3,26},{4,5},{5,12},{6,23},{7,30},{8,9},{9,0},{... | collective-permute-start | bytes 331784 | tf_op jit(solution)/shard_map/ppermute | solution.py:1117
  336.6 2.6 collective-permute-start.44
  339.3 6.3 %hidden_grads.3 = bf16[768,1536]{1,0:T(8,128)(2,1)} custom-call(s32[2]{0:T(128)} %pad_add_fusion.ids, bf16[512,768]{1,0:T(8,128)(2,1)} %pad_maximum_fusion.low, bf16[512,768]{1,0:T(8,128)(2,1)} %pad_maximum_fusion.1.grad, bf16[768,768]{1,0:T(8,128)(2,1)} %expand.3, bf16[768,768]{1,0:T(8,128)(2,1)} %reduce_ref.3), custom_call_target="tpu_custom_call" | custom-call | flops 2415919104 | bytes 6291456 | tf_op jit(solution)/shard_map/hidden_grads/pallas_call | solution.py:155
  346.2 6.6 %attend_back.3 = (bf16[8,32,1152]{2,1,0:T(8,128)(2,1)}, bf16[512,576]{1,0:T(8,128)(2,1)}) custom-call(s32[2]{0:T(128)} %pad_add_fusion.ids, s32[2]{0:T(128)} %broadcast.58.first_ref, s32[8,512]{1,0:T(8,128)} %broadcast_in_dim.60.row_ref, s32[512,1]{1,0:T(8,128)} %copy.36.rest_0_, bf16[512,576]{1,0:T(8,128)(2,1)} %get-tuple-element.313.rest_1_, ...), custom_call_target="tpu_custom_call" | custom-call | flops 251658240 | bytes 2197512 | tf_op jit(solution)/shard_map/attend_back/pallas_call | solution.py:155
  353.0 5.3 %project_grads.3 = (bf16[4,96,576]{2,1,0:T(8,128)(2,1)}, bf16[4,96,576]{2,1,0:T(8,128)(2,1)}) custom-call(s32[2]{0:T(128)} %pad_add_fusion.ids, bf16[512,576]{1,0:T(8,128)(2,1)} %get-tuple-element.384.dx_ref, bf16[64,768]{1,0:T(8,128)(2,1)} %get-tuple-element.242.rest_1_.rest_0_, bf16[64,768]{1,0:T(8,128)(2,1)} %copy-done.40, bf16[64,768]{1,0:T(8,128)(2,1)} %copy-done.37, ...), custom_call_target="tpu_custom_call" | custom-call | flops 452984832 | bytes 2260992 | tf_op jit(solution)/shard_map/project_grads/pallas_call | solution.py:155
  358.3 2.9 join.1
  364.2 3.5 all-to-all-start.4
  374.2 4.5 %collective-permute-done.49.rest_1_ = bf16[1,96,576]{2,1,0:T(8,128)(2,1)S(1)} collective-permute-done((bf16[1,96,576]{2,1,0:T(8,128)(2,1)}, bf16[1,96,576]{2,1,0:T(8,128)(2,1)S(1)}, u32[]{:S(2)}, u32[]{:S(2)}) %collective-permute-start.49) | collective-permute-done | bytes 110624 | tf_op jit(solution)/shard_map/ppermute | solution.py:1143
  379.6 2.9 unpack.2
  382.5 3.2 collective-permute-done.51.rest_3_
  390.8 7.4 %collective-permute-done.48.rest_3_ = bf16[96,1664]{1,0:T(8,128)(2,1)S(1)} collective-permute-done((bf16[96,1664]{1,0:T(8,128)(2,1)S(1)}, bf16[96,1664]{1,0:T(8,128)(2,1)S(1)}, u32[]{:S(2)}, u32[]{:S(2)}) %collective-permute-start.48) | collective-permute-done | bytes 319520 | tf_op jit(solution)/shard_map/ppermute | solution.py:1194
  406.0 2.9 collective-permute-start.59
  410.6 3.4 collective-permute-start.61
  414.0 6.0 %routed_post.1 = f32[512,768]{1,0:T(8,128)} custom-call(s32[2]{0:T(128)} %pad_add_fusion.ids, bf16[8,32,1152]{2,1,0:T(8,128)(2,1)} %copy-done.1, bf16[768,2304]{1,0:T(8,128)(2,1)} %rest_0_.7, f32[8,768]{1,0:T(8,128)} %get-tuple-element.268.rest_10_.vecs.rest_3_.rest_1_, bf16[128,768]{1,0:T(8,128)(2,1)} %get-tuple-element.267.rest_9_.picked.rest_5_.rest_2_, ...), custom_call_target="tpu_custom_call" | custom-call | flops 452984832 | bytes 8019968 | tf_op jit(solution)/shard_map/routed_post/pallas_call | solution.py:155
  428.1 2.9 unpack.3
  (308 shorter events, 112.4 us)
Async XLA Ops:
  7.2 37.8 %all-gather.13.cloned.1.call-start = ((), (), s32[]{:S(2)}) async-start(), calls=%async_computation.13 | async-start | bytes 1474560 | tf_op jit(solution)/shard_map/all_gather | solution.py:1238
  9.0 93.9 %all-gather.15.cloned.1.call-start = ((), (), s32[]{:S(2)}) async-start(), calls=%async_computation.14 | async-start | bytes 5898240 | tf_op jit(solution)/shard_map/all_gather | solution.py:1190
  45.0 94.5 %all-gather.17.cloned.1.call-start = ((), (), s32[]{:S(2)}) async-start(), calls=%async_computation.15 | async-start | bytes 1474560 | tf_op jit(solution)/shard_map/all_gather | solution.py:1319
  48.9 18.6 %collective-permute-start.14 = (bf16[128,768]{1,0:T(8,128)(2,1)}, bf16[128,768]{1,0:T(8,128)(2,1)S(1)}, u32[]{:S(2)}, u32[]{:S(2)}) collective-permute-start(bf16[128,768]{1,0:T(8,128)(2,1)} %get-tuple-element.368.rest_0_.low), channel_id=1, source_target_pairs={{0,1},{1,0},{2,3},{3,2},{4,5},{5,4},{6,7},{7,6},{8,9},{9,8},{10,11... | collective-permute-start | bytes 589832 | tf_op jit(solution)/shard_map/ppermute | solution.py:1143
  50.5 17.3 %collective-permute-start.15 = (bf16[128,768]{1,0:T(8,128)(2,1)}, bf16[128,768]{1,0:T(8,128)(2,1)S(1)}, u32[]{:S(2)}, u32[]{:S(2)}) collective-permute-start(bf16[128,768]{1,0:T(8,128)(2,1)} %get-tuple-element.368.rest_0_.low), channel_id=1, source_target_pairs={{0,2},{1,3},{2,0},{3,1},{4,6},{5,7},{6,4},{7,5},{8,10},{9,11},{10,... | collective-permute-start | bytes 589832 | tf_op jit(solution)/shard_map/ppermute | solution.py:1143
  53.1 14.7 %collective-permute-start.16 = (bf16[128,768]{1,0:T(8,128)(2,1)}, bf16[128,768]{1,0:T(8,128)(2,1)S(1)}, u32[]{:S(2)}, u32[]{:S(2)}) collective-permute-start(bf16[128,768]{1,0:T(8,128)(2,1)} %get-tuple-element.368.rest_0_.low), channel_id=1, source_target_pairs={{0,3},{1,2},{2,1},{3,0},{4,7},{5,6},{6,5},{7,4},{8,11},{9,10},{10,... | collective-permute-start | bytes 589832 | tf_op jit(solution)/shard_map/ppermute | solution.py:1143
  76.6 17.3 %collective-permute-start.18 = (bf16[128,768]{1,0:T(8,128)(2,1)}, bf16[128,768]{1,0:T(8,128)(2,1)S(1)}, u32[]{:S(2)}, u32[]{:S(2)}) collective-permute-start(bf16[128,768]{1,0:T(8,128)(2,1)} %get-tuple-element.286), channel_id=1, source_target_pairs={{0,2},{1,3},{2,0},{3,1},{4,6},{5,7},{6,4},{7,5},{8,10},{9,11},{10,... | collective-permute-start | bytes 589832 | tf_op jit(solution)/shard_map/ppermute | solution.py:1143
  77.5 16.4 %collective-permute-start.19 = (bf16[128,768]{1,0:T(8,128)(2,1)}, bf16[128,768]{1,0:T(8,128)(2,1)S(1)}, u32[]{:S(2)}, u32[]{:S(2)}) collective-permute-start(bf16[128,768]{1,0:T(8,128)(2,1)} %get-tuple-element.287), channel_id=1, source_target_pairs={{0,3},{1,2},{2,1},{3,0},{4,7},{5,6},{6,5},{7,4},{8,11},{9,10},{10,... | collective-permute-start | bytes 589832 | tf_op jit(solution)/shard_map/ppermute | solution.py:1143
  102.9 57.7 %collective-permute-start.27 = (bf16[4,4,2,96,768]{4,3,2,1,0:T(8,128)(2,1)}, bf16[4,4,2,96,768]{4,3,2,1,0:T(8,128)(2,1)}, u32[]{:S(2)}, u32[]{:S(2)}) collective-permute-start(bf16[4,4,2,96,768]{4,3,2,1,0:T(8,128)(2,1)} %bitcast.46), channel_id=1, source_target_pairs={{0,4},{4,0},{8,12},{12,8},{16,20},{20,16},{24,28},{28,24},{1,5},{5... | collective-permute-start | bytes 14155784 | tf_op jit(solution)/shard_map/ppermute | solution.py:1200
  102.9 100.3 %all-gather.9.cloned.1.call-start = ((), (), s32[]{:S(2)}) async-start(), calls=%async_computation.8 | async-start | bytes 3932160 | tf_op jit(solution)/shard_map/all_gather | solution.py:1332
  103.5 11.3 %collective-permute-start.23 = (bf16[256,768]{1,0:T(8,128)(2,1)}, bf16[256,768]{1,0:T(8,128)(2,1)S(1)}, u32[]{:S(2)}, u32[]{:S(2)}) collective-permute-start(bf16[256,768]{1,0:T(8,128)(2,1)} %get-tuple-element.295.rest_0_), channel_id=1, source_target_pairs={{0,16},{4,20},{8,24},{12,28},{16,0},{20,4},{24,8},{28,12},{1,17},{... | collective-permute-start | bytes 1179656 | tf_op jit(solution)/shard_map/ppermute | solution.py:1194
  111.2 11.9 %collective-permute-start.22 = (bf16[256,768]{1,0:T(8,128)(2,1)S(1)}, bf16[256,768]{1,0:T(8,128)(2,1)S(1)}, u32[]{:S(2)}, u32[]{:S(2)}) collective-permute-start(bf16[256,768]{1,0:T(8,128)(2,1)S(1)} %collective-permute-done.20.rest_1_), channel_id=1, source_target_pairs={{0,8},{4,12},{8,0},{12,4},{16,24},{20,28},{24,16},{28,20},{1,9},{5... | collective-permute-start | bytes 1179656 | tf_op jit(solution)/shard_map/ppermute | solution.py:1194
  112.7 18.9 %collective-permute-start.21 = (bf16[256,768]{1,0:T(8,128)(2,1)}, bf16[256,768]{1,0:T(8,128)(2,1)S(1)}, u32[]{:S(2)}, u32[]{:S(2)}) collective-permute-start(bf16[256,768]{1,0:T(8,128)(2,1)} %get-tuple-element.295.rest_0_), channel_id=1, source_target_pairs={{0,8},{4,12},{8,0},{12,4},{16,24},{20,28},{24,16},{28,20},{1,9},{5... | collective-permute-start | bytes 1179656 | tf_op jit(solution)/shard_map/ppermute | solution.py:1194
  113.3 18.3 %collective-permute-start.24 = (bf16[256,768]{1,0:T(8,128)(2,1)S(1)}, bf16[256,768]{1,0:T(8,128)(2,1)S(1)}, u32[]{:S(2)}, u32[]{:S(2)}) collective-permute-start(bf16[256,768]{1,0:T(8,128)(2,1)S(1)} %collective-permute-done.20.rest_1_), channel_id=1, source_target_pairs={{0,16},{4,20},{8,24},{12,28},{16,0},{20,4},{24,8},{28,12},{1,17},{... | collective-permute-start | bytes 1179656 | tf_op jit(solution)/shard_map/ppermute | solution.py:1194
  114.9 24.6 %collective-permute-start.25 = (bf16[256,768]{1,0:T(8,128)(2,1)S(1)}, bf16[256,768]{1,0:T(8,128)(2,1)S(1)}, u32[]{:S(2)}, u32[]{:S(2)}) collective-permute-start(bf16[256,768]{1,0:T(8,128)(2,1)S(1)} %collective-permute-done.23.rest_4_), channel_id=1, source_target_pairs={{0,8},{4,12},{8,0},{12,4},{16,24},{20,28},{24,16},{28,20},{1,9},{5... | collective-permute-start | bytes 1179656 | tf_op jit(solution)/shard_map/ppermute | solution.py:1194
  123.2 16.3 %collective-permute-start.26 = (bf16[256,768]{1,0:T(8,128)(2,1)S(1)}, bf16[256,768]{1,0:T(8,128)(2,1)S(1)}, u32[]{:S(2)}, u32[]{:S(2)}) collective-permute-start(bf16[256,768]{1,0:T(8,128)(2,1)S(1)} %collective-permute-done.22.rest_3_), channel_id=1, source_target_pairs={{0,16},{4,20},{8,24},{12,28},{16,0},{20,4},{24,8},{28,12},{1,17},{... | collective-permute-start | bytes 1179656 | tf_op jit(solution)/shard_map/ppermute | solution.py:1194
  139.5 132.8 %all-gather.11.cloned.1.call-start = ((), (), s32[]{:S(2)}) async-start(), calls=%async_computation.9 | async-start | bytes 3932160 | tf_op jit(solution)/shard_map/all_gather | solution.py:1346
  177.9 27.8 %collective-permute-start.28 = (bf16[1,4,2,96,768]{4,3,2,1,0:T(8,128)(2,1)S(1)}, bf16[1,4,2,96,768]{4,3,2,1,0:T(8,128)(2,1)S(1)}, u32[]{:S(2)}, u32[]{:S(2)}) collective-permute-start(bf16[1,4,2,96,768]{4,3,2,1,0:T(8,128)(2,1)S(1)} %bitcast.34), channel_id=1, source_target_pairs={{0,24},{4,28},{8,16},{12,20},{16,8},{20,12},{24,0},{28,4},{1,25},{... | collective-permute-start | bytes 3538952 | tf_op jit(solution)/shard_map/ppermute | solution.py:1194
  205.7 16.3 %all-to-all-start.1 = ((bf16[8,128,384]{2,1,0:T(8,128)(2,1)}), bf16[8,128,384]{2,1,0:T(8,128)(2,1)S(1)}, u32[]{:S(2)}, u32[]{:S(2)}) async-start(bf16[8,128,384]{2,1,0:T(8,128)(2,1)} %get-tuple-element.319), calls=%async_computation.1 | async-start | bytes 1572864 | tf_op jit(solution)/shard_map/all_to_all | solution.py:1349
  222.0 29.0 %collective-permute-start.29 = (bf16[1,4,2,96,768]{4,3,2,1,0:T(8,128)(2,1)S(1)}, bf16[1,4,2,96,768]{4,3,2,1,0:T(8,128)(2,1)S(1)}, u32[]{:S(2)}, u32[]{:S(2)}) collective-permute-start(bf16[1,4,2,96,768]{4,3,2,1,0:T(8,128)(2,1)S(1)} %bitcast.35), channel_id=1, source_target_pairs={{0,4},{4,0},{8,12},{12,8},{16,20},{20,16},{24,28},{28,24},{1,5},{5... | collective-permute-start | bytes 3538952 | tf_op jit(solution)/shard_map/ppermute | solution.py:1200
  222.0 29.0 %collective-permute-start.31 = (bf16[1,4,2,96,768]{4,3,2,1,0:T(8,128)(2,1)S(1)}, bf16[1,4,2,96,768]{4,3,2,1,0:T(8,128)(2,1)}, u32[]{:S(2)}, u32[]{:S(2)}) collective-permute-start(bf16[1,4,2,96,768]{4,3,2,1,0:T(8,128)(2,1)S(1)} %bitcast.36), channel_id=1, source_target_pairs={{0,8},{4,12},{8,0},{12,4},{16,24},{20,28},{24,16},{28,20},{1,9},{5... | collective-permute-start | bytes 3538952 | tf_op jit(solution)/shard_map/ppermute | solution.py:1194
  222.7 29.6 %collective-permute-start.32 = (bf16[1,4,2,96,768]{4,3,2,1,0:T(8,128)(2,1)S(1)}, bf16[1,4,2,96,768]{4,3,2,1,0:T(8,128)(2,1)}, u32[]{:S(2)}, u32[]{:S(2)}) collective-permute-start(bf16[1,4,2,96,768]{4,3,2,1,0:T(8,128)(2,1)S(1)} %bitcast.37), channel_id=1, source_target_pairs={{0,16},{4,20},{8,24},{12,28},{16,0},{20,4},{24,8},{28,12},{1,17},{... | collective-permute-start | bytes 3538952 | tf_op jit(solution)/shard_map/ppermute | solution.py:1194
  223.1 27.9 %collective-permute-start.30 = (bf16[4,96,768]{2,1,0:T(8,128)(2,1)}, bf16[4,96,768]{2,1,0:T(8,128)(2,1)S(1)}, u32[]{:S(2)}, u32[]{:S(2)}) collective-permute-start(bf16[4,96,768]{2,1,0:T(8,128)(2,1)} %get-tuple-element.331), channel_id=1, source_target_pairs={{0,4},{4,0},{8,12},{12,8},{16,20},{20,16},{24,28},{28,24},{1,5},{5... | collective-permute-start | bytes 1769480 | tf_op jit(solution)/shard_map/ppermute | solution.py:1200
  252.2 37.7 %all-to-all-start.2 = ((bf16[8,128,1152]{2,1,0:T(8,128)(2,1)}), bf16[8,128,1152]{2,1,0:T(8,128)(2,1)S(1)}, u32[]{:S(2)}, u32[]{:S(2)}) async-start(bf16[8,128,1152]{2,1,0:T(8,128)(2,1)} %get-tuple-element.334), calls=%async_computation.2 | async-start | bytes 4718592 | tf_op jit(solution)/shard_map/all_to_all | solution.py:1364
  260.4 68.3 %reduce-scatter.4.cloned.1.call-start = ((), (), s32[]{:S(2)}) async-start(), calls=%async_computation.10 | async-start | bytes 614400 | tf_op jit(solution)/shard_map/reduce_scatter | solution.py:1368
  267.7 20.1 %collective-permute-start.36 = (bf16[1,4,2,96,768]{4,3,2,1,0:T(8,128)(2,1)S(1)}, bf16[1,4,2,96,768]{4,3,2,1,0:T(8,128)(2,1)}, u32[]{:S(2)}, u32[]{:S(2)}) collective-permute-start(bf16[1,4,2,96,768]{4,3,2,1,0:T(8,128)(2,1)S(1)} %copy-done.4), channel_id=1, source_target_pairs={{0,4},{4,0},{8,12},{12,8},{16,20},{20,16},{24,28},{28,24},{1,5},{5... | collective-permute-start | bytes 3538952 | tf_op jit(solution)/shard_map/ppermute | solution.py:1200
  267.8 20.0 %collective-permute-start.34 = (bf16[1,4,2,96,768]{4,3,2,1,0:T(8,128)(2,1)}, bf16[1,4,2,96,768]{4,3,2,1,0:T(8,128)(2,1)}, u32[]{:S(2)}, u32[]{:S(2)}) collective-permute-start(bf16[1,4,2,96,768]{4,3,2,1,0:T(8,128)(2,1)} %collective-permute-done.31.rest_2_), channel_id=1, source_target_pairs={{0,4},{4,0},{8,12},{12,8},{16,20},{20,16},{24,28},{28,24},{1,5},{5... | collective-permute-start | bytes 3538952 | tf_op jit(solution)/shard_map/ppermute | solution.py:1200
  268.2 19.6 %collective-permute-start.35 = (bf16[1,4,2,96,768]{4,3,2,1,0:T(8,128)(2,1)}, bf16[1,4,2,96,768]{4,3,2,1,0:T(8,128)(2,1)}, u32[]{:S(2)}, u32[]{:S(2)}) collective-permute-start(bf16[1,4,2,96,768]{4,3,2,1,0:T(8,128)(2,1)} %collective-permute-done.32.rest_4_), channel_id=1, source_target_pairs={{0,4},{4,0},{8,12},{12,8},{16,20},{20,16},{24,28},{28,24},{1,5},{5... | collective-permute-start | bytes 3538952 | tf_op jit(solution)/shard_map/ppermute | solution.py:1200
  272.4 161.2 %reduce-scatter.6.cloned.1.call-start = ((), (), s32[]{:S(2)}) async-start(), calls=%async_computation.11 | async-start | bytes 2654208 | tf_op jit(solution)/shard_map/reduce_scatter | solution.py:1371
  299.8 16.4 %collective-permute-start.37 = (bf16[128,768]{1,0:T(8,128)(2,1)}, bf16[128,768]{1,0:T(8,128)(2,1)S(1)}, u32[]{:S(2)}, u32[]{:S(2)}) collective-permute-start(bf16[128,768]{1,0:T(8,128)(2,1)} %get-tuple-element.372.g_low), channel_id=1, source_target_pairs={{0,1},{1,0},{2,3},{3,2},{4,5},{5,4},{6,7},{7,6},{8,9},{9,8},{10,11... | collective-permute-start | bytes 589832 | tf_op jit(solution)/shard_map/ppermute | solution.py:1143
  303.5 16.5 %collective-permute-start.38 = (bf16[128,768]{1,0:T(8,128)(2,1)}, bf16[128,768]{1,0:T(8,128)(2,1)S(1)}, u32[]{:S(2)}, u32[]{:S(2)}) collective-permute-start(bf16[128,768]{1,0:T(8,128)(2,1)} %get-tuple-element.372.g_low), channel_id=1, source_target_pairs={{0,2},{1,3},{2,0},{3,1},{4,6},{5,7},{6,4},{7,5},{8,10},{9,11},{10,... | collective-permute-start | bytes 589832 | tf_op jit(solution)/shard_map/ppermute | solution.py:1143
  305.9 14.1 %collective-permute-start.39 = (bf16[128,768]{1,0:T(8,128)(2,1)}, bf16[128,768]{1,0:T(8,128)(2,1)S(1)}, u32[]{:S(2)}, u32[]{:S(2)}) collective-permute-start(bf16[128,768]{1,0:T(8,128)(2,1)} %get-tuple-element.372.g_low), channel_id=1, source_target_pairs={{0,3},{1,2},{2,1},{3,0},{4,7},{5,6},{6,5},{7,4},{8,11},{9,10},{10,... | collective-permute-start | bytes 589832 | tf_op jit(solution)/shard_map/ppermute | solution.py:1143
  323.4 29.5 %collective-permute-start.40 = (bf16[4,96,896]{2,1,0:T(8,128)(2,1)}, bf16[4,96,896]{2,1,0:T(8,128)(2,1)S(1)}, u32[]{:S(2)}, u32[]{:S(2)}) collective-permute-start(bf16[4,96,896]{2,1,0:T(8,128)(2,1)} %get-tuple-element.367), channel_id=1, source_target_pairs={{0,4},{4,0},{8,12},{12,8},{16,20},{20,16},{24,28},{28,24},{1,5},{5... | collective-permute-start | bytes 2064392 | tf_op jit(solution)/shard_map/ppermute | solution.py:1200
  323.4 22.2 %all-to-all-start.3 = ((bf16[8,32,384]{2,1,0:T(8,128)(2,1)}), bf16[8,32,384]{2,1,0:T(8,128)(2,1)S(1)}, u32[]{:S(2)}, u32[]{:S(2)}) async-start(bf16[8,32,384]{2,1,0:T(8,128)(2,1)} %get-tuple-element.359), calls=%async_computation.3 | async-start | bytes 393216 | tf_op jit(solution)/shard_map/all_to_all | solution.py:1402
  326.8 106.8 %reduce-scatter.8.cloned.1.call-start = ((), (), s32[]{:S(2)}) async-start(), calls=%async_computation.12 | async-start | bytes 2654208 | tf_op jit(solution)/shard_map/reduce_scatter | solution.py:1409
  328.7 24.1 %collective-permute-start.41 = (bf16[96,576]{1,0:T(8,128)(2,1)}, bf16[96,576]{1,0:T(8,128)(2,1)S(1)}, u32[]{:S(2)}, u32[]{:S(2)}) collective-permute-start(bf16[96,576]{1,0:T(8,128)(2,1)} %bitcast.50), channel_id=1, source_target_pairs={{0,0},{1,9},{2,18},{3,27},{4,4},{5,13},{6,22},{7,31},{8,8},{9,1},{... | collective-permute-start | bytes 331784 | tf_op jit(solution)/shard_map/ppermute | solution.py:1117
  330.3 22.6 %collective-permute-start.42 = (bf16[96,576]{1,0:T(8,128)(2,1)}, bf16[96,576]{1,0:T(8,128)(2,1)S(1)}, u32[]{:S(2)}, u32[]{:S(2)}) collective-permute-start(bf16[96,576]{1,0:T(8,128)(2,1)} %bitcast.51), channel_id=1, source_target_pairs={{0,1},{1,8},{2,19},{3,26},{4,5},{5,12},{6,23},{7,30},{8,9},{9,0},{... | collective-permute-start | bytes 331784 | tf_op jit(solution)/shard_map/ppermute | solution.py:1117
  335.7 17.2 %collective-permute-start.43 = (bf16[96,576]{1,0:T(8,128)(2,1)}, bf16[96,576]{1,0:T(8,128)(2,1)S(1)}, u32[]{:S(2)}, u32[]{:S(2)}) collective-permute-start(bf16[96,576]{1,0:T(8,128)(2,1)} %bitcast.52), channel_id=1, source_target_pairs={{0,2},{1,11},{2,16},{3,25},{4,6},{5,15},{6,20},{7,29},{8,10},{9,3}... | collective-permute-start | bytes 331784 | tf_op jit(solution)/shard_map/ppermute | solution.py:1117
  336.6 16.3 %collective-permute-start.44 = (bf16[96,576]{1,0:T(8,128)(2,1)}, bf16[96,576]{1,0:T(8,128)(2,1)S(1)}, u32[]{:S(2)}, u32[]{:S(2)}) collective-permute-start(bf16[96,576]{1,0:T(8,128)(2,1)} %bitcast.53), channel_id=1, source_target_pairs={{0,3},{1,10},{2,17},{3,24},{4,7},{5,14},{6,21},{7,28},{8,11},{9,2}... | collective-permute-start | bytes 331784 | tf_op jit(solution)/shard_map/ppermute | solution.py:1117
  364.2 45.7 %all-to-all-start.4 = ((bf16[8,32,1152]{2,1,0:T(8,128)(2,1)}), bf16[8,32,1152]{2,1,0:T(8,128)(2,1)S(1)}, u32[]{:S(2)}, u32[]{:S(2)}) async-start(bf16[8,32,1152]{2,1,0:T(8,128)(2,1)} %get-tuple-element.402), calls=%async_computation.5 | async-start | bytes 1179648 | tf_op jit(solution)/shard_map/all_to_all | solution.py:1418
  367.7 23.1 %collective-permute-start.46 = (bf16[96,1664]{1,0:T(8,128)(2,1)S(1)}, bf16[96,1664]{1,0:T(8,128)(2,1)S(1)}, u32[]{:S(2)}, u32[]{:S(2)}) collective-permute-start(bf16[96,1664]{1,0:T(8,128)(2,1)S(1)} %copy-done.68), channel_id=1, source_target_pairs={{0,8},{4,12},{8,0},{12,4},{16,24},{20,28},{24,16},{28,20},{1,9},{5... | collective-permute-start | bytes 958472 | tf_op jit(solution)/shard_map/ppermute | solution.py:1194
  369.6 21.2 %collective-permute-start.47 = (bf16[96,1664]{1,0:T(8,128)(2,1)S(1)}, bf16[96,1664]{1,0:T(8,128)(2,1)S(1)}, u32[]{:S(2)}, u32[]{:S(2)}) collective-permute-start(bf16[96,1664]{1,0:T(8,128)(2,1)S(1)} %copy-done.67), channel_id=1, source_target_pairs={{0,16},{4,20},{8,24},{12,28},{16,0},{20,4},{24,8},{28,12},{1,17},{... | collective-permute-start | bytes 958472 | tf_op jit(solution)/shard_map/ppermute | solution.py:1194
  371.1 27.1 %collective-permute-start.48 = (bf16[96,1664]{1,0:T(8,128)(2,1)S(1)}, bf16[96,1664]{1,0:T(8,128)(2,1)S(1)}, u32[]{:S(2)}, u32[]{:S(2)}) collective-permute-start(bf16[96,1664]{1,0:T(8,128)(2,1)S(1)} %copy-done.66), channel_id=1, source_target_pairs={{0,24},{4,28},{8,16},{12,20},{16,8},{20,12},{24,0},{28,4},{1,25},{... | collective-permute-start | bytes 958472 | tf_op jit(solution)/shard_map/ppermute | solution.py:1194
  404.5 19.0 %collective-permute-start.58 = (bf16[96,576]{1,0:T(8,128)(2,1)}, bf16[96,576]{1,0:T(8,128)(2,1)S(1)}, u32[]{:S(2)}, u32[]{:S(2)}) collective-permute-start(bf16[96,576]{1,0:T(8,128)(2,1)} %bitcast.40), channel_id=1, source_target_pairs={{0,0},{1,9},{2,18},{3,27},{4,4},{5,13},{6,22},{7,31},{8,8},{9,1},{... | collective-permute-start | bytes 331784 | tf_op jit(solution)/shard_map/ppermute | solution.py:1117
  406.0 18.5 %collective-permute-start.59 = (bf16[96,576]{1,0:T(8,128)(2,1)}, bf16[96,576]{1,0:T(8,128)(2,1)S(1)}, u32[]{:S(2)}, u32[]{:S(2)}) collective-permute-start(bf16[96,576]{1,0:T(8,128)(2,1)} %bitcast.41), channel_id=1, source_target_pairs={{0,1},{1,8},{2,19},{3,26},{4,5},{5,12},{6,23},{7,30},{8,9},{9,0},{... | collective-permute-start | bytes 331784 | tf_op jit(solution)/shard_map/ppermute | solution.py:1117
  409.0 11.1 %collective-permute-start.54 = (bf16[24,1664]{1,0:T(8,128)(2,1)}, bf16[24,1664]{1,0:T(8,128)(2,1)S(1)}, u32[]{:S(2)}, u32[]{:S(2)}) collective-permute-start(bf16[24,1664]{1,0:T(8,128)(2,1)} %get-tuple-element.425), channel_id=1, source_target_pairs={{0,3},{1,2},{2,1},{3,0},{4,7},{5,6},{6,5},{7,4},{8,11},{9,10},{10,... | collective-permute-start | bytes 239624 | tf_op jit(solution)/shard_map/ppermute | solution.py:1143
  409.8 16.9 %collective-permute-start.60 = (bf16[96,576]{1,0:T(8,128)(2,1)}, bf16[96,576]{1,0:T(8,128)(2,1)S(1)}, u32[]{:S(2)}, u32[]{:S(2)}) collective-permute-start(bf16[96,576]{1,0:T(8,128)(2,1)} %bitcast.42), channel_id=1, source_target_pairs={{0,2},{1,11},{2,16},{3,25},{4,6},{5,15},{6,20},{7,29},{8,10},{9,3}... | collective-permute-start | bytes 331784 | tf_op jit(solution)/shard_map/ppermute | solution.py:1117
  410.6 16.2 %collective-permute-start.61 = (bf16[96,576]{1,0:T(8,128)(2,1)}, bf16[96,576]{1,0:T(8,128)(2,1)S(1)}, u32[]{:S(2)}, u32[]{:S(2)}) collective-permute-start(bf16[96,576]{1,0:T(8,128)(2,1)} %bitcast.43), channel_id=1, source_target_pairs={{0,3},{1,10},{2,17},{3,24},{4,7},{5,14},{6,21},{7,28},{8,11},{9,2}... | collective-permute-start | bytes 331784 | tf_op jit(solution)/shard_map/ppermute | solution.py:1117
  (95 other events, 564.2 us)
Sparse Core Ops, SparseCore 0:
  10.2 33.1 all-gather.12
  45.2 57.6 all-gather.14
  105.0 30.4 all-gather.16
  139.6 63.5 all-gather.8
  205.9 65.5 all-gather.10
  273.6 23.6 reduce-scatter.3
  301.0 45.5 reduce-scatter.5
  353.1 49.1 reduce-scatter.7
